TPU v7x, 128 devices: a whole 4x4x4 slice. The times are simulated.
128 devices in a mesh: gx: 16 (over y, z), gy: 8 (over x, core).
Axes of the slice: x: 4, y: 4, z: 4, core: 2. Of those that a mesh axis runs over, the one named last changes fastest.
Arguments:
- block_list: int32 [256], P(('gx', 'gy')), may hold values from -1 to 255, as said below
- wet_levels: int32 [256, 1800], P(('gx', 'gy')), may hold values from 0 to 62, as said below
- mixing: float32 [256, 1800], P(('gx', 'gy')), may hold values from 0.5 to 2
- velocity: float32 [256, 2, 62, 1800], P(('gx', 'gy')), may hold values from -3 to 3
- tracers: float32 [256, 2, 62, 1800], P(('gx', 'gy')), may hold values from -6 to 6
- damping: float32 [320, 1440], P('gy', 'gx'), may hold values from 0.05 to 0.5
Outputs:
- new_tracers: float32 [256, 2, 62, 1800], P(('gx', 'gy'))
- surface_height: float32 [320, 1440], P('gy', 'gx')
Inputs may be any that keep to these rules, and one draw needn't show every extreme that they name: `block_list`: slots form runs of 2 (run j holds slots j * 2 to j * 2 + 1). With q = j // 8 and r = j % 8, run j names distinct blocks r * 32 + q * 2 + s with 0 <= s < 2, in any order, and -1 in its remaining slots. Every run names one block or more, and the last run names all 2. Blocks that no run names are land. `wet_levels`: 0 in every slot whose block_list entry is -1; some column has 62 wet levels.
All inputs are finite; a program needn't handle non-finite values.
Results may differ from a plain program's by a relative error of at most 0.0003.
Values sent between devices are 32-bit elements; how exact they have to be, the bound alone decides.
No kernel may reach another device: no remote copies, remote signals or barrier semaphores. Data moves between devices by JAX's collectives and lax.ppermute only.
A program may use at most 128 MiB of HBM per device.

v0:
```python
import math

import jax
import jax.numpy as jnp
from jax import lax
from jax.sharding import PartitionSpec as P

BX = 45
BY = 40
PASSES = 2
ITERS = 3


advect_rate = 0.25
mixing_rate = 0.015
salt_weight = 0.8
directions = ((0, 1), (0, -1), (1, 0), (-1, 0))


def with_halo(cells, sides, width):
    for axis, dim in sides:
        count = lax.axis_size(axis)
        head = lax.slice_in_dim(cells, 0, width, axis=dim)
        tail = lax.slice_in_dim(cells, cells.shape[dim] - width, cells.shape[dim], axis=dim)
        cells = jnp.concatenate(
            [
                lax.ppermute(tail, axis, [(i, (i + 1) % count) for i in range(count)]),
                cells,
                lax.ppermute(head, axis, [((i + 1) % count, i) for i in range(count)]),
            ],
            axis=dim,
        )
    return cells


def window(values, shrink, step_y, step_x):
    height = values.shape[-2]
    breadth = values.shape[-1]
    return values[
        ..., shrink + step_y : height - shrink + step_y, shrink + step_x : breadth - shrink + step_x
    ]


def laplace(values, wetness, shrink):
    centre = window(values, shrink, 0, 0)
    wet_centre = window(wetness, shrink, 0, 0)
    pieces = [
        wet_centre
        * window(wetness, shrink, step_y, step_x)
        * (window(values, shrink, step_y, step_x) - centre)
        for step_y, step_x in directions
    ]
    return pieces[0] + pieces[1] + pieces[2] + pieces[3]


def advect(values, wetness, eastward, northward):
    centre = window(values, 2, 0, 0)
    wet_centre = window(wetness, 2, 0, 0)

    def face_flux(speeds, step_y, step_x):
        face_speed = 0.5 * (window(speeds, 2, 0, 0) + window(speeds, 2, step_y, step_x))
        face_wet = wet_centre * window(wetness, 2, step_y, step_x)
        return face_wet * face_speed * (0.5 * (centre + window(values, 2, step_y, step_x)))

    return -(
        face_flux(eastward, 0, 1)
        - face_flux(eastward, 0, -1)
        + face_flux(northward, 1, 0)
        - face_flux(northward, -1, 0)
    )


def tracer_pass(padded, wetness, eastward, northward, mixing):
    first_lap = laplace(padded, wetness, 1)
    scaled = window(mixing, 1, 0, 0) * first_lap
    biharmonic = -laplace(scaled, window(wetness, 1, 0, 0), 1)
    return (
        window(padded, 2, 0, 0)
        + advect_rate * advect(padded, wetness, eastward, northward)
        + mixing_rate * biharmonic
    )


def to_strip(slot_values, selector):
    placed = jnp.einsum("ps,s...->p...", selector, slot_values, precision=lax.Precision.HIGHEST)
    slot_count = placed.shape[0]
    middle = placed.shape[1:-1]
    leading = len(middle)
    placed = placed.reshape((slot_count,) + middle + (BY, BX))
    axes_order = tuple(range(1, leading + 1)) + (leading + 1, 0, leading + 2)
    return placed.transpose(axes_order).reshape(middle + (BY, slot_count * BX))


def from_strip(strip_values, selector):
    slot_count = selector.shape[0]
    middle = strip_values.shape[:-2]
    leading = len(middle)
    blocks = strip_values.reshape(middle + (BY, slot_count, BX))
    axes_order = (leading + 1,) + tuple(range(leading)) + (leading, leading + 2)
    blocks = blocks.transpose(axes_order).reshape((slot_count,) + middle + (BY * BX,))
    return jnp.einsum("ps,p...->s...", selector, blocks, precision=lax.Precision.HIGHEST)


def per_device(block_list, wet_levels, mixing, velocity, tracers, damping):
    slot_count = block_list.shape[0]
    level_numbers = tracers.shape[2]
    present = block_list >= 0
    position = jnp.where(present, block_list % slot_count, -1)
    selector = (position[None, :] == jnp.arange(slot_count, dtype=jnp.int32)[:, None]).astype(
        jnp.float32
    )
    margin = 2
    flow_strip = to_strip(velocity, selector)
    flow_strip = flow_strip.reshape((2 * level_numbers,) + flow_strip.shape[2:])
    depth_strip = to_strip(wet_levels.astype(jnp.float32), selector)
    mixing_strip = to_strip(mixing, selector)
    static = jnp.concatenate([flow_strip, depth_strip[None], mixing_strip[None]], axis=0)
    padded_static = with_halo(static, (("gx", 2), ("gy", 1)), margin)
    row_index = lax.broadcasted_iota(jnp.int32, padded_static.shape[1:], 0)
    row_total = padded_static.shape[1]
    row_owner = lax.axis_index("gy")
    outside = (row_owner == 0) & (row_index < margin) | (row_owner == lax.axis_size("gy") - 1) & (
        row_index >= row_total - margin
    )
    depth_pad = jnp.where(outside, 0.0, padded_static[-2])
    mixing_pad = padded_static[-1]
    east_pad = padded_static[:level_numbers]
    north_pad = padded_static[level_numbers : 2 * level_numbers]
    current = to_strip(tracers, selector)
    for pass_index in range(PASSES):
        padded = with_halo(current, (("gx", 3), ("gy", 2)), margin)
        eastward = window(east_pad, 0, 0, 0)
        northward = window(north_pad, 0, 0, 0)
        depth_now = window(depth_pad, 0, 0, 0)
        mixing_now = window(mixing_pad, 0, 0, 0)
        advance_level_ids = lax.broadcasted_iota(jnp.int32, (level_numbers, 1, 1), 0)
        wetness = (advance_level_ids.astype(jnp.float32) < depth_now[None]).astype(jnp.float32)
        current = tracer_pass(padded, wetness, eastward, northward, mixing_now)
    inner_depth = window(depth_pad, margin, 0, 0)
    level_ids = lax.broadcasted_iota(jnp.int32, (level_numbers, 1, 1), 0)
    wet_inner = (level_ids.astype(jnp.float32) < inner_depth[None]).astype(jnp.float32)
    forcing = jnp.sum(wet_inner * (current[0] - salt_weight * current[1]), axis=0) / math.sqrt(
        level_numbers
    )
    height_pad = window(depth_pad, margin - 1, 0, 0)
    centre_depth = window(height_pad, 1, 0, 0)
    couplings = [
        jnp.minimum(centre_depth, window(height_pad, 1, step_y, step_x)) / level_numbers
        for step_y, step_x in directions
    ]
    diagonal = damping + (couplings[0] + couplings[1] + couplings[2] + couplings[3])

    def operate(values):
        padded = with_halo(values, (("gx", 1), ("gy", 0)), 1)
        beside = [
            couplings[number] * window(padded, 1, step_y, step_x)
            for number, (step_y, step_x) in enumerate(directions)
        ]
        return diagonal * values - (beside[0] + beside[1] + beside[2] + beside[3])

    def squares(residual):
        return lax.psum(jnp.sum(residual * residual), ("gx", "gy"))

    solution = jnp.zeros_like(forcing)
    residual = forcing
    direction = forcing
    norm_now = squares(residual)
    for iteration in range(ITERS):
        applied = operate(direction)
        step_size = norm_now / lax.psum(jnp.sum(direction * applied), ("gx", "gy"))
        solution = solution + step_size * direction
        residual = residual - step_size * applied
        norm_next = squares(residual)
        direction = residual + norm_next / norm_now * direction
        norm_now = norm_next
    restored = from_strip(current, selector)
    new_tracers = jnp.where(present[:, None, None, None], restored, tracers)
    return (new_tracers, solution)


def solution(mesh):
    return jax.shard_map(
        per_device,
        mesh=mesh,
        in_specs=(
            P(("gx", "gy")),
            P(("gx", "gy"), None),
            P(("gx", "gy"), None),
            P(("gx", "gy"), None, None, None),
            P(("gx", "gy"), None, None, None),
            P("gy", "gx"),
        ),
        out_specs=(P(("gx", "gy"), None, None, None), P("gy", "gx")),
        check_vma=False,
    )
```

profile of v0, /device:TPU:0, one launch (start us, length us, event | category | flops | bytes accessed | tf_op | source)
XLA Modules:
  0.0 577.9 jit_solution(15729175480442028371)
XLA Ops:
  1.4 6.8 %fusion.82 = f32[2,2,62,1800]{3,0,2,1:T(2,128)S(1)} fusion(f32[2,2,62,1800]{3,1,2,0:T(2,128)} %param.10, s32[2]{0:T(128)S(1)} %fusion.120), kind=kOutput, calls=%fused_computation.140 | convolution fusion | flops 10713604 | bytes 3571208 | tf_op jit(solution)/shard_map/ps,s...->p.../dot_general | solution.py:85
  9.7 5.0 reshape.59
  14.8 5.8 %copy.155 = f32[2,62,40,2,45]{1,2,4,3,0:T(8,128)} copy(f32[2,62,40,2,45]{4,2,1,0,3:T(8,128)} %bitcast.57) | data formatting | bytes 3571200 | tf_op jit(solution)/shard_map/transpose | solution.py:91
  33.5 5.1 fusion.60
  40.0 5.1 reshape.61
  45.1 8.8 %copy.159 = f32[2,62,40,2,45]{1,0,2,4,3:T(2,128)} copy(f32[2,62,40,2,45]{4,2,1,0,3:T(8,128)} %bitcast.54) | data formatting | bytes 3571200 | tf_op jit(solution)/shard_map/transpose | solution.py:91
  53.8 5.0 reshape_reshape.3
  60.1 5.8 %collective-permute-start.2 = (f32[126,40,2]{0,1,2:T(8,128)S(1)}, f32[126,40,2]{0,1,2:T(8,128)S(1)}, u32[]{:S(2)}, u32[]{:S(2)}) collective-permute-start(f32[126,40,2]{0,1,2:T(8,128)S(1)} %get-tuple-element.38), channel_id=1, source_target_pairs={{8,0},{16,8},{24,16},{32,24},{40,32},{48,40},{56,48},{64,56},{72,6... | collective-permute-start | bytes 120968 | tf_op jit(solution)/shard_map/ppermute | solution.py:29
  106.7 12.1 %fusion.10 = f32[2,62,42,92]{1,2,3,0:T(8,128)S(1)} fusion(f32[2,62,42,94]{1,2,3,0:T(8,128)} %get-tuple-element.46, f32[2,62,42,94]{1,2,3,0:T(8,128)} %get-tuple-element.45, f32[2,62,44,94]{1,2,3,0:T(8,128)} %pad_maximum_fusion.1, f32[62,42,92]{0,1,2:T(8,128)} %get-tuple-element.58, f32[62,42,92]{0,1,2:T(8,128)} %get-tuple-element.59, ...), kind=kLoop, calls=%fused_computation.21 | loop fusion | flops 5749632 | bytes 15347808 | tf_op jit(solution)/shard_map/mul | solution.py:75
  118.9 7.9 %fusion.73 = (f32[62,40,90]{0,1,2:T(8,128)}, f32[62,40,90]{0,1,2:T(8,128)}, f32[62,40,90]{0,1,2:T(8,128)}, f32[62,40,90]{0,1,2:T(8,128)}) fusion(f32[126,2,94]{0,1,2:T(2,128)S(1)} %collective-permute-done.4, f32[126,40,2]{0,1,2:T(8,128)S(1)} %collective-permute-done.2, f32[126,40,2]{0,1,2:T(8,128)S(1)} %collective-permute-done.1, ...), kind=kLoop, calls=%fused_computation.118 | loop fusion | flops 4464000 | bytes 9226944 | tf_op jit(solution)/shard_map/mul | solution.py:63
  126.8 5.2 fusion.81
  132.0 15.2 %fusion.42 = f32[2,62,40,90]{1,2,3,0:T(8,128)} fusion(f32[2,62,42,92]{1,2,3,0:T(8,128)S(1)} %fusion.10, f32[2,62,40,90]{1,2,3,0:T(8,128)} %bitcast.51, f32[2,62,42,94]{1,2,3,0:T(8,128)} %get-tuple-element.46, f32[2,62,42,94]{1,2,3,0:T(8,128)} %get-tuple-element.45, f32[2,62,40,2]{1,2,3,0:T(8,128)S(1)} %collective-permute-done.5, ...), kind=kLoop, calls=%fused_computation.65 | loop fusion | flops 13392000 | bytes 23292160 | tf_op jit(solution)/shard_map/add | solution.py:78
  148.2 5.3 collective-permute-start.8
  169.5 7.8 %fusion.2 = f32[2,62,42,92]{1,2,3,0:T(8,128)S(1)} fusion(f32[2,62,42,94]{1,2,3,0:T(8,128)} %get-tuple-element.42, f32[2,62,42,94]{1,2,3,0:T(8,128)} %get-tuple-element.41, f32[2,62,44,94]{1,2,3,0:T(8,128)S(1)} %pad_maximum_fusion.3, f32[62,42,92]{0,1,2:T(8,128)} %get-tuple-element.58, f32[62,42,92]{0,1,2:T(8,128)} %get-tuple-element.59, ...), kind=kLoop, calls=%fused_computation.9 | loop fusion | flops 5749632 | bytes 15347808 | tf_op jit(solution)/shard_map/mul | solution.py:75
  177.3 14.8 %fusion.20 = f32[2,62,40,90]{1,2,3,0:T(8,128)} fusion(f32[2,62,42,92]{1,2,3,0:T(8,128)S(1)} %fusion.2, f32[2,62,40,90]{1,2,3,0:T(8,128)} %fusion.42, f32[2,62,42,94]{1,2,3,0:T(8,128)} %get-tuple-element.42, f32[2,62,42,94]{1,2,3,0:T(8,128)} %get-tuple-element.41, f32[2,62,40,2]{1,2,3,0:T(8,128)S(1)} %collective-permute-done.9, ...), kind=kLoop, calls=%fused_computation.35 | loop fusion | flops 13392000 | bytes 23292160 | tf_op jit(solution)/shard_map/add | solution.py:78
  195.1 5.3 collective-permute-start.12
  207.6 65.1 %all-reduce = (f32[]{:T(128)}, f32[]{:T(128)}) all-reduce(f32[]{:T(128)} %get-tuple-element.15, f32[]{:T(128)} %get-tuple-element.14), channel_id=1, replica_groups=mesh['gx'=16,'gy'=8] {'gx','gy'}, use_global_device_ids=true, to_apply=%region_2.3 | all-reduce | flops 2 | bytes 16 | tf_op jit(solution)/shard_map/psum | solution.py:162
  274.7 62.0 %psum.44 = f32[]{:T(128)} all-reduce(f32[]{:T(128)} %get-tuple-element.20), channel_id=1, replica_groups=mesh['gx'=16,'gy'=8] {'gx','gy'}, use_global_device_ids=true, to_apply=%region_6.7 | all-reduce | flops 1 | bytes 8 | tf_op jit(solution)/shard_map/psum | solution.py:162
  351.4 64.5 %psum.45 = f32[]{:T(128)} all-reduce(f32[]{:T(128)} %get-tuple-element.18), channel_id=1, replica_groups=mesh['gx'=16,'gy'=8] {'gx','gy'}, use_global_device_ids=true, to_apply=%region_8.9 | all-reduce | flops 1 | bytes 8 | tf_op jit(solution)/shard_map/psum | solution.py:170
  417.9 62.2 %psum.46 = f32[]{:T(128)} all-reduce(f32[]{:T(128)} %multiply_reduce_fusion), channel_id=1, replica_groups=mesh['gx'=16,'gy'=8] {'gx','gy'}, use_global_device_ids=true, to_apply=%region_10.11 | all-reduce | flops 1 | bytes 8 | tf_op jit(solution)/shard_map/psum | solution.py:162
  487.2 5.7 copy.184
  492.9 6.4 %reshape.69 = f32[2,2,62,1800]{3,0,2,1:T(2,128)} reshape(f32[2,2,62,40,45]{4,3,0,2,1:T(8,128)} %copy.184) | data formatting | bytes 3571200 | tf_op jit(solution)/shard_map/reshape | solution.py:100
  500.9 6.4 %convolution_select_fusion = f32[2,2,62,1800]{3,0,2,1:T(2,128)S(1)} fusion(f32[2,2,62,1800]{3,0,2,1:T(2,128)} %reshape.69, pred[2]{0:T(512)(128)(4,1)S(1)} %broadcast_compare_fusion, f32[2,2,62,1800]{3,1,2,0:T(2,128)} %param.10, s32[2]{0:T(128)S(1)} %fusion.120), kind=kOutput, calls=%fused_computation.90 | convolution fusion | flops 11160004 | bytes 5356810 | tf_op jit(solution)/shard_map/ps,p...->s.../dot_general | solution.py:101
  510.3 65.2 %psum.47 = f32[]{:T(128)} all-reduce(f32[]{:T(128)} %fusion.88), channel_id=1, replica_groups=mesh['gx'=16,'gy'=8] {'gx','gy'}, use_global_device_ids=true, to_apply=%region_12.13 | all-reduce | flops 1 | bytes 8 | tf_op jit(solution)/shard_map/psum | solution.py:170
  (141 shorter events, 111.0 us)
Async XLA Ops:
  21.5 53.7 %collective-permute-start.5 = (f32[2,62,40,2]{1,2,3,0:T(8,128)S(1)}, f32[2,62,40,2]{1,2,3,0:T(8,128)S(1)}, u32[]{:S(2)}, u32[]{:S(2)}) collective-permute-start(f32[2,62,40,2]{1,2,3,0:T(8,128)S(1)} %get-tuple-element.51), channel_id=1, source_target_pairs={{0,8},{8,16},{16,24},{24,32},{32,40},{40,48},{48,56},{56,64},{64,7... | collective-permute-start | bytes 119048 | tf_op jit(solution)/shard_map/ppermute | solution.py:27
  23.6 51.6 %collective-permute-start = (f32[2,62,40,2]{1,2,3,0:T(8,128)S(1)}, f32[2,62,40,2]{1,2,3,0:T(8,128)S(1)}, u32[]{:S(2)}, u32[]{:S(2)}) collective-permute-start(f32[2,62,40,2]{1,2,3,0:T(8,128)S(1)} %get-tuple-element.52), channel_id=1, source_target_pairs={{8,0},{16,8},{24,16},{32,24},{40,32},{48,40},{56,48},{64,56},{72,6... | collective-permute-start | bytes 119048 | tf_op jit(solution)/shard_map/ppermute | solution.py:29
  60.0 18.3 %collective-permute-start.1 = (f32[126,40,2]{0,1,2:T(8,128)S(1)}, f32[126,40,2]{0,1,2:T(8,128)S(1)}, u32[]{:S(2)}, u32[]{:S(2)}) collective-permute-start(f32[126,40,2]{0,1,2:T(8,128)S(1)} %get-tuple-element.37), channel_id=1, source_target_pairs={{0,8},{8,16},{16,24},{24,32},{32,40},{40,48},{48,56},{56,64},{64,7... | collective-permute-start | bytes 120968 | tf_op jit(solution)/shard_map/ppermute | solution.py:27
  60.1 18.2 %collective-permute-start.2 = (f32[126,40,2]{0,1,2:T(8,128)S(1)}, f32[126,40,2]{0,1,2:T(8,128)S(1)}, u32[]{:S(2)}, u32[]{:S(2)}) collective-permute-start(f32[126,40,2]{0,1,2:T(8,128)S(1)} %get-tuple-element.38), channel_id=1, source_target_pairs={{8,0},{16,8},{24,16},{32,24},{40,32},{48,40},{56,48},{64,56},{72,6... | collective-permute-start | bytes 120968 | tf_op jit(solution)/shard_map/ppermute | solution.py:29
  76.9 4.8 collective-permute-start.6
  78.3 6.3 %collective-permute-start.7 = (f32[2,62,2,94]{1,2,3,0:T(2,128)S(1)}, f32[2,62,2,94]{1,2,3,0:T(2,128)S(1)}, u32[]{:S(2)}, u32[]{:S(2)}) collective-permute-start(f32[2,62,2,94]{1,2,3,0:T(2,128)S(1)} %get-tuple-element.48), channel_id=1, source_target_pairs={{0,1},{1,2},{2,3},{3,4},{4,5},{5,6},{6,7},{7,0},{8,9},{9,10},{10,1... | collective-permute-start | bytes 279752 | tf_op jit(solution)/shard_map/ppermute | solution.py:27
  78.8 12.6 %collective-permute-start.3 = (f32[126,2,94]{0,1,2:T(2,128)S(1)}, f32[126,2,94]{0,1,2:T(2,128)S(1)}, u32[]{:S(2)}, u32[]{:S(2)}) collective-permute-start(f32[126,2,94]{0,1,2:T(2,128)S(1)} %get-tuple-element.35), channel_id=1, source_target_pairs={{0,1},{1,2},{2,3},{3,4},{4,5},{5,6},{6,7},{7,0},{8,9},{9,10},{10,1... | collective-permute-start | bytes 284264 | tf_op jit(solution)/shard_map/ppermute | solution.py:27
  79.1 12.4 %collective-permute-start.4 = (f32[126,2,94]{0,1,2:T(2,128)S(1)}, f32[126,2,94]{0,1,2:T(2,128)S(1)}, u32[]{:S(2)}, u32[]{:S(2)}) collective-permute-start(f32[126,2,94]{0,1,2:T(2,128)S(1)} %get-tuple-element.36), channel_id=1, source_target_pairs={{1,0},{2,1},{3,2},{4,3},{5,4},{6,5},{7,6},{0,7},{9,8},{10,9},{11,1... | collective-permute-start | bytes 284264 | tf_op jit(solution)/shard_map/ppermute | solution.py:29
  148.1 7.9 %collective-permute-start.9 = (f32[2,62,40,2]{1,2,3,0:T(8,128)S(1)}, f32[2,62,40,2]{1,2,3,0:T(8,128)S(1)}, u32[]{:S(2)}, u32[]{:S(2)}) collective-permute-start(f32[2,62,40,2]{1,2,3,0:T(8,128)S(1)} %get-tuple-element.49), channel_id=1, source_target_pairs={{0,8},{8,16},{16,24},{24,32},{32,40},{40,48},{48,56},{56,64},{64,7... | collective-permute-start | bytes 119048 | tf_op jit(solution)/shard_map/ppermute | solution.py:27
  148.2 7.9 %collective-permute-start.8 = (f32[2,62,40,2]{1,2,3,0:T(8,128)S(1)}, f32[2,62,40,2]{1,2,3,0:T(8,128)S(1)}, u32[]{:S(2)}, u32[]{:S(2)}) collective-permute-start(f32[2,62,40,2]{1,2,3,0:T(8,128)S(1)} %get-tuple-element.50), channel_id=1, source_target_pairs={{8,0},{16,8},{24,16},{32,24},{40,32},{48,40},{56,48},{64,56},{72,6... | collective-permute-start | bytes 119048 | tf_op jit(solution)/shard_map/ppermute | solution.py:29
  157.8 3.2 collective-permute-start.10
  157.8 6.3 %collective-permute-start.11 = (f32[2,62,2,94]{1,2,3,0:T(2,128)S(1)}, f32[2,62,2,94]{1,2,3,0:T(2,128)S(1)}, u32[]{:S(2)}, u32[]{:S(2)}) collective-permute-start(f32[2,62,2,94]{1,2,3,0:T(2,128)S(1)} %get-tuple-element.44), channel_id=1, source_target_pairs={{0,1},{1,2},{2,3},{3,4},{4,5},{5,6},{6,7},{7,0},{8,9},{9,10},{10,1... | collective-permute-start | bytes 279752 | tf_op jit(solution)/shard_map/ppermute | solution.py:27
  195.1 6.9 %collective-permute-start.13 = (f32[40,1]{0,1:T(1,128)S(1)}, f32[40,1]{0,1:T(1,128)S(1)}, u32[]{:S(2)}, u32[]{:S(2)}) collective-permute-start(f32[40,1]{0,1:T(1,128)S(1)} %get-tuple-element.70), channel_id=1, source_target_pairs={{0,8},{8,16},{16,24},{24,32},{32,40},{40,48},{48,56},{56,64},{64,7... | collective-permute-start | bytes 488 | tf_op jit(solution)/shard_map/ppermute | solution.py:27
  195.1 6.8 %collective-permute-start.12 = (f32[40,1]{0,1:T(1,128)S(1)}, f32[40,1]{0,1:T(1,128)S(1)}, u32[]{:S(2)}, u32[]{:S(2)}) collective-permute-start(f32[40,1]{0,1:T(1,128)S(1)} %get-tuple-element.71), channel_id=1, source_target_pairs={{8,0},{16,8},{24,16},{32,24},{40,32},{48,40},{56,48},{64,56},{72,6... | collective-permute-start | bytes 488 | tf_op jit(solution)/shard_map/ppermute | solution.py:29
  202.1 1.8 collective-permute-start.14
  202.1 4.7 collective-permute-start.15
  338.1 6.9 %collective-permute-start.17 = (f32[40,1]{0,1:T(1,128)S(1)}, f32[40,1]{0,1:T(1,128)S(1)}, u32[]{:S(2)}, u32[]{:S(2)}) collective-permute-start(f32[40,1]{0,1:T(1,128)S(1)} %get-tuple-element.66), channel_id=1, source_target_pairs={{0,8},{8,16},{16,24},{24,32},{32,40},{40,48},{48,56},{56,64},{64,7... | collective-permute-start | bytes 488 | tf_op jit(solution)/shard_map/ppermute | solution.py:27
  339.6 5.5 collective-permute-start.16
  345.1 2.5 collective-permute-start.18
  345.9 4.7 collective-permute-start.19
  481.5 17.9 %collective-permute-start.21 = (f32[40,1]{0,1:T(1,128)S(1)}, f32[40,1]{0,1:T(1,128)S(1)}, u32[]{:S(2)}, u32[]{:S(2)}) collective-permute-start(f32[40,1]{0,1:T(1,128)S(1)} %get-tuple-element.62), channel_id=1, source_target_pairs={{0,8},{8,16},{16,24},{24,32},{32,40},{40,48},{48,56},{56,64},{64,7... | collective-permute-start | bytes 488 | tf_op jit(solution)/shard_map/ppermute | solution.py:27
  483.4 15.9 %collective-permute-start.20 = (f32[40,1]{0,1:T(1,128)S(1)}, f32[40,1]{0,1:T(1,128)S(1)}, u32[]{:S(2)}, u32[]{:S(2)}) collective-permute-start(f32[40,1]{0,1:T(1,128)S(1)} %get-tuple-element.63), channel_id=1, source_target_pairs={{8,0},{16,8},{24,16},{32,24},{40,32},{48,40},{56,48},{64,56},{72,6... | collective-permute-start | bytes 488 | tf_op jit(solution)/shard_map/ppermute | solution.py:29
  499.5 10.0 %collective-permute-start.22 = (f32[1,92]{0,1:T(8,128)S(1)}, f32[1,92]{0,1:T(8,128)S(1)}, u32[]{:S(2)}, u32[]{:S(2)}) collective-permute-start(f32[1,92]{0,1:T(8,128)S(1)} %get-tuple-element.60), channel_id=1, source_target_pairs={{1,0},{2,1},{3,2},{4,3},{5,4},{6,5},{7,6},{0,7},{9,8},{10,9},{11,1... | collective-permute-start | bytes 1112 | tf_op jit(solution)/shard_map/ppermute | solution.py:29
  500.9 8.6 %collective-permute-start.23 = (f32[1,92]{0,1:T(8,128)S(1)}, f32[1,92]{0,1:T(8,128)S(1)}, u32[]{:S(2)}, u32[]{:S(2)}) collective-permute-start(f32[1,92]{0,1:T(8,128)S(1)} %get-tuple-element.61), channel_id=1, source_target_pairs={{0,1},{1,2},{2,3},{3,4},{4,5},{5,6},{6,7},{7,0},{8,9},{9,10},{10,1... | collective-permute-start | bytes 1112 | tf_op jit(solution)/shard_map/ppermute | solution.py:27
  (17 other events, 451.9 us)
where the time goes:
time: 584 us; the launch traced here: 578 us
  blocking collectives  319 us (55%)
  other arithmetic  97.6 us (17%)
  local copies, waits for them, and re-layouts  71.4 us (12%)
  starting transfers between devices  42.4 us (7%)
  waiting for transfers between devices  20.4 us (3%)
  matrix products  18.8 us (3%)
  between operations  8.11 us (1%)
    psum x3, blocking collectives, squares(): return lax.psum(jnp.sum(residual * residual), ('gx', 'gy'))  189 us
    psum x2, blocking collectives, per_device(): step_size = norm_now / lax.psum(jnp.sum(direction * applied), ('gx', 'gy'))  130 us
    ppermute x12, starting transfers between devices, with_halo(): lax.ppermute(head, axis, [((i + 1) % count, i) for i in range(count)])  35.4 us
    add x2, other arithmetic, tracer_pass(): window(padded, 2, 0, 0)  30 us
    mul x2, other arithmetic, tracer_pass(): scaled = window(mixing, 1, 0, 0) * first_lap  20 us
    ppermute x12, waiting for transfers between devices, with_halo(): lax.ppermute(tail, axis, [(i, (i + 1) % count) for i in range(count)])  14.9 us
    transpose x2, local copies, waits for them, and re-layouts, to_strip(): return placed.transpose(axes_order).reshape(middle + (BY, slot_count * BX))  14.6 us
    concatenate x8, other arithmetic, with_halo(): jnp.concatenate([lax.ppermute(tail, axis, [(i, (i + 1) % count) for i in...  13.5 us
  transfers between devices with their start and end apart: 24, of which 9 were waited for; matrix products, arithmetic and copies ran while one was open for 13% of the time, Pallas kernels for 0%

commit v1 on v0

--- a/solution.py
+++ b/solution.py
@@ -99,6 +99,38 @@
     axes_order = (leading + 1,) + tuple(range(leading)) + (leading, leading + 2)
     blocks = blocks.transpose(axes_order).reshape((slot_count,) + middle + (BY * BX,))
     return jnp.einsum("ps,p...->s...", selector, blocks, precision=lax.Precision.HIGHEST)
+
+
+def quad_sum(values, axis, partner):
+    count = lax.axis_size(axis)
+    others = [
+        lax.ppermute(values, axis, [(i, partner(i, turn)) for i in range(count)])
+        for turn in range(1, 4)
+    ]
+    return (values + others[0]) + (others[1] + others[2])
+
+
+def total_over_devices(values):
+    values = values + lax.ppermute(values, "gy", [(i, i ^ 1) for i in range(lax.axis_size("gy"))])
+    values = quad_sum(values, "gy", lambda i, turn: i ^ (2 * turn))
+    values = quad_sum(values, "gx", lambda i, turn: i ^ turn)
+    return quad_sum(values, "gx", lambda i, turn: i ^ (4 * turn))
+
+
+def krylov_weights(moments):
+    m = [moments[k] for k in range(6)]
+    low10 = m[2] / m[1]
+    low20 = m[3] / m[1]
+    pivot1 = m[3] - low10 * m[2]
+    part21 = m[4] - low20 * m[2]
+    low21 = part21 / pivot1
+    pivot2 = m[5] - low20 * m[3] - low21 * part21
+    y1 = m[1] - low10 * m[0]
+    y2 = m[2] - low20 * m[0] - low21 * y1
+    z2 = y2 / pivot2
+    z1 = y1 / pivot1 - low21 * z2
+    z0 = m[0] / m[1] - low10 * z1 - low20 * z2
+    return z0, z1, z2
 
 
 def per_device(block_list, wet_levels, mixing, velocity, tracers, damping):
@@ -142,37 +174,37 @@
     forcing = jnp.sum(wet_inner * (current[0] - salt_weight * current[1]), axis=0) / math.sqrt(
         level_numbers
     )
-    height_pad = window(depth_pad, margin - 1, 0, 0)
-    centre_depth = window(height_pad, 1, 0, 0)
-    couplings = [
-        jnp.minimum(centre_depth, window(height_pad, 1, step_y, step_x)) / level_numbers
-        for step_y, step_x in directions
-    ]
-    diagonal = damping + (couplings[0] + couplings[1] + couplings[2] + couplings[3])
-
-    def operate(values):
-        padded = with_halo(values, (("gx", 1), ("gy", 0)), 1)
-        beside = [
-            couplings[number] * window(padded, 1, step_y, step_x)
-            for number, (step_y, step_x) in enumerate(directions)
-        ]
-        return diagonal * values - (beside[0] + beside[1] + beside[2] + beside[3])
-
-    def squares(residual):
-        return lax.psum(jnp.sum(residual * residual), ("gx", "gy"))
-
-    solution = jnp.zeros_like(forcing)
-    residual = forcing
-    direction = forcing
-    norm_now = squares(residual)
-    for iteration in range(ITERS):
-        applied = operate(direction)
-        step_size = norm_now / lax.psum(jnp.sum(direction * applied), ("gx", "gy"))
-        solution = solution + step_size * direction
-        residual = residual - step_size * applied
-        norm_next = squares(residual)
-        direction = residual + norm_next / norm_now * direction
-        norm_now = norm_next
+    reach = 3
+    surface = with_halo(
+        jnp.stack([forcing, inner_depth, damping]), (("gx", 2), ("gy", 1)), reach
+    )
+    surface_row = lax.broadcasted_iota(jnp.int32, surface.shape[1:], 0)
+    beyond = (row_owner == 0) & (surface_row < reach) | (row_owner == lax.axis_size("gy") - 1) & (
+        surface_row >= surface.shape[1] - reach
+    )
+    depth_wide = jnp.where(beyond, 0.0, surface[1])
+
+    def operate(values, cut):
+        depth_cut = window(depth_wide, cut, 0, 0)
+        damping_inner = window(surface[2], cut + 1, 0, 0)
+        centre = window(values, 1, 0, 0)
+        centre_depth = window(depth_cut, 1, 0, 0)
+        total = damping_inner * centre
+        for step_y, step_x in directions:
+            coupling = jnp.minimum(centre_depth, window(depth_cut, 1, step_y, step_x)) / level_numbers
+            total = total + coupling * (centre - window(values, 1, step_y, step_x))
+        return total
+
+    first = operate(surface[0], 0)
+    second = operate(first, 1)
+    third = operate(second, 2)
+    basis = [forcing, window(first, 2, 0, 0), window(second, 1, 0, 0), third]
+    moments = jnp.stack(
+        [jnp.sum(basis[k // 2] * basis[(k + 1) // 2]) for k in range(6)]
+    )
+    moments = total_over_devices(moments)
+    weights = krylov_weights(moments)
+    solution = weights[0] * basis[0] + weights[1] * basis[1] + weights[2] * basis[2]
     restored = from_strip(current, selector)
     new_tracers = jnp.where(present[:, None, None, None], restored, tracers)
     return (new_tracers, solution)

time: 584 us -> 269 us (0.46)
  blocking collectives: 319 us -> 0 us
    psum x5 -> x0, blocking collectives: 319 us -> none  [the longest x3 189 us: squares(): return lax.psum(jnp.sum(residual * residual), ('gx', 'gy'))]
    ppermute x0 -> x10, starting transfers between devices: none -> 12.4 us  [the longest x9 12.3 us: quad_sum(): lax.ppermute(values, axis, [(i, partner(i, turn)) for i in range(count)])]
    ppermute x12 -> x8, starting transfers between devices: 35.4 us -> 25.6 us  [with_halo(): lax.ppermute(head, axis, [((i + 1) % count, i) for i in range(count)])]
    ppermute x0 -> x10, waiting for transfers between devices: none -> 9.12 us  [the longest x9 8.01 us: quad_sum(): lax.ppermute(values, axis, [(i, partner(i, turn)) for i in range(count)])]
    ppermute x12 -> x8, waiting for transfers between devices: 14.9 us -> 8.28 us  [with_halo(): lax.ppermute(tail, axis, [(i, (i + 1) % count) for i in range(count)])]
    concatenate x8 -> x7, other arithmetic: 13.5 us -> 15.1 us  [with_halo(): jnp.concatenate([lax.ppermute(tail, axis, [(i, (i + 1) % count) for i in...]
  transfers between devices with their start and end apart: 24 -> 26, of which waited for: 9 -> 12; matrix products, arithmetic and copies ran while one was open for 13% -> 27% of each run, Pallas kernels for 0% -> 0%
where the time goes in v1:
time: 269 us; the launch traced here: 264 us
  other arithmetic  95.9 us (36%)
  local copies, waits for them, and re-layouts  76.2 us (28%)
  starting transfers between devices  41.5 us (15%)
  waiting for transfers between devices  19.9 us (7%)
  matrix products  18.8 us (7%)
  between operations  11.4 us (4%)
    add x2, other arithmetic, tracer_pass(): window(padded, 2, 0, 0)  29.5 us
    ppermute x8, starting transfers between devices, with_halo(): lax.ppermute(head, axis, [((i + 1) % count, i) for i in range(count)])  25.6 us
    mul x2, other arithmetic, tracer_pass(): scaled = window(mixing, 1, 0, 0) * first_lap  19.6 us
    concatenate x7, other arithmetic, with_halo(): jnp.concatenate([lax.ppermute(tail, axis, [(i, (i + 1) % count) for i in...  15.1 us
    transpose x2, local copies, waits for them, and re-layouts, to_strip(): return placed.transpose(axes_order).reshape(middle + (BY, slot_count * BX))  14.5 us
    mul x2, other arithmetic, face_flux(): face_wet * face_speed * (0.5 * (centre + window(values, 2, step_y, step_x)))  13.1 us
    dot_general x4, matrix products, to_strip(): jnp.einsum('ps,s...->p...', selector, slot_values, precision=lax.Precisio...  12.4 us
    reshape x2, local copies, waits for them, and re-layouts, from_strip(): blocks.transpose(axes_order).reshape((slot_count,) + middle + (BY * BX,))  12.4 us
  transfers between devices with their start and end apart: 26, of which 12 were waited for; matrix products, arithmetic and copies ran while one was open for 27% of the time, Pallas kernels for 0%

profile of v1, /device:TPU:0, one launch (start us, length us, event | category | flops | bytes accessed | tf_op | source)
XLA Modules:
  0.0 263.7 jit_solution(12266519197887598982)
XLA Ops:
  1.4 6.8 %fusion.82 = f32[2,2,62,1800]{3,0,2,1:T(2,128)S(1)} fusion(f32[2,2,62,1800]{3,1,2,0:T(2,128)} %param.10, s32[2]{0:T(128)S(1)} %fusion.129), kind=kOutput, calls=%fused_computation.140 | convolution fusion | flops 10713604 | bytes 3571208 | tf_op jit(solution)/shard_map/ps,s...->p.../dot_general | solution.py:85
  9.7 5.0 %reshape.68 = f32[2,2,62,40,45]{4,3,2,1,0:T(8,128)} reshape(f32[2,2,62,1800]{3,2,1,0:T(8,128)} %copy.89) | data formatting | bytes 3571200 | tf_op jit(solution)/shard_map/reshape | solution.py:89
  14.8 5.8 %copy.90 = f32[2,62,40,2,45]{1,2,4,3,0:T(8,128)} copy(f32[2,62,40,2,45]{4,2,1,0,3:T(8,128)} %bitcast.80) | data formatting | bytes 3571200 | tf_op jit(solution)/shard_map/transpose | solution.py:91
  23.6 4.9 %collective-permute-start = (f32[2,62,40,2]{1,2,3,0:T(8,128)S(1)}, f32[2,62,40,2]{1,2,3,0:T(8,128)S(1)}, u32[]{:S(2)}, u32[]{:S(2)}) collective-permute-start(f32[2,62,40,2]{1,2,3,0:T(8,128)S(1)} %get-tuple-element.47), channel_id=1, source_target_pairs={{8,0},{16,8},{24,16},{32,24},{40,32},{48,40},{56,48},{64,56},{72,6... | collective-permute-start | bytes 119048 | tf_op jit(solution)/shard_map/ppermute | solution.py:29
  33.5 5.1 %fusion.60 = f32[2,2,62,1800]{3,0,2,1:T(2,128)S(1)} fusion(f32[2,2,62,1800]{3,1,2,0:T(2,128)S(1)} %copy-done, s32[2]{0:T(128)S(1)} %fusion.129), kind=kOutput, calls=%fused_computation.97 | convolution fusion | flops 10713604 | bytes 3571208 | tf_op jit(solution)/shard_map/ps,s...->p.../dot_general | solution.py:85
  40.1 5.1 %reshape.70 = f32[2,2,62,40,45]{4,3,2,1,0:T(8,128)} reshape(f32[2,2,62,1800]{3,2,1,0:T(8,128)} %copy.93) | data formatting | bytes 3571200 | tf_op jit(solution)/shard_map/reshape | solution.py:89
  45.1 8.7 %copy.94 = f32[2,62,40,2,45]{1,0,2,4,3:T(2,128)} copy(f32[2,62,40,2,45]{4,2,1,0,3:T(8,128)} %bitcast.77) | data formatting | bytes 3571200 | tf_op jit(solution)/shard_map/transpose | solution.py:91
  53.8 5.0 %reshape_reshape.3 = f32[124,40,90]{0,1,2:T(8,128)} reshape(f32[2,62,40,2,45]{1,0,2,4,3:T(2,128)} %copy.94) | data formatting | bytes 3571200 | tf_op jit(solution)/shard_map/reshape;reshape | solution.py:146
  60.0 5.8 %collective-permute-start.2 = (f32[126,40,2]{0,1,2:T(8,128)S(1)}, f32[126,40,2]{0,1,2:T(8,128)S(1)}, u32[]{:S(2)}, u32[]{:S(2)}) collective-permute-start(f32[126,40,2]{0,1,2:T(8,128)S(1)} %get-tuple-element.33), channel_id=1, source_target_pairs={{8,0},{16,8},{24,16},{32,24},{40,32},{48,40},{56,48},{64,56},{72,6... | collective-permute-start | bytes 120968 | tf_op jit(solution)/shard_map/ppermute | solution.py:29
  84.5 4.1 %pad_maximum_fusion = (f32[2,62,42,94]{1,2,3,0:T(8,128)}, f32[2,62,42,94]{1,2,3,0:T(8,128)}) fusion(f32[2,62,2,94]{1,2,3,0:T(2,128)S(1)} %collective-permute-done.6, f32[2,62,40,2]{1,2,3,0:T(8,128)S(1)} %collective-permute-done, f32[2,62,40,90]{1,2,3,0:T(8,128)S(1)} %bitcast.75, f32[2,62,40,2]{1,2,3,0:T(8,128)S(1)} %collective-permute-done.5, ...), kind=kLoop, calls=%fused_computation | loop fusion | flops 2937312 | bytes 5967872 | tf_op jit(solution)/shard_map/concatenate | solution.py:25
  92.6 4.1 %fusion.139 = (f32[1,44,94]{0,1,2:T(8,128)}, f32[1,44,94]{0,1,2:T(8,128)}, f32[1,44,94]{0,1,2:T(8,128)}) fusion(f32[126,44,94]{0,1,2:T(8,128)S(1)} %pad_maximum_fusion.8, pred[44]{0:T(512)(128)(4,1)S(1)} %and_or_fusion.1), kind=kLoop, calls=%fused_computation.266 | loop fusion | flops 4136 | bytes 82764 | tf_op jit(solution)/shard_map/slice | solution.py:157
  108.9 11.7 %fusion.10 = f32[2,62,42,92]{1,2,3,0:T(8,128)S(1)} fusion(f32[2,62,42,94]{1,2,3,0:T(8,128)} %get-tuple-element.41, f32[2,62,42,94]{1,2,3,0:T(8,128)} %get-tuple-element.40, f32[2,62,44,94]{1,2,3,0:T(8,128)} %pad_maximum_fusion.1, f32[62,42,92]{0,1,2:T(8,128)} %get-tuple-element.53, f32[62,42,92]{0,1,2:T(8,128)} %get-tuple-element.54, ...), kind=kLoop, calls=%fused_computation.21 | loop fusion | flops 5749632 | bytes 15347808 | tf_op jit(solution)/shard_map/mul | solution.py:75
  120.7 7.9 %fusion.73 = (f32[62,40,90]{0,1,2:T(8,128)}, f32[62,40,90]{0,1,2:T(8,128)}, f32[62,40,90]{0,1,2:T(8,128)}, f32[62,40,90]{0,1,2:T(8,128)}) fusion(f32[126,2,94]{0,1,2:T(2,128)S(1)} %collective-permute-done.4, f32[126,40,2]{0,1,2:T(8,128)S(1)} %collective-permute-done.2, f32[126,40,2]{0,1,2:T(8,128)S(1)} %collective-permute-done.1, ...), kind=kLoop, calls=%fused_computation.118 | loop fusion | flops 4464000 | bytes 9226944 | tf_op jit(solution)/shard_map/mul | solution.py:63
  128.6 5.2 %fusion.81 = (f32[62,40,90]{0,1,2:T(8,128)}, f32[62,40,90]{0,1,2:T(8,128)}, f32[62,40,90]{0,1,2:T(8,128)}, f32[62,40,90]{0,1,2:T(8,128)}) fusion(f32[126,40,2]{0,1,2:T(8,128)S(1)} %collective-permute-done.2, f32[1,40,90]{0,1,2:T(8,128)S(1)} %copy-done.6, f32[1,40,90]{0,1,2:T(8,128)S(1)} %copy-done.4, f32[124,40,90]{0,1,2:T(8,128)S(1)} %copy-done.8, ...), kind=kLoop, calls=%fused_computation.136 | loop fusion | flops 3571200 | bytes 9037440 | tf_op jit(solution)/shard_map/mul | solution.py:63
  133.8 15.3 %fusion.42 = f32[2,62,40,90]{1,2,3,0:T(8,128)} fusion(f32[2,62,42,92]{1,2,3,0:T(8,128)S(1)} %fusion.10, f32[2,62,40,90]{1,2,3,0:T(8,128)} %bitcast.74, f32[2,62,42,94]{1,2,3,0:T(8,128)} %get-tuple-element.41, f32[2,62,42,94]{1,2,3,0:T(8,128)} %get-tuple-element.40, f32[2,62,40,2]{1,2,3,0:T(8,128)S(1)} %collective-permute-done.5, ...), kind=kLoop, calls=%fused_computation.65 | loop fusion | flops 13392000 | bytes 23292160 | tf_op jit(solution)/shard_map/add | solution.py:78
  150.1 5.3 %collective-permute-start.8 = (f32[2,62,40,2]{1,2,3,0:T(8,128)S(1)}, f32[2,62,40,2]{1,2,3,0:T(8,128)S(1)}, u32[]{:S(2)}, u32[]{:S(2)}) collective-permute-start(f32[2,62,40,2]{1,2,3,0:T(8,128)S(1)} %get-tuple-element.45), channel_id=1, source_target_pairs={{8,0},{16,8},{24,16},{32,24},{40,32},{48,40},{56,48},{64,56},{72,6... | collective-permute-start | bytes 119048 | tf_op jit(solution)/shard_map/ppermute | solution.py:29
  168.3 4.2 %pad_maximum_fusion.2 = (f32[2,62,42,94]{1,2,3,0:T(8,128)}, f32[2,62,42,94]{1,2,3,0:T(8,128)}) fusion(f32[2,62,2,94]{1,2,3,0:T(2,128)S(1)} %collective-permute-done.10, f32[2,62,40,2]{1,2,3,0:T(8,128)S(1)} %collective-permute-done.8, f32[2,62,40,90]{1,2,3,0:T(8,128)S(1)} %copy-done.3, f32[2,62,40,2]{1,2,3,0:T(8,128)S(1)} %collective-permute-done.9, ...), kind=kLoop, calls=%fused_computation.3 | loop fusion | flops 2937312 | bytes 5967872 | tf_op jit(solution)/shard_map/concatenate | solution.py:25
  172.5 7.8 %fusion.2 = f32[2,62,42,92]{1,2,3,0:T(8,128)S(1)} fusion(f32[2,62,42,94]{1,2,3,0:T(8,128)} %get-tuple-element.37, f32[2,62,42,94]{1,2,3,0:T(8,128)} %get-tuple-element.36, f32[2,62,44,94]{1,2,3,0:T(8,128)S(1)} %pad_maximum_fusion.3, f32[62,42,92]{0,1,2:T(8,128)} %get-tuple-element.53, f32[62,42,92]{0,1,2:T(8,128)} %get-tuple-element.54, ...), kind=kLoop, calls=%fused_computation.9 | loop fusion | flops 5749632 | bytes 15347808 | tf_op jit(solution)/shard_map/mul | solution.py:75
  180.4 14.2 %fusion.20 = f32[2,62,40,90]{1,2,3,0:T(8,128)} fusion(f32[2,62,42,92]{1,2,3,0:T(8,128)S(1)} %fusion.2, f32[2,62,40,90]{1,2,3,0:T(8,128)} %fusion.42, f32[2,62,42,94]{1,2,3,0:T(8,128)} %get-tuple-element.37, f32[2,62,42,94]{1,2,3,0:T(8,128)} %get-tuple-element.36, f32[2,62,40,2]{1,2,3,0:T(8,128)S(1)} %collective-permute-done.9, ...), kind=kLoop, calls=%fused_computation.35 | loop fusion | flops 13392000 | bytes 23292160 | tf_op jit(solution)/shard_map/add | solution.py:78
  197.7 5.4 %collective-permute-start.13 = (f32[3,40,3]{2,1,0:T(8,128)S(1)}, f32[3,40,3]{2,1,0:T(8,128)S(1)}, u32[]{:S(2)}, u32[]{:S(2)}) collective-permute-start(f32[3,40,3]{2,1,0:T(8,128)S(1)} %get-tuple-element.60), channel_id=1, source_target_pairs={{8,0},{16,8},{24,16},{32,24},{40,32},{48,40},{56,48},{64,56},{72,6... | collective-permute-start | bytes 4328 | tf_op jit(solution)/shard_map/ppermute | solution.py:29
  203.1 6.0 %copy.122 = f32[2,2,62,40,45]{4,3,0,2,1:T(8,128)} copy(f32[2,2,62,40,45]{2,3,4,0,1:T(8,128)} %bitcast.79) | data formatting | bytes 3571200 | tf_op jit(solution)/shard_map/reshape | solution.py:100
  209.1 6.4 %reshape.78 = f32[2,2,62,1800]{3,0,2,1:T(2,128)} reshape(f32[2,2,62,40,45]{4,3,0,2,1:T(8,128)} %copy.122) | data formatting | bytes 3571200 | tf_op jit(solution)/shard_map/reshape | solution.py:100
  216.4 6.4 %convolution_select_fusion = f32[2,2,62,1800]{3,0,2,1:T(2,128)S(1)} fusion(f32[2,2,62,1800]{3,0,2,1:T(2,128)} %reshape.78, pred[2]{0:T(512)(128)(4,1)S(1)} %broadcast_compare_fusion, f32[2,2,62,1800]{3,1,2,0:T(2,128)} %param.10, s32[2]{0:T(128)S(1)} %fusion.129), kind=kOutput, calls=%fused_computation.90 | convolution fusion | flops 11160004 | bytes 5356810 | tf_op jit(solution)/shard_map/ps,p...->s.../dot_general | solution.py:101
  239.4 4.0 %collective-permute-start.20 = (f32[6]{0:T(128)S(1)}, f32[6]{0:T(128)S(1)}, u32[]{:S(2)}, u32[]{:S(2)}) collective-permute-start(f32[6]{0:T(128)S(1)} %add_add_fusion.2), channel_id=1, source_target_pairs={{0,8},{8,0},{16,24},{24,16},{32,40},{40,32},{48,56},{56,48},{64,72... | collective-permute-start | bytes 80 | tf_op jit(solution)/shard_map/ppermute | solution.py:107
  (146 shorter events, 91.9 us)
Async XLA Ops:
  21.5 53.6 %collective-permute-start.5 = (f32[2,62,40,2]{1,2,3,0:T(8,128)S(1)}, f32[2,62,40,2]{1,2,3,0:T(8,128)S(1)}, u32[]{:S(2)}, u32[]{:S(2)}) collective-permute-start(f32[2,62,40,2]{1,2,3,0:T(8,128)S(1)} %get-tuple-element.46), channel_id=1, source_target_pairs={{0,8},{8,16},{16,24},{24,32},{32,40},{40,48},{48,56},{56,64},{64,7... | collective-permute-start | bytes 119048 | tf_op jit(solution)/shard_map/ppermute | solution.py:27
  23.6 51.5 %collective-permute-start = (f32[2,62,40,2]{1,2,3,0:T(8,128)S(1)}, f32[2,62,40,2]{1,2,3,0:T(8,128)S(1)}, u32[]{:S(2)}, u32[]{:S(2)}) collective-permute-start(f32[2,62,40,2]{1,2,3,0:T(8,128)S(1)} %get-tuple-element.47), channel_id=1, source_target_pairs={{8,0},{16,8},{24,16},{32,24},{40,32},{48,40},{56,48},{64,56},{72,6... | collective-permute-start | bytes 119048 | tf_op jit(solution)/shard_map/ppermute | solution.py:29
  60.0 18.3 %collective-permute-start.1 = (f32[126,40,2]{0,1,2:T(8,128)S(1)}, f32[126,40,2]{0,1,2:T(8,128)S(1)}, u32[]{:S(2)}, u32[]{:S(2)}) collective-permute-start(f32[126,40,2]{0,1,2:T(8,128)S(1)} %get-tuple-element.32), channel_id=1, source_target_pairs={{0,8},{8,16},{16,24},{24,32},{32,40},{40,48},{48,56},{56,64},{64,7... | collective-permute-start | bytes 120968 | tf_op jit(solution)/shard_map/ppermute | solution.py:27
  60.0 18.2 %collective-permute-start.2 = (f32[126,40,2]{0,1,2:T(8,128)S(1)}, f32[126,40,2]{0,1,2:T(8,128)S(1)}, u32[]{:S(2)}, u32[]{:S(2)}) collective-permute-start(f32[126,40,2]{0,1,2:T(8,128)S(1)} %get-tuple-element.33), channel_id=1, source_target_pairs={{8,0},{16,8},{24,16},{32,24},{40,32},{48,40},{56,48},{64,56},{72,6... | collective-permute-start | bytes 120968 | tf_op jit(solution)/shard_map/ppermute | solution.py:29
  76.8 4.8 %collective-permute-start.6 = (f32[2,62,2,94]{1,2,3,0:T(2,128)S(1)}, f32[2,62,2,94]{1,2,3,0:T(2,128)S(1)}, u32[]{:S(2)}, u32[]{:S(2)}) collective-permute-start(f32[2,62,2,94]{1,2,3,0:T(2,128)S(1)} %get-tuple-element.42), channel_id=1, source_target_pairs={{1,0},{2,1},{3,2},{4,3},{5,4},{6,5},{7,6},{0,7},{9,8},{10,9},{11,1... | collective-permute-start | bytes 279752 | tf_op jit(solution)/shard_map/ppermute | solution.py:29
  78.2 6.3 %collective-permute-start.7 = (f32[2,62,2,94]{1,2,3,0:T(2,128)S(1)}, f32[2,62,2,94]{1,2,3,0:T(2,128)S(1)}, u32[]{:S(2)}, u32[]{:S(2)}) collective-permute-start(f32[2,62,2,94]{1,2,3,0:T(2,128)S(1)} %get-tuple-element.43), channel_id=1, source_target_pairs={{0,1},{1,2},{2,3},{3,4},{4,5},{5,6},{6,7},{7,0},{8,9},{9,10},{10,1... | collective-permute-start | bytes 279752 | tf_op jit(solution)/shard_map/ppermute | solution.py:27
  78.7 12.6 %collective-permute-start.3 = (f32[126,2,94]{0,1,2:T(2,128)S(1)}, f32[126,2,94]{0,1,2:T(2,128)S(1)}, u32[]{:S(2)}, u32[]{:S(2)}) collective-permute-start(f32[126,2,94]{0,1,2:T(2,128)S(1)} %get-tuple-element.30), channel_id=1, source_target_pairs={{0,1},{1,2},{2,3},{3,4},{4,5},{5,6},{6,7},{7,0},{8,9},{9,10},{10,1... | collective-permute-start | bytes 284264 | tf_op jit(solution)/shard_map/ppermute | solution.py:27
  79.0 12.3 %collective-permute-start.4 = (f32[126,2,94]{0,1,2:T(2,128)S(1)}, f32[126,2,94]{0,1,2:T(2,128)S(1)}, u32[]{:S(2)}, u32[]{:S(2)}) collective-permute-start(f32[126,2,94]{0,1,2:T(2,128)S(1)} %get-tuple-element.31), channel_id=1, source_target_pairs={{1,0},{2,1},{3,2},{4,3},{5,4},{6,5},{7,6},{0,7},{9,8},{10,9},{11,1... | collective-permute-start | bytes 284264 | tf_op jit(solution)/shard_map/ppermute | solution.py:29
  150.0 7.8 %collective-permute-start.9 = (f32[2,62,40,2]{1,2,3,0:T(8,128)S(1)}, f32[2,62,40,2]{1,2,3,0:T(8,128)S(1)}, u32[]{:S(2)}, u32[]{:S(2)}) collective-permute-start(f32[2,62,40,2]{1,2,3,0:T(8,128)S(1)} %get-tuple-element.44), channel_id=1, source_target_pairs={{0,8},{8,16},{16,24},{24,32},{32,40},{40,48},{48,56},{56,64},{64,7... | collective-permute-start | bytes 119048 | tf_op jit(solution)/shard_map/ppermute | solution.py:27
  150.1 7.8 %collective-permute-start.8 = (f32[2,62,40,2]{1,2,3,0:T(8,128)S(1)}, f32[2,62,40,2]{1,2,3,0:T(8,128)S(1)}, u32[]{:S(2)}, u32[]{:S(2)}) collective-permute-start(f32[2,62,40,2]{1,2,3,0:T(8,128)S(1)} %get-tuple-element.45), channel_id=1, source_target_pairs={{8,0},{16,8},{24,16},{32,24},{40,32},{48,40},{56,48},{64,56},{72,6... | collective-permute-start | bytes 119048 | tf_op jit(solution)/shard_map/ppermute | solution.py:29
  159.4 6.3 %collective-permute-start.11 = (f32[2,62,2,94]{1,2,3,0:T(2,128)S(1)}, f32[2,62,2,94]{1,2,3,0:T(2,128)S(1)}, u32[]{:S(2)}, u32[]{:S(2)}) collective-permute-start(f32[2,62,2,94]{1,2,3,0:T(2,128)S(1)} %get-tuple-element.39), channel_id=1, source_target_pairs={{0,1},{1,2},{2,3},{3,4},{4,5},{5,6},{6,7},{7,0},{8,9},{9,10},{10,1... | collective-permute-start | bytes 279752 | tf_op jit(solution)/shard_map/ppermute | solution.py:27
  197.6 17.9 %collective-permute-start.12 = (f32[3,40,3]{2,1,0:T(8,128)S(1)}, f32[3,40,3]{2,1,0:T(8,128)S(1)}, u32[]{:S(2)}, u32[]{:S(2)}) collective-permute-start(f32[3,40,3]{2,1,0:T(8,128)S(1)} %get-tuple-element.59), channel_id=1, source_target_pairs={{0,8},{8,16},{16,24},{24,32},{32,40},{40,48},{48,56},{56,64},{64,7... | collective-permute-start | bytes 4328 | tf_op jit(solution)/shard_map/ppermute | solution.py:27
  197.7 17.9 %collective-permute-start.13 = (f32[3,40,3]{2,1,0:T(8,128)S(1)}, f32[3,40,3]{2,1,0:T(8,128)S(1)}, u32[]{:S(2)}, u32[]{:S(2)}) collective-permute-start(f32[3,40,3]{2,1,0:T(8,128)S(1)} %get-tuple-element.60), channel_id=1, source_target_pairs={{8,0},{16,8},{24,16},{32,24},{40,32},{48,40},{56,48},{64,56},{72,6... | collective-permute-start | bytes 4328 | tf_op jit(solution)/shard_map/ppermute | solution.py:29
  215.9 9.2 %collective-permute-start.15 = (f32[3,3,96]{1,2,0:T(8,128)S(1)}, f32[3,3,96]{1,2,0:T(8,128)S(1)}, u32[]{:S(2)}, u32[]{:S(2)}) collective-permute-start(f32[3,3,96]{1,2,0:T(8,128)S(1)} %copy.112), channel_id=1, source_target_pairs={{1,0},{2,1},{3,2},{4,3},{5,4},{6,5},{7,6},{0,7},{9,8},{10,9},{11,1... | collective-permute-start | bytes 10376 | tf_op jit(solution)/shard_map/ppermute | solution.py:29
  215.9 9.2 %collective-permute-start.14 = (f32[3,3,96]{1,2,0:T(8,128)S(1)}, f32[3,3,96]{1,2,0:T(8,128)S(1)}, u32[]{:S(2)}, u32[]{:S(2)}) collective-permute-start(f32[3,3,96]{1,2,0:T(8,128)S(1)} %copy.111), channel_id=1, source_target_pairs={{0,1},{1,2},{2,3},{3,4},{4,5},{5,6},{6,7},{7,0},{8,9},{9,10},{10,1... | collective-permute-start | bytes 10376 | tf_op jit(solution)/shard_map/ppermute | solution.py:27
  231.6 4.8 %collective-permute-start.19 = (f32[6]{0:T(128)S(1)}, f32[6]{0:T(128)S(1)}, u32[]{:S(2)}, u32[]{:S(2)}) collective-permute-start(f32[6]{0:T(128)S(1)} %add.215), channel_id=1, source_target_pairs={{0,6},{1,7},{2,4},{3,5},{4,2},{5,3},{6,0},{7,1},{8,14},{9,15},{10,... | collective-permute-start | bytes 80 | tf_op jit(solution)/shard_map/ppermute | solution.py:107
  234.1 5.0 %collective-permute-start.18 = (f32[6]{0:T(128)S(1)}, f32[6]{0:T(128)S(1)}, u32[]{:S(2)}, u32[]{:S(2)}) collective-permute-start(f32[6]{0:T(128)S(1)} %add.215), channel_id=1, source_target_pairs={{0,4},{1,5},{2,6},{3,7},{4,0},{5,1},{6,2},{7,3},{8,12},{9,13},{10,... | collective-permute-start | bytes 80 | tf_op jit(solution)/shard_map/ppermute | solution.py:107
  234.1 5.0 %collective-permute-start.17 = (f32[6]{0:T(128)S(1)}, f32[6]{0:T(128)S(1)}, u32[]{:S(2)}, u32[]{:S(2)}) collective-permute-start(f32[6]{0:T(128)S(1)} %add.215), channel_id=1, source_target_pairs={{0,2},{1,3},{2,0},{3,1},{4,6},{5,7},{6,4},{7,5},{8,10},{9,11},{10,... | collective-permute-start | bytes 80 | tf_op jit(solution)/shard_map/ppermute | solution.py:107
  239.2 4.8 %collective-permute-start.22 = (f32[6]{0:T(128)S(1)}, f32[6]{0:T(128)S(1)}, u32[]{:S(2)}, u32[]{:S(2)}) collective-permute-start(f32[6]{0:T(128)S(1)} %add_add_fusion.2), channel_id=1, source_target_pairs={{0,24},{8,16},{16,8},{24,0},{32,56},{40,48},{48,40},{56,32},{64,88... | collective-permute-start | bytes 80 | tf_op jit(solution)/shard_map/ppermute | solution.py:107
  239.3 5.1 %collective-permute-start.21 = (f32[6]{0:T(128)S(1)}, f32[6]{0:T(128)S(1)}, u32[]{:S(2)}, u32[]{:S(2)}) collective-permute-start(f32[6]{0:T(128)S(1)} %add_add_fusion.2), channel_id=1, source_target_pairs={{0,16},{8,24},{16,0},{24,8},{32,48},{40,56},{48,32},{56,40},{64,80... | collective-permute-start | bytes 80 | tf_op jit(solution)/shard_map/ppermute | solution.py:107
  239.4 5.5 %collective-permute-start.20 = (f32[6]{0:T(128)S(1)}, f32[6]{0:T(128)S(1)}, u32[]{:S(2)}, u32[]{:S(2)}) collective-permute-start(f32[6]{0:T(128)S(1)} %add_add_fusion.2), channel_id=1, source_target_pairs={{0,8},{8,0},{16,24},{24,16},{32,40},{40,32},{48,56},{56,48},{64,72... | collective-permute-start | bytes 80 | tf_op jit(solution)/shard_map/ppermute | solution.py:107
  244.9 4.8 %collective-permute-start.25 = (f32[6]{0:T(128)S(1)}, f32[6]{0:T(128)S(1)}, u32[]{:S(2)}, u32[]{:S(2)}) collective-permute-start(f32[6]{0:T(128)S(1)} %add_add_fusion.1), channel_id=1, source_target_pairs={{0,96},{8,104},{16,112},{24,120},{32,64},{40,72},{48,80},{56,88},{... | collective-permute-start | bytes 80 | tf_op jit(solution)/shard_map/ppermute | solution.py:107
  246.9 5.0 %collective-permute-start.24 = (f32[6]{0:T(128)S(1)}, f32[6]{0:T(128)S(1)}, u32[]{:S(2)}, u32[]{:S(2)}) collective-permute-start(f32[6]{0:T(128)S(1)} %add_add_fusion.1), channel_id=1, source_target_pairs={{0,64},{8,72},{16,80},{24,88},{32,96},{40,104},{48,112},{56,120},{... | collective-permute-start | bytes 80 | tf_op jit(solution)/shard_map/ppermute | solution.py:107
  246.9 5.0 %collective-permute-start.23 = (f32[6]{0:T(128)S(1)}, f32[6]{0:T(128)S(1)}, u32[]{:S(2)}, u32[]{:S(2)}) collective-permute-start(f32[6]{0:T(128)S(1)} %add_add_fusion.1), channel_id=1, source_target_pairs={{0,32},{8,40},{16,48},{24,56},{32,0},{40,8},{48,16},{56,24},{64,96... | collective-permute-start | bytes 80 | tf_op jit(solution)/shard_map/ppermute | solution.py:107
  (19 other events, 199.7 us)

commit v2 on v0

v2 whole, which is shorter than its diff:
```python
import functools
import math

import jax
import jax.numpy as jnp
from jax import lax
from jax.experimental import pallas as pl
from jax.experimental.pallas import tpu as pltpu
from jax.sharding import PartitionSpec as P

BX = 45
BY = 40
CELLS = BX * BY
LEVELS = 62
LANES = 128
TILES = 8
REACH = 7
ROWS = BY + 2 * REACH
BASE = 8
WIDE = 2 * BX
NS = 21
EW = 13
SURFACE = 56

advect_rate = 0.25
mixing_rate = 0.015
salt_weight = 0.8


def lane_ids():
    return lax.broadcasted_iota(jnp.int32, (8, LANES), 1)


def merge(parts, lane):
    flat = []
    for low, width, value in parts:
        low %= LANES
        if low + width > LANES:
            flat.append((low, value))
            flat.append((0, value))
        else:
            flat.append((low, value))
    flat.sort(key=lambda part: part[0])
    result = flat[0][1]
    last = result
    for low, value in flat[1:]:
        if value is last:
            continue
        result = jnp.where(lane >= low, value, result)
        last = value
    return result


def turn(value, shift):
    shift %= LANES
    return pltpu.roll(value, shift, 1) if shift else value


class Source:
    def __init__(self, own, up=None, down=None, west=None, east=None):
        self.load = {"own": own, "up": up, "down": down, "west": west, "east": east}
        self.kept = {}

    def tile(self, kind, position, number):
        key = (kind, position, number)
        if kind in ("west", "east"):
            key = (kind, 0, number)
        elif kind == "up" and number == 14:
            key = (kind, position, 11)
        if key not in self.kept:
            self.kept[key] = self.fetch(*key)
        return self.kept[key]

    def fetch(self, kind, position, number):
        load = self.load[kind]
        if kind == "own":
            return load(position, number)
        if kind in ("west", "east"):
            return load(number)
        shift = 120 if kind == "up" else 8
        first = 12 if kind == "up" else 0
        if first <= number <= first + 1:
            return turn(load(1 + 2 * position + number - first), shift)
        return turn(load(0), shift + 64 * position)

    def cells(self, position, start, width):
        parts = []
        at = start
        while at < start + width:
            if at < 0:
                number = (at + CELLS) // LANES
                end = min(start + width, 0, (number + 1) * LANES - CELLS)
                value = self.tile("up", position, number)
            elif at < CELLS:
                number = at // LANES
                end = min(start + width, CELLS, (number + 1) * LANES)
                value = self.tile("own", position, number)
            else:
                number = (at - CELLS) // LANES
                end = min(start + width, (number + 1) * LANES + CELLS)
                value = self.tile("down", position, number)
            parts.append((at, end - at, value))
            at = end
        return parts


def west_edge(row):
    if row == 45:
        return 2, 0, 1
    if -6 <= row <= 44:
        return (row + 6) // 17, 0, REACH
    return None


def east_edge(row):
    if row == -6:
        return 0, 6, 1
    if -5 <= row <= 45:
        return (row + 5) // 17, 0, REACH
    return None


def pack_columns(source, lane):
    east, west = [], []
    for group in range(3):
        parts = []
        for row in range(-6, 46):
            number, first, count = east_edge(row)
            if number == group:
                parts += source.cells(1, BX * row + BX - REACH + first, count)
        east.append(merge(parts, lane))
        parts = []
        for row in range(-6, 46):
            number, first, count = west_edge(row)
            if number == group:
                parts += source.cells(0, BX * row + first, count)
        west.append(merge(parts, lane))
    return east, west


def strip_rows(source, lane):
    turned = {}

    def combined(r):
        if r in turned:
            return turned[r]
        parts = []
        if east_edge(r - 1):
            number, first, count = east_edge(r - 1)
            value = source.tile("west", 0, number)
            parts.append((BX * r - REACH + first, count, value))
        if -REACH <= r < BY + REACH:
            parts += source.cells(0, BX * r, BX)
        if -REACH <= r + 1 < BY + REACH:
            parts += source.cells(1, BX * (r + 1), BX)
        if west_edge(r + 2):
            number, first, count = west_edge(r + 2)
            value = source.tile("east", 0, number)
            parts.append((BX * (r + 2) + first, count, value))
        turned[r] = turn(merge(parts, lane), BASE - BX * r)
        return turned[r]

    for row in range(-REACH, BY + REACH):
        value = combined(row)
        if east_edge(row):
            value = jnp.where(lane < BASE, combined(row + 1), value)
        value = jnp.where(lane < BASE + BX, value, combined(row - 1))
        if west_edge(row):
            value = jnp.where(lane < BASE + WIDE, value, combined(row - 2))
        yield row, value


def slot_swap(block_list):
    first = block_list[0]
    return jnp.where(first >= 0, first & 1, 1 - (block_list[1] & 1))


def field_loader(ref, which, swap):
    def load(position, number):
        slot = swap if position == 0 else 1 - swap
        if number < 14:
            return ref[slot, which, :, number * LANES : (number + 1) * LANES]
        return turn(ref[slot, which, :, CELLS - LANES : CELLS], CELLS % LANES)

    return load


def column_loader(wet_levels, mixing, swap):
    def load(position, number):
        slot = swap if position == 0 else 1 - swap
        low = number * LANES if number < 14 else CELLS - LANES
        both = wet_levels[:, low : low + LANES].astype(jnp.float32)
        depth = jnp.where(slot == 0, both[0:1, :], both[1:2, :])
        both = mixing[:, low : low + LANES]
        mix = jnp.where(slot == 0, both[0:1, :], both[1:2, :])
        sublane = lax.broadcasted_iota(jnp.int32, (8, LANES), 0)
        value = jnp.where(
            sublane == 0, jnp.broadcast_to(depth, (8, LANES)), jnp.broadcast_to(mix, (8, LANES))
        )
        return value if number < 14 else turn(value, CELLS % LANES)

    return load


def pack_rows(load, lane):
    ends = [jnp.where(lane < 8, load(p, 14), load(p, 11)) for p in range(2)]
    mixed = jnp.where((lane >= 13) & (lane < 72), turn(ends[1], 64), ends[0])
    up = [mixed, load(0, 12), load(0, 13), load(1, 12), load(1, 13)]
    mixed = jnp.where(lane < 64, load(0, 2), turn(load(1, 2), 64))
    down = [mixed, load(0, 0), load(0, 1), load(1, 0), load(1, 1)]
    return up, down


def rows_kernel(block_list, wet_levels, mixing, damping, velocity, tracers, up, down, padded):
    lane = lane_ids()
    swap = slot_swap(block_list)
    step = pl.program_id(0)
    for field in range(4):
        load = field_loader(tracers if field < 2 else velocity, field % 2, swap)
        ups, downs = pack_rows(load, lane)
        for number in range(5):
            up[0, 5 * field + number] = ups[number]
            down[0, 5 * field + number] = downs[number]

    @pl.when(step == 0)
    def _():
        padded[...] = jnp.zeros_like(padded)
        padded[:, 0:WIDE] = damping[...]

    load = column_loader(wet_levels, mixing, swap)
    for number in range(5):

        @pl.when(step == number)
        def _():
            ups, downs = pack_rows(load, lane)
            up[0, NS - 1] = ups[number]
            down[0, NS - 1] = downs[number]

    @pl.when(step >= 5)
    def _():
        up[0, NS - 1] = padded[BY - 8 : BY, :]
        down[0, NS - 1] = padded[0:8, :]


def columns_kernel(
    block_list, wet_levels, mixing, damping, velocity, tracers, up, down, up_extra, down_extra,
    east, west, padded,
):
    lane = lane_ids()
    swap = slot_swap(block_list)
    step = pl.program_id(0)
    for field in range(4):
        source = Source(
            field_loader(tracers if field < 2 else velocity, field % 2, swap),
            lambda number, field=field: up[0, 5 * field + number],
            lambda number, field=field: down[0, 5 * field + number],
        )
        easts, wests = pack_columns(source, lane)
        for number in range(3):
            east[0, 3 * field + number] = easts[number]
            west[0, 3 * field + number] = wests[number]

    @pl.when(step == 0)
    def _():
        padded[...] = jnp.zeros_like(padded)
        padded[:, 0:WIDE] = damping[...]

    for number in range(3):

        @pl.when(step == number)
        def _():
            source = Source(
                column_loader(wet_levels, mixing, swap),
                lambda tile: up_extra[tile, 0],
                lambda tile: down_extra[tile, 0],
            )
            easts, wests = pack_columns(source, lane)
            east[0, EW - 1] = easts[number]
            west[0, EW - 1] = wests[number]

    @pl.when(step >= 3)
    def _():
        tiles = [up_extra[5, 0]]
        tiles += [padded[8 * j : 8 * j + 8, :] for j in range(5)]
        tiles += [down_extra[5, 0]]
        east[0, EW - 1] = merge([(2 * j, 2, turn(t, 2 * j - WIDE + 2)) for j, t in enumerate(tiles)], lane)
        west[0, EW - 1] = merge([(2 * j, 2, turn(t, 2 * j)) for j, t in enumerate(tiles)], lane)


def advance(fields, read, write, low, high, levels, shared, lane):
    depth_east, depth_north, mix = shared
    zero = jnp.zeros((8, LANES), jnp.float32)
    row0 = low - 1
    now = [read(n, row0) for n in range(2)]
    below = [read(n, row0 - 1) for n in range(2)]
    wet_north = levels < depth_north[row0 - 1 + REACH]
    drop = [jnp.where(wet_north, now[n] - below[n], zero) for n in range(2)]
    scaled = [None, None]
    flow = [None, None]
    held = [None, None]
    gone = None
    for row in range(row0, high + 2):
        at = row + REACH
        wet_east = levels < depth_east[at]
        wet_north = levels < depth_north[at]
        mixing = mix[at]
        above = [read(n, row + 1) for n in range(2)]
        fresh = []
        kept = []
        for n in range(2):
            beside = turn(now[n], LANES - 1)
            step_east = jnp.where(wet_east, beside - now[n], zero)
            rise = jnp.where(wet_north, above[n] - now[n], zero)
            lap = (step_east - turn(step_east, 1)) + (rise - drop[n])
            fresh.append(mixing * lap)
            drop[n] = rise
            kept.append(beside + now[n])
        if row > row0:
            old_east, old_north, old_row = gone
            flow_east = fields[2, old_row + REACH]
            flow_east = flow_east + turn(flow_east, LANES - 1)
            flow_north = fields[3, old_row + REACH] + fields[3, at]
            for n in range(2):
                beside = turn(scaled[n], LANES - 1)
                east = jnp.where(old_east, flow_east * held[n] + (beside - scaled[n]), zero)
                north = jnp.where(
                    old_north, flow_north * (below[n] + now[n]) + (fresh[n] - scaled[n]), zero
                )
                if old_row >= low:
                    out = below[n] - ((east - turn(east, 1)) + (north - flow[n]))
                    write(n, old_row, out)
                flow[n] = north
        gone = (wet_east, wet_north, row)
        scaled = fresh
        held = kept
        below = now
        now = above


def surface_operator(values, couple_east, couple_north, damping):
    east = couple_east * (values - turn(values, LANES - 1))
    north = couple_north * (values - pltpu.roll(values, SURFACE - 1, 0))
    return damping * values + ((east - turn(east, 1)) + (north - pltpu.roll(north, 1, 0)))


def main_kernel(
    block_list, wet_levels, mixing, damping, velocity, tracers,
    up, down, from_west, from_east, up_extra, down_extra, west_extra, east_extra,
    new_tracers, basis, moments,
    fields, halfway, depth, depth_east, depth_north, mix, forcing, surface, depths, dampings,
):
    lane = lane_ids()
    swap = slot_swap(block_list)
    step = pl.program_id(0)

    @pl.when(step == 0)
    def _():
        source = Source(
            column_loader(wet_levels, mixing, swap),
            lambda tile: up_extra[tile, 0],
            lambda tile: down_extra[tile, 0],
            lambda tile: west_extra[tile, 0],
            lambda tile: east_extra[tile, 0],
        )
        depths[...] = jnp.zeros_like(depths)
        last = None
        for row, value in strip_rows(source, lane):
            here = jnp.broadcast_to(value[0:1, :], (8, LANES))
            depth[row + REACH] = here
            depth_east[row + REACH] = jnp.minimum(here, turn(here, LANES - 1))
            mix[row + REACH] = mixing_rate * jnp.broadcast_to(value[1:2, :], (8, LANES))
            depths[row + 8 : row + 9, :] = value[0:1, :]
            if last is not None:
                depth_north[row + REACH - 1] = jnp.minimum(here, last)
            last = here
        forcing[...] = jnp.zeros_like(forcing)

    for field in range(4):
        source = Source(
            field_loader(tracers if field < 2 else velocity, field % 2, swap),
            lambda number, field=field: up[0, 5 * field + number],
            lambda number, field=field: down[0, 5 * field + number],
            lambda number, field=field: from_west[0, 3 * field + number],
            lambda number, field=field: from_east[0, 3 * field + number],
        )
        for row, value in strip_rows(source, lane):
            fields[field, row + REACH] = value if field < 2 else (0.25 * advect_rate) * value

    levels = (lax.broadcasted_iota(jnp.int32, (8, LANES), 0) + 8 * step).astype(jnp.float32)
    shared = (depth_east, depth_north, mix)

    def read_first(n, row):
        return fields[n, row + REACH]

    def write_first(n, row, value):
        halfway[n, row + REACH] = value

    advance(fields, read_first, write_first, -5, 44, levels, shared, lane)

    def read_second(n, row):
        return halfway[n, row + REACH]

    def write_second(n, row, value):
        fields[n, row + REACH] = value

    advance(fields, read_second, write_second, -3, 42, levels, shared, lane)

    for row in range(-3, 43):
        at = row + REACH
        part = fields[0, at] - salt_weight * fields[1, at]
        forcing[at] += jnp.where(levels < depth[at], part, 0.0)

    for n in range(2):
        turned = {}

        def back(r, n=n, turned=turned):
            if r not in turned:
                value = jnp.where(lane < BASE + BX, fields[n, r + REACH], fields[n, r + 1 + REACH])
                turned[r] = turn(value, BX * r - BASE)
            return turned[r]

        for number in range(15):
            for position in range(2):
                slot = swap if position == 0 else 1 - swap
                first, end = number * LANES, min((number + 1) * LANES, CELLS)
                parts = []
                for row in range(first // BX, (end - 1) // BX + 1):
                    low = max(row * BX, first)
                    parts.append((low, min((row + 1) * BX, end) - low, back(row - position)))
                value = merge(parts, lane)
                new_tracers[slot, n, :, first:end] = value[:, 0 : end - first]

    @pl.when(step == TILES - 1)
    def _():
        surface[...] = jnp.zeros_like(surface)
        for row in range(-3, 43):
            total = jnp.sum(forcing[row + REACH], axis=0, keepdims=True)
            surface[row + 8 : row + 9, :] = total * (1.0 / math.sqrt(LEVELS))
        dampings[...] = jnp.zeros_like(dampings)
        dampings[8 : 8 + BY, 0:WIDE] = damping[...]
        dampings[0:8, :] = up_extra[5, 0]
        dampings[8 + BY : 16 + BY, :] = down_extra[5, 0]
        for j in range(7):
            value = turn(dampings[8 * j : 8 * j + 8, :], BASE)
            value = jnp.where(lane < BASE, turn(west_extra[3, 0], BASE - 2 - 2 * j), value)
            value = jnp.where(lane < BASE + WIDE, value, turn(east_extra[3, 0], BASE + WIDE - 2 * j))
            dampings[8 * j : 8 * j + 8, :] = value
        here = depths[...]
        couple_east = jnp.minimum(here, turn(here, LANES - 1)) * (1.0 / LEVELS)
        couple_north = jnp.minimum(here, pltpu.roll(here, SURFACE - 1, 0)) * (1.0 / LEVELS)
        diagonal = dampings[...]
        powers = [surface[...]]
        for _ in range(3):
            powers.append(surface_operator(powers[-1], couple_east, couple_north, diagonal))
        row_id = lax.broadcasted_iota(jnp.int32, (SURFACE, LANES), 0)
        lane_id = lax.broadcasted_iota(jnp.int32, (SURFACE, LANES), 1)
        own = (row_id >= 8) & (row_id < 8 + BY) & (lane_id >= BASE) & (lane_id < BASE + WIDE)
        moments[...] = jnp.zeros_like(moments)
        for k in range(6):
            product = jnp.where(own, powers[k // 2] * powers[(k + 1) // 2], 0.0)
            moments[k : k + 1, :] = jnp.sum(product, axis=0, keepdims=True)
        for k in range(3):
            basis[k] = turn(powers[k], LANES - BASE)[8 : 8 + BY, :]


def finish_kernel(moments, basis, out):
    totals = jnp.sum(moments[...], axis=1, keepdims=True)
    m = [totals[k : k + 1, :] for k in range(6)]
    low10 = m[2] / m[1]
    low20 = m[3] / m[1]
    pivot1 = m[3] - low10 * m[2]
    part21 = m[4] - low20 * m[2]
    low21 = part21 / pivot1
    pivot2 = m[5] - low20 * m[3] - low21 * part21
    y1 = m[1] - low10 * m[0]
    y2 = m[2] - low20 * m[0] - low21 * y1
    z2 = y2 / pivot2
    z1 = y1 / pivot1 - low21 * z2
    z0 = m[0] / m[1] - low10 * z1 - low20 * z2
    value = z0 * basis[0] + z1 * basis[1] + z2 * basis[2]
    out[...] = value[:, 0:WIDE]


def quad_sum(values, axis, partner):
    count = lax.axis_size(axis)
    others = [
        lax.ppermute(values, axis, [(i, partner(i, turn)) for i in range(count)])
        for turn in range(1, 4)
    ]
    return (values + others[0]) + (others[1] + others[2])


def total_over_devices(values):
    values = values + lax.ppermute(values, "gy", [(i, i ^ 1) for i in range(lax.axis_size("gy"))])
    values = quad_sum(values, "gy", lambda i, turn: i ^ (2 * turn))
    values = quad_sum(values, "gx", lambda i, turn: i ^ turn)
    return quad_sum(values, "gx", lambda i, turn: i ^ (4 * turn))


def whole(shape):
    return pl.BlockSpec(shape, lambda k: (0,) * len(shape))


def per_device(block_list, wet_levels, mixing, velocity, tracers, damping):
    f32 = jnp.float32
    slots, fields_each, levels, cells = tracers.shape
    params = pltpu.CompilerParams(
        dimension_semantics=("arbitrary",), vmem_limit_bytes=40 * 1024 * 1024
    )
    level_block = pl.BlockSpec((slots, fields_each, 8, cells), lambda k: (0, 0, k, 0))
    rows_block = pl.BlockSpec((1, NS, 8, LANES), lambda k: (k, 0, 0, 0))
    columns_block = pl.BlockSpec((1, EW, 8, LANES), lambda k: (k, 0, 0, 0))
    rows_extra = pl.BlockSpec((TILES, 1, 8, LANES), lambda k: (0, NS - 1, 0, 0))
    columns_extra = pl.BlockSpec((TILES, 1, 8, LANES), lambda k: (0, EW - 1, 0, 0))
    own_specs = [
        pl.BlockSpec(memory_space=pltpu.SMEM),
        whole(wet_levels.shape),
        whole(mixing.shape),
        whole(damping.shape),
        level_block,
        level_block,
    ]
    own = (block_list, wet_levels, mixing, damping, velocity, tracers)
    rows_type = jax.ShapeDtypeStruct((TILES, NS, 8, LANES), f32)
    columns_type = jax.ShapeDtypeStruct((TILES, EW, 8, LANES), f32)

    up, down = pl.pallas_call(
        rows_kernel,
        grid=(TILES,),
        in_specs=own_specs,
        out_specs=[rows_block, rows_block],
        out_shape=[rows_type, rows_type],
        scratch_shapes=[pltpu.VMEM((BY, LANES), f32)],
        compiler_params=params,
        name="pack_rows",
    )(*own)
    rows_total = lax.axis_size("gy")
    up = lax.ppermute(up, "gy", [(i, i + 1) for i in range(rows_total - 1)])
    down = lax.ppermute(down, "gy", [(i + 1, i) for i in range(rows_total - 1)])

    east, west = pl.pallas_call(
        columns_kernel,
        grid=(TILES,),
        in_specs=own_specs + [rows_block, rows_block, rows_extra, rows_extra],
        out_specs=[columns_block, columns_block],
        out_shape=[columns_type, columns_type],
        scratch_shapes=[pltpu.VMEM((BY, LANES), f32)],
        compiler_params=params,
        name="pack_columns",
    )(*own, up, down, up, down)
    columns_total = lax.axis_size("gx")
    from_west = lax.ppermute(east, "gx", [(i, (i + 1) % columns_total) for i in range(columns_total)])
    from_east = lax.ppermute(west, "gx", [((i + 1) % columns_total, i) for i in range(columns_total)])

    row_store = pltpu.VMEM((ROWS, 8, LANES), f32)
    new_tracers, basis, moments = pl.pallas_call(
        main_kernel,
        grid=(TILES,),
        in_specs=own_specs
        + [rows_block, rows_block, columns_block, columns_block]
        + [rows_extra, rows_extra, columns_extra, columns_extra],
        out_specs=[level_block, whole((3, BY, LANES)), whole((8, LANES))],
        out_shape=[
            jax.ShapeDtypeStruct(tracers.shape, f32),
            jax.ShapeDtypeStruct((3, BY, LANES), f32),
            jax.ShapeDtypeStruct((8, LANES), f32),
        ],
        scratch_shapes=[
            pltpu.VMEM((4, ROWS, 8, LANES), f32),
            pltpu.VMEM((2, ROWS, 8, LANES), f32),
            row_store,
            row_store,
            row_store,
            row_store,
            row_store,
            pltpu.VMEM((SURFACE, LANES), f32),
            pltpu.VMEM((SURFACE, LANES), f32),
            pltpu.VMEM((SURFACE, LANES), f32),
        ],
        compiler_params=params,
        name="advance",
    )(*own, up, down, from_west, from_east, up, down, from_west, from_east)

    moments = total_over_devices(moments)
    height = pl.pallas_call(
        finish_kernel,
        out_shape=jax.ShapeDtypeStruct((BY, WIDE), f32),
        name="finish",
    )(moments, basis)
    return (new_tracers, height)


def solution(mesh):
    return jax.shard_map(
        per_device,
        mesh=mesh,
        in_specs=(
            P(("gx", "gy")),
            P(("gx", "gy"), None),
            P(("gx", "gy"), None),
            P(("gx", "gy"), None, None, None),
            P(("gx", "gy"), None, None, None),
            P("gy", "gx"),
        ),
        out_specs=(P(("gx", "gy"), None, None, None), P("gy", "gx")),
        check_vma=False,
    )
```

time: 584 us -> 147 us (0.25); the launches traced: 578 us -> 147 us
  blocking collectives: 319 us -> 0 us
  other arithmetic: 97.6 us -> 0.61 us
  Pallas kernels: 0 us -> 87.1 us
  local copies, waits for them, and re-layouts: 71.4 us -> 5.54 us
  matrix products: 18.8 us -> 0 us
  starting transfers between devices: 42.4 us -> 33.5 us
  between operations: 8.11 us -> 0.72 us
    psum x5 -> x0, blocking collectives: 319 us -> none  [the longest x3 189 us: squares(): return lax.psum(jnp.sum(residual * residual), ('gx', 'gy'))]
    pallas_call x0 -> x4, Pallas kernels: none -> 87.1 us  [the longest x1 79.6 us: per_device(): pl.pallas_call(main_kernel, grid=(TILES,), in_specs=own_specs + [rows_blo...]
    mul x5 -> x0, other arithmetic: 36.9 us -> none  [the longest x2 20 us: tracer_pass(): scaled = window(mixing, 1, 0, 0) * first_lap]
    add x5 -> x4, other arithmetic: 30 us -> 0.61 us  [the longest x3 0.61 us: quad_sum(): return values + others[0] + (others[1] + others[2])]
    reshape x8 -> x0, local copies, waits for them, and re-layouts: 22.6 us -> none  [the longest x2 12.2 us: from_strip(): blocks.transpose(axes_order).reshape((slot_count,) + middle + (BY * BX,))]
    dot_general x5 -> x0, matrix products: 18.8 us -> none  [the longest x4 12.4 us: to_strip(): jnp.einsum('ps,s...->p...', selector, slot_values, precision=lax.Precisio...]
    transpose x2 -> x0, local copies, waits for them, and re-layouts: 14.6 us -> none  [to_strip(): return placed.transpose(axes_order).reshape(middle + (BY, slot_count * BX))]
    slice x15 -> x0, local copies, waits for them, and re-layouts: 14.2 us -> none  [the longest x6 9.54 us: window(): values[..., shrink + step_y:height - shrink + step_y, shrink + step_x:bre...]
  transfers between devices with their start and end apart: 24 -> 14, of which waited for: 9 -> 9; matrix products, arithmetic and copies ran while one was open for 13% -> 2% of each run, Pallas kernels for 0% -> 0%
where the time goes in v2:
time: 147 us
  Pallas kernels  87.1 us (59%)
  starting transfers between devices  33.5 us (23%)
  waiting for transfers between devices  19.3 us (13%)
  local copies, waits for them, and re-layouts  5.54 us (4%)
    pallas_call x1, Pallas kernels, per_device(): pl.pallas_call(main_kernel, grid=(TILES,), in_specs=own_specs + [rows_blo...  79.6 us
    ppermute x9, starting transfers between devices, quad_sum(): lax.ppermute(values, axis, [(i, partner(i, turn)) for i in range(count)])  16 us
    ppermute x1, starting transfers between devices, total_over_devices(): lax.ppermute(values, 'gy', [(i, i ^ 1) for i in range(lax.axis_size('gy'))])  8.22 us
    ppermute x9, waiting for transfers between devices, quad_sum(): lax.ppermute(values, axis, [(i, partner(i, turn)) for i in range(count)])  7.95 us
    ppermute x1, waiting for transfers between devices, per_device(): lax.ppermute(east, 'gx', [(i, (i + 1) % columns_total) for i in range(col...  6.03 us
    unnamed x15, local copies, waits for them, and re-layouts  5.54 us
    ppermute x1, starting transfers between devices, per_device(): lax.ppermute(west, 'gx', [((i + 1) % columns_total, i) for i in range(col...  4.65 us
    ppermute x1, waiting for transfers between devices, per_device(): down = lax.ppermute(down, 'gy', [(i + 1, i) for i in range(rows_total - 1)])  4.09 us
  transfers between devices with their start and end apart: 14, of which 9 were waited for; matrix products, arithmetic and copies ran while one was open for 2% of the time, Pallas kernels for 0%

profile of v2, /device:TPU:0, one launch (start us, length us, event | category | flops | bytes accessed | tf_op | source)
XLA Modules:
  0.0 146.7 jit_solution(16654752663719713513)
XLA Ops:
  0.6 1.8 %copy.12.velocity = f32[2,2,62,1800]{3,2,1,0:T(8,128)S(1)} copy(f32[2,2,62,1800]{3,1,2,0:T(2,128)} %param.9) | data formatting | bytes 3571200 | tf_op args[3]
  3.5 3.0 %pack_rows.1 = (f32[8,21,8,128]{3,2,1,0:T(8,128)S(1)}, f32[8,21,8,128]{3,2,1,0:T(8,128)S(1)}) custom-call(s32[2]{0:T(128)S(1)} %copy-done.4, s32[2,1800]{1,0:T(2,128)S(1)} %copy-done.1, f32[2,1800]{1,0:T(2,128)S(1)} %copy-done.2, f32[40,90]{1,0:T(8,128)S(1)} %copy-done, f32[2,2,62,1800]{3,2,1,0:T(8,128)S(1)} %copy.12.velocity, ...), custom_call_target="tpu_custom_call" | custom-call | tf_op jit(solution)/shard_map/pack_rows/pallas_call | solution.py:527
  6.4 1.3 collective-permute-start
  7.8 1.3 collective-permute-start.1
  9.5 4.1 %collective-permute-done.1.down.down_extra = f32[8,21,8,128]{3,2,1,0:T(8,128)S(1)} collective-permute-done((f32[8,21,8,128]{3,2,1,0:T(8,128)S(1)}, f32[8,21,8,128]{3,2,1,0:T(8,128)S(1)}, u32[]{:S(2)}, u32[]{:S(2)}) %collective-permute-start.1) | collective-permute-done | bytes 688160 | tf_op jit(solution)/shard_map/ppermute | solution.py:539
  13.6 2.9 %pack_columns.1 = (f32[8,13,8,128]{3,2,1,0:T(8,128)S(1)}, f32[8,13,8,128]{3,2,1,0:T(8,128)S(1)}) custom-call(s32[2]{0:T(128)S(1)} %copy-done.4, s32[2,1800]{1,0:T(2,128)S(1)} %copy-done.1, f32[2,1800]{1,0:T(2,128)S(1)} %copy-done.2, f32[40,90]{1,0:T(8,128)S(1)} %copy-done, f32[2,2,62,1800]{3,2,1,0:T(8,128)S(1)} %copy.12.velocity, ...), custom_call_target="tpu_custom_call" | custom-call | tf_op jit(solution)/shard_map/pack_columns/pallas_call | solution.py:541
  16.5 2.0 %collective-permute-start.2 = (f32[8,13,8,128]{3,2,1,0:T(8,128)S(1)}, f32[8,13,8,128]{3,2,1,0:T(8,128)S(1)}, u32[]{:S(2)}, u32[]{:S(2)}) collective-permute-start(f32[8,13,8,128]{3,2,1,0:T(8,128)S(1)} %get-tuple-element.11), channel_id=1, source_target_pairs={{0,8},{8,16},{16,24},{24,32},{32,40},{40,48},{48,56},{56,64},{64,7... | collective-permute-start | bytes 1277960 | tf_op jit(solution)/shard_map/ppermute | solution.py:552
  18.5 4.7 %collective-permute-start.3 = (f32[8,13,8,128]{3,2,1,0:T(8,128)S(1)}, f32[8,13,8,128]{3,2,1,0:T(8,128)S(1)}, u32[]{:S(2)}, u32[]{:S(2)}) collective-permute-start(f32[8,13,8,128]{3,2,1,0:T(8,128)S(1)} %get-tuple-element.12), channel_id=1, source_target_pairs={{8,0},{16,8},{24,16},{32,24},{40,32},{48,40},{56,48},{64,56},{72,6... | collective-permute-start | bytes 1277960 | tf_op jit(solution)/shard_map/ppermute | solution.py:553
  23.2 6.0 %collective-permute-done.2.from_west.west_extra = f32[8,13,8,128]{3,2,1,0:T(8,128)S(1)} collective-permute-done((f32[8,13,8,128]{3,2,1,0:T(8,128)S(1)}, f32[8,13,8,128]{3,2,1,0:T(8,128)S(1)}, u32[]{:S(2)}, u32[]{:S(2)}) %collective-permute-start.2) | collective-permute-done | bytes 426016 | tf_op jit(solution)/shard_map/ppermute | solution.py:552
  29.2 79.6 %advance.1 = (f32[2,2,62,1800]{3,2,1,0:T(8,128)S(1)}, f32[3,40,128]{2,1,0:T(8,128)S(1)}, f32[8,128]{1,0:T(8,128)S(1)}) custom-call(s32[2]{0:T(128)S(1)} %copy-done.4, s32[2,1800]{1,0:T(2,128)S(1)} %copy-done.1, f32[2,1800]{1,0:T(2,128)S(1)} %copy-done.2, f32[40,90]{1,0:T(8,128)S(1)} %copy-done, f32[2,2,62,1800]{3,2,1,0:T(8,128)S(1)} %copy.12.velocity, ...), custom_call_target="tpu_custom_call" | custom-call | tf_op jit(solution)/shard_map/advance/pallas_call | solution.py:556
  108.8 8.2 %collective-permute-start.4 = (f32[8,128]{1,0:T(8,128)S(1)}, f32[8,128]{1,0:T(8,128)S(1)}, u32[]{:S(2)}, u32[]{:S(2)}) collective-permute-start(f32[8,128]{1,0:T(8,128)S(1)} %get-tuple-element.14), channel_id=1, source_target_pairs={{0,1},{1,0},{2,3},{3,2},{4,5},{5,4},{6,7},{7,6},{8,9},{9,8},{10,11... | collective-permute-start | bytes 12296 | tf_op jit(solution)/shard_map/ppermute | solution.py:494
  117.0 0.8 collective-permute-done.4
  117.9 1.9 %collective-permute-start.7 = (f32[8,128]{1,0:T(8,128)S(1)}, f32[8,128]{1,0:T(8,128)S(1)}, u32[]{:S(2)}, u32[]{:S(2)}) collective-permute-start(f32[8,128]{1,0:T(8,128)S(1)} %add.30), channel_id=1, source_target_pairs={{0,6},{1,7},{2,4},{3,5},{4,2},{5,3},{6,0},{7,1},{8,14},{9,15},{10,... | collective-permute-start | bytes 12296 | tf_op jit(solution)/shard_map/ppermute | solution.py:487
  119.8 4.8 %collective-permute-start.6 = (f32[8,128]{1,0:T(8,128)S(1)}, f32[8,128]{1,0:T(8,128)S(1)}, u32[]{:S(2)}, u32[]{:S(2)}) collective-permute-start(f32[8,128]{1,0:T(8,128)S(1)} %add.30), channel_id=1, source_target_pairs={{0,4},{1,5},{2,6},{3,7},{4,0},{5,1},{6,2},{7,3},{8,12},{9,13},{10,... | collective-permute-start | bytes 12296 | tf_op jit(solution)/shard_map/ppermute | solution.py:487
  124.6 1.6 %collective-permute-done.6 = f32[8,128]{1,0:T(8,128)S(1)} collective-permute-done((f32[8,128]{1,0:T(8,128)S(1)}, f32[8,128]{1,0:T(8,128)S(1)}, u32[]{:S(2)}, u32[]{:S(2)}) %collective-permute-start.6) | collective-permute-done | bytes 4128 | tf_op jit(solution)/shard_map/ppermute | solution.py:487
  126.2 2.0 %collective-permute-done.5 = f32[8,128]{1,0:T(8,128)S(1)} collective-permute-done((f32[8,128]{1,0:T(8,128)S(1)}, f32[8,128]{1,0:T(8,128)S(1)}, u32[]{:S(2)}, u32[]{:S(2)}) %collective-permute-start.5) | collective-permute-done | bytes 4128 | tf_op jit(solution)/shard_map/ppermute | solution.py:487
  128.2 1.9 %collective-permute-start.10 = (f32[8,128]{1,0:T(8,128)S(1)}, f32[8,128]{1,0:T(8,128)S(1)}, u32[]{:S(2)}, u32[]{:S(2)}) collective-permute-start(f32[8,128]{1,0:T(8,128)S(1)} %add_add_fusion.2), channel_id=1, source_target_pairs={{0,24},{8,16},{16,8},{24,0},{32,56},{40,48},{48,40},{56,32},{64,88... | collective-permute-start | bytes 12296 | tf_op jit(solution)/shard_map/ppermute | solution.py:487
  130.1 2.2 %collective-permute-start.8 = (f32[8,128]{1,0:T(8,128)S(1)}, f32[8,128]{1,0:T(8,128)S(1)}, u32[]{:S(2)}, u32[]{:S(2)}) collective-permute-start(f32[8,128]{1,0:T(8,128)S(1)} %add_add_fusion.2), channel_id=1, source_target_pairs={{0,8},{8,0},{16,24},{24,16},{32,40},{40,32},{48,56},{56,48},{64,72... | collective-permute-start | bytes 12296 | tf_op jit(solution)/shard_map/ppermute | solution.py:487
  133.1 2.2 %collective-permute-done.9 = f32[8,128]{1,0:T(8,128)S(1)} collective-permute-done((f32[8,128]{1,0:T(8,128)S(1)}, f32[8,128]{1,0:T(8,128)S(1)}, u32[]{:S(2)}, u32[]{:S(2)}) %collective-permute-start.9) | collective-permute-done | bytes 4128 | tf_op jit(solution)/shard_map/ppermute | solution.py:487
  135.2 4.2 %collective-permute-start.13 = (f32[8,128]{1,0:T(8,128)S(1)}, f32[8,128]{1,0:T(8,128)S(1)}, u32[]{:S(2)}, u32[]{:S(2)}) collective-permute-start(f32[8,128]{1,0:T(8,128)S(1)} %add_add_fusion.1), channel_id=1, source_target_pairs={{0,96},{8,104},{16,112},{24,120},{32,64},{40,72},{48,80},{56,88},{... | collective-permute-start | bytes 12296 | tf_op jit(solution)/shard_map/ppermute | solution.py:487
  139.4 0.9 collective-permute-start.11
  140.4 2.7 %copy.14 = f32[2,2,62,1800]{3,1,2,0:T(2,128)} copy(f32[2,2,62,1800]{3,2,1,0:T(8,128)S(1)} %get-tuple-element.16) | data formatting | bytes 3571200
  143.1 1.4 collective-permute-done.12
  145.1 1.6 %finish.1 = f32[40,90]{1,0:T(8,128)} custom-call(f32[8,128]{1,0:T(8,128)} %add_add_fusion.moments, f32[3,40,128]{2,1,0:T(8,128)} %copy-done.3), custom_call_target="tpu_custom_call" | custom-call | tf_op jit(solution)/shard_map/finish/pallas_call | solution.py:585
  (27 shorter events, 2.8 us)
Async XLA Ops:
  0.6 2.1 %copy-start.5 = (f32[2,2,62,1800]{3,1,2,0:T(2,128)S(1)}, f32[2,2,62,1800]{3,1,2,0:T(2,128)}, u32[]{:S(2)}) copy-start(f32[2,2,62,1800]{3,1,2,0:T(2,128)} %param.10) | copy-start | bytes 5356804
  2.7 0.7 copy-start
  2.7 0.7 copy-start.1
  2.7 0.7 copy-start.2
  2.7 0.7 copy-start.4
  6.4 3.1 %collective-permute-start = (f32[8,21,8,128]{3,2,1,0:T(8,128)S(1)}, f32[8,21,8,128]{3,2,1,0:T(8,128)S(1)}, u32[]{:S(2)}, u32[]{:S(2)}) collective-permute-start(f32[8,21,8,128]{3,2,1,0:T(8,128)S(1)} %get-tuple-element.9), channel_id=1, source_target_pairs={{0,1},{1,2},{2,3},{3,4},{4,5},{5,6},{6,7},{8,9},{9,10},{10,11},{11... | collective-permute-start | bytes 2064392 | tf_op jit(solution)/shard_map/ppermute | solution.py:538
  7.8 5.8 %collective-permute-start.1 = (f32[8,21,8,128]{3,2,1,0:T(8,128)S(1)}, f32[8,21,8,128]{3,2,1,0:T(8,128)S(1)}, u32[]{:S(2)}, u32[]{:S(2)}) collective-permute-start(f32[8,21,8,128]{3,2,1,0:T(8,128)S(1)} %get-tuple-element.10), channel_id=1, source_target_pairs={{1,0},{2,1},{3,2},{4,3},{5,4},{6,5},{7,6},{9,8},{10,9},{11,10},{12... | collective-permute-start | bytes 2064392 | tf_op jit(solution)/shard_map/ppermute | solution.py:539
  16.5 12.7 %collective-permute-start.2 = (f32[8,13,8,128]{3,2,1,0:T(8,128)S(1)}, f32[8,13,8,128]{3,2,1,0:T(8,128)S(1)}, u32[]{:S(2)}, u32[]{:S(2)}) collective-permute-start(f32[8,13,8,128]{3,2,1,0:T(8,128)S(1)} %get-tuple-element.11), channel_id=1, source_target_pairs={{0,8},{8,16},{16,24},{24,32},{32,40},{40,48},{48,56},{56,64},{64,7... | collective-permute-start | bytes 1277960 | tf_op jit(solution)/shard_map/ppermute | solution.py:552
  18.5 10.7 %collective-permute-start.3 = (f32[8,13,8,128]{3,2,1,0:T(8,128)S(1)}, f32[8,13,8,128]{3,2,1,0:T(8,128)S(1)}, u32[]{:S(2)}, u32[]{:S(2)}) collective-permute-start(f32[8,13,8,128]{3,2,1,0:T(8,128)S(1)} %get-tuple-element.12), channel_id=1, source_target_pairs={{8,0},{16,8},{24,16},{32,24},{40,32},{48,40},{56,48},{64,56},{72,6... | collective-permute-start | bytes 1277960 | tf_op jit(solution)/shard_map/ppermute | solution.py:553
  108.8 36.3 %copy-start.3 = (f32[3,40,128]{2,1,0:T(8,128)}, f32[3,40,128]{2,1,0:T(8,128)S(1)}, u32[]{:S(2)}) copy-start(f32[3,40,128]{2,1,0:T(8,128)S(1)} %get-tuple-element.15.basis) | copy-start | bytes 184324
  108.8 9.0 %collective-permute-start.4 = (f32[8,128]{1,0:T(8,128)S(1)}, f32[8,128]{1,0:T(8,128)S(1)}, u32[]{:S(2)}, u32[]{:S(2)}) collective-permute-start(f32[8,128]{1,0:T(8,128)S(1)} %get-tuple-element.14), channel_id=1, source_target_pairs={{0,1},{1,0},{2,3},{3,2},{4,5},{5,4},{6,7},{7,6},{8,9},{9,8},{10,11... | collective-permute-start | bytes 12296 | tf_op jit(solution)/shard_map/ppermute | solution.py:494
  117.9 6.8 %collective-permute-start.7 = (f32[8,128]{1,0:T(8,128)S(1)}, f32[8,128]{1,0:T(8,128)S(1)}, u32[]{:S(2)}, u32[]{:S(2)}) collective-permute-start(f32[8,128]{1,0:T(8,128)S(1)} %add.30), channel_id=1, source_target_pairs={{0,6},{1,7},{2,4},{3,5},{4,2},{5,3},{6,0},{7,1},{8,14},{9,15},{10,... | collective-permute-start | bytes 12296 | tf_op jit(solution)/shard_map/ppermute | solution.py:487
  119.8 6.4 %collective-permute-start.6 = (f32[8,128]{1,0:T(8,128)S(1)}, f32[8,128]{1,0:T(8,128)S(1)}, u32[]{:S(2)}, u32[]{:S(2)}) collective-permute-start(f32[8,128]{1,0:T(8,128)S(1)} %add.30), channel_id=1, source_target_pairs={{0,4},{1,5},{2,6},{3,7},{4,0},{5,1},{6,2},{7,3},{8,12},{9,13},{10,... | collective-permute-start | bytes 12296 | tf_op jit(solution)/shard_map/ppermute | solution.py:487
  124.6 3.6 %collective-permute-start.5 = (f32[8,128]{1,0:T(8,128)S(1)}, f32[8,128]{1,0:T(8,128)S(1)}, u32[]{:S(2)}, u32[]{:S(2)}) collective-permute-start(f32[8,128]{1,0:T(8,128)S(1)} %add.30), channel_id=1, source_target_pairs={{0,2},{1,3},{2,0},{3,1},{4,6},{5,7},{6,4},{7,5},{8,10},{9,11},{10,... | collective-permute-start | bytes 12296 | tf_op jit(solution)/shard_map/ppermute | solution.py:487
  128.2 4.8 %collective-permute-start.10 = (f32[8,128]{1,0:T(8,128)S(1)}, f32[8,128]{1,0:T(8,128)S(1)}, u32[]{:S(2)}, u32[]{:S(2)}) collective-permute-start(f32[8,128]{1,0:T(8,128)S(1)} %add_add_fusion.2), channel_id=1, source_target_pairs={{0,24},{8,16},{16,8},{24,0},{32,56},{40,48},{48,40},{56,32},{64,88... | collective-permute-start | bytes 12296 | tf_op jit(solution)/shard_map/ppermute | solution.py:487
  130.1 5.1 %collective-permute-start.9 = (f32[8,128]{1,0:T(8,128)S(1)}, f32[8,128]{1,0:T(8,128)S(1)}, u32[]{:S(2)}, u32[]{:S(2)}) collective-permute-start(f32[8,128]{1,0:T(8,128)S(1)} %add_add_fusion.2), channel_id=1, source_target_pairs={{0,16},{8,24},{16,0},{24,8},{32,48},{40,56},{48,32},{56,40},{64,80... | collective-permute-start | bytes 12296 | tf_op jit(solution)/shard_map/ppermute | solution.py:487
  130.1 5.1 %collective-permute-start.8 = (f32[8,128]{1,0:T(8,128)S(1)}, f32[8,128]{1,0:T(8,128)S(1)}, u32[]{:S(2)}, u32[]{:S(2)}) collective-permute-start(f32[8,128]{1,0:T(8,128)S(1)} %add_add_fusion.2), channel_id=1, source_target_pairs={{0,8},{8,0},{16,24},{24,16},{32,40},{40,32},{48,56},{56,48},{64,72... | collective-permute-start | bytes 12296 | tf_op jit(solution)/shard_map/ppermute | solution.py:487
  135.2 7.8 %collective-permute-start.13 = (f32[8,128]{1,0:T(8,128)S(1)}, f32[8,128]{1,0:T(8,128)S(1)}, u32[]{:S(2)}, u32[]{:S(2)}) collective-permute-start(f32[8,128]{1,0:T(8,128)S(1)} %add_add_fusion.1), channel_id=1, source_target_pairs={{0,96},{8,104},{16,112},{24,120},{32,64},{40,72},{48,80},{56,88},{... | collective-permute-start | bytes 12296 | tf_op jit(solution)/shard_map/ppermute | solution.py:487
  139.4 5.1 %collective-permute-start.12 = (f32[8,128]{1,0:T(8,128)S(1)}, f32[8,128]{1,0:T(8,128)S(1)}, u32[]{:S(2)}, u32[]{:S(2)}) collective-permute-start(f32[8,128]{1,0:T(8,128)S(1)} %add_add_fusion.1), channel_id=1, source_target_pairs={{0,64},{8,72},{16,80},{24,88},{32,96},{40,104},{48,112},{56,120},{... | collective-permute-start | bytes 12296 | tf_op jit(solution)/shard_map/ppermute | solution.py:487
  139.4 5.1 %collective-permute-start.11 = (f32[8,128]{1,0:T(8,128)S(1)}, f32[8,128]{1,0:T(8,128)S(1)}, u32[]{:S(2)}, u32[]{:S(2)}) collective-permute-start(f32[8,128]{1,0:T(8,128)S(1)} %add_add_fusion.1), channel_id=1, source_target_pairs={{0,32},{8,40},{16,48},{24,56},{32,0},{40,8},{48,16},{56,24},{64,96... | collective-permute-start | bytes 12296 | tf_op jit(solution)/shard_map/ppermute | solution.py:487

commit v3 on v2

--- a/solution.py
+++ b/solution.py
@@ -16,6 +16,7 @@
 TILES = 8
 REACH = 7
 ROWS = BY + 2 * REACH
+AHEAD = 26
 BASE = 8
 WIDE = 2 * BX
 NS = 21
@@ -287,54 +288,72 @@
         west[0, EW - 1] = merge([(2 * j, 2, turn(t, 2 * j)) for j, t in enumerate(tiles)], lane)
 
 
-def advance(fields, read, write, low, high, levels, shared, lane):
+def staggered(low, high, phases):
+    state = {}
+    rows = range(low, high + 1)
+    for time in range(low, high + 1 + AHEAD * (len(phases) - 1)):
+        for number in reversed(range(len(phases))):
+            row = time - number * AHEAD
+            if row in rows:
+                phases[number](row + REACH, state)
+
+
+def advance(values, fields, out, low, high, levels, shared, scratch):
     depth_east, depth_north, mix = shared
-    zero = jnp.zeros((8, LANES), jnp.float32)
-    row0 = low - 1
-    now = [read(n, row0) for n in range(2)]
-    below = [read(n, row0 - 1) for n in range(2)]
-    wet_north = levels < depth_north[row0 - 1 + REACH]
-    drop = [jnp.where(wet_north, now[n] - below[n], zero) for n in range(2)]
-    scaled = [None, None]
-    flow = [None, None]
-    held = [None, None]
-    gone = None
-    for row in range(row0, high + 2):
-        at = row + REACH
-        wet_east = levels < depth_east[at]
-        wet_north = levels < depth_north[at]
-        mixing = mix[at]
-        above = [read(n, row + 1) for n in range(2)]
-        fresh = []
-        kept = []
+    scaled, held = scratch
+
+    def rise(n, at):
+        return jnp.where(levels < depth_north[at], values[n, at + 1] - values[n, at], 0.0)
+
+    def look_east(at, state):
         for n in range(2):
-            beside = turn(now[n], LANES - 1)
-            step_east = jnp.where(wet_east, beside - now[n], zero)
-            rise = jnp.where(wet_north, above[n] - now[n], zero)
-            lap = (step_east - turn(step_east, 1)) + (rise - drop[n])
-            fresh.append(mixing * lap)
-            drop[n] = rise
-            kept.append(beside + now[n])
-        if row > row0:
-            old_east, old_north, old_row = gone
-            flow_east = fields[2, old_row + REACH]
-            flow_east = flow_east + turn(flow_east, LANES - 1)
-            flow_north = fields[3, old_row + REACH] + fields[3, at]
-            for n in range(2):
-                beside = turn(scaled[n], LANES - 1)
-                east = jnp.where(old_east, flow_east * held[n] + (beside - scaled[n]), zero)
-                north = jnp.where(
-                    old_north, flow_north * (below[n] + now[n]) + (fresh[n] - scaled[n]), zero
-                )
-                if old_row >= low:
-                    out = below[n] - ((east - turn(east, 1)) + (north - flow[n]))
-                    write(n, old_row, out)
-                flow[n] = north
-        gone = (wet_east, wet_north, row)
-        scaled = fresh
-        held = kept
-        below = now
-        now = above
+            state[n, at] = turn(values[n, at], LANES - 1)
+
+    def step_east(at, state):
+        wet = levels < depth_east[at]
+        for n in range(2):
+            here, beside = values[n, at], state[n, at]
+            step = jnp.where(wet, beside - here, 0.0)
+            state[n, at] = step, turn(step, 1)
+            held[n, at] = beside + here
+
+    def scale(at, state):
+        for n in range(2):
+            step, back = state.pop((n, at))
+            drop = state.pop(n) if n in state else rise(n, at - 1)
+            state[n] = rise(n, at)
+            scaled[n, at] = mix[at] * ((step - back) + (state[n] - drop))
+
+    staggered(low - 1, high + 1, (look_east, step_east, scale))
+
+    def north_flow(n, at):
+        flow = fields[3, at] + fields[3, at + 1]
+        step = scaled[n, at + 1] - scaled[n, at]
+        both = flow * (values[n, at] + values[n, at + 1]) + step
+        return jnp.where(levels < depth_north[at], both, 0.0)
+
+    def look_east_again(at, state):
+        flow = fields[2, at]
+        state["flow", at] = turn(flow, LANES - 1)
+        for n in range(2):
+            state[n, at] = turn(scaled[n, at], LANES - 1)
+
+    def east_flow(at, state):
+        wet = levels < depth_east[at]
+        flow = fields[2, at] + state.pop(("flow", at))
+        for n in range(2):
+            both = flow * held[n, at] + (state[n, at] - scaled[n, at])
+            both = jnp.where(wet, both, 0.0)
+            state[n, at] = both, turn(both, 1)
+
+    def change(at, state):
+        for n in range(2):
+            east, back = state.pop((n, at))
+            south = state.pop(n) if n in state else north_flow(n, at - 1)
+            state[n] = north_flow(n, at)
+            out[n, at] = values[n, at] - ((east - back) + (state[n] - south))
+
+    staggered(low, high, (look_east_again, east_flow, change))
 
 
 def surface_operator(values, couple_east, couple_north, damping):
@@ -347,7 +366,7 @@
     block_list, wet_levels, mixing, damping, velocity, tracers,
     up, down, from_west, from_east, up_extra, down_extra, west_extra, east_extra,
     new_tracers, basis, moments,
-    fields, halfway, depth, depth_east, depth_north, mix, forcing, surface, depths, dampings,
+    fields, halfway, scaled, held, depth, depth_east, depth_north, mix, forcing, surface, depths, dampings,
 ):
     lane = lane_ids()
     swap = slot_swap(block_list)
@@ -389,21 +408,9 @@
     levels = (lax.broadcasted_iota(jnp.int32, (8, LANES), 0) + 8 * step).astype(jnp.float32)
     shared = (depth_east, depth_north, mix)
 
-    def read_first(n, row):
-        return fields[n, row + REACH]
-
-    def write_first(n, row, value):
-        halfway[n, row + REACH] = value
-
-    advance(fields, read_first, write_first, -5, 44, levels, shared, lane)
-
-    def read_second(n, row):
-        return halfway[n, row + REACH]
-
-    def write_second(n, row, value):
-        fields[n, row + REACH] = value
-
-    advance(fields, read_second, write_second, -3, 42, levels, shared, lane)
+    scratch = (scaled, held)
+    advance(fields, fields, halfway, -5, 44, levels, shared, scratch)
+    advance(halfway, fields, fields, -3, 42, levels, shared, scratch)
 
     for row in range(-3, 43):
         at = row + REACH
@@ -568,6 +575,8 @@
         scratch_shapes=[
             pltpu.VMEM((4, ROWS, 8, LANES), f32),
             pltpu.VMEM((2, ROWS, 8, LANES), f32),
+            pltpu.VMEM((2, ROWS, 8, LANES), f32),
+            pltpu.VMEM((2, ROWS, 8, LANES), f32),
             row_store,
             row_store,
             row_store,

time: 147 us -> 94.3 us (0.64)
  Pallas kernels: 87.1 us -> 34.4 us
    pallas_call x1, Pallas kernels: 79.6 us -> 27 us  [per_device(): pl.pallas_call(main_kernel, grid=(TILES,), in_specs=own_specs + [rows_blo...]
  transfers between devices with their start and end apart: 14 -> 14, of which waited for: 9 -> 9; matrix products, arithmetic and copies ran while one was open for 2% -> 3% of each run, Pallas kernels for 0% -> 0%
where the time goes in v3:
time: 94.3 us; the launch traced here: 94.1 us
  Pallas kernels  34.4 us (36%)
  starting transfers between devices  33.5 us (36%)
  waiting for transfers between devices  19.3 us (20%)
  local copies, waits for them, and re-layouts  5.54 us (6%)
    pallas_call x1, Pallas kernels, per_device(): pl.pallas_call(main_kernel, grid=(TILES,), in_specs=own_specs + [rows_blo...  27 us
    ppermute x9, starting transfers between devices, quad_sum(): lax.ppermute(values, axis, [(i, partner(i, turn)) for i in range(count)])  16 us
    ppermute x1, starting transfers between devices, total_over_devices(): lax.ppermute(values, 'gy', [(i, i ^ 1) for i in range(lax.axis_size('gy'))])  8.22 us
    ppermute x9, waiting for transfers between devices, quad_sum(): lax.ppermute(values, axis, [(i, partner(i, turn)) for i in range(count)])  7.95 us
    ppermute x1, waiting for transfers between devices, per_device(): lax.ppermute(east, 'gx', [(i, (i + 1) % columns_total) for i in range(col...  6.03 us
    unnamed x15, local copies, waits for them, and re-layouts  5.54 us
    ppermute x1, starting transfers between devices, per_device(): lax.ppermute(west, 'gx', [((i + 1) % columns_total, i) for i in range(col...  4.65 us
    ppermute x1, waiting for transfers between devices, per_device(): down = lax.ppermute(down, 'gy', [(i + 1, i) for i in range(rows_total - 1)])  4.09 us
  transfers between devices with their start and end apart: 14, of which 9 were waited for; matrix products, arithmetic and copies ran while one was open for 3% of the time, Pallas kernels for 0%

profile of v3, /device:TPU:0, one launch (start us, length us, event | category | flops | bytes accessed | tf_op | source)
XLA Modules:
  0.0 94.1 jit_solution(9170382614553919289)
XLA Ops:
  0.6 1.8 %copy.12.velocity = f32[2,2,62,1800]{3,2,1,0:T(8,128)S(1)} copy(f32[2,2,62,1800]{3,1,2,0:T(2,128)} %param.9) | data formatting | bytes 3571200 | tf_op args[3]
  3.5 3.0 %pack_rows.1 = (f32[8,21,8,128]{3,2,1,0:T(8,128)S(1)}, f32[8,21,8,128]{3,2,1,0:T(8,128)S(1)}) custom-call(s32[2]{0:T(128)S(1)} %copy-done.4, s32[2,1800]{1,0:T(2,128)S(1)} %copy-done.1, f32[2,1800]{1,0:T(2,128)S(1)} %copy-done.2, f32[40,90]{1,0:T(8,128)S(1)} %copy-done, f32[2,2,62,1800]{3,2,1,0:T(8,128)S(1)} %copy.12.velocity, ...), custom_call_target="tpu_custom_call" | custom-call | tf_op jit(solution)/shard_map/pack_rows/pallas_call | solution.py:534
  6.4 1.3 %collective-permute-start = (f32[8,21,8,128]{3,2,1,0:T(8,128)S(1)}, f32[8,21,8,128]{3,2,1,0:T(8,128)S(1)}, u32[]{:S(2)}, u32[]{:S(2)}) collective-permute-start(f32[8,21,8,128]{3,2,1,0:T(8,128)S(1)} %get-tuple-element.9), channel_id=1, source_target_pairs={{0,1},{1,2},{2,3},{3,4},{4,5},{5,6},{6,7},{8,9},{9,10},{10,11},{11... | collective-permute-start | bytes 2064392 | tf_op jit(solution)/shard_map/ppermute | solution.py:545
  7.8 1.3 %collective-permute-start.1 = (f32[8,21,8,128]{3,2,1,0:T(8,128)S(1)}, f32[8,21,8,128]{3,2,1,0:T(8,128)S(1)}, u32[]{:S(2)}, u32[]{:S(2)}) collective-permute-start(f32[8,21,8,128]{3,2,1,0:T(8,128)S(1)} %get-tuple-element.10), channel_id=1, source_target_pairs={{1,0},{2,1},{3,2},{4,3},{5,4},{6,5},{7,6},{9,8},{10,9},{11,10},{12... | collective-permute-start | bytes 2064392 | tf_op jit(solution)/shard_map/ppermute | solution.py:546
  9.5 4.1 %collective-permute-done.1.down.down_extra = f32[8,21,8,128]{3,2,1,0:T(8,128)S(1)} collective-permute-done((f32[8,21,8,128]{3,2,1,0:T(8,128)S(1)}, f32[8,21,8,128]{3,2,1,0:T(8,128)S(1)}, u32[]{:S(2)}, u32[]{:S(2)}) %collective-permute-start.1) | collective-permute-done | bytes 688160 | tf_op jit(solution)/shard_map/ppermute | solution.py:546
  13.6 2.9 %pack_columns.1 = (f32[8,13,8,128]{3,2,1,0:T(8,128)S(1)}, f32[8,13,8,128]{3,2,1,0:T(8,128)S(1)}) custom-call(s32[2]{0:T(128)S(1)} %copy-done.4, s32[2,1800]{1,0:T(2,128)S(1)} %copy-done.1, f32[2,1800]{1,0:T(2,128)S(1)} %copy-done.2, f32[40,90]{1,0:T(8,128)S(1)} %copy-done, f32[2,2,62,1800]{3,2,1,0:T(8,128)S(1)} %copy.12.velocity, ...), custom_call_target="tpu_custom_call" | custom-call | tf_op jit(solution)/shard_map/pack_columns/pallas_call | solution.py:548
  16.5 2.0 %collective-permute-start.2 = (f32[8,13,8,128]{3,2,1,0:T(8,128)S(1)}, f32[8,13,8,128]{3,2,1,0:T(8,128)S(1)}, u32[]{:S(2)}, u32[]{:S(2)}) collective-permute-start(f32[8,13,8,128]{3,2,1,0:T(8,128)S(1)} %get-tuple-element.11), channel_id=1, source_target_pairs={{0,8},{8,16},{16,24},{24,32},{32,40},{40,48},{48,56},{56,64},{64,7... | collective-permute-start | bytes 1277960 | tf_op jit(solution)/shard_map/ppermute | solution.py:559
  18.5 4.7 %collective-permute-start.3 = (f32[8,13,8,128]{3,2,1,0:T(8,128)S(1)}, f32[8,13,8,128]{3,2,1,0:T(8,128)S(1)}, u32[]{:S(2)}, u32[]{:S(2)}) collective-permute-start(f32[8,13,8,128]{3,2,1,0:T(8,128)S(1)} %get-tuple-element.12), channel_id=1, source_target_pairs={{8,0},{16,8},{24,16},{32,24},{40,32},{48,40},{56,48},{64,56},{72,6... | collective-permute-start | bytes 1277960 | tf_op jit(solution)/shard_map/ppermute | solution.py:560
  23.2 6.0 %collective-permute-done.2.from_west.west_extra = f32[8,13,8,128]{3,2,1,0:T(8,128)S(1)} collective-permute-done((f32[8,13,8,128]{3,2,1,0:T(8,128)S(1)}, f32[8,13,8,128]{3,2,1,0:T(8,128)S(1)}, u32[]{:S(2)}, u32[]{:S(2)}) %collective-permute-start.2) | collective-permute-done | bytes 426016 | tf_op jit(solution)/shard_map/ppermute | solution.py:559
  29.2 27.0 %advance.1 = (f32[2,2,62,1800]{3,2,1,0:T(8,128)S(1)}, f32[3,40,128]{2,1,0:T(8,128)S(1)}, f32[8,128]{1,0:T(8,128)S(1)}) custom-call(s32[2]{0:T(128)S(1)} %copy-done.4, s32[2,1800]{1,0:T(2,128)S(1)} %copy-done.1, f32[2,1800]{1,0:T(2,128)S(1)} %copy-done.2, f32[40,90]{1,0:T(8,128)S(1)} %copy-done, f32[2,2,62,1800]{3,2,1,0:T(8,128)S(1)} %copy.12.velocity, ...), custom_call_target="tpu_custom_call" | custom-call | tf_op jit(solution)/shard_map/advance/pallas_call | solution.py:563
  56.2 8.2 %collective-permute-start.4 = (f32[8,128]{1,0:T(8,128)S(1)}, f32[8,128]{1,0:T(8,128)S(1)}, u32[]{:S(2)}, u32[]{:S(2)}) collective-permute-start(f32[8,128]{1,0:T(8,128)S(1)} %get-tuple-element.14), channel_id=1, source_target_pairs={{0,1},{1,0},{2,3},{3,2},{4,5},{5,4},{6,7},{7,6},{8,9},{9,8},{10,11... | collective-permute-start | bytes 12296 | tf_op jit(solution)/shard_map/ppermute | solution.py:501
  64.4 0.8 collective-permute-done.4
  65.2 1.9 %collective-permute-start.7 = (f32[8,128]{1,0:T(8,128)S(1)}, f32[8,128]{1,0:T(8,128)S(1)}, u32[]{:S(2)}, u32[]{:S(2)}) collective-permute-start(f32[8,128]{1,0:T(8,128)S(1)} %add.30), channel_id=1, source_target_pairs={{0,6},{1,7},{2,4},{3,5},{4,2},{5,3},{6,0},{7,1},{8,14},{9,15},{10,... | collective-permute-start | bytes 12296 | tf_op jit(solution)/shard_map/ppermute | solution.py:494
  67.1 4.8 %collective-permute-start.6 = (f32[8,128]{1,0:T(8,128)S(1)}, f32[8,128]{1,0:T(8,128)S(1)}, u32[]{:S(2)}, u32[]{:S(2)}) collective-permute-start(f32[8,128]{1,0:T(8,128)S(1)} %add.30), channel_id=1, source_target_pairs={{0,4},{1,5},{2,6},{3,7},{4,0},{5,1},{6,2},{7,3},{8,12},{9,13},{10,... | collective-permute-start | bytes 12296 | tf_op jit(solution)/shard_map/ppermute | solution.py:494
  72.0 1.6 %collective-permute-done.6 = f32[8,128]{1,0:T(8,128)S(1)} collective-permute-done((f32[8,128]{1,0:T(8,128)S(1)}, f32[8,128]{1,0:T(8,128)S(1)}, u32[]{:S(2)}, u32[]{:S(2)}) %collective-permute-start.6) | collective-permute-done | bytes 4128 | tf_op jit(solution)/shard_map/ppermute | solution.py:494
  73.5 2.0 %collective-permute-done.5 = f32[8,128]{1,0:T(8,128)S(1)} collective-permute-done((f32[8,128]{1,0:T(8,128)S(1)}, f32[8,128]{1,0:T(8,128)S(1)}, u32[]{:S(2)}, u32[]{:S(2)}) %collective-permute-start.5) | collective-permute-done | bytes 4128 | tf_op jit(solution)/shard_map/ppermute | solution.py:494
  75.6 1.9 %collective-permute-start.10 = (f32[8,128]{1,0:T(8,128)S(1)}, f32[8,128]{1,0:T(8,128)S(1)}, u32[]{:S(2)}, u32[]{:S(2)}) collective-permute-start(f32[8,128]{1,0:T(8,128)S(1)} %add_add_fusion.2), channel_id=1, source_target_pairs={{0,24},{8,16},{16,8},{24,0},{32,56},{40,48},{48,40},{56,32},{64,88... | collective-permute-start | bytes 12296 | tf_op jit(solution)/shard_map/ppermute | solution.py:494
  77.5 2.2 %collective-permute-start.8 = (f32[8,128]{1,0:T(8,128)S(1)}, f32[8,128]{1,0:T(8,128)S(1)}, u32[]{:S(2)}, u32[]{:S(2)}) collective-permute-start(f32[8,128]{1,0:T(8,128)S(1)} %add_add_fusion.2), channel_id=1, source_target_pairs={{0,8},{8,0},{16,24},{24,16},{32,40},{40,32},{48,56},{56,48},{64,72... | collective-permute-start | bytes 12296 | tf_op jit(solution)/shard_map/ppermute | solution.py:494
  80.4 2.2 %collective-permute-done.9 = f32[8,128]{1,0:T(8,128)S(1)} collective-permute-done((f32[8,128]{1,0:T(8,128)S(1)}, f32[8,128]{1,0:T(8,128)S(1)}, u32[]{:S(2)}, u32[]{:S(2)}) %collective-permute-start.9) | collective-permute-done | bytes 4128 | tf_op jit(solution)/shard_map/ppermute | solution.py:494
  82.6 4.2 %collective-permute-start.13 = (f32[8,128]{1,0:T(8,128)S(1)}, f32[8,128]{1,0:T(8,128)S(1)}, u32[]{:S(2)}, u32[]{:S(2)}) collective-permute-start(f32[8,128]{1,0:T(8,128)S(1)} %add_add_fusion.1), channel_id=1, source_target_pairs={{0,96},{8,104},{16,112},{24,120},{32,64},{40,72},{48,80},{56,88},{... | collective-permute-start | bytes 12296 | tf_op jit(solution)/shard_map/ppermute | solution.py:494
  86.8 0.9 %collective-permute-start.11 = (f32[8,128]{1,0:T(8,128)S(1)}, f32[8,128]{1,0:T(8,128)S(1)}, u32[]{:S(2)}, u32[]{:S(2)}) collective-permute-start(f32[8,128]{1,0:T(8,128)S(1)} %add_add_fusion.1), channel_id=1, source_target_pairs={{0,32},{8,40},{16,48},{24,56},{32,0},{40,8},{48,16},{56,24},{64,96... | collective-permute-start | bytes 12296 | tf_op jit(solution)/shard_map/ppermute | solution.py:494
  87.7 2.7 %copy.14 = f32[2,2,62,1800]{3,1,2,0:T(2,128)} copy(f32[2,2,62,1800]{3,2,1,0:T(8,128)S(1)} %get-tuple-element.16) | data formatting | bytes 3571200
  90.4 1.4 %collective-permute-done.12 = f32[8,128]{1,0:T(8,128)S(1)} collective-permute-done((f32[8,128]{1,0:T(8,128)S(1)}, f32[8,128]{1,0:T(8,128)S(1)}, u32[]{:S(2)}, u32[]{:S(2)}) %collective-permute-start.12) | collective-permute-done | bytes 4128 | tf_op jit(solution)/shard_map/ppermute | solution.py:494
  92.5 1.6 %finish.1 = f32[40,90]{1,0:T(8,128)} custom-call(f32[8,128]{1,0:T(8,128)} %add_add_fusion.moments, f32[3,40,128]{2,1,0:T(8,128)} %copy-done.3), custom_call_target="tpu_custom_call" | custom-call | tf_op jit(solution)/shard_map/finish/pallas_call | solution.py:594
  (27 shorter events, 2.8 us)
Async XLA Ops:
  0.6 2.1 %copy-start.5 = (f32[2,2,62,1800]{3,1,2,0:T(2,128)S(1)}, f32[2,2,62,1800]{3,1,2,0:T(2,128)}, u32[]{:S(2)}) copy-start(f32[2,2,62,1800]{3,1,2,0:T(2,128)} %param.10) | copy-start | bytes 5356804
  2.7 0.7 copy-start
  2.7 0.7 copy-start.1
  2.7 0.7 copy-start.2
  2.7 0.7 copy-start.4
  6.4 3.1 %collective-permute-start = (f32[8,21,8,128]{3,2,1,0:T(8,128)S(1)}, f32[8,21,8,128]{3,2,1,0:T(8,128)S(1)}, u32[]{:S(2)}, u32[]{:S(2)}) collective-permute-start(f32[8,21,8,128]{3,2,1,0:T(8,128)S(1)} %get-tuple-element.9), channel_id=1, source_target_pairs={{0,1},{1,2},{2,3},{3,4},{4,5},{5,6},{6,7},{8,9},{9,10},{10,11},{11... | collective-permute-start | bytes 2064392 | tf_op jit(solution)/shard_map/ppermute | solution.py:545
  7.8 5.8 %collective-permute-start.1 = (f32[8,21,8,128]{3,2,1,0:T(8,128)S(1)}, f32[8,21,8,128]{3,2,1,0:T(8,128)S(1)}, u32[]{:S(2)}, u32[]{:S(2)}) collective-permute-start(f32[8,21,8,128]{3,2,1,0:T(8,128)S(1)} %get-tuple-element.10), channel_id=1, source_target_pairs={{1,0},{2,1},{3,2},{4,3},{5,4},{6,5},{7,6},{9,8},{10,9},{11,10},{12... | collective-permute-start | bytes 2064392 | tf_op jit(solution)/shard_map/ppermute | solution.py:546
  16.5 12.7 %collective-permute-start.2 = (f32[8,13,8,128]{3,2,1,0:T(8,128)S(1)}, f32[8,13,8,128]{3,2,1,0:T(8,128)S(1)}, u32[]{:S(2)}, u32[]{:S(2)}) collective-permute-start(f32[8,13,8,128]{3,2,1,0:T(8,128)S(1)} %get-tuple-element.11), channel_id=1, source_target_pairs={{0,8},{8,16},{16,24},{24,32},{32,40},{40,48},{48,56},{56,64},{64,7... | collective-permute-start | bytes 1277960 | tf_op jit(solution)/shard_map/ppermute | solution.py:559
  18.5 10.7 %collective-permute-start.3 = (f32[8,13,8,128]{3,2,1,0:T(8,128)S(1)}, f32[8,13,8,128]{3,2,1,0:T(8,128)S(1)}, u32[]{:S(2)}, u32[]{:S(2)}) collective-permute-start(f32[8,13,8,128]{3,2,1,0:T(8,128)S(1)} %get-tuple-element.12), channel_id=1, source_target_pairs={{8,0},{16,8},{24,16},{32,24},{40,32},{48,40},{56,48},{64,56},{72,6... | collective-permute-start | bytes 1277960 | tf_op jit(solution)/shard_map/ppermute | solution.py:560
  56.1 36.3 %copy-start.3 = (f32[3,40,128]{2,1,0:T(8,128)}, f32[3,40,128]{2,1,0:T(8,128)S(1)}, u32[]{:S(2)}) copy-start(f32[3,40,128]{2,1,0:T(8,128)S(1)} %get-tuple-element.15.basis) | copy-start | bytes 184324
  56.2 9.0 %collective-permute-start.4 = (f32[8,128]{1,0:T(8,128)S(1)}, f32[8,128]{1,0:T(8,128)S(1)}, u32[]{:S(2)}, u32[]{:S(2)}) collective-permute-start(f32[8,128]{1,0:T(8,128)S(1)} %get-tuple-element.14), channel_id=1, source_target_pairs={{0,1},{1,0},{2,3},{3,2},{4,5},{5,4},{6,7},{7,6},{8,9},{9,8},{10,11... | collective-permute-start | bytes 12296 | tf_op jit(solution)/shard_map/ppermute | solution.py:501
  65.2 6.8 %collective-permute-start.7 = (f32[8,128]{1,0:T(8,128)S(1)}, f32[8,128]{1,0:T(8,128)S(1)}, u32[]{:S(2)}, u32[]{:S(2)}) collective-permute-start(f32[8,128]{1,0:T(8,128)S(1)} %add.30), channel_id=1, source_target_pairs={{0,6},{1,7},{2,4},{3,5},{4,2},{5,3},{6,0},{7,1},{8,14},{9,15},{10,... | collective-permute-start | bytes 12296 | tf_op jit(solution)/shard_map/ppermute | solution.py:494
  67.1 6.4 %collective-permute-start.6 = (f32[8,128]{1,0:T(8,128)S(1)}, f32[8,128]{1,0:T(8,128)S(1)}, u32[]{:S(2)}, u32[]{:S(2)}) collective-permute-start(f32[8,128]{1,0:T(8,128)S(1)} %add.30), channel_id=1, source_target_pairs={{0,4},{1,5},{2,6},{3,7},{4,0},{5,1},{6,2},{7,3},{8,12},{9,13},{10,... | collective-permute-start | bytes 12296 | tf_op jit(solution)/shard_map/ppermute | solution.py:494
  72.0 3.6 %collective-permute-start.5 = (f32[8,128]{1,0:T(8,128)S(1)}, f32[8,128]{1,0:T(8,128)S(1)}, u32[]{:S(2)}, u32[]{:S(2)}) collective-permute-start(f32[8,128]{1,0:T(8,128)S(1)} %add.30), channel_id=1, source_target_pairs={{0,2},{1,3},{2,0},{3,1},{4,6},{5,7},{6,4},{7,5},{8,10},{9,11},{10,... | collective-permute-start | bytes 12296 | tf_op jit(solution)/shard_map/ppermute | solution.py:494
  75.6 4.8 %collective-permute-start.10 = (f32[8,128]{1,0:T(8,128)S(1)}, f32[8,128]{1,0:T(8,128)S(1)}, u32[]{:S(2)}, u32[]{:S(2)}) collective-permute-start(f32[8,128]{1,0:T(8,128)S(1)} %add_add_fusion.2), channel_id=1, source_target_pairs={{0,24},{8,16},{16,8},{24,0},{32,56},{40,48},{48,40},{56,32},{64,88... | collective-permute-start | bytes 12296 | tf_op jit(solution)/shard_map/ppermute | solution.py:494
  77.5 5.1 %collective-permute-start.9 = (f32[8,128]{1,0:T(8,128)S(1)}, f32[8,128]{1,0:T(8,128)S(1)}, u32[]{:S(2)}, u32[]{:S(2)}) collective-permute-start(f32[8,128]{1,0:T(8,128)S(1)} %add_add_fusion.2), channel_id=1, source_target_pairs={{0,16},{8,24},{16,0},{24,8},{32,48},{40,56},{48,32},{56,40},{64,80... | collective-permute-start | bytes 12296 | tf_op jit(solution)/shard_map/ppermute | solution.py:494
  77.5 5.1 %collective-permute-start.8 = (f32[8,128]{1,0:T(8,128)S(1)}, f32[8,128]{1,0:T(8,128)S(1)}, u32[]{:S(2)}, u32[]{:S(2)}) collective-permute-start(f32[8,128]{1,0:T(8,128)S(1)} %add_add_fusion.2), channel_id=1, source_target_pairs={{0,8},{8,0},{16,24},{24,16},{32,40},{40,32},{48,56},{56,48},{64,72... | collective-permute-start | bytes 12296 | tf_op jit(solution)/shard_map/ppermute | solution.py:494
  82.6 7.8 %collective-permute-start.13 = (f32[8,128]{1,0:T(8,128)S(1)}, f32[8,128]{1,0:T(8,128)S(1)}, u32[]{:S(2)}, u32[]{:S(2)}) collective-permute-start(f32[8,128]{1,0:T(8,128)S(1)} %add_add_fusion.1), channel_id=1, source_target_pairs={{0,96},{8,104},{16,112},{24,120},{32,64},{40,72},{48,80},{56,88},{... | collective-permute-start | bytes 12296 | tf_op jit(solution)/shard_map/ppermute | solution.py:494
  86.8 5.1 %collective-permute-start.12 = (f32[8,128]{1,0:T(8,128)S(1)}, f32[8,128]{1,0:T(8,128)S(1)}, u32[]{:S(2)}, u32[]{:S(2)}) collective-permute-start(f32[8,128]{1,0:T(8,128)S(1)} %add_add_fusion.1), channel_id=1, source_target_pairs={{0,64},{8,72},{16,80},{24,88},{32,96},{40,104},{48,112},{56,120},{... | collective-permute-start | bytes 12296 | tf_op jit(solution)/shard_map/ppermute | solution.py:494
  86.8 5.1 %collective-permute-start.11 = (f32[8,128]{1,0:T(8,128)S(1)}, f32[8,128]{1,0:T(8,128)S(1)}, u32[]{:S(2)}, u32[]{:S(2)}) collective-permute-start(f32[8,128]{1,0:T(8,128)S(1)} %add_add_fusion.1), channel_id=1, source_target_pairs={{0,32},{8,40},{16,48},{24,56},{32,0},{40,8},{48,16},{56,24},{64,96... | collective-permute-start | bytes 12296 | tf_op jit(solution)/shard_map/ppermute | solution.py:494

commit v4 on v3

v4 whole, which is shorter than its diff:
```python
import functools
import math

import jax
import jax.numpy as jnp
from jax import lax
from jax.experimental import pallas as pl
from jax.experimental.pallas import tpu as pltpu
from jax.sharding import PartitionSpec as P

BX = 45
BY = 40
CELLS = BX * BY
LEVELS = 62
LANES = 128
TILES = 8
REACH = 7
ROWS = BY + 2 * REACH
AHEAD = 26
BASE = 8
WIDE = 2 * BX
NS = 29
EW = 13
SURFACE = 56

advect_rate = 0.25
mixing_rate = 0.015
salt_weight = 0.8


def lane_ids():
    return lax.broadcasted_iota(jnp.int32, (8, LANES), 1)


def merge(parts, lane):
    flat = []
    for low, width, value in parts:
        low %= LANES
        if low + width > LANES:
            flat.append((low, value))
            flat.append((0, value))
        else:
            flat.append((low, value))
    flat.sort(key=lambda part: part[0])
    result = flat[0][1]
    last = result
    for low, value in flat[1:]:
        if value is last:
            continue
        result = jnp.where(lane >= low, value, result)
        last = value
    return result


def turn(value, shift):
    shift %= LANES
    return pltpu.roll(value, shift, 1) if shift else value


class Source:
    def __init__(self, own, west=None, east=None):
        self.load = {"own": own, "west": west, "east": east}
        self.kept = {}

    def tile(self, kind, position, number):
        key = (kind, position, number)
        if key not in self.kept:
            load = self.load[kind]
            self.kept[key] = load(position, number) if kind == "own" else load(number)
        return self.kept[key]

    def cells(self, position, start, width):
        parts = []
        at = start
        while at < start + width:
            number = at // LANES
            end = min(start + width, (number + 1) * LANES)
            parts.append((at, end - at, self.tile("own", position, number)))
            at = end
        return parts


def pack_columns(source, lane):
    east, west = [], []
    for group in range(3):
        rows = range(17 * group, min(17 * group + 17, BY))
        east.append(merge([c for r in rows for c in source.cells(1, BX * r + BX - REACH, REACH)], lane))
        west.append(merge([c for r in rows for c in source.cells(0, BX * r, REACH)], lane))
    return east, west


def strip_rows(source, lane):
    turned = {}

    def combined(r):
        if r in turned:
            return turned[r]
        parts = []
        if 0 <= r - 1 < BY:
            parts.append((BX * r - REACH, REACH, source.tile("west", 0, (r - 1) // 17)))
        if 0 <= r < BY:
            parts += source.cells(0, BX * r, BX)
        if 0 <= r + 1 < BY:
            parts += source.cells(1, BX * (r + 1), BX)
        if 0 <= r + 2 < BY:
            parts.append((BX * (r + 2), REACH, source.tile("east", 0, (r + 2) // 17)))
        turned[r] = turn(merge(parts, lane), BASE - BX * r)
        return turned[r]

    for row in range(BY):
        value = jnp.where(lane < BASE, combined(row + 1), combined(row))
        value = jnp.where(lane < BASE + BX, value, combined(row - 1))
        yield row, jnp.where(lane < BASE + WIDE, value, combined(row - 2))


def slot_swap(block_list):
    first = block_list[0]
    return jnp.where(first >= 0, first & 1, 1 - (block_list[1] & 1))


def field_loader(ref, which, swap):
    def load(position, number):
        slot = swap if position == 0 else 1 - swap
        if number < 14:
            return ref[slot, which, :, number * LANES : (number + 1) * LANES]
        return turn(ref[slot, which, :, CELLS - LANES : CELLS], CELLS % LANES)

    return load


def column_loader(wet_levels, mixing, swap):
    def load(position, number):
        slot = swap if position == 0 else 1 - swap
        low = number * LANES if number < 14 else CELLS - LANES
        both = wet_levels[:, low : low + LANES].astype(jnp.float32)
        depth = jnp.where(slot == 0, both[0:1, :], both[1:2, :])
        both = mixing[:, low : low + LANES]
        mix = jnp.where(slot == 0, both[0:1, :], both[1:2, :])
        sublane = lax.broadcasted_iota(jnp.int32, (8, LANES), 0)
        value = jnp.where(
            sublane == 0, jnp.broadcast_to(depth, (8, LANES)), jnp.broadcast_to(mix, (8, LANES))
        )
        return value if number < 14 else turn(value, CELLS % LANES)

    return load


def columns_kernel(block_list, wet_levels, mixing, damping, velocity, tracers, east, west, padded):
    lane = lane_ids()
    swap = slot_swap(block_list)
    step = pl.program_id(0)
    for field in range(4):
        source = Source(field_loader(tracers if field < 2 else velocity, field % 2, swap))
        easts, wests = pack_columns(source, lane)
        for number in range(3):
            east[0, 3 * field + number] = easts[number]
            west[0, 3 * field + number] = wests[number]

    for number in range(3):

        @pl.when(step == number)
        def _():
            easts, wests = pack_columns(Source(column_loader(wet_levels, mixing, swap)), lane)
            east[0, EW - 1] = easts[number]
            west[0, EW - 1] = wests[number]

    @pl.when(step >= 3)
    def _():
        padded[...] = jnp.zeros_like(padded)
        padded[:, 0:WIDE] = damping[...]
        tiles = [padded[8 * j : 8 * j + 8, :] for j in range(5)]
        east[0, EW - 1] = merge([(2 * j, 2, turn(t, 2 * j - WIDE + 2)) for j, t in enumerate(tiles)], lane)
        west[0, EW - 1] = merge([(2 * j, 2, turn(t, 2 * j)) for j, t in enumerate(tiles)], lane)


def strips_kernel(
    block_list, wet_levels, mixing, damping, velocity, tracers,
    from_west, from_east, west_extra, east_extra,
    fields, columns, up, down, padded,
):
    lane = lane_ids()
    swap = slot_swap(block_list)
    step = pl.program_id(0)

    @pl.when(step == 0)
    def _():
        padded[...] = jnp.zeros_like(padded)
        padded[:, 0:WIDE] = damping[...]
        for j in range(5):
            value = turn(padded[8 * j : 8 * j + 8, :], BASE)
            value = jnp.where(lane < BASE, turn(west_extra[3, 0], BASE - 2 - 2 * j), value)
            value = jnp.where(lane < BASE + WIDE, value, turn(east_extra[3, 0], BASE + WIDE - 2 * j))
            padded[8 * j : 8 * j + 8, :] = value
        source = Source(
            column_loader(wet_levels, mixing, swap),
            lambda tile: west_extra[tile, 0],
            lambda tile: east_extra[tile, 0],
        )
        sublane = lax.broadcasted_iota(jnp.int32, (8, LANES), 0)
        for row, value in strip_rows(source, lane):
            damp = jnp.broadcast_to(padded[row : row + 1, :], (8, LANES))
            columns[row] = jnp.where(sublane == 2, damp, value)

    for field in range(4):
        source = Source(
            field_loader(tracers if field < 2 else velocity, field % 2, swap),
            lambda number, field=field: from_west[0, 3 * field + number],
            lambda number, field=field: from_east[0, 3 * field + number],
        )
        for row, value in strip_rows(source, lane):
            value = value if field < 2 else (0.25 * advect_rate) * value
            fields[0, field, row] = value
            if row < REACH:
                down[0, REACH * field + row] = value
            if row >= BY - REACH:
                up[0, REACH * field + row - (BY - REACH)] = value
    row = jnp.minimum(step, REACH - 1)
    down[0, NS - 1] = columns[row]
    up[0, NS - 1] = columns[BY - REACH + row]


def staggered(spans, phases):
    state = {}
    length = max(high - low + 1 for low, high in spans)
    ahead = min(AHEAD, length)
    for time in range(length + ahead * (len(phases) - 1)):
        for number in reversed(range(len(phases))):
            for span, (low, high) in enumerate(spans):
                row = low + time - number * ahead
                if low <= row <= high:
                    phases[number](span, row, state)


class Band:
    def __init__(self, low, high, read, write, eastward, northward):
        self.low, self.high, self.read, self.write = low, high, read, write
        self.eastward, self.northward = eastward, northward


def advance(bands, levels, shared, scratch):
    depth_east, depth_north, mix = shared
    scaled, held = scratch

    def rise(band, n, row):
        read = bands[band].read
        return jnp.where(levels < depth_north(row), read(n, row + 1) - read(n, row), 0.0)

    def look_east(band, row, state):
        for n in range(2):
            state[band, n, row] = turn(bands[band].read(n, row), LANES - 1)

    def step_east(band, row, state):
        wet = levels < depth_east(row)
        for n in range(2):
            here, beside = bands[band].read(n, row), state[band, n, row]
            step = jnp.where(wet, beside - here, 0.0)
            state[band, n, row] = step, turn(step, 1)
            held[n, row + REACH] = beside + here

    def scale(band, row, state):
        for n in range(2):
            step, back = state.pop((band, n, row))
            drop = state.pop((band, n)) if (band, n) in state else rise(band, n, row - 1)
            state[band, n] = rise(band, n, row)
            scaled[n, row + REACH] = mix(row) * ((step - back) + (state[band, n] - drop))

    staggered([(b.low - 1, b.high + 1) for b in bands], (look_east, step_east, scale))

    def north_flow(band, n, row):
        read, northward = bands[band].read, bands[band].northward
        step = scaled[n, row + 1 + REACH] - scaled[n, row + REACH]
        both = (northward(row) + northward(row + 1)) * (read(n, row) + read(n, row + 1)) + step
        return jnp.where(levels < depth_north(row), both, 0.0)

    def look_east_again(band, row, state):
        state[band, "flow", row] = turn(bands[band].eastward(row), LANES - 1)
        for n in range(2):
            state[band, n, row] = turn(scaled[n, row + REACH], LANES - 1)

    def east_flow(band, row, state):
        wet = levels < depth_east(row)
        flow = bands[band].eastward(row) + state.pop((band, "flow", row))
        for n in range(2):
            at = row + REACH
            both = flow * held[n, at] + (state[band, n, row] - scaled[n, at])
            both = jnp.where(wet, both, 0.0)
            state[band, n, row] = both, turn(both, 1)

    def change(band, row, state):
        for n in range(2):
            east, back = state.pop((band, n, row))
            south = state.pop((band, n)) if (band, n) in state else north_flow(band, n, row - 1)
            state[band, n] = north_flow(band, n, row)
            result = bands[band].read(n, row) - ((east - back) + (state[band, n] - south))
            bands[band].write(n, row, result)

    staggered([(b.low, b.high) for b in bands], (look_east_again, east_flow, change))


def level_ids(step):
    return (lax.broadcasted_iota(jnp.int32, (8, LANES), 0) + 8 * step).astype(jnp.float32)


def spread_columns(column, rows, depth, depth_east, depth_north, mix):
    last = None
    for row in rows:
        value = column(row)
        here = jnp.broadcast_to(value[0:1, :], (8, LANES))
        depth[row + REACH] = here
        depth_east[row + REACH] = jnp.minimum(here, turn(here, LANES - 1))
        mix[row + REACH] = mixing_rate * jnp.broadcast_to(value[1:2, :], (8, LANES))
        if last is not None:
            depth_north[row + REACH - 1] = jnp.minimum(here, last)
        last = here


def contribution(levels, depth, warm, salt):
    return jnp.where(levels < depth, warm - salt_weight * salt, 0.0)


def inner_kernel(
    fields, columns, halfway, moved, forcing,
    middle, depth, depth_east, depth_north, mix, scaled, held,
):
    step = pl.program_id(0)

    @pl.when(step == 0)
    def _():
        spread_columns(lambda row: columns[row], range(BY), depth, depth_east, depth_north, mix)
        forcing[...] = jnp.zeros_like(forcing)

    levels = level_ids(step)
    shared = (
        lambda row: depth_east[row + REACH],
        lambda row: depth_north[row + REACH],
        lambda row: mix[row + REACH],
    )

    def write_middle(n, row, value):
        middle[n, row] = value
        if row < 6:
            halfway[0, n, row - 2] = value
        if row >= 34:
            halfway[0, n, row - 30] = value

    def write_moved(n, row, value):
        moved[0, n, row - 4] = value

    def eastward(row):
        return fields[0, 2, row]

    def northward(row):
        return fields[0, 3, row]

    first = Band(2, 37, lambda n, row: fields[0, n, row], write_middle, eastward, northward)
    second = Band(4, 35, lambda n, row: middle[n, row], write_moved, eastward, northward)
    advance([first], levels, shared, (scaled, held))
    advance([second], levels, shared, (scaled, held))
    for row in range(4, 36):
        forcing[row] += contribution(
            levels, depth[row + REACH], moved[0, 0, row - 4], moved[0, 1, row - 4]
        )


def surface_operator(values, couple_east, couple_north, damping):
    east = couple_east * (values - turn(values, LANES - 1))
    north = couple_north * (values - pltpu.roll(values, SURFACE - 1, 0))
    return damping * values + ((east - turn(east, 1)) + (north - pltpu.roll(north, 1, 0)))


def outer_kernel(
    low_fields, high_fields, columns, up, down, up_extra, down_extra, halfway, inner_forcing,
    moved, basis, moments,
    middle, beyond, depth, depth_east, depth_north, mix, scaled, held, forcing, surface, depths, dampings,
):
    step = pl.program_id(0)

    def column(row):
        if row < 0:
            return up_extra[row + REACH, 0]
        if row >= BY:
            return down_extra[row - BY, 0]
        return columns[row]

    rows = range(-REACH, BY + REACH)

    @pl.when(step == 0)
    def _():
        spread_columns(column, rows, depth, depth_east, depth_north, mix)
        forcing[...] = jnp.zeros_like(forcing)

    levels = level_ids(step)
    shared = (
        lambda row: depth_east[row + REACH],
        lambda row: depth_north[row + REACH],
        lambda row: mix[row + REACH],
    )

    def field(number, row):
        if row < 0:
            return up[0, REACH * number + row + REACH]
        if row >= BY:
            return down[0, REACH * number + row - BY]
        return low_fields[0, number, row] if row < 10 else high_fields[0, number, row - 30]

    def read_middle(n, row):
        if 2 <= row < 6:
            return halfway[0, n, row - 2]
        if 34 <= row < 38:
            return halfway[0, n, row - 30]
        return middle[n, row + REACH]

    def write_middle(n, row, value):
        middle[n, row + REACH] = value

    def write_beyond(n, row, value):
        beyond[n, row + REACH] = value
        if 0 <= row < 4:
            moved[0, n, row] = value
        if 36 <= row < BY:
            moved[0, n, row - 32] = value

    def eastward(row):
        return field(2, row)

    def northward(row):
        return field(3, row)

    bands = [Band(low, high, field, write_middle, eastward, northward) for low, high in ((-5, 1), (38, 44))]
    advance(bands, levels, shared, (scaled, held))
    bands = [
        Band(low, high, read_middle, write_beyond, eastward, northward) for low, high in ((-3, 3), (36, 42))
    ]
    advance(bands, levels, shared, (scaled, held))
    for row in (*range(-3, 4), *range(36, 43)):
        at = row + REACH
        forcing[at] += contribution(levels, depth[at], beyond[0, at], beyond[1, at])

    @pl.when(step == TILES - 1)
    def _():
        surface[...] = jnp.zeros_like(surface)
        for row in range(-3, 43):
            part = inner_forcing[row] if 4 <= row < 36 else forcing[row + REACH]
            total = jnp.sum(part, axis=0, keepdims=True)
            surface[row + 8 : row + 9, :] = total * (1.0 / math.sqrt(LEVELS))
        depths[...] = jnp.zeros_like(depths)
        dampings[...] = jnp.zeros_like(dampings)
        for row in rows:
            value = column(row)
            depths[row + 8 : row + 9, :] = value[0:1, :]
            dampings[row + 8 : row + 9, :] = value[2:3, :]
        here = depths[...]
        couple_east = jnp.minimum(here, turn(here, LANES - 1)) * (1.0 / LEVELS)
        couple_north = jnp.minimum(here, pltpu.roll(here, SURFACE - 1, 0)) * (1.0 / LEVELS)
        diagonal = dampings[...]
        powers = [surface[...]]
        for _ in range(3):
            powers.append(surface_operator(powers[-1], couple_east, couple_north, diagonal))
        row_id = lax.broadcasted_iota(jnp.int32, (SURFACE, LANES), 0)
        lane_id = lax.broadcasted_iota(jnp.int32, (SURFACE, LANES), 1)
        own = (row_id >= 8) & (row_id < 8 + BY) & (lane_id >= BASE) & (lane_id < BASE + WIDE)
        moments[...] = jnp.zeros_like(moments)
        for k in range(6):
            product = jnp.where(own, powers[k // 2] * powers[(k + 1) // 2], 0.0)
            moments[k : k + 1, :] = jnp.sum(product, axis=0, keepdims=True)
        for k in range(3):
            basis[k] = turn(powers[k], LANES - BASE)[8 : 8 + BY, :]


def slots_kernel(block_list, moved, edges, new_tracers):
    lane = lane_ids()
    swap = slot_swap(block_list)
    for n in range(2):
        turned = {}

        def strip(row, n=n):
            row = min(max(row, 0), BY - 1)
            if row < 4:
                return edges[0, n, row]
            return edges[0, n, row - 32] if row >= 36 else moved[0, n, row - 4]

        def back(r, strip=strip, turned=turned):
            if r not in turned:
                value = jnp.where(lane < BASE + BX, strip(r), strip(r + 1))
                turned[r] = turn(value, BX * r - BASE)
            return turned[r]

        for number in range(15):
            for position in range(2):
                slot = swap if position == 0 else 1 - swap
                first, end = number * LANES, min((number + 1) * LANES, CELLS)
                parts = []
                for row in range(first // BX, (end - 1) // BX + 1):
                    low = max(row * BX, first)
                    parts.append((low, min((row + 1) * BX, end) - low, back(row - position)))
                value = merge(parts, lane)
                new_tracers[slot, n, :, first:end] = value[:, 0 : end - first]


def finish_kernel(moments, basis, out):
    totals = jnp.sum(moments[...], axis=1, keepdims=True)
    m = [totals[k : k + 1, :] for k in range(6)]
    low10 = m[2] / m[1]
    low20 = m[3] / m[1]
    pivot1 = m[3] - low10 * m[2]
    part21 = m[4] - low20 * m[2]
    low21 = part21 / pivot1
    pivot2 = m[5] - low20 * m[3] - low21 * part21
    y1 = m[1] - low10 * m[0]
    y2 = m[2] - low20 * m[0] - low21 * y1
    z2 = y2 / pivot2
    z1 = y1 / pivot1 - low21 * z2
    z0 = m[0] / m[1] - low10 * z1 - low20 * z2
    value = z0 * basis[0] + z1 * basis[1] + z2 * basis[2]
    out[...] = value[:, 0:WIDE]


def quad_sum(values, axis, partner):
    count = lax.axis_size(axis)
    others = [
        lax.ppermute(values, axis, [(i, partner(i, turn)) for i in range(count)])
        for turn in range(1, 4)
    ]
    return (values + others[0]) + (others[1] + others[2])


def total_over_devices(values):
    values = values + lax.ppermute(values, "gy", [(i, i ^ 1) for i in range(lax.axis_size("gy"))])
    values = quad_sum(values, "gy", lambda i, turn: i ^ (2 * turn))
    values = quad_sum(values, "gx", lambda i, turn: i ^ turn)
    return quad_sum(values, "gx", lambda i, turn: i ^ (4 * turn))


def whole(shape):
    return pl.BlockSpec(shape, lambda k: (0,) * len(shape))


def per_device(block_list, wet_levels, mixing, velocity, tracers, damping):
    f32 = jnp.float32
    slots, fields_each, levels, cells = tracers.shape
    params = pltpu.CompilerParams(
        dimension_semantics=("arbitrary",), vmem_limit_bytes=40 * 1024 * 1024
    )
    level_block = pl.BlockSpec((slots, fields_each, 8, cells), lambda k: (0, 0, k, 0))

    def tiles(*shape):
        zeros = (0,) * (len(shape) + 2)
        return (
            pl.BlockSpec((1, *shape, 8, LANES), lambda k: (k, *zeros)),
            jax.ShapeDtypeStruct((TILES, *shape, 8, LANES), f32),
        )

    rows_block, rows_type = tiles(NS)
    columns_block, columns_type = tiles(EW)
    rows_extra = pl.BlockSpec((TILES, 1, 8, LANES), lambda k: (0, NS - 1, 0, 0))
    columns_extra = pl.BlockSpec((TILES, 1, 8, LANES), lambda k: (0, EW - 1, 0, 0))
    own_specs = [
        pl.BlockSpec(memory_space=pltpu.SMEM),
        whole(wet_levels.shape),
        whole(mixing.shape),
        whole(damping.shape),
        level_block,
        level_block,
    ]
    own = (block_list, wet_levels, mixing, damping, velocity, tracers)

    east, west = pl.pallas_call(
        columns_kernel,
        grid=(TILES,),
        in_specs=own_specs,
        out_specs=[columns_block, columns_block],
        out_shape=[columns_type, columns_type],
        scratch_shapes=[pltpu.VMEM((BY, LANES), f32)],
        compiler_params=params,
        name="pack_columns",
    )(*own)
    columns_total = lax.axis_size("gx")
    from_west = lax.ppermute(east, "gx", [(i, (i + 1) % columns_total) for i in range(columns_total)])
    from_east = lax.ppermute(west, "gx", [((i + 1) % columns_total, i) for i in range(columns_total)])

    fields_block, fields_type = tiles(4, BY)
    column_shape = (BY, 8, LANES)
    fields, columns, up, down = pl.pallas_call(
        strips_kernel,
        grid=(TILES,),
        in_specs=own_specs + [columns_block, columns_block, columns_extra, columns_extra],
        out_specs=[fields_block, whole(column_shape), rows_block, rows_block],
        out_shape=[fields_type, jax.ShapeDtypeStruct(column_shape, f32), rows_type, rows_type],
        scratch_shapes=[pltpu.VMEM((BY, LANES), f32)],
        compiler_params=params,
        name="strips",
    )(*own, from_west, from_east, from_west, from_east)
    rows_total = lax.axis_size("gy")
    from_below = lax.ppermute(up, "gy", [(i, i + 1) for i in range(rows_total - 1)])
    from_above = lax.ppermute(down, "gy", [(i + 1, i) for i in range(rows_total - 1)])

    row_store = pltpu.VMEM((ROWS, 8, LANES), f32)
    pair_store = pltpu.VMEM((2, ROWS, 8, LANES), f32)
    halfway_block, halfway_type = tiles(2, 8)
    moved_block, moved_type = tiles(2, 32)
    halfway, moved, forcing = pl.pallas_call(
        inner_kernel,
        grid=(TILES,),
        in_specs=[fields_block, whole(column_shape)],
        out_specs=[halfway_block, moved_block, whole(column_shape)],
        out_shape=[halfway_type, moved_type, jax.ShapeDtypeStruct(column_shape, f32)],
        scratch_shapes=[pair_store] + [row_store] * 4 + [pair_store] * 2,
        compiler_params=params,
        cost_estimate=pl.CostEstimate(flops=60_000_000, bytes_accessed=10_000_000, transcendentals=0),
        name="inner_rows",
    )(fields, columns)

    low_block = pl.BlockSpec((1, 4, 10, 8, LANES), lambda k: (k, 0, 0, 0, 0))
    high_block = pl.BlockSpec((1, 4, 10, 8, LANES), lambda k: (k, 0, 3, 0, 0))
    edges, basis, moments = pl.pallas_call(
        outer_kernel,
        grid=(TILES,),
        in_specs=[low_block, high_block, whole(column_shape), rows_block, rows_block]
        + [rows_extra, rows_extra, halfway_block, whole(column_shape)],
        out_specs=[halfway_block, whole((3, BY, LANES)), whole((8, LANES))],
        out_shape=[
            halfway_type,
            jax.ShapeDtypeStruct((3, BY, LANES), f32),
            jax.ShapeDtypeStruct((8, LANES), f32),
        ],
        scratch_shapes=[pair_store] * 2
        + [row_store] * 4
        + [pair_store] * 2
        + [row_store]
        + [pltpu.VMEM((SURFACE, LANES), f32)] * 3,
        compiler_params=params,
        name="outer_rows",
    )(fields, fields, columns, from_below, from_above, from_below, from_above, halfway, forcing)

    new_tracers = pl.pallas_call(
        slots_kernel,
        grid=(TILES,),
        in_specs=[pl.BlockSpec(memory_space=pltpu.SMEM), moved_block, halfway_block],
        out_specs=level_block,
        out_shape=jax.ShapeDtypeStruct(tracers.shape, f32),
        compiler_params=params,
        cost_estimate=pl.CostEstimate(flops=4_000_000, bytes_accessed=4_000_000, transcendentals=0),
        name="to_slots",
    )(block_list, moved, edges)

    moments = total_over_devices(moments)
    height = pl.pallas_call(
        finish_kernel,
        out_shape=jax.ShapeDtypeStruct((BY, WIDE), f32),
        name="finish",
    )(moments, basis)
    return (new_tracers, height)


def solution(mesh):
    return jax.shard_map(
        per_device,
        mesh=mesh,
        in_specs=(
            P(("gx", "gy")),
            P(("gx", "gy"), None),
            P(("gx", "gy"), None),
            P(("gx", "gy"), None, None, None),
            P(("gx", "gy"), None, None, None),
            P("gy", "gx"),
        ),
        out_specs=(P(("gx", "gy"), None, None, None), P("gy", "gx")),
        check_vma=False,
    )
```

time: 94.3 us -> 79.2 us (0.84)
  Pallas kernels: 34.4 us -> 24.4 us
  waiting for transfers between devices: 19.3 us -> 16.1 us
  starting transfers between devices: 33.5 us -> 31.4 us
    pallas_call x3 -> x5, Pallas kernels: 32.8 us -> 22.8 us  [the longest x1 7.33 us: per_device(): pl.pallas_call(inner_kernel, grid=(TILES,), in_specs=[fields_block, whole...]
    ppermute x2, waiting for transfers between devices: 4.5 us -> 0.01 us  [the longest x1 0.01 us: per_device(): lax.ppermute(up, 'gy', [(i, i + 1) for i in range(rows_total - 1)])]
    ppermute x1, waiting for transfers between devices: 6.03 us -> 9.73 us  [per_device(): lax.ppermute(east, 'gx', [(i, (i + 1) % columns_total) for i in range(col...]
    ppermute x9, starting transfers between devices: 16 us -> 13.4 us  [quad_sum(): lax.ppermute(values, axis, [(i, partner(i, turn)) for i in range(count)])]
    ppermute x9, waiting for transfers between devices: 7.95 us -> 5.58 us  [quad_sum(): lax.ppermute(values, axis, [(i, partner(i, turn)) for i in range(count)])]
  transfers between devices with their start and end apart: 14 -> 14, of which waited for: 9 -> 7; matrix products, arithmetic and copies ran while one was open for 3% -> 3% of each run, Pallas kernels for 0% -> 12%
where the time goes in v4:
time: 79.2 us; the launch traced here: 78.9 us
  starting transfers between devices  31.4 us (40%)
  Pallas kernels  24.4 us (31%)
  waiting for transfers between devices  16.1 us (20%)
  local copies, waits for them, and re-layouts  5.54 us (7%)
    ppermute x9, starting transfers between devices, quad_sum(): lax.ppermute(values, axis, [(i, partner(i, turn)) for i in range(count)])  13.4 us
    ppermute x1, waiting for transfers between devices, per_device(): lax.ppermute(east, 'gx', [(i, (i + 1) % columns_total) for i in range(col...  9.73 us
    ppermute x1, starting transfers between devices, total_over_devices(): lax.ppermute(values, 'gy', [(i, i ^ 1) for i in range(lax.axis_size('gy'))])  8.62 us
    pallas_call x1, Pallas kernels, per_device(): pl.pallas_call(inner_kernel, grid=(TILES,), in_specs=[fields_block, whole...  7.33 us
    pallas_call x1, Pallas kernels, per_device(): pl.pallas_call(outer_kernel, grid=(TILES,), in_specs=[low_block, high_blo...  5.85 us
    ppermute x9, waiting for transfers between devices, quad_sum(): lax.ppermute(values, axis, [(i, partner(i, turn)) for i in range(count)])  5.58 us
    unnamed x15, local copies, waits for them, and re-layouts  5.54 us
    pallas_call x1, Pallas kernels, per_device(): pl.pallas_call(strips_kernel, grid=(TILES,), in_specs=own_specs + [column...  4.81 us
  transfers between devices with their start and end apart: 14, of which 7 were waited for; matrix products, arithmetic and copies ran while one was open for 3% of the time, Pallas kernels for 12%

profile of v4, /device:TPU:0, one launch (start us, length us, event | category | flops | bytes accessed | tf_op | source)
XLA Modules:
  0.0 78.9 jit_solution(10998108978250336973)
XLA Ops:
  0.6 1.8 %copy.10.velocity = f32[2,2,62,1800]{3,2,1,0:T(8,128)S(1)} copy(f32[2,2,62,1800]{3,1,2,0:T(2,128)} %param.9) | data formatting | bytes 3571200 | tf_op args[3]
  3.5 2.8 %pack_columns.1 = (f32[8,13,8,128]{3,2,1,0:T(8,128)S(1)}, f32[8,13,8,128]{3,2,1,0:T(8,128)S(1)}) custom-call(s32[2]{0:T(128)S(1)} %copy-done.4, s32[2,1800]{1,0:T(2,128)S(1)} %copy-done.1, f32[2,1800]{1,0:T(2,128)S(1)} %copy-done.2, f32[40,90]{1,0:T(8,128)S(1)} %copy-done, f32[2,2,62,1800]{3,2,1,0:T(8,128)S(1)} %copy.10.velocity, ...), custom_call_target="tpu_custom_call" | custom-call | tf_op jit(solution)/shard_map/pack_columns/pallas_call | solution.py:567
  6.2 2.1 %collective-permute-start = (f32[8,13,8,128]{3,2,1,0:T(8,128)S(1)}, f32[8,13,8,128]{3,2,1,0:T(8,128)S(1)}, u32[]{:S(2)}, u32[]{:S(2)}) collective-permute-start(f32[8,13,8,128]{3,2,1,0:T(8,128)S(1)} %get-tuple-element.14), channel_id=1, source_target_pairs={{0,8},{8,16},{16,24},{24,32},{32,40},{40,48},{48,56},{56,64},{64,7... | collective-permute-start | bytes 1277960 | tf_op jit(solution)/shard_map/ppermute | solution.py:578
  8.3 4.7 %collective-permute-start.1 = (f32[8,13,8,128]{3,2,1,0:T(8,128)S(1)}, f32[8,13,8,128]{3,2,1,0:T(8,128)S(1)}, u32[]{:S(2)}, u32[]{:S(2)}) collective-permute-start(f32[8,13,8,128]{3,2,1,0:T(8,128)S(1)} %get-tuple-element.15), channel_id=1, source_target_pairs={{8,0},{16,8},{24,16},{32,24},{40,32},{48,40},{56,48},{64,56},{72,6... | collective-permute-start | bytes 1277960 | tf_op jit(solution)/shard_map/ppermute | solution.py:579
  13.0 9.7 %collective-permute-done.from_west.west_extra = f32[8,13,8,128]{3,2,1,0:T(8,128)S(1)} collective-permute-done((f32[8,13,8,128]{3,2,1,0:T(8,128)S(1)}, f32[8,13,8,128]{3,2,1,0:T(8,128)S(1)}, u32[]{:S(2)}, u32[]{:S(2)}) %collective-permute-start) | collective-permute-done | bytes 426016 | tf_op jit(solution)/shard_map/ppermute | solution.py:578
  22.7 4.8 %strips.1 = (f32[8,4,40,8,128]{4,3,2,1,0:T(8,128)S(1)}, f32[40,8,128]{2,1,0:T(8,128)S(1)}, f32[8,29,8,128]{3,2,1,0:T(8,128)S(1)}, f32[8,29,8,128]{3,2,1,0:T(8,128)S(1)}) custom-call(s32[2]{0:T(128)S(1)} %copy-done.4, s32[2,1800]{1,0:T(2,128)S(1)} %copy-done.1, f32[2,1800]{1,0:T(2,128)S(1)} %copy-done.2, f32[40,90]{1,0:T(8,128)S(1)} %copy-done, ...), custom_call_target="tpu_custom_call" | custom-call | tf_op jit(solution)/shard_map/strips/pallas_call | solution.py:583
  27.5 1.4 %collective-permute-start.2 = (f32[8,29,8,128]{3,2,1,0:T(8,128)S(1)}, f32[8,29,8,128]{3,2,1,0:T(8,128)S(1)}, u32[]{:S(2)}, u32[]{:S(2)}) collective-permute-start(f32[8,29,8,128]{3,2,1,0:T(8,128)S(1)} %get-tuple-element.19), channel_id=1, source_target_pairs={{0,1},{1,2},{2,3},{3,4},{4,5},{5,6},{6,7},{8,9},{9,10},{10,11},{11... | collective-permute-start | bytes 2850824 | tf_op jit(solution)/shard_map/ppermute | solution.py:594
  28.9 1.3 %collective-permute-start.3 = (f32[8,29,8,128]{3,2,1,0:T(8,128)S(1)}, f32[8,29,8,128]{3,2,1,0:T(8,128)S(1)}, u32[]{:S(2)}, u32[]{:S(2)}) collective-permute-start(f32[8,29,8,128]{3,2,1,0:T(8,128)S(1)} %get-tuple-element.20), channel_id=1, source_target_pairs={{1,0},{2,1},{3,2},{4,3},{5,4},{6,5},{7,6},{9,8},{10,9},{11,10},{12... | collective-permute-start | bytes 2850824 | tf_op jit(solution)/shard_map/ppermute | solution.py:595
  30.2 7.3 %inner_rows.1 = (f32[8,2,8,8,128]{4,3,2,1,0:T(8,128)S(1)}, f32[8,2,32,8,128]{4,3,2,1,0:T(8,128)S(1)}, f32[40,8,128]{2,1,0:T(8,128)S(1)}) custom-call(f32[8,4,40,8,128]{4,3,2,1,0:T(8,128)S(1)} %get-tuple-element.16.fields.low_fields.high_fields, f32[40,8,128]{2,1,0:T(8,128)S(1)} %get-tuple-element.17.columns), custom_call_target="tpu_custom_call" | custom-call | flops 60000000 | bytes 10000000 | tf_op jit(solution)/shard_map/inner_rows/pallas_call | solution.py:601
  37.5 5.9 %outer_rows.1 = (f32[8,2,8,8,128]{4,3,2,1,0:T(8,128)S(1)}, f32[3,40,128]{2,1,0:T(8,128)S(1)}, f32[8,128]{1,0:T(8,128)S(1)}) custom-call(f32[8,4,40,8,128]{4,3,2,1,0:T(8,128)S(1)} %get-tuple-element.16.fields.low_fields.high_fields, f32[8,4,40,8,128]{4,3,2,1,0:T(8,128)S(1)} %get-tuple-element.16.fields.low_fields.high_fields, ...), custom_call_target="tpu_custom_call" | custom-call | tf_op jit(solution)/shard_map/outer_rows/pallas_call | solution.py:615
  43.4 8.6 %collective-permute-start.4 = (f32[8,128]{1,0:T(8,128)S(1)}, f32[8,128]{1,0:T(8,128)S(1)}, u32[]{:S(2)}, u32[]{:S(2)}) collective-permute-start(f32[8,128]{1,0:T(8,128)S(1)} %get-tuple-element.24), channel_id=1, source_target_pairs={{0,1},{1,0},{2,3},{3,2},{4,5},{5,4},{6,7},{7,6},{8,9},{9,8},{10,11... | collective-permute-start | bytes 12296 | tf_op jit(solution)/shard_map/ppermute | solution.py:528
  52.0 0.8 %collective-permute-done.4 = f32[8,128]{1,0:T(8,128)S(1)} collective-permute-done((f32[8,128]{1,0:T(8,128)S(1)}, f32[8,128]{1,0:T(8,128)S(1)}, u32[]{:S(2)}, u32[]{:S(2)}) %collective-permute-start.4) | collective-permute-done | bytes 4128 | tf_op jit(solution)/shard_map/ppermute | solution.py:528
  52.8 1.3 %collective-permute-start.7 = (f32[8,128]{1,0:T(8,128)S(1)}, f32[8,128]{1,0:T(8,128)S(1)}, u32[]{:S(2)}, u32[]{:S(2)}) collective-permute-start(f32[8,128]{1,0:T(8,128)S(1)} %add.30), channel_id=1, source_target_pairs={{0,6},{1,7},{2,4},{3,5},{4,2},{5,3},{6,0},{7,1},{8,14},{9,15},{10,... | collective-permute-start | bytes 12296 | tf_op jit(solution)/shard_map/ppermute | solution.py:521
  54.2 2.2 %collective-permute-start.6 = (f32[8,128]{1,0:T(8,128)S(1)}, f32[8,128]{1,0:T(8,128)S(1)}, u32[]{:S(2)}, u32[]{:S(2)}) collective-permute-start(f32[8,128]{1,0:T(8,128)S(1)} %add.30), channel_id=1, source_target_pairs={{0,4},{1,5},{2,6},{3,7},{4,0},{5,1},{6,2},{7,3},{8,12},{9,13},{10,... | collective-permute-start | bytes 12296 | tf_op jit(solution)/shard_map/ppermute | solution.py:521
  56.9 0.7 collective-permute-done.7
  57.7 1.6 %collective-permute-done.6 = f32[8,128]{1,0:T(8,128)S(1)} collective-permute-done((f32[8,128]{1,0:T(8,128)S(1)}, f32[8,128]{1,0:T(8,128)S(1)}, u32[]{:S(2)}, u32[]{:S(2)}) %collective-permute-start.6) | collective-permute-done | bytes 4128 | tf_op jit(solution)/shard_map/ppermute | solution.py:521
  60.0 1.5 %collective-permute-start.10 = (f32[8,128]{1,0:T(8,128)S(1)}, f32[8,128]{1,0:T(8,128)S(1)}, u32[]{:S(2)}, u32[]{:S(2)}) collective-permute-start(f32[8,128]{1,0:T(8,128)S(1)} %add_add_fusion.2), channel_id=1, source_target_pairs={{0,24},{8,16},{16,8},{24,0},{32,56},{40,48},{48,40},{56,32},{64,88... | collective-permute-start | bytes 12296 | tf_op jit(solution)/shard_map/ppermute | solution.py:521
  61.5 2.6 %collective-permute-start.8 = (f32[8,128]{1,0:T(8,128)S(1)}, f32[8,128]{1,0:T(8,128)S(1)}, u32[]{:S(2)}, u32[]{:S(2)}) collective-permute-start(f32[8,128]{1,0:T(8,128)S(1)} %add_add_fusion.2), channel_id=1, source_target_pairs={{0,8},{8,0},{16,24},{24,16},{32,40},{40,32},{48,56},{56,48},{64,72... | collective-permute-start | bytes 12296 | tf_op jit(solution)/shard_map/ppermute | solution.py:521
  64.8 1.8 %collective-permute-done.9 = f32[8,128]{1,0:T(8,128)S(1)} collective-permute-done((f32[8,128]{1,0:T(8,128)S(1)}, f32[8,128]{1,0:T(8,128)S(1)}, u32[]{:S(2)}, u32[]{:S(2)}) %collective-permute-start.9) | collective-permute-done | bytes 4128 | tf_op jit(solution)/shard_map/ppermute | solution.py:521
  66.6 4.3 %collective-permute-start.13 = (f32[8,128]{1,0:T(8,128)S(1)}, f32[8,128]{1,0:T(8,128)S(1)}, u32[]{:S(2)}, u32[]{:S(2)}) collective-permute-start(f32[8,128]{1,0:T(8,128)S(1)} %add_add_fusion.1), channel_id=1, source_target_pairs={{0,96},{8,104},{16,112},{24,120},{32,64},{40,72},{48,80},{56,88},{... | collective-permute-start | bytes 12296 | tf_op jit(solution)/shard_map/ppermute | solution.py:521
  70.9 0.9 %collective-permute-start.11 = (f32[8,128]{1,0:T(8,128)S(1)}, f32[8,128]{1,0:T(8,128)S(1)}, u32[]{:S(2)}, u32[]{:S(2)}) collective-permute-start(f32[8,128]{1,0:T(8,128)S(1)} %add_add_fusion.1), channel_id=1, source_target_pairs={{0,32},{8,40},{16,48},{24,56},{32,0},{40,8},{48,16},{56,24},{64,96... | collective-permute-start | bytes 12296 | tf_op jit(solution)/shard_map/ppermute | solution.py:521
  71.9 2.1 %to_slots.1 = f32[2,2,62,1800]{3,2,1,0:T(8,128)S(1)} custom-call(s32[2]{0:T(128)S(1)} %copy-done.4, f32[8,2,32,8,128]{4,3,2,1,0:T(8,128)S(1)} %get-tuple-element.18.moved, f32[8,2,8,8,128]{4,3,2,1,0:T(8,128)S(1)} %get-tuple-element.23.edges), custom_call_target="tpu_custom_call" | custom-call | flops 4000000 | bytes 4000000 | tf_op jit(solution)/shard_map/to_slots/pallas_call | solution.py:635
  74.0 2.7 %copy.12 = f32[2,2,62,1800]{3,1,2,0:T(2,128)} copy(f32[2,2,62,1800]{3,2,1,0:T(8,128)S(1)} %to_slots.1) | data formatting | bytes 3571200
  77.3 1.6 %finish.1 = f32[40,90]{1,0:T(8,128)} custom-call(f32[8,128]{1,0:T(8,128)} %add_add_fusion.moments, f32[3,40,128]{2,1,0:T(8,128)} %copy-done.3), custom_call_target="tpu_custom_call" | custom-call | tf_op jit(solution)/shard_map/finish/pallas_call | solution.py:647
  (29 shorter events, 3.6 us)
Async XLA Ops:
  0.6 2.1 %copy-start.5 = (f32[2,2,62,1800]{3,1,2,0:T(2,128)S(1)}, f32[2,2,62,1800]{3,1,2,0:T(2,128)}, u32[]{:S(2)}) copy-start(f32[2,2,62,1800]{3,1,2,0:T(2,128)} %param.10) | copy-start | bytes 5356804
  2.7 0.7 copy-start
  2.7 0.7 copy-start.1
  2.7 0.7 copy-start.2
  2.7 0.7 copy-start.4
  6.2 16.4 %collective-permute-start = (f32[8,13,8,128]{3,2,1,0:T(8,128)S(1)}, f32[8,13,8,128]{3,2,1,0:T(8,128)S(1)}, u32[]{:S(2)}, u32[]{:S(2)}) collective-permute-start(f32[8,13,8,128]{3,2,1,0:T(8,128)S(1)} %get-tuple-element.14), channel_id=1, source_target_pairs={{0,8},{8,16},{16,24},{24,32},{32,40},{40,48},{48,56},{56,64},{64,7... | collective-permute-start | bytes 1277960 | tf_op jit(solution)/shard_map/ppermute | solution.py:578
  8.3 14.4 %collective-permute-start.1 = (f32[8,13,8,128]{3,2,1,0:T(8,128)S(1)}, f32[8,13,8,128]{3,2,1,0:T(8,128)S(1)}, u32[]{:S(2)}, u32[]{:S(2)}) collective-permute-start(f32[8,13,8,128]{3,2,1,0:T(8,128)S(1)} %get-tuple-element.15), channel_id=1, source_target_pairs={{8,0},{16,8},{24,16},{32,24},{40,32},{48,40},{56,48},{64,56},{72,6... | collective-permute-start | bytes 1277960 | tf_op jit(solution)/shard_map/ppermute | solution.py:579
  27.5 10.0 %collective-permute-start.2 = (f32[8,29,8,128]{3,2,1,0:T(8,128)S(1)}, f32[8,29,8,128]{3,2,1,0:T(8,128)S(1)}, u32[]{:S(2)}, u32[]{:S(2)}) collective-permute-start(f32[8,29,8,128]{3,2,1,0:T(8,128)S(1)} %get-tuple-element.19), channel_id=1, source_target_pairs={{0,1},{1,2},{2,3},{3,4},{4,5},{5,6},{6,7},{8,9},{9,10},{10,11},{11... | collective-permute-start | bytes 2850824 | tf_op jit(solution)/shard_map/ppermute | solution.py:594
  28.9 8.7 %collective-permute-start.3 = (f32[8,29,8,128]{3,2,1,0:T(8,128)S(1)}, f32[8,29,8,128]{3,2,1,0:T(8,128)S(1)}, u32[]{:S(2)}, u32[]{:S(2)}) collective-permute-start(f32[8,29,8,128]{3,2,1,0:T(8,128)S(1)} %get-tuple-element.20), channel_id=1, source_target_pairs={{1,0},{2,1},{3,2},{4,3},{5,4},{6,5},{7,6},{9,8},{10,9},{11,10},{12... | collective-permute-start | bytes 2850824 | tf_op jit(solution)/shard_map/ppermute | solution.py:595
  43.4 30.6 %copy-start.3 = (f32[3,40,128]{2,1,0:T(8,128)}, f32[3,40,128]{2,1,0:T(8,128)S(1)}, u32[]{:S(2)}) copy-start(f32[3,40,128]{2,1,0:T(8,128)S(1)} %get-tuple-element.25.basis) | copy-start | bytes 184324
  43.4 9.4 %collective-permute-start.4 = (f32[8,128]{1,0:T(8,128)S(1)}, f32[8,128]{1,0:T(8,128)S(1)}, u32[]{:S(2)}, u32[]{:S(2)}) collective-permute-start(f32[8,128]{1,0:T(8,128)S(1)} %get-tuple-element.24), channel_id=1, source_target_pairs={{0,1},{1,0},{2,3},{3,2},{4,5},{5,4},{6,7},{7,6},{8,9},{9,8},{10,11... | collective-permute-start | bytes 12296 | tf_op jit(solution)/shard_map/ppermute | solution.py:528
  52.8 4.8 %collective-permute-start.7 = (f32[8,128]{1,0:T(8,128)S(1)}, f32[8,128]{1,0:T(8,128)S(1)}, u32[]{:S(2)}, u32[]{:S(2)}) collective-permute-start(f32[8,128]{1,0:T(8,128)S(1)} %add.30), channel_id=1, source_target_pairs={{0,6},{1,7},{2,4},{3,5},{4,2},{5,3},{6,0},{7,1},{8,14},{9,15},{10,... | collective-permute-start | bytes 12296 | tf_op jit(solution)/shard_map/ppermute | solution.py:521
  54.2 5.1 %collective-permute-start.6 = (f32[8,128]{1,0:T(8,128)S(1)}, f32[8,128]{1,0:T(8,128)S(1)}, u32[]{:S(2)}, u32[]{:S(2)}) collective-permute-start(f32[8,128]{1,0:T(8,128)S(1)} %add.30), channel_id=1, source_target_pairs={{0,4},{1,5},{2,6},{3,7},{4,0},{5,1},{6,2},{7,3},{8,12},{9,13},{10,... | collective-permute-start | bytes 12296 | tf_op jit(solution)/shard_map/ppermute | solution.py:521
  56.4 3.6 %collective-permute-start.5 = (f32[8,128]{1,0:T(8,128)S(1)}, f32[8,128]{1,0:T(8,128)S(1)}, u32[]{:S(2)}, u32[]{:S(2)}) collective-permute-start(f32[8,128]{1,0:T(8,128)S(1)} %add.30), channel_id=1, source_target_pairs={{0,2},{1,3},{2,0},{3,1},{4,6},{5,7},{6,4},{7,5},{8,10},{9,11},{10,... | collective-permute-start | bytes 12296 | tf_op jit(solution)/shard_map/ppermute | solution.py:521
  60.0 4.8 %collective-permute-start.10 = (f32[8,128]{1,0:T(8,128)S(1)}, f32[8,128]{1,0:T(8,128)S(1)}, u32[]{:S(2)}, u32[]{:S(2)}) collective-permute-start(f32[8,128]{1,0:T(8,128)S(1)} %add_add_fusion.2), channel_id=1, source_target_pairs={{0,24},{8,16},{16,8},{24,0},{32,56},{40,48},{48,40},{56,32},{64,88... | collective-permute-start | bytes 12296 | tf_op jit(solution)/shard_map/ppermute | solution.py:521
  61.5 5.1 %collective-permute-start.9 = (f32[8,128]{1,0:T(8,128)S(1)}, f32[8,128]{1,0:T(8,128)S(1)}, u32[]{:S(2)}, u32[]{:S(2)}) collective-permute-start(f32[8,128]{1,0:T(8,128)S(1)} %add_add_fusion.2), channel_id=1, source_target_pairs={{0,16},{8,24},{16,0},{24,8},{32,48},{40,56},{48,32},{56,40},{64,80... | collective-permute-start | bytes 12296 | tf_op jit(solution)/shard_map/ppermute | solution.py:521
  61.5 5.1 %collective-permute-start.8 = (f32[8,128]{1,0:T(8,128)S(1)}, f32[8,128]{1,0:T(8,128)S(1)}, u32[]{:S(2)}, u32[]{:S(2)}) collective-permute-start(f32[8,128]{1,0:T(8,128)S(1)} %add_add_fusion.2), channel_id=1, source_target_pairs={{0,8},{8,0},{16,24},{24,16},{32,40},{40,32},{48,56},{56,48},{64,72... | collective-permute-start | bytes 12296 | tf_op jit(solution)/shard_map/ppermute | solution.py:521
  66.6 10.1 %collective-permute-start.13 = (f32[8,128]{1,0:T(8,128)S(1)}, f32[8,128]{1,0:T(8,128)S(1)}, u32[]{:S(2)}, u32[]{:S(2)}) collective-permute-start(f32[8,128]{1,0:T(8,128)S(1)} %add_add_fusion.1), channel_id=1, source_target_pairs={{0,96},{8,104},{16,112},{24,120},{32,64},{40,72},{48,80},{56,88},{... | collective-permute-start | bytes 12296 | tf_op jit(solution)/shard_map/ppermute | solution.py:521
  70.9 5.8 %collective-permute-start.12 = (f32[8,128]{1,0:T(8,128)S(1)}, f32[8,128]{1,0:T(8,128)S(1)}, u32[]{:S(2)}, u32[]{:S(2)}) collective-permute-start(f32[8,128]{1,0:T(8,128)S(1)} %add_add_fusion.1), channel_id=1, source_target_pairs={{0,64},{8,72},{16,80},{24,88},{32,96},{40,104},{48,112},{56,120},{... | collective-permute-start | bytes 12296 | tf_op jit(solution)/shard_map/ppermute | solution.py:521
  70.9 5.8 %collective-permute-start.11 = (f32[8,128]{1,0:T(8,128)S(1)}, f32[8,128]{1,0:T(8,128)S(1)}, u32[]{:S(2)}, u32[]{:S(2)}) collective-permute-start(f32[8,128]{1,0:T(8,128)S(1)} %add_add_fusion.1), channel_id=1, source_target_pairs={{0,32},{8,40},{16,48},{24,56},{32,0},{40,8},{48,16},{56,24},{64,96... | collective-permute-start | bytes 12296 | tf_op jit(solution)/shard_map/ppermute | solution.py:521

commit v5 on v4

--- a/solution.py
+++ b/solution.py
@@ -58,15 +58,13 @@
 
 
 class Source:
-    def __init__(self, own, west=None, east=None):
-        self.load = {"own": own, "west": west, "east": east}
+    def __init__(self, load):
+        self.load = load
         self.kept = {}
 
-    def tile(self, kind, position, number):
-        key = (kind, position, number)
+    def tile(self, *key):
         if key not in self.kept:
-            load = self.load[kind]
-            self.kept[key] = load(position, number) if kind == "own" else load(number)
+            self.kept[key] = self.load(*key)
         return self.kept[key]
 
     def cells(self, position, start, width):
@@ -75,7 +73,7 @@
         while at < start + width:
             number = at // LANES
             end = min(start + width, (number + 1) * LANES)
-            parts.append((at, end - at, self.tile("own", position, number)))
+            parts.append((at, end - at, self.tile(position, number)))
             at = end
         return parts
 
@@ -93,24 +91,42 @@
     turned = {}
 
     def combined(r):
-        if r in turned:
-            return turned[r]
-        parts = []
-        if 0 <= r - 1 < BY:
-            parts.append((BX * r - REACH, REACH, source.tile("west", 0, (r - 1) // 17)))
-        if 0 <= r < BY:
-            parts += source.cells(0, BX * r, BX)
-        if 0 <= r + 1 < BY:
-            parts += source.cells(1, BX * (r + 1), BX)
-        if 0 <= r + 2 < BY:
-            parts.append((BX * (r + 2), REACH, source.tile("east", 0, (r + 2) // 17)))
-        turned[r] = turn(merge(parts, lane), BASE - BX * r)
+        if r not in turned:
+            parts = source.cells(0, BX * r, BX) if r >= 0 else []
+            if r + 1 < BY:
+                parts += source.cells(1, BX * (r + 1), BX)
+            turned[r] = turn(merge(parts, lane), BASE - BX * r)
         return turned[r]
 
+    for r in range(-1, BY):
+        combined(r)
     for row in range(BY):
-        value = jnp.where(lane < BASE, combined(row + 1), combined(row))
-        value = jnp.where(lane < BASE + BX, value, combined(row - 1))
-        yield row, jnp.where(lane < BASE + WIDE, value, combined(row - 2))
+        yield row, jnp.where(lane < BASE + BX, combined(row), combined(row - 1))
+
+
+def beside_rows(rows, west, east, lane):
+    turned = {}
+
+    def combined(r):
+        if r not in turned:
+            low, high = (BX * r - REACH) % LANES, BX * (r + 2) % LANES
+            if not 0 <= r - 1 < BY:
+                value = east((r + 2) // 17)
+            elif not 0 <= r + 2 < BY:
+                value = west((r - 1) // 17)
+            elif low < high:
+                inside = lane < high if high + REACH <= LANES else (lane >= low) & (lane < high)
+                value = jnp.where(inside, west((r - 1) // 17), east((r + 2) // 17))
+            else:
+                inside = lane < low if low + REACH <= LANES else (lane >= high) & (lane < low)
+                value = jnp.where(inside, east((r + 2) // 17), west((r - 1) // 17))
+            turned[r] = turn(value, BASE - BX * r)
+        return turned[r]
+
+    for r in sorted({row + 1 for row in rows} | {row - 2 for row in rows}):
+        combined(r)
+    for row in rows:
+        yield row, combined(row + 1), combined(row - 2)
 
 
 def slot_swap(block_list):
@@ -118,12 +134,21 @@
     return jnp.where(first >= 0, first & 1, 1 - (block_list[1] & 1))
 
 
-def field_loader(ref, which, swap):
+def over_level_blocks(work):
+    def body(block, carry):
+        work(block, pl.ds(pl.multiple_of(8 * block, 8), 8))
+        return carry
+
+    lax.fori_loop(0, TILES - 1, body, 0)
+    work(TILES - 1, pl.ds(LEVELS - 8, 8))
+
+
+def field_loader(ref, which, levels, swap):
     def load(position, number):
         slot = swap if position == 0 else 1 - swap
         if number < 14:
-            return ref[slot, which, :, number * LANES : (number + 1) * LANES]
-        return turn(ref[slot, which, :, CELLS - LANES : CELLS], CELLS % LANES)
+            return ref[slot, which, levels, number * LANES : (number + 1) * LANES]
+        return turn(ref[slot, which, levels, CELLS - LANES : CELLS], CELLS % LANES)
 
     return load
 
@@ -148,75 +173,100 @@
 def columns_kernel(block_list, wet_levels, mixing, damping, velocity, tracers, east, west, padded):
     lane = lane_ids()
     swap = slot_swap(block_list)
-    step = pl.program_id(0)
-    for field in range(4):
-        source = Source(field_loader(tracers if field < 2 else velocity, field % 2, swap))
-        easts, wests = pack_columns(source, lane)
-        for number in range(3):
-            east[0, 3 * field + number] = easts[number]
-            west[0, 3 * field + number] = wests[number]
-
-    for number in range(3):
-
-        @pl.when(step == number)
-        def _():
-            easts, wests = pack_columns(Source(column_loader(wet_levels, mixing, swap)), lane)
-            east[0, EW - 1] = easts[number]
-            west[0, EW - 1] = wests[number]
-
-    @pl.when(step >= 3)
-    def _():
-        padded[...] = jnp.zeros_like(padded)
-        padded[:, 0:WIDE] = damping[...]
-        tiles = [padded[8 * j : 8 * j + 8, :] for j in range(5)]
-        east[0, EW - 1] = merge([(2 * j, 2, turn(t, 2 * j - WIDE + 2)) for j, t in enumerate(tiles)], lane)
-        west[0, EW - 1] = merge([(2 * j, 2, turn(t, 2 * j)) for j, t in enumerate(tiles)], lane)
-
-
-def strips_kernel(
-    block_list, wet_levels, mixing, damping, velocity, tracers,
-    from_west, from_east, west_extra, east_extra,
-    fields, columns, up, down, padded,
-):
+
+    def work(block, levels):
+        for field in range(4):
+            ref = tracers if field < 2 else velocity
+            easts, wests = pack_columns(Source(field_loader(ref, field % 2, levels, swap)), lane)
+            scale = 1.0 if field < 2 else 0.25 * advect_rate
+            for number in range(3):
+                east[block, 3 * field + number] = easts[number] * scale
+                west[block, 3 * field + number] = wests[number] * scale
+
+    over_level_blocks(work)
+    easts, wests = pack_columns(Source(column_loader(wet_levels, mixing, swap)), lane)
+    padded[...] = jnp.zeros_like(padded)
+    padded[:, 0:WIDE] = damping[...]
+    tiles = [padded[8 * j : 8 * j + 8, :] for j in range(5)]
+    easts.append(merge([(2 * j, 2, turn(t, 2 * j - WIDE + 2)) for j, t in enumerate(tiles)], lane))
+    wests.append(merge([(2 * j, 2, turn(t, 2 * j)) for j, t in enumerate(tiles)], lane))
+    for block in range(TILES):
+        east[block, EW - 1] = easts[min(block, 3)]
+        west[block, EW - 1] = wests[min(block, 3)]
+
+
+def strips_kernel(block_list, wet_levels, mixing, damping, velocity, tracers, fields, columns, padded):
     lane = lane_ids()
     swap = slot_swap(block_list)
-    step = pl.program_id(0)
-
-    @pl.when(step == 0)
-    def _():
-        padded[...] = jnp.zeros_like(padded)
-        padded[:, 0:WIDE] = damping[...]
-        for j in range(5):
-            value = turn(padded[8 * j : 8 * j + 8, :], BASE)
-            value = jnp.where(lane < BASE, turn(west_extra[3, 0], BASE - 2 - 2 * j), value)
-            value = jnp.where(lane < BASE + WIDE, value, turn(east_extra[3, 0], BASE + WIDE - 2 * j))
-            padded[8 * j : 8 * j + 8, :] = value
-        source = Source(
-            column_loader(wet_levels, mixing, swap),
-            lambda tile: west_extra[tile, 0],
-            lambda tile: east_extra[tile, 0],
-        )
-        sublane = lax.broadcasted_iota(jnp.int32, (8, LANES), 0)
-        for row, value in strip_rows(source, lane):
-            damp = jnp.broadcast_to(padded[row : row + 1, :], (8, LANES))
-            columns[row] = jnp.where(sublane == 2, damp, value)
-
-    for field in range(4):
-        source = Source(
-            field_loader(tracers if field < 2 else velocity, field % 2, swap),
-            lambda number, field=field: from_west[0, 3 * field + number],
-            lambda number, field=field: from_east[0, 3 * field + number],
-        )
-        for row, value in strip_rows(source, lane):
-            value = value if field < 2 else (0.25 * advect_rate) * value
-            fields[0, field, row] = value
-            if row < REACH:
-                down[0, REACH * field + row] = value
-            if row >= BY - REACH:
-                up[0, REACH * field + row - (BY - REACH)] = value
-    row = jnp.minimum(step, REACH - 1)
-    down[0, NS - 1] = columns[row]
-    up[0, NS - 1] = columns[BY - REACH + row]
+    padded[...] = jnp.zeros_like(padded)
+    padded[:, 0:WIDE] = damping[...]
+    for j in range(5):
+        padded[8 * j : 8 * j + 8, :] = turn(padded[8 * j : 8 * j + 8, :], BASE)
+    sublane = lax.broadcasted_iota(jnp.int32, (8, LANES), 0)
+    for row, value in strip_rows(Source(column_loader(wet_levels, mixing, swap)), lane):
+        damp = jnp.broadcast_to(padded[row : row + 1, :], (8, LANES))
+        columns[row] = jnp.where(sublane == 2, damp, value)
+
+    def work(block, levels):
+        for field in range(4):
+            ref = tracers if field < 2 else velocity
+            for row, value in strip_rows(Source(field_loader(ref, field % 2, levels, swap)), lane):
+                fields[block, field, row] = value if field < 2 else (0.25 * advect_rate) * value
+
+    over_level_blocks(work)
+
+
+def place_halos(own_fields, own_columns, from_west, from_east, low_damp, high_damp, rows, put):
+    lane = lane_ids()
+    sublane = lax.broadcasted_iota(jnp.int32, (8, LANES), 0)
+    for j in range(5):
+        low_damp[8 * j : 8 * j + 8, :] = turn(from_west[3, EW - 1], BASE - 2 - 2 * j)
+        high_damp[8 * j : 8 * j + 8, :] = turn(from_east[3, EW - 1], BASE + WIDE - 2 * j)
+    sides = beside_rows(rows, lambda t: from_west[t, EW - 1], lambda t: from_east[t, EW - 1], lane)
+    for row, west, east in sides:
+        west = jnp.where(sublane == 2, jnp.broadcast_to(low_damp[row : row + 1, :], (8, LANES)), west)
+        east = jnp.where(sublane == 2, jnp.broadcast_to(high_damp[row : row + 1, :], (8, LANES)), east)
+        value = jnp.where(lane < BASE, west, own_columns[row])
+        put(0, 4, row, jnp.where(lane < BASE + WIDE, value, east))
+
+    def work(block, carry):
+        for field in range(4):
+            sides = beside_rows(
+                rows,
+                lambda t, field=field: from_west[block, 3 * field + t],
+                lambda t, field=field: from_east[block, 3 * field + t],
+                lane,
+            )
+            for row, west, east in sides:
+                value = jnp.where(lane < BASE, west, own_fields[block, field, row])
+                put(block, field, row, jnp.where(lane < BASE + WIDE, value, east))
+        return carry
+
+    lax.fori_loop(0, TILES, work, 0)
+
+
+def row_message_kernel(own_fields, own_columns, from_west, from_east, up, down, low_damp, high_damp):
+    def put(block, field, row, value):
+        target, row = (down, row) if row < REACH else (up, row - (BY - REACH))
+        if field == 4:
+            target[row, NS - 1] = value
+        else:
+            target[block, REACH * field + row] = value
+
+    up[TILES - 1, NS - 1] = jnp.zeros((8, LANES), jnp.float32)
+    down[TILES - 1, NS - 1] = jnp.zeros((8, LANES), jnp.float32)
+    rows = (*range(REACH), *range(BY - REACH, BY))
+    place_halos(own_fields, own_columns, from_west, from_east, low_damp, high_damp, rows, put)
+
+
+def halo_kernel(own_fields, own_columns, from_west, from_east, fields, columns, low_damp, high_damp):
+    def put(block, field, row, value):
+        if field == 4:
+            columns[row] = value
+        else:
+            fields[block, field, row] = value
+
+    place_halos(own_fields, own_columns, from_west, from_east, low_damp, high_damp, range(BY), put)
 
 
 def staggered(spans, phases):
@@ -298,7 +348,11 @@
 
 
 def level_ids(step):
-    return (lax.broadcasted_iota(jnp.int32, (8, LANES), 0) + 8 * step).astype(jnp.float32)
+    sublane = lax.broadcasted_iota(jnp.int32, (8, LANES), 0)
+    last = step == TILES - 1
+    twice = last & (sublane < 8 * TILES - LEVELS)
+    numbers = sublane + jnp.where(last, LEVELS - 8, 8 * step)
+    return jnp.where(twice, LEVELS, numbers).astype(jnp.float32)
 
 
 def spread_columns(column, rows, depth, depth_east, depth_north, mix):
@@ -467,38 +521,76 @@
             basis[k] = turn(powers[k], LANES - BASE)[8 : 8 + BY, :]
 
 
-def slots_kernel(block_list, moved, edges, new_tracers):
+def to_slots(numbers, start, rows, load, block_list, out):
     lane = lane_ids()
     swap = slot_swap(block_list)
-    for n in range(2):
-        turned = {}
-
-        def strip(row, n=n):
-            row = min(max(row, 0), BY - 1)
-            if row < 4:
-                return edges[0, n, row]
-            return edges[0, n, row - 32] if row >= 36 else moved[0, n, row - 4]
-
-        def back(r, strip=strip, turned=turned):
-            if r not in turned:
-                value = jnp.where(lane < BASE + BX, strip(r), strip(r + 1))
-                turned[r] = turn(value, BX * r - BASE)
-            return turned[r]
-
-        for number in range(15):
-            for position in range(2):
-                slot = swap if position == 0 else 1 - swap
-                first, end = number * LANES, min((number + 1) * LANES, CELLS)
-                parts = []
-                for row in range(first // BX, (end - 1) // BX + 1):
-                    low = max(row * BX, first)
-                    parts.append((low, min((row + 1) * BX, end) - low, back(row - position)))
-                value = merge(parts, lane)
-                new_tracers[slot, n, :, first:end] = value[:, 0 : end - first]
-
-
-def finish_kernel(moments, basis, out):
-    totals = jnp.sum(moments[...], axis=1, keepdims=True)
+    cells = [c for t in numbers for c in range(t * LANES, min((t + 1) * LANES, CELLS))]
+    wanted = sorted({c // BX - p for c in cells for p in range(2)})
+
+    def work(block, last):
+        for n in range(2):
+            turned = {}
+
+            def strip(row, n=n):
+                return load(block, n, min(max(row, rows[0]), rows[1]))
+
+            def back(r, strip=strip, turned=turned):
+                if r not in turned:
+                    value = jnp.where(lane < BASE + BX, strip(r), strip(r + 1))
+                    turned[r] = turn(value, BX * r - BASE)
+                return turned[r]
+
+            for r in wanted:
+                back(r)
+            for number in numbers:
+                for position in range(2):
+                    slot = swap if position == 0 else 1 - swap
+                    first, end = number * LANES, min((number + 1) * LANES, CELLS)
+                    parts = []
+                    for row in range(first // BX, (end - 1) // BX + 1):
+                        low = max(row * BX, first)
+                        parts.append((low, min((row + 1) * BX, end) - low, back(row - position)))
+                    value = merge(parts, lane)[:, 0 : end - first]
+                    if last:
+                        rest = value[8 * TILES - LEVELS : 8]
+                        out[slot, 8 * TILES - 8 : LEVELS, n, first - start : end - start] = rest
+                    else:
+                        out[slot, pl.ds(8 * block, 8), n, first - start : end - start] = value
+
+    def body(block, carry):
+        work(block, False)
+        return carry
+
+    lax.fori_loop(0, TILES - 1, body, 0)
+    work(TILES - 1, True)
+
+
+def inner_slots_kernel(block_list, moved, out, cells, semaphore):
+    to_slots(range(2, 12), 2 * LANES, (4, 35), lambda block, n, row: moved[block, n, row - 4], block_list, cells)
+    copy = pltpu.make_async_copy(cells, out.at[:, :, :, 2 * LANES : 12 * LANES], semaphore)
+    copy.start()
+    copy.wait()
+
+
+def outer_slots_kernel(block_list, moved, edges, inner, out, low, high, low_semaphore, high_semaphore):
+    def load(block, n, row):
+        if 4 <= row < 36:
+            return moved[block, n, row - 4]
+        return edges[block, n, row if row < 4 else row - 32]
+
+    to_slots((0, 1), 0, (0, BY - 1), load, block_list, low)
+    low_copy = pltpu.make_async_copy(low, out.at[:, :, :, 0 : 2 * LANES], low_semaphore)
+    low_copy.start()
+    to_slots((12, 13, 14), 12 * LANES, (0, BY - 1), load, block_list, high)
+    high_copy = pltpu.make_async_copy(high, out.at[:, :, :, 12 * LANES : CELLS], high_semaphore)
+    high_copy.start()
+    low_copy.wait()
+    high_copy.wait()
+
+
+def finish_kernel(first, second, third, fourth, basis, out):
+    moments = (first[...] + second[...]) + (third[...] + fourth[...])
+    totals = jnp.sum(moments, axis=1, keepdims=True)
     m = [totals[k : k + 1, :] for k in range(6)]
     low10 = m[2] / m[1]
     low20 = m[3] / m[1]
@@ -515,20 +607,33 @@
     out[...] = value[:, 0:WIDE]
 
 
-def quad_sum(values, axis, partner):
+def quad(values, axis, partner):
     count = lax.axis_size(axis)
     others = [
         lax.ppermute(values, axis, [(i, partner(i, turn)) for i in range(count)])
         for turn in range(1, 4)
     ]
-    return (values + others[0]) + (others[1] + others[2])
-
-
-def total_over_devices(values):
+    return [values, *others]
+
+
+def quad_sum(values, axis, partner):
+    four = quad(values, axis, partner)
+    return (four[0] + four[1]) + (four[2] + four[3])
+
+
+def terms_over_devices(values):
     values = values + lax.ppermute(values, "gy", [(i, i ^ 1) for i in range(lax.axis_size("gy"))])
     values = quad_sum(values, "gy", lambda i, turn: i ^ (2 * turn))
     values = quad_sum(values, "gx", lambda i, turn: i ^ turn)
-    return quad_sum(values, "gx", lambda i, turn: i ^ (4 * turn))
+    return quad(values, "gx", lambda i, turn: i ^ (4 * turn))
+
+
+def held_in_vmem(arrays):
+    return [pltpu.with_memory_space_constraint(a, pltpu.VMEM) for a in arrays]
+
+
+def vmem(kind):
+    return pltpu.VMEM(kind.shape, kind.dtype)
 
 
 def whole(shape):
@@ -541,7 +646,6 @@
     params = pltpu.CompilerParams(
         dimension_semantics=("arbitrary",), vmem_limit_bytes=40 * 1024 * 1024
     )
-    level_block = pl.BlockSpec((slots, fields_each, 8, cells), lambda k: (0, 0, k, 0))
 
     def tiles(*shape):
         zeros = (0,) * (len(shape) + 2)
@@ -551,27 +655,20 @@
         )
 
     rows_block, rows_type = tiles(NS)
-    columns_block, columns_type = tiles(EW)
+    _, columns_type = tiles(EW)
     rows_extra = pl.BlockSpec((TILES, 1, 8, LANES), lambda k: (0, NS - 1, 0, 0))
-    columns_extra = pl.BlockSpec((TILES, 1, 8, LANES), lambda k: (0, EW - 1, 0, 0))
-    own_specs = [
-        pl.BlockSpec(memory_space=pltpu.SMEM),
-        whole(wet_levels.shape),
-        whole(mixing.shape),
-        whole(damping.shape),
-        level_block,
-        level_block,
-    ]
-    own = (block_list, wet_levels, mixing, damping, velocity, tracers)
+    in_vmem = pl.BlockSpec(memory_space=pltpu.VMEM)
+    own_specs = [pl.BlockSpec(memory_space=pltpu.SMEM)] + [in_vmem] * 5
+    own = (block_list, *held_in_vmem((wet_levels, mixing, damping, velocity, tracers)))
+    whole_params = pltpu.CompilerParams(vmem_limit_bytes=40 * 1024 * 1024)
 
     east, west = pl.pallas_call(
         columns_kernel,
-        grid=(TILES,),
         in_specs=own_specs,
-        out_specs=[columns_block, columns_block],
-        out_shape=[columns_type, columns_type],
+        out_specs=[in_vmem] * 2,
+        out_shape=[vmem(columns_type)] * 2,
         scratch_shapes=[pltpu.VMEM((BY, LANES), f32)],
-        compiler_params=params,
+        compiler_params=whole_params,
         name="pack_columns",
     )(*own)
     columns_total = lax.axis_size("gx")
@@ -580,16 +677,37 @@
 
     fields_block, fields_type = tiles(4, BY)
     column_shape = (BY, 8, LANES)
-    fields, columns, up, down = pl.pallas_call(
+    column_type = jax.ShapeDtypeStruct(column_shape, f32)
+    own_strips = pl.pallas_call(
         strips_kernel,
-        grid=(TILES,),
-        in_specs=own_specs + [columns_block, columns_block, columns_extra, columns_extra],
-        out_specs=[fields_block, whole(column_shape), rows_block, rows_block],
-        out_shape=[fields_type, jax.ShapeDtypeStruct(column_shape, f32), rows_type, rows_type],
+        in_specs=own_specs,
+        out_specs=[in_vmem] * 2,
+        out_shape=[vmem(fields_type), vmem(column_type)],
         scratch_shapes=[pltpu.VMEM((BY, LANES), f32)],
-        compiler_params=params,
+        compiler_params=whole_params,
+        cost_estimate=pl.CostEstimate(flops=30_000_000, bytes_accessed=9_000_000, transcendentals=0),
         name="strips",
-    )(*own, from_west, from_east, from_west, from_east)
+    )(*own)
+    with_halos = held_in_vmem((*own_strips, from_west, from_east))
+    up, down = pl.pallas_call(
+        row_message_kernel,
+        in_specs=[in_vmem] * 4,
+        out_specs=[in_vmem] * 2,
+        out_shape=[vmem(rows_type)] * 2,
+        scratch_shapes=[pltpu.VMEM((BY, LANES), f32)] * 2,
+        compiler_params=whole_params,
+        name="row_message",
+    )(*with_halos)
+    fields, columns = pl.pallas_call(
+        halo_kernel,
+        in_specs=[in_vmem] * 4,
+        out_specs=[in_vmem] * 2,
+        out_shape=[vmem(fields_type), vmem(column_type)],
+        scratch_shapes=[pltpu.VMEM((BY, LANES), f32)] * 2,
+        compiler_params=whole_params,
+        cost_estimate=pl.CostEstimate(flops=30_000_000, bytes_accessed=9_000_000, transcendentals=0),
+        name="halos",
+    )(*with_halos)
     rows_total = lax.axis_size("gy")
     from_below = lax.ppermute(up, "gy", [(i, i + 1) for i in range(rows_total - 1)])
     from_above = lax.ppermute(down, "gy", [(i + 1, i) for i in range(rows_total - 1)])
@@ -609,6 +727,22 @@
         cost_estimate=pl.CostEstimate(flops=60_000_000, bytes_accessed=10_000_000, transcendentals=0),
         name="inner_rows",
     )(fields, columns)
+
+    slots_type = jax.ShapeDtypeStruct((slots, levels, fields_each, cells), f32)
+    inner_slots = pl.pallas_call(
+        inner_slots_kernel,
+        in_specs=[pl.BlockSpec(memory_space=pltpu.SMEM), in_vmem],
+        out_specs=pl.BlockSpec(memory_space=pl.ANY),
+        out_shape=slots_type,
+        scratch_shapes=[
+            pltpu.VMEM((slots, levels, fields_each, 10 * LANES), f32),
+            pltpu.SemaphoreType.DMA,
+        ],
+        compiler_params=whole_params,
+        cost_estimate=pl.CostEstimate(flops=20_000_000, bytes_accessed=6_000_000, transcendentals=0),
+        name="inner_slots",
+    )(block_list, moved)
+    inner_slots, forcing = lax.optimization_barrier((inner_slots, forcing))
 
     low_block = pl.BlockSpec((1, 4, 10, 8, LANES), lambda k: (k, 0, 0, 0, 0))
     high_block = pl.BlockSpec((1, 4, 10, 8, LANES), lambda k: (k, 0, 3, 0, 0))
@@ -633,22 +767,30 @@
     )(fields, fields, columns, from_below, from_above, from_below, from_above, halfway, forcing)
 
     new_tracers = pl.pallas_call(
-        slots_kernel,
-        grid=(TILES,),
-        in_specs=[pl.BlockSpec(memory_space=pltpu.SMEM), moved_block, halfway_block],
-        out_specs=level_block,
-        out_shape=jax.ShapeDtypeStruct(tracers.shape, f32),
-        compiler_params=params,
-        cost_estimate=pl.CostEstimate(flops=4_000_000, bytes_accessed=4_000_000, transcendentals=0),
-        name="to_slots",
-    )(block_list, moved, edges)
-
-    moments = total_over_devices(moments)
+        outer_slots_kernel,
+        in_specs=[pl.BlockSpec(memory_space=pltpu.SMEM), in_vmem, in_vmem]
+        + [pl.BlockSpec(memory_space=pl.ANY)],
+        out_specs=pl.BlockSpec(memory_space=pl.ANY),
+        out_shape=slots_type,
+        scratch_shapes=[
+            pltpu.VMEM((slots, levels, fields_each, 2 * LANES), f32),
+            pltpu.VMEM((slots, levels, fields_each, cells - 12 * LANES), f32),
+            pltpu.SemaphoreType.DMA,
+            pltpu.SemaphoreType.DMA,
+        ],
+        input_output_aliases={3: 0},
+        compiler_params=whole_params,
+        cost_estimate=pl.CostEstimate(flops=2_000_000, bytes_accessed=2_000_000, transcendentals=0),
+        name="outer_slots",
+    )(block_list, moved, edges, inner_slots)
+    new_tracers = jnp.transpose(new_tracers, (0, 2, 1, 3))
+
+    moments = terms_over_devices(moments)
     height = pl.pallas_call(
         finish_kernel,
         out_shape=jax.ShapeDtypeStruct((BY, WIDE), f32),
         name="finish",
-    )(moments, basis)
+    )(*moments, basis)
     return (new_tracers, height)
 
 

time: 79.2 us -> 74.4 us (0.939)
  Pallas kernels: 24.4 us -> 29.6 us
  starting transfers between devices: 31.4 us -> 26.7 us
  waiting for transfers between devices: 16.1 us -> 13.5 us
  local copies, waits for them, and re-layouts: 5.54 us -> 3.42 us
    pallas_call x3 -> x6, Pallas kernels: 9.66 us -> 15.1 us  [the longest x1 4 us: per_device(): pl.pallas_call(strips_kernel, in_specs=own_specs, out_specs=[in_vmem] * 2...]
    ppermute x10, starting transfers between devices: 22.1 us -> 17.4 us  [the longest x9 13.5 us: quad(): lax.ppermute(values, axis, [(i, partner(i, turn)) for i in range(count)])]
    ppermute x1, waiting for transfers between devices: 9.73 us -> 5.72 us  [per_device(): lax.ppermute(east, 'gx', [(i, (i + 1) % columns_total) for i in range(col...]
    unnamed x15 -> x22, local copies, waits for them, and re-layouts: 5.54 us -> 3.42 us
    ppermute x10, waiting for transfers between devices: 6.4 us -> 7.81 us  [the longest x9 6.99 us: quad(): lax.ppermute(values, axis, [(i, partner(i, turn)) for i in range(count)])]
  transfers between devices with their start and end apart: 14 -> 14, of which waited for: 7 -> 7; matrix products, arithmetic and copies ran while one was open for 3% -> 0% of each run, Pallas kernels for 12% -> 26%
where the time goes in v5:
time: 74.4 us; the launch traced here: 74.1 us
  Pallas kernels  29.6 us (40%)
  starting transfers between devices  26.7 us (36%)
  waiting for transfers between devices  13.5 us (18%)
  local copies, waits for them, and re-layouts  3.42 us (5%)
  between operations  0.83 us (1%)
    ppermute x9, starting transfers between devices, quad(): lax.ppermute(values, axis, [(i, partner(i, turn)) for i in range(count)])  13.5 us
    ppermute x9, waiting for transfers between devices, quad(): lax.ppermute(values, axis, [(i, partner(i, turn)) for i in range(count)])  6.99 us
    pallas_call x1, Pallas kernels, per_device(): pl.pallas_call(inner_kernel, grid=(TILES,), in_specs=[fields_block, whole...  6.96 us
    pallas_call x1, Pallas kernels, per_device(): pl.pallas_call(outer_kernel, grid=(TILES,), in_specs=[low_block, high_blo...  5.88 us
    ppermute x1, waiting for transfers between devices, per_device(): lax.ppermute(east, 'gx', [(i, (i + 1) % columns_total) for i in range(col...  5.72 us
    ppermute x1, starting transfers between devices, per_device(): lax.ppermute(west, 'gx', [((i + 1) % columns_total, i) for i in range(col...  4.65 us
    pallas_call x1, Pallas kernels, per_device(): pl.pallas_call(strips_kernel, in_specs=own_specs, out_specs=[in_vmem] * 2...  4 us
    ppermute x1, starting transfers between devices, terms_over_devices(): lax.ppermute(values, 'gy', [(i, i ^ 1) for i in range(lax.axis_size('gy'))])  3.84 us
  transfers between devices with their start and end apart: 14, of which 7 were waited for; matrix products, arithmetic and copies ran while one was open for 0% of the time, Pallas kernels for 26%

profile of v5, /device:TPU:0, one launch (start us, length us, event | category | flops | bytes accessed | tf_op | source)
XLA Modules:
  0.0 74.1 jit_solution(8696076863830837512)
XLA Ops:
  0.6 1.8 %copy.9.velocity = f32[2,2,62,1800]{3,2,1,0:T(8,128)S(1)} copy(f32[2,2,62,1800]{3,1,2,0:T(2,128)} %param.9) | data formatting | bytes 3571200 | tf_op args[3]
  3.5 1.8 %pack_columns.1 = (f32[8,13,8,128]{3,2,1,0:T(8,128)S(1)}, f32[8,13,8,128]{3,2,1,0:T(8,128)S(1)}) custom-call(s32[2]{0:T(128)S(1)} %copy-done.4, s32[2,1800]{1,0:T(2,128)S(1)} %copy-done.1, f32[2,1800]{1,0:T(2,128)S(1)} %copy-done.2, f32[40,90]{1,0:T(8,128)S(1)} %copy-done, f32[2,2,62,1800]{3,2,1,0:T(8,128)S(1)} %copy.9.velocity, ...), custom_call_target="tpu_custom_call" | custom-call | tf_op jit(solution)/shard_map/pack_columns/pallas_call | solution.py:665
  5.3 2.1 %collective-permute-start = (f32[8,13,8,128]{3,2,1,0:T(8,128)S(1)}, f32[8,13,8,128]{3,2,1,0:T(8,128)S(1)}, u32[]{:S(2)}, u32[]{:S(2)}) collective-permute-start(f32[8,13,8,128]{3,2,1,0:T(8,128)S(1)} %get-tuple-element.20), channel_id=1, source_target_pairs={{0,8},{8,16},{16,24},{24,32},{32,40},{40,48},{48,56},{56,64},{64,7... | collective-permute-start | bytes 1277960 | tf_op jit(solution)/shard_map/ppermute | solution.py:675
  7.4 4.7 %collective-permute-start.1 = (f32[8,13,8,128]{3,2,1,0:T(8,128)S(1)}, f32[8,13,8,128]{3,2,1,0:T(8,128)S(1)}, u32[]{:S(2)}, u32[]{:S(2)}) collective-permute-start(f32[8,13,8,128]{3,2,1,0:T(8,128)S(1)} %get-tuple-element.21), channel_id=1, source_target_pairs={{8,0},{16,8},{24,16},{32,24},{40,32},{48,40},{56,48},{64,56},{72,6... | collective-permute-start | bytes 1277960 | tf_op jit(solution)/shard_map/ppermute | solution.py:676
  12.0 4.0 %strips.1 = (f32[8,4,40,8,128]{4,3,2,1,0:T(8,128)S(1)}, f32[40,8,128]{2,1,0:T(8,128)S(1)}) custom-call(s32[2]{0:T(128)S(1)} %copy-done.4, s32[2,1800]{1,0:T(2,128)S(1)} %copy-done.1, f32[2,1800]{1,0:T(2,128)S(1)} %copy-done.2, f32[40,90]{1,0:T(8,128)S(1)} %copy-done, f32[2,2,62,1800]{3,2,1,0:T(8,128)S(1)} %copy.9.velocity, f32[2,2,62,1800]{3,2,1,0:T(8,128)S(1)} %copy.10.tracers), custom_call_target="tpu_custom_call" | custom-call | flops 30000000 | bytes 9000000 | tf_op jit(solution)/shard_map/strips/pallas_call | solution.py:681
  16.0 5.7 %collective-permute-done.from_west = f32[8,13,8,128]{3,2,1,0:T(8,128)S(1)} collective-permute-done((f32[8,13,8,128]{3,2,1,0:T(8,128)S(1)}, f32[8,13,8,128]{3,2,1,0:T(8,128)S(1)}, u32[]{:S(2)}, u32[]{:S(2)}) %collective-permute-start) | collective-permute-done | bytes 426016 | tf_op jit(solution)/shard_map/ppermute | solution.py:675
  21.8 1.3 %row_message.1 = (f32[8,29,8,128]{3,2,1,0:T(8,128)S(1)}, f32[8,29,8,128]{3,2,1,0:T(8,128)S(1)}) custom-call(f32[8,4,40,8,128]{4,3,2,1,0:T(8,128)S(1)} %get-tuple-element.18.own_fields, f32[40,8,128]{2,1,0:T(8,128)S(1)} %get-tuple-element.19.own_columns, f32[8,13,8,128]{3,2,1,0:T(8,128)S(1)} %collective-permute-done.from_west, ...), custom_call_target="tpu_custom_call" | custom-call | tf_op jit(solution)/shard_map/row_message/pallas_call | solution.py:692
  23.0 1.4 %collective-permute-start.2 = (f32[8,29,8,128]{3,2,1,0:T(8,128)S(1)}, f32[8,29,8,128]{3,2,1,0:T(8,128)S(1)}, u32[]{:S(2)}, u32[]{:S(2)}) collective-permute-start(f32[8,29,8,128]{3,2,1,0:T(8,128)S(1)} %get-tuple-element.25), channel_id=1, source_target_pairs={{0,1},{1,2},{2,3},{3,4},{4,5},{5,6},{6,7},{8,9},{9,10},{10,11},{11... | collective-permute-start | bytes 2850824 | tf_op jit(solution)/shard_map/ppermute | solution.py:712
  24.4 1.3 %collective-permute-start.3 = (f32[8,29,8,128]{3,2,1,0:T(8,128)S(1)}, f32[8,29,8,128]{3,2,1,0:T(8,128)S(1)}, u32[]{:S(2)}, u32[]{:S(2)}) collective-permute-start(f32[8,29,8,128]{3,2,1,0:T(8,128)S(1)} %get-tuple-element.26), channel_id=1, source_target_pairs={{1,0},{2,1},{3,2},{4,3},{5,4},{6,5},{7,6},{9,8},{10,9},{11,10},{12... | collective-permute-start | bytes 2850824 | tf_op jit(solution)/shard_map/ppermute | solution.py:713
  25.7 2.1 %halos.1 = (f32[8,4,40,8,128]{4,3,2,1,0:T(8,128)S(1)}, f32[40,8,128]{2,1,0:T(8,128)S(1)}) custom-call(f32[8,4,40,8,128]{4,3,2,1,0:T(8,128)S(1)} %get-tuple-element.18.own_fields, f32[40,8,128]{2,1,0:T(8,128)S(1)} %get-tuple-element.19.own_columns, f32[8,13,8,128]{3,2,1,0:T(8,128)S(1)} %collective-permute-done.from_west, ...), custom_call_target="tpu_custom_call" | custom-call | flops 30000000 | bytes 9000000 | tf_op jit(solution)/shard_map/halos/pallas_call | solution.py:701
  27.8 7.0 %inner_rows.1 = (f32[8,2,8,8,128]{4,3,2,1,0:T(8,128)S(1)}, f32[8,2,32,8,128]{4,3,2,1,0:T(8,128)S(1)}, f32[40,8,128]{2,1,0:T(8,128)S(1)}) custom-call(f32[8,4,40,8,128]{4,3,2,1,0:T(8,128)S(1)} %get-tuple-element.22.fields.low_fields.high_fields, f32[40,8,128]{2,1,0:T(8,128)S(1)} %get-tuple-element.23.columns), custom_call_target="tpu_custom_call" | custom-call | flops 60000000 | bytes 10000000 | tf_op jit(solution)/shard_map/inner_rows/pallas_call | solution.py:719
  34.8 3.0 %inner_slots.1.inner = f32[2,62,2,1800]{3,2,1,0:T(2,128)} custom-call(s32[2]{0:T(128)S(1)} %copy-done.4, f32[8,2,32,8,128]{4,3,2,1,0:T(8,128)S(1)} %get-tuple-element.24.moved), custom_call_target="tpu_custom_call" | custom-call | flops 20000000 | bytes 6000000 | tf_op jit(solution)/shard_map/inner_slots/pallas_call | solution.py:732
  37.8 5.9 %outer_rows.1 = (f32[8,2,8,8,128]{4,3,2,1,0:T(8,128)S(1)}, f32[3,40,128]{2,1,0:T(8,128)S(1)}, f32[8,128]{1,0:T(8,128)S(1)}) custom-call(f32[8,4,40,8,128]{4,3,2,1,0:T(8,128)S(1)} %get-tuple-element.22.fields.low_fields.high_fields, f32[8,4,40,8,128]{4,3,2,1,0:T(8,128)S(1)} %get-tuple-element.22.fields.low_fields.high_fields, ...), custom_call_target="tpu_custom_call" | custom-call | tf_op jit(solution)/shard_map/outer_rows/pallas_call | solution.py:749
  43.7 3.8 %collective-permute-start.4 = (f32[8,128]{1,0:T(8,128)S(1)}, f32[8,128]{1,0:T(8,128)S(1)}, u32[]{:S(2)}, u32[]{:S(2)}) collective-permute-start(f32[8,128]{1,0:T(8,128)S(1)} %get-tuple-element.32), channel_id=1, source_target_pairs={{0,1},{1,0},{2,3},{3,2},{4,5},{5,4},{6,7},{7,6},{8,9},{9,8},{10,11... | collective-permute-start | bytes 12296 | tf_op jit(solution)/shard_map/ppermute | solution.py:625
  48.4 2.3 %collective-permute-start.7 = (f32[8,128]{1,0:T(8,128)S(1)}, f32[8,128]{1,0:T(8,128)S(1)}, u32[]{:S(2)}, u32[]{:S(2)}) collective-permute-start(f32[8,128]{1,0:T(8,128)S(1)} %add.21), channel_id=1, source_target_pairs={{0,6},{1,7},{2,4},{3,5},{4,2},{5,3},{6,0},{7,1},{8,14},{9,15},{10,... | collective-permute-start | bytes 12296 | tf_op jit(solution)/shard_map/ppermute | solution.py:613
  50.7 1.3 %collective-permute-start.6 = (f32[8,128]{1,0:T(8,128)S(1)}, f32[8,128]{1,0:T(8,128)S(1)}, u32[]{:S(2)}, u32[]{:S(2)}) collective-permute-start(f32[8,128]{1,0:T(8,128)S(1)} %add.21), channel_id=1, source_target_pairs={{0,4},{1,5},{2,6},{3,7},{4,0},{5,1},{6,2},{7,3},{8,12},{9,13},{10,... | collective-permute-start | bytes 12296 | tf_op jit(solution)/shard_map/ppermute | solution.py:613
  53.2 2.6 %collective-permute-done.6 = f32[8,128]{1,0:T(8,128)S(1)} collective-permute-done((f32[8,128]{1,0:T(8,128)S(1)}, f32[8,128]{1,0:T(8,128)S(1)}, u32[]{:S(2)}, u32[]{:S(2)}) %collective-permute-start.6) | collective-permute-done | bytes 4128 | tf_op jit(solution)/shard_map/ppermute | solution.py:613
  55.8 1.6 %collective-permute-start.10 = (f32[8,128]{1,0:T(8,128)S(1)}, f32[8,128]{1,0:T(8,128)S(1)}, u32[]{:S(2)}, u32[]{:S(2)}) collective-permute-start(f32[8,128]{1,0:T(8,128)S(1)} %add_add_fusion.1), channel_id=1, source_target_pairs={{0,24},{8,16},{16,8},{24,0},{32,56},{40,48},{48,40},{56,32},{64,88... | collective-permute-start | bytes 12296 | tf_op jit(solution)/shard_map/ppermute | solution.py:613
  57.4 2.6 %collective-permute-start.8 = (f32[8,128]{1,0:T(8,128)S(1)}, f32[8,128]{1,0:T(8,128)S(1)}, u32[]{:S(2)}, u32[]{:S(2)}) collective-permute-start(f32[8,128]{1,0:T(8,128)S(1)} %add_add_fusion.1), channel_id=1, source_target_pairs={{0,8},{8,0},{16,24},{24,16},{32,40},{40,32},{48,56},{56,48},{64,72... | collective-permute-start | bytes 12296 | tf_op jit(solution)/shard_map/ppermute | solution.py:613
  60.7 1.8 %collective-permute-done.9 = f32[8,128]{1,0:T(8,128)S(1)} collective-permute-done((f32[8,128]{1,0:T(8,128)S(1)}, f32[8,128]{1,0:T(8,128)S(1)}, u32[]{:S(2)}, u32[]{:S(2)}) %collective-permute-start.9) | collective-permute-done | bytes 4128 | tf_op jit(solution)/shard_map/ppermute | solution.py:613
  62.5 4.3 %collective-permute-start.13 = (f32[8,128]{1,0:T(8,128)S(1)}, f32[8,128]{1,0:T(8,128)S(1)}, u32[]{:S(2)}, u32[]{:S(2)}) collective-permute-start(f32[8,128]{1,0:T(8,128)S(1)} %add_add_fusion.first), channel_id=1, source_target_pairs={{0,96},{8,104},{16,112},{24,120},{32,64},{40,72},{48,80},{56,88},{... | collective-permute-start | bytes 12296 | tf_op jit(solution)/shard_map/ppermute | solution.py:613
  67.7 2.9 %outer_slots.1 = f32[2,62,2,1800]{3,2,1,0:T(2,128)} custom-call(s32[2]{0:T(128)S(1)} %copy-done.4, f32[8,2,32,8,128]{4,3,2,1,0:T(8,128)S(1)} %get-tuple-element.24.moved, f32[8,2,8,8,128]{4,3,2,1,0:T(8,128)S(1)} %get-tuple-element.30.edges, f32[2,62,2,1800]{3,2,1,0:T(2,128)} %inner_slots.1.inner), custom_call_target="tpu_custom_call", output_to_operand_aliasing={{}: (3, {})} | custom-call | flops 2000000 | bytes 2000000 | tf_op jit(solution)/shard_map/outer_slots/pallas_call | solution.py:769
  70.7 1.2 %collective-permute-done.12.third = f32[8,128]{1,0:T(8,128)S(1)} collective-permute-done((f32[8,128]{1,0:T(8,128)S(1)}, f32[8,128]{1,0:T(8,128)S(1)}, u32[]{:S(2)}, u32[]{:S(2)}) %collective-permute-start.12) | collective-permute-done | bytes 4128 | tf_op jit(solution)/shard_map/ppermute | solution.py:613
  72.5 1.6 %finish.1 = f32[40,90]{1,0:T(8,128)} custom-call(f32[8,128]{1,0:T(8,128)} %copy-done.6, f32[8,128]{1,0:T(8,128)} %copy-done.9, f32[8,128]{1,0:T(8,128)} %copy-done.8, f32[8,128]{1,0:T(8,128)} %copy-done.7, f32[3,40,128]{2,1,0:T(8,128)} %copy-done.3), custom_call_target="tpu_custom_call" | custom-call | tf_op jit(solution)/shard_map/finish/pallas_call | solution.py:789
  (38 shorter events, 5.4 us)
Async XLA Ops:
  0.6 2.1 %copy-start.5 = (f32[2,2,62,1800]{3,1,2,0:T(2,128)S(1)}, f32[2,2,62,1800]{3,1,2,0:T(2,128)}, u32[]{:S(2)}) copy-start(f32[2,2,62,1800]{3,1,2,0:T(2,128)} %param.10) | copy-start | bytes 5356804
  2.7 0.7 copy-start
  2.7 0.7 copy-start.1
  2.7 0.7 %copy-start.2 = (f32[2,1800]{1,0:T(2,128)S(1)}, f32[2,1800]{1,0:T(2,128)}, u32[]{:S(2)}) copy-start(f32[2,1800]{1,0:T(2,128)} %mixing.3) | copy-start | bytes 43204
  2.7 0.7 %copy-start.4 = (s32[2]{0:T(128)S(1)}, s32[2]{0:T(128)}, u32[]{:S(2)}) copy-start(s32[2]{0:T(128)} %block_list.7) | copy-start | bytes 28
  5.3 16.5 %collective-permute-start = (f32[8,13,8,128]{3,2,1,0:T(8,128)S(1)}, f32[8,13,8,128]{3,2,1,0:T(8,128)S(1)}, u32[]{:S(2)}, u32[]{:S(2)}) collective-permute-start(f32[8,13,8,128]{3,2,1,0:T(8,128)S(1)} %get-tuple-element.20), channel_id=1, source_target_pairs={{0,8},{8,16},{16,24},{24,32},{32,40},{40,48},{48,56},{56,64},{64,7... | collective-permute-start | bytes 1277960 | tf_op jit(solution)/shard_map/ppermute | solution.py:675
  7.4 14.4 %collective-permute-start.1 = (f32[8,13,8,128]{3,2,1,0:T(8,128)S(1)}, f32[8,13,8,128]{3,2,1,0:T(8,128)S(1)}, u32[]{:S(2)}, u32[]{:S(2)}) collective-permute-start(f32[8,13,8,128]{3,2,1,0:T(8,128)S(1)} %get-tuple-element.21), channel_id=1, source_target_pairs={{8,0},{16,8},{24,16},{32,24},{40,32},{48,40},{56,48},{64,56},{72,6... | collective-permute-start | bytes 1277960 | tf_op jit(solution)/shard_map/ppermute | solution.py:676
  23.0 14.8 %collective-permute-start.2 = (f32[8,29,8,128]{3,2,1,0:T(8,128)S(1)}, f32[8,29,8,128]{3,2,1,0:T(8,128)S(1)}, u32[]{:S(2)}, u32[]{:S(2)}) collective-permute-start(f32[8,29,8,128]{3,2,1,0:T(8,128)S(1)} %get-tuple-element.25), channel_id=1, source_target_pairs={{0,1},{1,2},{2,3},{3,4},{4,5},{5,6},{6,7},{8,9},{9,10},{10,11},{11... | collective-permute-start | bytes 2850824 | tf_op jit(solution)/shard_map/ppermute | solution.py:712
  24.4 13.4 %collective-permute-start.3 = (f32[8,29,8,128]{3,2,1,0:T(8,128)S(1)}, f32[8,29,8,128]{3,2,1,0:T(8,128)S(1)}, u32[]{:S(2)}, u32[]{:S(2)}) collective-permute-start(f32[8,29,8,128]{3,2,1,0:T(8,128)S(1)} %get-tuple-element.26), channel_id=1, source_target_pairs={{1,0},{2,1},{3,2},{4,3},{5,4},{6,5},{7,6},{9,8},{10,9},{11,10},{12... | collective-permute-start | bytes 2850824 | tf_op jit(solution)/shard_map/ppermute | solution.py:713
  43.7 26.9 %copy-start.3 = (f32[3,40,128]{2,1,0:T(8,128)}, f32[3,40,128]{2,1,0:T(8,128)S(1)}, u32[]{:S(2)}) copy-start(f32[3,40,128]{2,1,0:T(8,128)S(1)} %get-tuple-element.33.basis) | copy-start | bytes 184324
  43.7 4.7 %collective-permute-start.4 = (f32[8,128]{1,0:T(8,128)S(1)}, f32[8,128]{1,0:T(8,128)S(1)}, u32[]{:S(2)}, u32[]{:S(2)}) collective-permute-start(f32[8,128]{1,0:T(8,128)S(1)} %get-tuple-element.32), channel_id=1, source_target_pairs={{0,1},{1,0},{2,3},{3,2},{4,5},{5,4},{6,7},{7,6},{8,9},{9,8},{10,11... | collective-permute-start | bytes 12296 | tf_op jit(solution)/shard_map/ppermute | solution.py:625
  48.4 4.8 %collective-permute-start.7 = (f32[8,128]{1,0:T(8,128)S(1)}, f32[8,128]{1,0:T(8,128)S(1)}, u32[]{:S(2)}, u32[]{:S(2)}) collective-permute-start(f32[8,128]{1,0:T(8,128)S(1)} %add.21), channel_id=1, source_target_pairs={{0,6},{1,7},{2,4},{3,5},{4,2},{5,3},{6,0},{7,1},{8,14},{9,15},{10,... | collective-permute-start | bytes 12296 | tf_op jit(solution)/shard_map/ppermute | solution.py:613
  50.7 5.1 %collective-permute-start.6 = (f32[8,128]{1,0:T(8,128)S(1)}, f32[8,128]{1,0:T(8,128)S(1)}, u32[]{:S(2)}, u32[]{:S(2)}) collective-permute-start(f32[8,128]{1,0:T(8,128)S(1)} %add.21), channel_id=1, source_target_pairs={{0,4},{1,5},{2,6},{3,7},{4,0},{5,1},{6,2},{7,3},{8,12},{9,13},{10,... | collective-permute-start | bytes 12296 | tf_op jit(solution)/shard_map/ppermute | solution.py:613
  52.0 3.8 %collective-permute-start.5 = (f32[8,128]{1,0:T(8,128)S(1)}, f32[8,128]{1,0:T(8,128)S(1)}, u32[]{:S(2)}, u32[]{:S(2)}) collective-permute-start(f32[8,128]{1,0:T(8,128)S(1)} %add.21), channel_id=1, source_target_pairs={{0,2},{1,3},{2,0},{3,1},{4,6},{5,7},{6,4},{7,5},{8,10},{9,11},{10,... | collective-permute-start | bytes 12296 | tf_op jit(solution)/shard_map/ppermute | solution.py:613
  55.8 4.9 %collective-permute-start.10 = (f32[8,128]{1,0:T(8,128)S(1)}, f32[8,128]{1,0:T(8,128)S(1)}, u32[]{:S(2)}, u32[]{:S(2)}) collective-permute-start(f32[8,128]{1,0:T(8,128)S(1)} %add_add_fusion.1), channel_id=1, source_target_pairs={{0,24},{8,16},{16,8},{24,0},{32,56},{40,48},{48,40},{56,32},{64,88... | collective-permute-start | bytes 12296 | tf_op jit(solution)/shard_map/ppermute | solution.py:613
  57.4 5.1 %collective-permute-start.9 = (f32[8,128]{1,0:T(8,128)S(1)}, f32[8,128]{1,0:T(8,128)S(1)}, u32[]{:S(2)}, u32[]{:S(2)}) collective-permute-start(f32[8,128]{1,0:T(8,128)S(1)} %add_add_fusion.1), channel_id=1, source_target_pairs={{0,16},{8,24},{16,0},{24,8},{32,48},{40,56},{48,32},{56,40},{64,80... | collective-permute-start | bytes 12296 | tf_op jit(solution)/shard_map/ppermute | solution.py:613
  57.4 5.1 %collective-permute-start.8 = (f32[8,128]{1,0:T(8,128)S(1)}, f32[8,128]{1,0:T(8,128)S(1)}, u32[]{:S(2)}, u32[]{:S(2)}) collective-permute-start(f32[8,128]{1,0:T(8,128)S(1)} %add_add_fusion.1), channel_id=1, source_target_pairs={{0,8},{8,0},{16,24},{24,16},{32,40},{40,32},{48,56},{56,48},{64,72... | collective-permute-start | bytes 12296 | tf_op jit(solution)/shard_map/ppermute | solution.py:613
  62.5 8.2 %copy-start.6 = (f32[8,128]{1,0:T(8,128)}, f32[8,128]{1,0:T(8,128)S(1)}, u32[]{:S(2)}) copy-start(f32[8,128]{1,0:T(8,128)S(1)} %add_add_fusion.first) | copy-start | bytes 12292
  62.5 8.2 %collective-permute-start.13 = (f32[8,128]{1,0:T(8,128)S(1)}, f32[8,128]{1,0:T(8,128)S(1)}, u32[]{:S(2)}, u32[]{:S(2)}) collective-permute-start(f32[8,128]{1,0:T(8,128)S(1)} %add_add_fusion.first), channel_id=1, source_target_pairs={{0,96},{8,104},{16,112},{24,120},{32,64},{40,72},{48,80},{56,88},{... | collective-permute-start | bytes 12296 | tf_op jit(solution)/shard_map/ppermute | solution.py:613
  66.8 5.1 %collective-permute-start.12 = (f32[8,128]{1,0:T(8,128)S(1)}, f32[8,128]{1,0:T(8,128)S(1)}, u32[]{:S(2)}, u32[]{:S(2)}) collective-permute-start(f32[8,128]{1,0:T(8,128)S(1)} %add_add_fusion.first), channel_id=1, source_target_pairs={{0,64},{8,72},{16,80},{24,88},{32,96},{40,104},{48,112},{56,120},{... | collective-permute-start | bytes 12296 | tf_op jit(solution)/shard_map/ppermute | solution.py:613
  66.8 5.1 %collective-permute-start.11 = (f32[8,128]{1,0:T(8,128)S(1)}, f32[8,128]{1,0:T(8,128)S(1)}, u32[]{:S(2)}, u32[]{:S(2)}) collective-permute-start(f32[8,128]{1,0:T(8,128)S(1)} %add_add_fusion.first), channel_id=1, source_target_pairs={{0,32},{8,40},{16,48},{24,56},{32,0},{40,8},{48,16},{56,24},{64,96... | collective-permute-start | bytes 12296 | tf_op jit(solution)/shard_map/ppermute | solution.py:613
  70.7 1.2 %copy-start.7 = (f32[8,128]{1,0:T(8,128)}, f32[8,128]{1,0:T(8,128)S(1)}, u32[]{:S(2)}) copy-start(f32[8,128]{1,0:T(8,128)S(1)} %collective-permute-done.13.fourth) | copy-start | bytes 12292
  71.9 0.6 copy-start.8
  71.9 0.6 copy-start.9

commit v6 on v5

--- a/solution.py
+++ b/solution.py
@@ -16,6 +16,7 @@
 TILES = 8
 REACH = 7
 ROWS = BY + 2 * REACH
+PARTS = 2
 AHEAD = 26
 BASE = 8
 WIDE = 2 * BX
@@ -282,57 +283,58 @@
 
 
 class Band:
-    def __init__(self, low, high, read, write, eastward, northward):
+    def __init__(self, low, high, read, write, eastward, northward, levels, part=0):
         self.low, self.high, self.read, self.write = low, high, read, write
         self.eastward, self.northward = eastward, northward
-
-
-def advance(bands, levels, shared, scratch):
+        self.levels, self.part = levels, 2 * part
+
+
+def advance(bands, shared, scratch):
     depth_east, depth_north, mix = shared
     scaled, held = scratch
 
     def rise(band, n, row):
         read = bands[band].read
-        return jnp.where(levels < depth_north(row), read(n, row + 1) - read(n, row), 0.0)
+        return jnp.where(bands[band].levels < depth_north(row), read(n, row + 1) - read(n, row), 0.0)
 
     def look_east(band, row, state):
         for n in range(2):
             state[band, n, row] = turn(bands[band].read(n, row), LANES - 1)
 
     def step_east(band, row, state):
-        wet = levels < depth_east(row)
+        wet = bands[band].levels < depth_east(row)
         for n in range(2):
             here, beside = bands[band].read(n, row), state[band, n, row]
             step = jnp.where(wet, beside - here, 0.0)
             state[band, n, row] = step, turn(step, 1)
-            held[n, row + REACH] = beside + here
+            held[bands[band].part + n, row + REACH] = beside + here
 
     def scale(band, row, state):
         for n in range(2):
             step, back = state.pop((band, n, row))
             drop = state.pop((band, n)) if (band, n) in state else rise(band, n, row - 1)
             state[band, n] = rise(band, n, row)
-            scaled[n, row + REACH] = mix(row) * ((step - back) + (state[band, n] - drop))
+            scaled[bands[band].part + n, row + REACH] = mix(row) * ((step - back) + (state[band, n] - drop))
 
     staggered([(b.low - 1, b.high + 1) for b in bands], (look_east, step_east, scale))
 
     def north_flow(band, n, row):
         read, northward = bands[band].read, bands[band].northward
-        step = scaled[n, row + 1 + REACH] - scaled[n, row + REACH]
+        step = scaled[bands[band].part + n, row + 1 + REACH] - scaled[bands[band].part + n, row + REACH]
         both = (northward(row) + northward(row + 1)) * (read(n, row) + read(n, row + 1)) + step
-        return jnp.where(levels < depth_north(row), both, 0.0)
+        return jnp.where(bands[band].levels < depth_north(row), both, 0.0)
 
     def look_east_again(band, row, state):
         state[band, "flow", row] = turn(bands[band].eastward(row), LANES - 1)
         for n in range(2):
-            state[band, n, row] = turn(scaled[n, row + REACH], LANES - 1)
+            state[band, n, row] = turn(scaled[bands[band].part + n, row + REACH], LANES - 1)
 
     def east_flow(band, row, state):
-        wet = levels < depth_east(row)
+        wet = bands[band].levels < depth_east(row)
         flow = bands[band].eastward(row) + state.pop((band, "flow", row))
         for n in range(2):
             at = row + REACH
-            both = flow * held[n, at] + (state[band, n, row] - scaled[n, at])
+            both = flow * held[bands[band].part + n, at] + (state[band, n, row] - scaled[bands[band].part + n, at])
             both = jnp.where(wet, both, 0.0)
             state[band, n, row] = both, turn(both, 1)
 
@@ -406,10 +408,10 @@
     def northward(row):
         return fields[0, 3, row]
 
-    first = Band(2, 37, lambda n, row: fields[0, n, row], write_middle, eastward, northward)
-    second = Band(4, 35, lambda n, row: middle[n, row], write_moved, eastward, northward)
-    advance([first], levels, shared, (scaled, held))
-    advance([second], levels, shared, (scaled, held))
+    first = Band(2, 37, lambda n, row: fields[0, n, row], write_middle, eastward, northward, levels)
+    second = Band(4, 35, lambda n, row: middle[n, row], write_moved, eastward, northward, levels)
+    advance([first], shared, (scaled, held))
+    advance([second], shared, (scaled, held))
     for row in range(4, 36):
         forcing[row] += contribution(
             levels, depth[row + REACH], moved[0, 0, row - 4], moved[0, 1, row - 4]
@@ -443,54 +445,52 @@
         spread_columns(column, rows, depth, depth_east, depth_north, mix)
         forcing[...] = jnp.zeros_like(forcing)
 
-    levels = level_ids(step)
     shared = (
         lambda row: depth_east[row + REACH],
         lambda row: depth_north[row + REACH],
         lambda row: mix[row + REACH],
     )
-
-    def field(number, row):
-        if row < 0:
-            return up[0, REACH * number + row + REACH]
-        if row >= BY:
-            return down[0, REACH * number + row - BY]
-        return low_fields[0, number, row] if row < 10 else high_fields[0, number, row - 30]
-
-    def read_middle(n, row):
-        if 2 <= row < 6:
-            return halfway[0, n, row - 2]
-        if 34 <= row < 38:
-            return halfway[0, n, row - 30]
-        return middle[n, row + REACH]
-
-    def write_middle(n, row, value):
-        middle[n, row + REACH] = value
-
-    def write_beyond(n, row, value):
-        beyond[n, row + REACH] = value
-        if 0 <= row < 4:
-            moved[0, n, row] = value
-        if 36 <= row < BY:
-            moved[0, n, row - 32] = value
-
-    def eastward(row):
-        return field(2, row)
-
-    def northward(row):
-        return field(3, row)
-
-    bands = [Band(low, high, field, write_middle, eastward, northward) for low, high in ((-5, 1), (38, 44))]
-    advance(bands, levels, shared, (scaled, held))
-    bands = [
-        Band(low, high, read_middle, write_beyond, eastward, northward) for low, high in ((-3, 3), (36, 42))
-    ]
-    advance(bands, levels, shared, (scaled, held))
+    first, second = [], []
+    for part in range(PARTS):
+        levels = level_ids(PARTS * step + part)
+
+        def field(number, row, part=part):
+            if row < 0:
+                return up[part, REACH * number + row + REACH]
+            if row >= BY:
+                return down[part, REACH * number + row - BY]
+            return low_fields[part, number, row] if row < 10 else high_fields[part, number, row - 30]
+
+        def read_middle(n, row, part=part):
+            if 2 <= row < 6:
+                return halfway[part, n, row - 2]
+            if 34 <= row < 38:
+                return halfway[part, n, row - 30]
+            return middle[2 * part + n, row + REACH]
+
+        def write_middle(n, row, value, part=part):
+            middle[2 * part + n, row + REACH] = value
+
+        def write_beyond(n, row, value, part=part):
+            beyond[2 * part + n, row + REACH] = value
+            if 0 <= row < 4:
+                moved[part, n, row] = value
+            if 36 <= row < BY:
+                moved[part, n, row - 32] = value
+
+        flows = (functools.partial(field, 2), functools.partial(field, 3), levels, part)
+        first += [Band(low, high, field, write_middle, *flows) for low, high in ((-5, 1), (38, 44))]
+        second += [Band(low, high, read_middle, write_beyond, *flows) for low, high in ((-3, 3), (36, 42))]
+    advance(first, shared, (scaled, held))
+    advance(second, shared, (scaled, held))
     for row in (*range(-3, 4), *range(36, 43)):
         at = row + REACH
-        forcing[at] += contribution(levels, depth[at], beyond[0, at], beyond[1, at])
-
-    @pl.when(step == TILES - 1)
+        for part in range(PARTS):
+            forcing[at] += contribution(
+                second[2 * part].levels, depth[at], beyond[2 * part, at], beyond[2 * part + 1, at]
+            )
+
+    @pl.when(step == TILES // PARTS - 1)
     def _():
         surface[...] = jnp.zeros_like(surface)
         for row in range(-3, 43):
@@ -572,20 +572,17 @@
     copy.wait()
 
 
-def outer_slots_kernel(block_list, moved, edges, inner, out, low, high, low_semaphore, high_semaphore):
+def outer_slots_kernel(numbers, block_list, moved, edges, inner, out, cells, semaphore):
     def load(block, n, row):
         if 4 <= row < 36:
             return moved[block, n, row - 4]
         return edges[block, n, row if row < 4 else row - 32]
 
-    to_slots((0, 1), 0, (0, BY - 1), load, block_list, low)
-    low_copy = pltpu.make_async_copy(low, out.at[:, :, :, 0 : 2 * LANES], low_semaphore)
-    low_copy.start()
-    to_slots((12, 13, 14), 12 * LANES, (0, BY - 1), load, block_list, high)
-    high_copy = pltpu.make_async_copy(high, out.at[:, :, :, 12 * LANES : CELLS], high_semaphore)
-    high_copy.start()
-    low_copy.wait()
-    high_copy.wait()
+    start, end = numbers[0] * LANES, min((numbers[-1] + 1) * LANES, CELLS)
+    to_slots(numbers, start, (0, BY - 1), load, block_list, cells)
+    copy = pltpu.make_async_copy(cells, out.at[:, :, :, start:end], semaphore)
+    copy.start()
+    copy.wait()
 
 
 def finish_kernel(first, second, third, fourth, basis, out):
@@ -621,11 +618,13 @@
     return (four[0] + four[1]) + (four[2] + four[3])
 
 
-def terms_over_devices(values):
+def terms_over_devices(values, beside):
     values = values + lax.ppermute(values, "gy", [(i, i ^ 1) for i in range(lax.axis_size("gy"))])
     values = quad_sum(values, "gy", lambda i, turn: i ^ (2 * turn))
+    values, done = lax.optimization_barrier((values, beside[0]()))
     values = quad_sum(values, "gx", lambda i, turn: i ^ turn)
-    return quad(values, "gx", lambda i, turn: i ^ (4 * turn))
+    values, done = lax.optimization_barrier((values, beside[1](done)))
+    return quad(values, "gx", lambda i, turn: i ^ (4 * turn)), done
 
 
 def held_in_vmem(arrays):
@@ -654,7 +653,7 @@
             jax.ShapeDtypeStruct((TILES, *shape, 8, LANES), f32),
         )
 
-    rows_block, rows_type = tiles(NS)
+    _, rows_type = tiles(NS)
     _, columns_type = tiles(EW)
     rows_extra = pl.BlockSpec((TILES, 1, 8, LANES), lambda k: (0, NS - 1, 0, 0))
     in_vmem = pl.BlockSpec(memory_space=pltpu.VMEM)
@@ -744,53 +743,59 @@
     )(block_list, moved)
     inner_slots, forcing = lax.optimization_barrier((inner_slots, forcing))
 
-    low_block = pl.BlockSpec((1, 4, 10, 8, LANES), lambda k: (k, 0, 0, 0, 0))
-    high_block = pl.BlockSpec((1, 4, 10, 8, LANES), lambda k: (k, 0, 3, 0, 0))
+    low_block = pl.BlockSpec((PARTS, 4, 10, 8, LANES), lambda k: (k, 0, 0, 0, 0))
+    high_block = pl.BlockSpec((PARTS, 4, 10, 8, LANES), lambda k: (k, 0, 3, 0, 0))
+    part_rows = pl.BlockSpec((PARTS, NS, 8, LANES), lambda k: (k, 0, 0, 0))
+    part_halfway = pl.BlockSpec((PARTS, 2, 8, 8, LANES), lambda k: (k, 0, 0, 0, 0))
+    parts_store = pltpu.VMEM((2 * PARTS, ROWS, 8, LANES), f32)
     edges, basis, moments = pl.pallas_call(
         outer_kernel,
-        grid=(TILES,),
-        in_specs=[low_block, high_block, whole(column_shape), rows_block, rows_block]
-        + [rows_extra, rows_extra, halfway_block, whole(column_shape)],
-        out_specs=[halfway_block, whole((3, BY, LANES)), whole((8, LANES))],
+        grid=(TILES // PARTS,),
+        in_specs=[low_block, high_block, whole(column_shape), part_rows, part_rows]
+        + [rows_extra, rows_extra, part_halfway, whole(column_shape)],
+        out_specs=[part_halfway, whole((3, BY, LANES)), whole((8, LANES))],
         out_shape=[
             halfway_type,
             jax.ShapeDtypeStruct((3, BY, LANES), f32),
             jax.ShapeDtypeStruct((8, LANES), f32),
         ],
-        scratch_shapes=[pair_store] * 2
+        scratch_shapes=[parts_store] * 2
         + [row_store] * 4
-        + [pair_store] * 2
+        + [parts_store] * 2
         + [row_store]
         + [pltpu.VMEM((SURFACE, LANES), f32)] * 3,
         compiler_params=params,
         name="outer_rows",
     )(fields, fields, columns, from_below, from_above, from_below, from_above, halfway, forcing)
 
-    new_tracers = pl.pallas_call(
-        outer_slots_kernel,
-        in_specs=[pl.BlockSpec(memory_space=pltpu.SMEM), in_vmem, in_vmem]
-        + [pl.BlockSpec(memory_space=pl.ANY)],
-        out_specs=pl.BlockSpec(memory_space=pl.ANY),
-        out_shape=slots_type,
-        scratch_shapes=[
-            pltpu.VMEM((slots, levels, fields_each, 2 * LANES), f32),
-            pltpu.VMEM((slots, levels, fields_each, cells - 12 * LANES), f32),
-            pltpu.SemaphoreType.DMA,
-            pltpu.SemaphoreType.DMA,
-        ],
-        input_output_aliases={3: 0},
-        compiler_params=whole_params,
-        cost_estimate=pl.CostEstimate(flops=2_000_000, bytes_accessed=2_000_000, transcendentals=0),
-        name="outer_slots",
-    )(block_list, moved, edges, inner_slots)
+    def outer_slots(numbers, before):
+        width = min((numbers[-1] + 1) * LANES, cells) - numbers[0] * LANES
+        return pl.pallas_call(
+            functools.partial(outer_slots_kernel, numbers),
+            in_specs=[pl.BlockSpec(memory_space=pltpu.SMEM), in_vmem, in_vmem]
+            + [pl.BlockSpec(memory_space=pl.ANY)],
+            out_specs=pl.BlockSpec(memory_space=pl.ANY),
+            out_shape=slots_type,
+            scratch_shapes=[
+                pltpu.VMEM((slots, levels, fields_each, width), f32),
+                pltpu.SemaphoreType.DMA,
+            ],
+            input_output_aliases={3: 0},
+            compiler_params=whole_params,
+            cost_estimate=pl.CostEstimate(flops=2_000_000, bytes_accessed=2_000_000, transcendentals=0),
+            name="outer_slots",
+        )(block_list, moved, edges, before)
+
+    beside = (lambda: outer_slots((0, 1), inner_slots), lambda before: outer_slots((12, 13, 14), before))
+    moments, new_tracers = terms_over_devices(moments, beside)
     new_tracers = jnp.transpose(new_tracers, (0, 2, 1, 3))
-
-    moments = terms_over_devices(moments)
     height = pl.pallas_call(
         finish_kernel,
+        in_specs=[in_vmem] * 5,
+        out_specs=in_vmem,
         out_shape=jax.ShapeDtypeStruct((BY, WIDE), f32),
         name="finish",
-    )(*moments, basis)
+    )(*held_in_vmem((*moments, basis)))
     return (new_tracers, height)
 
 

time: 74.4 us -> 71.1 us (0.956)
  Pallas kernels: 29.6 us -> 28.3 us
    pallas_call x3 -> x4, Pallas kernels: 10.4 us -> 9.1 us  [the longest x1 4.19 us: per_device(): pl.pallas_call(outer_kernel, grid=(TILES // PARTS,), in_specs=[low_block,...]
    unnamed x22 -> x12, local copies, waits for them, and re-layouts: 3.42 us -> 2.82 us
  transfers between devices with their start and end apart: 14 -> 14, of which waited for: 7 -> 6; matrix products, arithmetic and copies ran while one was open for 0% -> 0% of each run, Pallas kernels for 26% -> 29%
where the time goes in v6:
time: 71.1 us; the launch traced here: 70.9 us
  Pallas kernels  28.3 us (40%)
  starting transfers between devices  26 us (37%)
  waiting for transfers between devices  13 us (18%)
  local copies, waits for them, and re-layouts  2.82 us (4%)
  between operations  0.81 us (1%)
    ppermute x9, starting transfers between devices, quad(): lax.ppermute(values, axis, [(i, partner(i, turn)) for i in range(count)])  12.8 us
    pallas_call x1, Pallas kernels, per_device(): pl.pallas_call(inner_kernel, grid=(TILES,), in_specs=[fields_block, whole...  6.96 us
    ppermute x9, waiting for transfers between devices, quad(): lax.ppermute(values, axis, [(i, partner(i, turn)) for i in range(count)])  6.4 us
    ppermute x1, waiting for transfers between devices, per_device(): lax.ppermute(east, 'gx', [(i, (i + 1) % columns_total) for i in range(col...  5.72 us
    ppermute x1, starting transfers between devices, per_device(): lax.ppermute(west, 'gx', [((i + 1) % columns_total, i) for i in range(col...  4.65 us
    pallas_call x1, Pallas kernels, per_device(): pl.pallas_call(outer_kernel, grid=(TILES // PARTS,), in_specs=[low_block,...  4.19 us
    pallas_call x2, Pallas kernels, outer_slots(): pl.pallas_call(functools.partial(outer_slots_kernel, numbers), in_specs=[...  4.15 us
    pallas_call x1, Pallas kernels, per_device(): pl.pallas_call(strips_kernel, in_specs=own_specs, out_specs=[in_vmem] * 2...  4 us
  transfers between devices with their start and end apart: 14, of which 6 were waited for; matrix products, arithmetic and copies ran while one was open for 0% of the time, Pallas kernels for 29%

profile of v6, /device:TPU:0, one launch (start us, length us, event | category | flops | bytes accessed | tf_op | source)
XLA Modules:
  0.0 70.9 jit_solution(6926021831339841793)
XLA Ops:
  0.6 1.8 %copy.10.velocity = f32[2,2,62,1800]{3,2,1,0:T(8,128)S(1)} copy(f32[2,2,62,1800]{3,1,2,0:T(2,128)} %param.9) | data formatting | bytes 3571200 | tf_op args[3]
  3.5 1.8 %pack_columns.1 = (f32[8,13,8,128]{3,2,1,0:T(8,128)S(1)}, f32[8,13,8,128]{3,2,1,0:T(8,128)S(1)}) custom-call(s32[2]{0:T(128)S(1)} %copy-done.3, s32[2,1800]{1,0:T(2,128)S(1)} %copy-done.1, f32[2,1800]{1,0:T(2,128)S(1)} %copy-done.2, f32[40,90]{1,0:T(8,128)S(1)} %copy-done, f32[2,2,62,1800]{3,2,1,0:T(8,128)S(1)} %copy.10.velocity, ...), custom_call_target="tpu_custom_call" | custom-call | tf_op jit(solution)/shard_map/pack_columns/pallas_call | solution.py:664
  5.3 2.1 %collective-permute-start = (f32[8,13,8,128]{3,2,1,0:T(8,128)S(1)}, f32[8,13,8,128]{3,2,1,0:T(8,128)S(1)}, u32[]{:S(2)}, u32[]{:S(2)}) collective-permute-start(f32[8,13,8,128]{3,2,1,0:T(8,128)S(1)} %get-tuple-element.24), channel_id=1, source_target_pairs={{0,8},{8,16},{16,24},{24,32},{32,40},{40,48},{48,56},{56,64},{64,7... | collective-permute-start | bytes 1277960 | tf_op jit(solution)/shard_map/ppermute | solution.py:674
  7.4 4.7 %collective-permute-start.1 = (f32[8,13,8,128]{3,2,1,0:T(8,128)S(1)}, f32[8,13,8,128]{3,2,1,0:T(8,128)S(1)}, u32[]{:S(2)}, u32[]{:S(2)}) collective-permute-start(f32[8,13,8,128]{3,2,1,0:T(8,128)S(1)} %get-tuple-element.25), channel_id=1, source_target_pairs={{8,0},{16,8},{24,16},{32,24},{40,32},{48,40},{56,48},{64,56},{72,6... | collective-permute-start | bytes 1277960 | tf_op jit(solution)/shard_map/ppermute | solution.py:675
  12.0 4.0 %strips.1 = (f32[8,4,40,8,128]{4,3,2,1,0:T(8,128)S(1)}, f32[40,8,128]{2,1,0:T(8,128)S(1)}) custom-call(s32[2]{0:T(128)S(1)} %copy-done.3, s32[2,1800]{1,0:T(2,128)S(1)} %copy-done.1, f32[2,1800]{1,0:T(2,128)S(1)} %copy-done.2, f32[40,90]{1,0:T(8,128)S(1)} %copy-done, f32[2,2,62,1800]{3,2,1,0:T(8,128)S(1)} %copy.10.velocity, f32[2,2,62,1800]{3,2,1,0:T(8,128)S(1)} %copy.11.tracers), custom_call_target="tpu_custom_call" | custom-call | flops 30000000 | bytes 9000000 | tf_op jit(solution)/shard_map/strips/pallas_call | solution.py:680
  16.0 5.7 %collective-permute-done.from_west = f32[8,13,8,128]{3,2,1,0:T(8,128)S(1)} collective-permute-done((f32[8,13,8,128]{3,2,1,0:T(8,128)S(1)}, f32[8,13,8,128]{3,2,1,0:T(8,128)S(1)}, u32[]{:S(2)}, u32[]{:S(2)}) %collective-permute-start) | collective-permute-done | bytes 426016 | tf_op jit(solution)/shard_map/ppermute | solution.py:674
  21.8 1.3 %row_message.1 = (f32[8,29,8,128]{3,2,1,0:T(8,128)S(1)}, f32[8,29,8,128]{3,2,1,0:T(8,128)S(1)}) custom-call(f32[8,4,40,8,128]{4,3,2,1,0:T(8,128)S(1)} %get-tuple-element.22.own_fields, f32[40,8,128]{2,1,0:T(8,128)S(1)} %get-tuple-element.23.own_columns, f32[8,13,8,128]{3,2,1,0:T(8,128)S(1)} %collective-permute-done.from_west, ...), custom_call_target="tpu_custom_call" | custom-call | tf_op jit(solution)/shard_map/row_message/pallas_call | solution.py:691
  23.0 1.4 %collective-permute-start.2 = (f32[8,29,8,128]{3,2,1,0:T(8,128)S(1)}, f32[8,29,8,128]{3,2,1,0:T(8,128)S(1)}, u32[]{:S(2)}, u32[]{:S(2)}) collective-permute-start(f32[8,29,8,128]{3,2,1,0:T(8,128)S(1)} %get-tuple-element.28), channel_id=1, source_target_pairs={{0,1},{1,2},{2,3},{3,4},{4,5},{5,6},{6,7},{8,9},{9,10},{10,11},{11... | collective-permute-start | bytes 2850824 | tf_op jit(solution)/shard_map/ppermute | solution.py:711
  24.4 1.3 %collective-permute-start.3 = (f32[8,29,8,128]{3,2,1,0:T(8,128)S(1)}, f32[8,29,8,128]{3,2,1,0:T(8,128)S(1)}, u32[]{:S(2)}, u32[]{:S(2)}) collective-permute-start(f32[8,29,8,128]{3,2,1,0:T(8,128)S(1)} %get-tuple-element.29), channel_id=1, source_target_pairs={{1,0},{2,1},{3,2},{4,3},{5,4},{6,5},{7,6},{9,8},{10,9},{11,10},{12... | collective-permute-start | bytes 2850824 | tf_op jit(solution)/shard_map/ppermute | solution.py:712
  25.7 2.1 %halos.1 = (f32[8,4,40,8,128]{4,3,2,1,0:T(8,128)S(1)}, f32[40,8,128]{2,1,0:T(8,128)S(1)}) custom-call(f32[8,4,40,8,128]{4,3,2,1,0:T(8,128)S(1)} %get-tuple-element.22.own_fields, f32[40,8,128]{2,1,0:T(8,128)S(1)} %get-tuple-element.23.own_columns, f32[8,13,8,128]{3,2,1,0:T(8,128)S(1)} %collective-permute-done.from_west, ...), custom_call_target="tpu_custom_call" | custom-call | flops 30000000 | bytes 9000000 | tf_op jit(solution)/shard_map/halos/pallas_call | solution.py:700
  27.8 7.0 %inner_rows.1 = (f32[8,2,8,8,128]{4,3,2,1,0:T(8,128)S(1)}, f32[8,2,32,8,128]{4,3,2,1,0:T(8,128)S(1)}, f32[40,8,128]{2,1,0:T(8,128)S(1)}) custom-call(f32[8,4,40,8,128]{4,3,2,1,0:T(8,128)S(1)} %get-tuple-element.26.fields.low_fields.high_fields, f32[40,8,128]{2,1,0:T(8,128)S(1)} %get-tuple-element.27.columns), custom_call_target="tpu_custom_call" | custom-call | flops 60000000 | bytes 10000000 | tf_op jit(solution)/shard_map/inner_rows/pallas_call | solution.py:718
  34.8 3.0 %inner_slots.1.inner = f32[2,62,2,1800]{3,2,1,0:T(2,128)} custom-call(s32[2]{0:T(128)S(1)} %copy-done.3, f32[8,2,32,8,128]{4,3,2,1,0:T(8,128)S(1)} %get-tuple-element.31.moved), custom_call_target="tpu_custom_call" | custom-call | flops 20000000 | bytes 6000000 | tf_op jit(solution)/shard_map/inner_slots/pallas_call | solution.py:731
  37.8 4.2 %outer_rows.1 = (f32[8,2,8,8,128]{4,3,2,1,0:T(8,128)S(1)}, f32[3,40,128]{2,1,0:T(8,128)S(1)}, f32[8,128]{1,0:T(8,128)S(1)}) custom-call(f32[8,4,40,8,128]{4,3,2,1,0:T(8,128)S(1)} %get-tuple-element.26.fields.low_fields.high_fields, f32[8,4,40,8,128]{4,3,2,1,0:T(8,128)S(1)} %get-tuple-element.26.fields.low_fields.high_fields, ...), custom_call_target="tpu_custom_call" | custom-call | tf_op jit(solution)/shard_map/outer_rows/pallas_call | solution.py:751
  42.0 3.8 %collective-permute-start.4 = (f32[8,128]{1,0:T(8,128)S(1)}, f32[8,128]{1,0:T(8,128)S(1)}, u32[]{:S(2)}, u32[]{:S(2)}) collective-permute-start(f32[8,128]{1,0:T(8,128)S(1)} %get-tuple-element.34), channel_id=1, source_target_pairs={{0,1},{1,0},{2,3},{3,2},{4,5},{5,4},{6,7},{7,6},{8,9},{9,8},{10,11... | collective-permute-start | bytes 12296 | tf_op jit(solution)/shard_map/ppermute | solution.py:622
  46.7 2.7 %collective-permute-start.6 = (f32[8,128]{1,0:T(8,128)S(1)}, f32[8,128]{1,0:T(8,128)S(1)}, u32[]{:S(2)}, u32[]{:S(2)}) collective-permute-start(f32[8,128]{1,0:T(8,128)S(1)} %add.21), channel_id=1, source_target_pairs={{0,4},{1,5},{2,6},{3,7},{4,0},{5,1},{6,2},{7,3},{8,12},{9,13},{10,... | collective-permute-start | bytes 12296 | tf_op jit(solution)/shard_map/ppermute | solution.py:610
  49.4 1.4 %collective-permute-start.7 = (f32[8,128]{1,0:T(8,128)S(1)}, f32[8,128]{1,0:T(8,128)S(1)}, u32[]{:S(2)}, u32[]{:S(2)}) collective-permute-start(f32[8,128]{1,0:T(8,128)S(1)} %add.21), channel_id=1, source_target_pairs={{0,6},{1,7},{2,4},{3,5},{4,2},{5,3},{6,0},{7,1},{8,14},{9,15},{10,... | collective-permute-start | bytes 12296 | tf_op jit(solution)/shard_map/ppermute | solution.py:610
  50.9 2.0 %outer_slots.2.inner = f32[2,62,2,1800]{3,2,1,0:T(2,128)} custom-call(s32[2]{0:T(128)S(1)} %copy-done.3, f32[8,2,32,8,128]{4,3,2,1,0:T(8,128)S(1)} %get-tuple-element.31.moved, f32[8,2,8,8,128]{4,3,2,1,0:T(8,128)S(1)} %get-tuple-element.35.edges, f32[2,62,2,1800]{3,2,1,0:T(2,128)} %inner_slots.1.inner), custom_call_target="tpu_custom_call", output_to_operand_aliasing={{}: (3, {})} | custom-call | flops 2000000 | bytes 2000000 | tf_op jit(solution)/shard_map/outer_slots/pallas_call | solution.py:773
  52.9 1.4 %collective-permute-done.7 = f32[8,128]{1,0:T(8,128)S(1)} collective-permute-done((f32[8,128]{1,0:T(8,128)S(1)}, f32[8,128]{1,0:T(8,128)S(1)}, u32[]{:S(2)}, u32[]{:S(2)}) %collective-permute-start.7) | collective-permute-done | bytes 4128 | tf_op jit(solution)/shard_map/ppermute | solution.py:610
  56.1 1.9 %collective-permute-start.8 = (f32[8,128]{1,0:T(8,128)S(1)}, f32[8,128]{1,0:T(8,128)S(1)}, u32[]{:S(2)}, u32[]{:S(2)}) collective-permute-start(f32[8,128]{1,0:T(8,128)S(1)} %add_add_fusion.1), channel_id=1, source_target_pairs={{0,8},{8,0},{16,24},{24,16},{32,40},{40,32},{48,56},{56,48},{64,72... | collective-permute-start | bytes 12296 | tf_op jit(solution)/shard_map/ppermute | solution.py:610
  58.0 2.1 %outer_slots.3 = f32[2,62,2,1800]{3,2,1,0:T(2,128)} custom-call(s32[2]{0:T(128)S(1)} %copy-done.3, f32[8,2,32,8,128]{4,3,2,1,0:T(8,128)S(1)} %get-tuple-element.31.moved, f32[8,2,8,8,128]{4,3,2,1,0:T(8,128)S(1)} %get-tuple-element.35.edges, f32[2,62,2,1800]{3,2,1,0:T(2,128)} %outer_slots.2.inner), custom_call_target="tpu_custom_call", output_to_operand_aliasing={{}: (3, {})} | custom-call | flops 2000000 | bytes 2000000 | tf_op jit(solution)/shard_map/outer_slots/pallas_call | solution.py:773
  60.2 1.3 %collective-permute-start.11 = (f32[8,128]{1,0:T(8,128)S(1)}, f32[8,128]{1,0:T(8,128)S(1)}, u32[]{:S(2)}, u32[]{:S(2)}) collective-permute-start(f32[8,128]{1,0:T(8,128)S(1)} %add_add_fusion.first), channel_id=1, source_target_pairs={{0,32},{8,40},{16,48},{24,56},{32,0},{40,8},{48,16},{56,24},{64,96... | collective-permute-start | bytes 12296 | tf_op jit(solution)/shard_map/ppermute | solution.py:610
  61.4 3.9 %collective-permute-start.12 = (f32[8,128]{1,0:T(8,128)S(1)}, f32[8,128]{1,0:T(8,128)S(1)}, u32[]{:S(2)}, u32[]{:S(2)}) collective-permute-start(f32[8,128]{1,0:T(8,128)S(1)} %add_add_fusion.first), channel_id=1, source_target_pairs={{0,64},{8,72},{16,80},{24,88},{32,96},{40,104},{48,112},{56,120},{... | collective-permute-start | bytes 12296 | tf_op jit(solution)/shard_map/ppermute | solution.py:610
  65.4 1.6 %collective-permute-done.12.third = f32[8,128]{1,0:T(8,128)S(1)} collective-permute-done((f32[8,128]{1,0:T(8,128)S(1)}, f32[8,128]{1,0:T(8,128)S(1)}, u32[]{:S(2)}, u32[]{:S(2)}) %collective-permute-start.12) | collective-permute-done | bytes 4128 | tf_op jit(solution)/shard_map/ppermute | solution.py:610
  67.0 3.2 %collective-permute-done.13.fourth = f32[8,128]{1,0:T(8,128)S(1)} collective-permute-done((f32[8,128]{1,0:T(8,128)S(1)}, f32[8,128]{1,0:T(8,128)S(1)}, u32[]{:S(2)}, u32[]{:S(2)}) %collective-permute-start.13) | collective-permute-done | bytes 4128 | tf_op jit(solution)/shard_map/ppermute | solution.py:610
  (29 shorter events, 4.4 us)
Async XLA Ops:
  0.6 2.1 %copy-start.4 = (f32[2,2,62,1800]{3,1,2,0:T(2,128)S(1)}, f32[2,2,62,1800]{3,1,2,0:T(2,128)}, u32[]{:S(2)}) copy-start(f32[2,2,62,1800]{3,1,2,0:T(2,128)} %param.10) | copy-start | bytes 5356804
  2.7 0.7 %copy-start = (f32[40,90]{1,0:T(8,128)S(1)}, f32[40,90]{1,0:T(8,128)}, u32[]{:S(2)}) copy-start(f32[40,90]{1,0:T(8,128)} %damping.3) | copy-start | bytes 43204
  2.7 0.7 %copy-start.1 = (s32[2,1800]{1,0:T(2,128)S(1)}, s32[2,1800]{1,0:T(2,128)}, u32[]{:S(2)}) copy-start(s32[2,1800]{1,0:T(2,128)} %wet_levels.3) | copy-start | bytes 43204
  2.7 0.7 %copy-start.2 = (f32[2,1800]{1,0:T(2,128)S(1)}, f32[2,1800]{1,0:T(2,128)}, u32[]{:S(2)}) copy-start(f32[2,1800]{1,0:T(2,128)} %mixing.3) | copy-start | bytes 43204
  2.7 0.7 %copy-start.3 = (s32[2]{0:T(128)S(1)}, s32[2]{0:T(128)}, u32[]{:S(2)}) copy-start(s32[2]{0:T(128)} %block_list.9) | copy-start | bytes 28
  5.3 16.5 %collective-permute-start = (f32[8,13,8,128]{3,2,1,0:T(8,128)S(1)}, f32[8,13,8,128]{3,2,1,0:T(8,128)S(1)}, u32[]{:S(2)}, u32[]{:S(2)}) collective-permute-start(f32[8,13,8,128]{3,2,1,0:T(8,128)S(1)} %get-tuple-element.24), channel_id=1, source_target_pairs={{0,8},{8,16},{16,24},{24,32},{32,40},{40,48},{48,56},{56,64},{64,7... | collective-permute-start | bytes 1277960 | tf_op jit(solution)/shard_map/ppermute | solution.py:674
  7.4 14.4 %collective-permute-start.1 = (f32[8,13,8,128]{3,2,1,0:T(8,128)S(1)}, f32[8,13,8,128]{3,2,1,0:T(8,128)S(1)}, u32[]{:S(2)}, u32[]{:S(2)}) collective-permute-start(f32[8,13,8,128]{3,2,1,0:T(8,128)S(1)} %get-tuple-element.25), channel_id=1, source_target_pairs={{8,0},{16,8},{24,16},{32,24},{40,32},{48,40},{56,48},{64,56},{72,6... | collective-permute-start | bytes 1277960 | tf_op jit(solution)/shard_map/ppermute | solution.py:675
  23.0 14.8 %collective-permute-start.2 = (f32[8,29,8,128]{3,2,1,0:T(8,128)S(1)}, f32[8,29,8,128]{3,2,1,0:T(8,128)S(1)}, u32[]{:S(2)}, u32[]{:S(2)}) collective-permute-start(f32[8,29,8,128]{3,2,1,0:T(8,128)S(1)} %get-tuple-element.28), channel_id=1, source_target_pairs={{0,1},{1,2},{2,3},{3,4},{4,5},{5,6},{6,7},{8,9},{9,10},{10,11},{11... | collective-permute-start | bytes 2850824 | tf_op jit(solution)/shard_map/ppermute | solution.py:711
  24.4 13.4 %collective-permute-start.3 = (f32[8,29,8,128]{3,2,1,0:T(8,128)S(1)}, f32[8,29,8,128]{3,2,1,0:T(8,128)S(1)}, u32[]{:S(2)}, u32[]{:S(2)}) collective-permute-start(f32[8,29,8,128]{3,2,1,0:T(8,128)S(1)} %get-tuple-element.29), channel_id=1, source_target_pairs={{1,0},{2,1},{3,2},{4,3},{5,4},{6,5},{7,6},{9,8},{10,9},{11,10},{12... | collective-permute-start | bytes 2850824 | tf_op jit(solution)/shard_map/ppermute | solution.py:712
  42.0 4.7 %collective-permute-start.4 = (f32[8,128]{1,0:T(8,128)S(1)}, f32[8,128]{1,0:T(8,128)S(1)}, u32[]{:S(2)}, u32[]{:S(2)}) collective-permute-start(f32[8,128]{1,0:T(8,128)S(1)} %get-tuple-element.34), channel_id=1, source_target_pairs={{0,1},{1,0},{2,3},{3,2},{4,5},{5,4},{6,7},{7,6},{8,9},{9,8},{10,11... | collective-permute-start | bytes 12296 | tf_op jit(solution)/shard_map/ppermute | solution.py:622
  46.7 6.2 %collective-permute-start.6 = (f32[8,128]{1,0:T(8,128)S(1)}, f32[8,128]{1,0:T(8,128)S(1)}, u32[]{:S(2)}, u32[]{:S(2)}) collective-permute-start(f32[8,128]{1,0:T(8,128)S(1)} %add.21), channel_id=1, source_target_pairs={{0,4},{1,5},{2,6},{3,7},{4,0},{5,1},{6,2},{7,3},{8,12},{9,13},{10,... | collective-permute-start | bytes 12296 | tf_op jit(solution)/shard_map/ppermute | solution.py:610
  49.4 4.8 %collective-permute-start.7 = (f32[8,128]{1,0:T(8,128)S(1)}, f32[8,128]{1,0:T(8,128)S(1)}, u32[]{:S(2)}, u32[]{:S(2)}) collective-permute-start(f32[8,128]{1,0:T(8,128)S(1)} %add.21), channel_id=1, source_target_pairs={{0,6},{1,7},{2,4},{3,5},{4,2},{5,3},{6,0},{7,1},{8,14},{9,15},{10,... | collective-permute-start | bytes 12296 | tf_op jit(solution)/shard_map/ppermute | solution.py:610
  50.9 3.6 %collective-permute-start.5 = (f32[8,128]{1,0:T(8,128)S(1)}, f32[8,128]{1,0:T(8,128)S(1)}, u32[]{:S(2)}, u32[]{:S(2)}) collective-permute-start(f32[8,128]{1,0:T(8,128)S(1)} %add.21), channel_id=1, source_target_pairs={{0,2},{1,3},{2,0},{3,1},{4,6},{5,7},{6,4},{7,5},{8,10},{9,11},{10,... | collective-permute-start | bytes 12296 | tf_op jit(solution)/shard_map/ppermute | solution.py:610
  54.5 5.6 %collective-permute-start.9 = (f32[8,128]{1,0:T(8,128)S(1)}, f32[8,128]{1,0:T(8,128)S(1)}, u32[]{:S(2)}, u32[]{:S(2)}) collective-permute-start(f32[8,128]{1,0:T(8,128)S(1)} %add_add_fusion.1), channel_id=1, source_target_pairs={{0,16},{8,24},{16,0},{24,8},{32,48},{40,56},{48,32},{56,40},{64,80... | collective-permute-start | bytes 12296 | tf_op jit(solution)/shard_map/ppermute | solution.py:610
  55.0 5.2 %collective-permute-start.10 = (f32[8,128]{1,0:T(8,128)S(1)}, f32[8,128]{1,0:T(8,128)S(1)}, u32[]{:S(2)}, u32[]{:S(2)}) collective-permute-start(f32[8,128]{1,0:T(8,128)S(1)} %add_add_fusion.1), channel_id=1, source_target_pairs={{0,24},{8,16},{16,8},{24,0},{32,56},{40,48},{48,40},{56,32},{64,88... | collective-permute-start | bytes 12296 | tf_op jit(solution)/shard_map/ppermute | solution.py:610
  56.1 4.1 %collective-permute-start.8 = (f32[8,128]{1,0:T(8,128)S(1)}, f32[8,128]{1,0:T(8,128)S(1)}, u32[]{:S(2)}, u32[]{:S(2)}) collective-permute-start(f32[8,128]{1,0:T(8,128)S(1)} %add_add_fusion.1), channel_id=1, source_target_pairs={{0,8},{8,0},{16,24},{24,16},{32,40},{40,32},{48,56},{56,48},{64,72... | collective-permute-start | bytes 12296 | tf_op jit(solution)/shard_map/ppermute | solution.py:610
  60.2 5.2 %collective-permute-start.11 = (f32[8,128]{1,0:T(8,128)S(1)}, f32[8,128]{1,0:T(8,128)S(1)}, u32[]{:S(2)}, u32[]{:S(2)}) collective-permute-start(f32[8,128]{1,0:T(8,128)S(1)} %add_add_fusion.first), channel_id=1, source_target_pairs={{0,32},{8,40},{16,48},{24,56},{32,0},{40,8},{48,16},{56,24},{64,96... | collective-permute-start | bytes 12296 | tf_op jit(solution)/shard_map/ppermute | solution.py:610
  61.4 5.5 %collective-permute-start.12 = (f32[8,128]{1,0:T(8,128)S(1)}, f32[8,128]{1,0:T(8,128)S(1)}, u32[]{:S(2)}, u32[]{:S(2)}) collective-permute-start(f32[8,128]{1,0:T(8,128)S(1)} %add_add_fusion.first), channel_id=1, source_target_pairs={{0,64},{8,72},{16,80},{24,88},{32,96},{40,104},{48,112},{56,120},{... | collective-permute-start | bytes 12296 | tf_op jit(solution)/shard_map/ppermute | solution.py:610
  65.4 4.8 %collective-permute-start.13 = (f32[8,128]{1,0:T(8,128)S(1)}, f32[8,128]{1,0:T(8,128)S(1)}, u32[]{:S(2)}, u32[]{:S(2)}) collective-permute-start(f32[8,128]{1,0:T(8,128)S(1)} %add_add_fusion.first), channel_id=1, source_target_pairs={{0,96},{8,104},{16,112},{24,120},{32,64},{40,72},{48,80},{56,88},{... | collective-permute-start | bytes 12296 | tf_op jit(solution)/shard_map/ppermute | solution.py:610

commit v7 on v6

--- a/solution.py
+++ b/solution.py
@@ -20,8 +20,10 @@
 AHEAD = 26
 BASE = 8
 WIDE = 2 * BX
-NS = 29
-EW = 13
+NS = 27
+FIELD_AT = (0, 7, 14, 20)
+EW = 11
+SHARED = 16
 SURFACE = 56
 
 advect_rate = 0.25
@@ -105,6 +107,13 @@
         yield row, jnp.where(lane < BASE + BX, combined(row), combined(row - 1))
 
 
+def message_tiles(message, block, field):
+    tiles = [message[block, 2 * field], message[block, 2 * field + 1]]
+    last = message[block, 8 + field // 2]
+    tiles.append(turn(last, LANES - SHARED) if field % 2 else last)
+    return lambda number: tiles[number]
+
+
 def beside_rows(rows, west, east, lane):
     turned = {}
 
@@ -176,13 +185,22 @@
     swap = slot_swap(block_list)
 
     def work(block, levels):
+        lasts = []
         for field in range(4):
             ref = tracers if field < 2 else velocity
             easts, wests = pack_columns(Source(field_loader(ref, field % 2, levels, swap)), lane)
             scale = 1.0 if field < 2 else 0.25 * advect_rate
-            for number in range(3):
-                east[block, 3 * field + number] = easts[number] * scale
-                west[block, 3 * field + number] = wests[number] * scale
+            for number in range(2):
+                east[block, 2 * field + number] = easts[number] * scale
+                west[block, 2 * field + number] = wests[number] * scale
+            lasts.append((easts[2] * scale, wests[2] * scale))
+        for pair in range(2):
+            for side, message in enumerate((east, west)):
+                first = BX - REACH if side == 0 else 0
+                lows = [BX * row + first for row in range(34, BY)]
+                one, two = lasts[2 * pair][side], turn(lasts[2 * pair + 1][side], SHARED)
+                parts = [(low, REACH, one) for low in lows] + [(low + SHARED, REACH, two) for low in lows]
+                message[block, 8 + pair] = merge(parts, lane)
 
     over_level_blocks(work)
     easts, wests = pack_columns(Source(column_loader(wet_levels, mixing, swap)), lane)
@@ -234,8 +252,8 @@
         for field in range(4):
             sides = beside_rows(
                 rows,
-                lambda t, field=field: from_west[block, 3 * field + t],
-                lambda t, field=field: from_east[block, 3 * field + t],
+                message_tiles(from_west, block, field),
+                message_tiles(from_east, block, field),
                 lane,
             )
             for row, west, east in sides:
@@ -246,18 +264,35 @@
     lax.fori_loop(0, TILES, work, 0)
 
 
-def row_message_kernel(own_fields, own_columns, from_west, from_east, up, down, low_damp, high_damp):
-    def put(block, field, row, value):
-        target, row = (down, row) if row < REACH else (up, row - (BY - REACH))
-        if field == 4:
-            target[row, NS - 1] = value
-        else:
-            target[block, REACH * field + row] = value
-
-    up[TILES - 1, NS - 1] = jnp.zeros((8, LANES), jnp.float32)
-    down[TILES - 1, NS - 1] = jnp.zeros((8, LANES), jnp.float32)
-    rows = (*range(REACH), *range(BY - REACH, BY))
-    place_halos(own_fields, own_columns, from_west, from_east, low_damp, high_damp, rows, put)
+def row_message_kernel(parity, own_fields, own_columns, from_west, from_east, chip, link, low_damp, high_damp):
+    def write(up, down):
+        def put(block, field, row, value):
+            if row < REACH:
+                target, number = down, row
+            else:
+                target, number = up, row - (BY - REACH)
+            if field == 4:
+                target[number, NS - 1] = value
+            elif field < 2:
+                target[block, FIELD_AT[field] + number] = value
+            elif row < REACH - 1:
+                target[block, FIELD_AT[field] + number] = value
+            elif row > BY - REACH:
+                target[block, FIELD_AT[field] + number - 1] = value
+
+        rows = (*range(REACH), *range(BY - REACH, BY))
+        place_halos(own_fields, own_columns, from_west, from_east, low_damp, high_damp, rows, put)
+
+    for message in (chip, link):
+        message[TILES - 1, NS - 1] = jnp.zeros((8, LANES), jnp.float32)
+
+    @pl.when(parity[0] == 0)
+    def _():
+        write(chip, link)
+
+    @pl.when(parity[0] != 0)
+    def _():
+        write(link, chip)
 
 
 def halo_kernel(own_fields, own_columns, from_west, from_east, fields, columns, low_damp, high_damp):
@@ -424,7 +459,17 @@
     return damping * values + ((east - turn(east, 1)) + (north - pltpu.roll(north, 1, 0)))
 
 
-def outer_kernel(
+def outer_kernel(parity, low_fields, high_fields, columns, chip, link, chip_extra, link_extra, *others):
+    @pl.when(parity[0] == 0)
+    def _():
+        outer_rows(low_fields, high_fields, columns, link, chip, link_extra, chip_extra, *others)
+
+    @pl.when(parity[0] != 0)
+    def _():
+        outer_rows(low_fields, high_fields, columns, chip, link, chip_extra, link_extra, *others)
+
+
+def outer_rows(
     low_fields, high_fields, columns, up, down, up_extra, down_extra, halfway, inner_forcing,
     moved, basis, moments,
     middle, beyond, depth, depth_east, depth_north, mix, scaled, held, forcing, surface, depths, dampings,
@@ -456,9 +501,9 @@
 
         def field(number, row, part=part):
             if row < 0:
-                return up[part, REACH * number + row + REACH]
+                return up[part, FIELD_AT[number] + row + (REACH if number < 2 else REACH - 1)]
             if row >= BY:
-                return down[part, REACH * number + row - BY]
+                return down[part, FIELD_AT[number] + row - BY]
             return low_fields[part, number, row] if row < 10 else high_fields[part, number, row - 30]
 
         def read_middle(n, row, part=part):
@@ -521,52 +566,49 @@
             basis[k] = turn(powers[k], LANES - BASE)[8 : 8 + BY, :]
 
 
-def to_slots(numbers, start, rows, load, block_list, out):
+def to_slots(numbers, start, rows, load, block_list, out, group):
     lane = lane_ids()
     swap = slot_swap(block_list)
     cells = [c for t in numbers for c in range(t * LANES, min((t + 1) * LANES, CELLS))]
     wanted = sorted({c // BX - p for c in cells for p in range(2)})
 
-    def work(block, last):
-        for n in range(2):
-            turned = {}
-
-            def strip(row, n=n):
-                return load(block, n, min(max(row, rows[0]), rows[1]))
-
-            def back(r, strip=strip, turned=turned):
-                if r not in turned:
-                    value = jnp.where(lane < BASE + BX, strip(r), strip(r + 1))
-                    turned[r] = turn(value, BX * r - BASE)
-                return turned[r]
-
-            for r in wanted:
-                back(r)
-            for number in numbers:
-                for position in range(2):
-                    slot = swap if position == 0 else 1 - swap
-                    first, end = number * LANES, min((number + 1) * LANES, CELLS)
-                    parts = []
-                    for row in range(first // BX, (end - 1) // BX + 1):
-                        low = max(row * BX, first)
-                        parts.append((low, min((row + 1) * BX, end) - low, back(row - position)))
-                    value = merge(parts, lane)[:, 0 : end - first]
-                    if last:
-                        rest = value[8 * TILES - LEVELS : 8]
-                        out[slot, 8 * TILES - 8 : LEVELS, n, first - start : end - start] = rest
-                    else:
-                        out[slot, pl.ds(8 * block, 8), n, first - start : end - start] = value
-
-    def body(block, carry):
-        work(block, False)
+    def work(blocks):
+        turned = {}
+        chosen = list(enumerate(blocks))
+        for index, (block, last) in chosen:
+            for n in range(2):
+                for r in wanted:
+                    low, high = (min(max(row, rows[0]), rows[1]) for row in (r, r + 1))
+                    value = jnp.where(lane < BASE + BX, load(block, n, low), load(block, n, high))
+                    turned[index, n, r] = turn(value, BX * r - BASE)
+        for index, (block, last) in chosen:
+            for n in range(2):
+                for number in numbers:
+                    for position in range(2):
+                        slot = swap if position == 0 else 1 - swap
+                        first, end = number * LANES, min((number + 1) * LANES, CELLS)
+                        parts = []
+                        for row in range(first // BX, (end - 1) // BX + 1):
+                            low = max(row * BX, first)
+                            width = min((row + 1) * BX, end) - low
+                            parts.append((low, width, turned[index, n, row - position]))
+                        value = merge(parts, lane)[:, 0 : end - first]
+                        if last:
+                            rest = value[8 * TILES - LEVELS : 8]
+                            out[slot, 8 * TILES - 8 : LEVELS, n, first - start : end - start] = rest
+                        else:
+                            out[slot, pl.ds(8 * block, 8), n, first - start : end - start] = value
+
+    def body(index, carry):
+        work([(group * index + i, False) for i in range(group)])
         return carry
 
-    lax.fori_loop(0, TILES - 1, body, 0)
-    work(TILES - 1, True)
+    lax.fori_loop(0, TILES // group - 1, body, 0)
+    work([(block, block == TILES - 1) for block in range(TILES - group, TILES)])
 
 
 def inner_slots_kernel(block_list, moved, out, cells, semaphore):
-    to_slots(range(2, 12), 2 * LANES, (4, 35), lambda block, n, row: moved[block, n, row - 4], block_list, cells)
+    to_slots(range(2, 12), 2 * LANES, (4, 35), lambda block, n, row: moved[block, n, row - 4], block_list, cells, 1)
     copy = pltpu.make_async_copy(cells, out.at[:, :, :, 2 * LANES : 12 * LANES], semaphore)
     copy.start()
     copy.wait()
@@ -579,7 +621,7 @@
         return edges[block, n, row if row < 4 else row - 32]
 
     start, end = numbers[0] * LANES, min((numbers[-1] + 1) * LANES, CELLS)
-    to_slots(numbers, start, (0, BY - 1), load, block_list, cells)
+    to_slots(numbers, start, (0, BY - 1), load, block_list, cells, 2)
     copy = pltpu.make_async_copy(cells, out.at[:, :, :, start:end], semaphore)
     copy.start()
     copy.wait()
@@ -688,15 +730,16 @@
         name="strips",
     )(*own)
     with_halos = held_in_vmem((*own_strips, from_west, from_east))
-    up, down = pl.pallas_call(
+    parity = (lax.axis_index("gy") & 1).astype(jnp.int32).reshape(1)
+    chip, link = pl.pallas_call(
         row_message_kernel,
-        in_specs=[in_vmem] * 4,
+        in_specs=[pl.BlockSpec(memory_space=pltpu.SMEM)] + [in_vmem] * 4,
         out_specs=[in_vmem] * 2,
         out_shape=[vmem(rows_type)] * 2,
         scratch_shapes=[pltpu.VMEM((BY, LANES), f32)] * 2,
         compiler_params=whole_params,
         name="row_message",
-    )(*with_halos)
+    )(parity, *with_halos)
     fields, columns = pl.pallas_call(
         halo_kernel,
         in_specs=[in_vmem] * 4,
@@ -708,8 +751,10 @@
         name="halos",
     )(*with_halos)
     rows_total = lax.axis_size("gy")
-    from_below = lax.ppermute(up, "gy", [(i, i + 1) for i in range(rows_total - 1)])
-    from_above = lax.ppermute(down, "gy", [(i + 1, i) for i in range(rows_total - 1)])
+    pairs = [(i, i ^ 1) for i in range(rows_total)]
+    from_chip = lax.ppermute(chip, "gy", pairs)
+    pairs = [pair for i in range(1, rows_total - 1, 2) for pair in ((i, i + 1), (i + 1, i))]
+    from_link = lax.ppermute(link, "gy", pairs)
 
     row_store = pltpu.VMEM((ROWS, 8, LANES), f32)
     pair_store = pltpu.VMEM((2, ROWS, 8, LANES), f32)
@@ -751,7 +796,8 @@
     edges, basis, moments = pl.pallas_call(
         outer_kernel,
         grid=(TILES // PARTS,),
-        in_specs=[low_block, high_block, whole(column_shape), part_rows, part_rows]
+        in_specs=[pl.BlockSpec(memory_space=pltpu.SMEM), low_block, high_block, whole(column_shape)]
+        + [part_rows, part_rows]
         + [rows_extra, rows_extra, part_halfway, whole(column_shape)],
         out_specs=[part_halfway, whole((3, BY, LANES)), whole((8, LANES))],
         out_shape=[
@@ -766,7 +812,7 @@
         + [pltpu.VMEM((SURFACE, LANES), f32)] * 3,
         compiler_params=params,
         name="outer_rows",
-    )(fields, fields, columns, from_below, from_above, from_below, from_above, halfway, forcing)
+    )(parity, fields, fields, columns, from_chip, from_link, from_chip, from_link, halfway, forcing)
 
     def outer_slots(numbers, before):
         width = min((numbers[-1] + 1) * LANES, cells) - numbers[0] * LANES

time: 71.1 us -> 68.9 us (0.969)
  starting transfers between devices: 26 us -> 23.4 us
  waiting for transfers between devices: 13 us -> 10.5 us
  local copies, waits for them, and re-layouts: 2.82 us -> 4.37 us
  Pallas kernels: 28.3 us -> 29.6 us
    ppermute x1, waiting for transfers between devices: 5.72 us -> 2.99 us  [per_device(): lax.ppermute(east, 'gx', [(i, (i + 1) % columns_total) for i in range(col...]
    ppermute x2, starting transfers between devices: 2.64 us -> 0.8 us  [the longest x1 0.72 us: per_device(): from_link = lax.ppermute(link, 'gy', pairs)]
    unnamed x12 -> x16, local copies, waits for them, and re-layouts: 2.82 us -> 4.37 us
    pallas_call x1, Pallas kernels: 1.82 us -> 3.19 us  [per_device(): pl.pallas_call(columns_kernel, in_specs=own_specs, out_specs=[in_vmem] *...]
    ppermute x1, starting transfers between devices: 3.84 us -> 2.88 us  [terms_over_devices(): lax.ppermute(values, 'gy', [(i, i ^ 1) for i in range(lax.axis_size('gy'))])]
where the time goes in v7:
time: 68.9 us; the launch traced here: 68.7 us
  Pallas kernels  29.6 us (43%)
  starting transfers between devices  23.4 us (34%)
  waiting for transfers between devices  10.5 us (15%)
  local copies, waits for them, and re-layouts  4.37 us (6%)
  between operations  0.8 us (1%)
    ppermute x9, starting transfers between devices, quad(): lax.ppermute(values, axis, [(i, partner(i, turn)) for i in range(count)])  13.1 us
    pallas_call x1, Pallas kernels, per_device(): pl.pallas_call(inner_kernel, grid=(TILES,), in_specs=[fields_block, whole...  6.96 us
    ppermute x9, waiting for transfers between devices, quad(): lax.ppermute(values, axis, [(i, partner(i, turn)) for i in range(count)])  6.69 us
    ppermute x1, starting transfers between devices, per_device(): lax.ppermute(west, 'gx', [((i + 1) % columns_total, i) for i in range(col...  4.64 us
    unnamed x16, local copies, waits for them, and re-layouts  4.37 us
    pallas_call x1, Pallas kernels, per_device(): pl.pallas_call(outer_kernel, grid=(TILES // PARTS,), in_specs=[pl.BlockSp...  4.19 us
    pallas_call x1, Pallas kernels, per_device(): pl.pallas_call(strips_kernel, in_specs=own_specs, out_specs=[in_vmem] * 2...  4.01 us
    pallas_call x2, Pallas kernels, outer_slots(): pl.pallas_call(functools.partial(outer_slots_kernel, numbers), in_specs=[...  3.55 us
  transfers between devices with their start and end apart: 14, of which 6 were waited for; matrix products, arithmetic and copies ran while one was open for 0% of the time, Pallas kernels for 29%

profile of v7, /device:TPU:0, one launch (start us, length us, event | category | flops | bytes accessed | tf_op | source)
XLA Modules:
  0.0 68.7 jit_solution(7121287242745858174)
XLA Ops:
  0.6 1.8 %copy.10.velocity = f32[2,2,62,1800]{3,2,1,0:T(8,128)S(1)} copy(f32[2,2,62,1800]{3,1,2,0:T(2,128)} %param.9) | data formatting | bytes 3571200 | tf_op args[3]
  3.5 3.2 %pack_columns.1 = (f32[8,11,8,128]{3,2,1,0:T(8,128)}, f32[8,11,8,128]{3,2,1,0:T(8,128)}) custom-call(s32[2]{0:T(128)S(1)} %copy-done.5, s32[2,1800]{1,0:T(2,128)S(1)} %copy-done.3, f32[2,1800]{1,0:T(2,128)S(1)} %copy-done.4, f32[40,90]{1,0:T(8,128)S(1)} %copy-done.2, f32[2,2,62,1800]{3,2,1,0:T(8,128)S(1)} %copy.10.velocity, f32[2,2,62,1800]{3,2,1,0:T(8,128)S(1)} %copy.11.tracers), custom_call_target="tpu_custom_call" | custom-call | tf_op jit(solution)/shard_map/pack_columns/pallas_call | solution.py:706
  6.7 2.0 %collective-permute-start = (f32[8,11,8,128]{3,2,1,0:T(8,128)}, f32[8,11,8,128]{3,2,1,0:T(8,128)S(1)}, u32[]{:S(2)}, u32[]{:S(2)}) collective-permute-start(f32[8,11,8,128]{3,2,1,0:T(8,128)} %get-tuple-element.24), channel_id=1, source_target_pairs={{0,8},{8,16},{16,24},{24,32},{32,40},{40,48},{48,56},{56,64},{64,7... | collective-permute-start | bytes 1081352 | tf_op jit(solution)/shard_map/ppermute | solution.py:716
  8.7 4.6 %collective-permute-start.1 = (f32[8,11,8,128]{3,2,1,0:T(8,128)}, f32[8,11,8,128]{3,2,1,0:T(8,128)S(1)}, u32[]{:S(2)}, u32[]{:S(2)}) collective-permute-start(f32[8,11,8,128]{3,2,1,0:T(8,128)} %get-tuple-element.25), channel_id=1, source_target_pairs={{8,0},{16,8},{24,16},{32,24},{40,32},{48,40},{56,48},{64,56},{72,6... | collective-permute-start | bytes 1081352 | tf_op jit(solution)/shard_map/ppermute | solution.py:717
  13.3 1.5 %copy-done.1 = f32[2,2,62,1800]{3,2,1,0:T(8,128)S(1)} copy-done((f32[2,2,62,1800]{3,2,1,0:T(8,128)S(1)}, f32[2,2,62,1800]{3,2,1,0:T(8,128)}, u32[]{:S(2)}) %copy-start.1) | copy-done | bytes 1785624
  14.9 4.0 %strips.1 = (f32[8,4,40,8,128]{4,3,2,1,0:T(8,128)S(1)}, f32[40,8,128]{2,1,0:T(8,128)S(1)}) custom-call(s32[2]{0:T(128)S(1)} %copy-done.5, s32[2,1800]{1,0:T(2,128)S(1)} %copy-done.3, f32[2,1800]{1,0:T(2,128)S(1)} %copy-done.4, f32[40,90]{1,0:T(8,128)S(1)} %copy-done.2, f32[2,2,62,1800]{3,2,1,0:T(8,128)S(1)} %copy.10.velocity, f32[2,2,62,1800]{3,2,1,0:T(8,128)S(1)} %copy-done.1), custom_call_target="tpu_custom_call" | custom-call | flops 30000000 | bytes 9000000 | tf_op jit(solution)/shard_map/strips/pallas_call | solution.py:722
  18.9 3.0 %collective-permute-done.from_west = f32[8,11,8,128]{3,2,1,0:T(8,128)S(1)} collective-permute-done((f32[8,11,8,128]{3,2,1,0:T(8,128)}, f32[8,11,8,128]{3,2,1,0:T(8,128)S(1)}, u32[]{:S(2)}, u32[]{:S(2)}) %collective-permute-start) | collective-permute-done | bytes 360480 | tf_op jit(solution)/shard_map/ppermute | solution.py:716
  21.9 1.4 %row_message.1 = (f32[8,27,8,128]{3,2,1,0:T(8,128)S(1)}, f32[8,27,8,128]{3,2,1,0:T(8,128)S(1)}) custom-call(s32[1]{0:T(128)} %bitcast.parity, f32[8,4,40,8,128]{4,3,2,1,0:T(8,128)S(1)} %get-tuple-element.22.own_fields, f32[40,8,128]{2,1,0:T(8,128)S(1)} %get-tuple-element.23.own_columns, f32[8,11,8,128]{3,2,1,0:T(8,128)S(1)} %collective-permute-done.from_west, ...), custom_call_target="tpu_custom_call" | custom-call | tf_op jit(solution)/shard_map/row_message/pallas_call | solution.py:734
  24.1 2.4 %halos.1 = (f32[8,4,40,8,128]{4,3,2,1,0:T(8,128)S(1)}, f32[40,8,128]{2,1,0:T(8,128)S(1)}) custom-call(f32[8,4,40,8,128]{4,3,2,1,0:T(8,128)S(1)} %get-tuple-element.22.own_fields, f32[40,8,128]{2,1,0:T(8,128)S(1)} %get-tuple-element.23.own_columns, f32[8,11,8,128]{3,2,1,0:T(8,128)S(1)} %collective-permute-done.from_west, ...), custom_call_target="tpu_custom_call" | custom-call | flops 30000000 | bytes 9000000 | tf_op jit(solution)/shard_map/halos/pallas_call | solution.py:743
  26.6 7.0 %inner_rows.1 = (f32[8,2,8,8,128]{4,3,2,1,0:T(8,128)S(1)}, f32[8,2,32,8,128]{4,3,2,1,0:T(8,128)S(1)}, f32[40,8,128]{2,1,0:T(8,128)S(1)}) custom-call(f32[8,4,40,8,128]{4,3,2,1,0:T(8,128)S(1)} %get-tuple-element.26.fields.low_fields.high_fields, f32[40,8,128]{2,1,0:T(8,128)S(1)} %get-tuple-element.27.columns), custom_call_target="tpu_custom_call" | custom-call | flops 60000000 | bytes 10000000 | tf_op jit(solution)/shard_map/inner_rows/pallas_call | solution.py:763
  33.5 3.0 %inner_slots.1.inner = f32[2,62,2,1800]{3,2,1,0:T(2,128)} custom-call(s32[2]{0:T(128)S(1)} %copy-done.5, f32[8,2,32,8,128]{4,3,2,1,0:T(8,128)S(1)} %get-tuple-element.31.moved), custom_call_target="tpu_custom_call" | custom-call | flops 20000000 | bytes 6000000 | tf_op jit(solution)/shard_map/inner_slots/pallas_call | solution.py:776
  36.6 4.2 %outer_rows.1 = (f32[8,2,8,8,128]{4,3,2,1,0:T(8,128)S(1)}, f32[3,40,128]{2,1,0:T(8,128)S(1)}, f32[8,128]{1,0:T(8,128)S(1)}) custom-call(s32[1]{0:T(128)} %bitcast.parity, f32[8,4,40,8,128]{4,3,2,1,0:T(8,128)S(1)} %get-tuple-element.26.fields.low_fields.high_fields, f32[8,4,40,8,128]{4,3,2,1,0:T(8,128)S(1)} %get-tuple-element.26.fields.low_fields.high_fields, ...), custom_call_target="tpu_custom_call" | custom-call | tf_op jit(solution)/shard_map/outer_rows/pallas_call | solution.py:796
  40.8 2.9 %collective-permute-start.4 = (f32[8,128]{1,0:T(8,128)S(1)}, f32[8,128]{1,0:T(8,128)S(1)}, u32[]{:S(2)}, u32[]{:S(2)}) collective-permute-start(f32[8,128]{1,0:T(8,128)S(1)} %get-tuple-element.34), channel_id=1, source_target_pairs={{0,1},{1,0},{2,3},{3,2},{4,5},{5,4},{6,7},{7,6},{8,9},{9,8},{10,11... | collective-permute-start | bytes 12296 | tf_op jit(solution)/shard_map/ppermute | solution.py:664
  44.5 2.7 %collective-permute-start.6 = (f32[8,128]{1,0:T(8,128)S(1)}, f32[8,128]{1,0:T(8,128)S(1)}, u32[]{:S(2)}, u32[]{:S(2)}) collective-permute-start(f32[8,128]{1,0:T(8,128)S(1)} %add.21), channel_id=1, source_target_pairs={{0,4},{1,5},{2,6},{3,7},{4,0},{5,1},{6,2},{7,3},{8,12},{9,13},{10,... | collective-permute-start | bytes 12296 | tf_op jit(solution)/shard_map/ppermute | solution.py:652
  47.2 1.4 %collective-permute-start.7 = (f32[8,128]{1,0:T(8,128)S(1)}, f32[8,128]{1,0:T(8,128)S(1)}, u32[]{:S(2)}, u32[]{:S(2)}) collective-permute-start(f32[8,128]{1,0:T(8,128)S(1)} %add.21), channel_id=1, source_target_pairs={{0,6},{1,7},{2,4},{3,5},{4,2},{5,3},{6,0},{7,1},{8,14},{9,15},{10,... | collective-permute-start | bytes 12296 | tf_op jit(solution)/shard_map/ppermute | solution.py:652
  48.7 1.7 %outer_slots.2.inner = f32[2,62,2,1800]{3,2,1,0:T(2,128)} custom-call(s32[2]{0:T(128)S(1)} %copy-done.5, f32[8,2,32,8,128]{4,3,2,1,0:T(8,128)S(1)} %get-tuple-element.31.moved, f32[8,2,8,8,128]{4,3,2,1,0:T(8,128)S(1)} %get-tuple-element.35.edges, f32[2,62,2,1800]{3,2,1,0:T(2,128)} %inner_slots.1.inner), custom_call_target="tpu_custom_call", output_to_operand_aliasing={{}: (3, {})} | custom-call | flops 2000000 | bytes 2000000 | tf_op jit(solution)/shard_map/outer_slots/pallas_call | solution.py:819
  50.4 1.6 %collective-permute-done.7 = f32[8,128]{1,0:T(8,128)S(1)} collective-permute-done((f32[8,128]{1,0:T(8,128)S(1)}, f32[8,128]{1,0:T(8,128)S(1)}, u32[]{:S(2)}, u32[]{:S(2)}) %collective-permute-start.7) | collective-permute-done | bytes 4128 | tf_op jit(solution)/shard_map/ppermute | solution.py:652
  52.8 1.1 %collective-permute-start.10 = (f32[8,128]{1,0:T(8,128)S(1)}, f32[8,128]{1,0:T(8,128)S(1)}, u32[]{:S(2)}, u32[]{:S(2)}) collective-permute-start(f32[8,128]{1,0:T(8,128)S(1)} %add_add_fusion.1), channel_id=1, source_target_pairs={{0,24},{8,16},{16,8},{24,0},{32,56},{40,48},{48,40},{56,32},{64,88... | collective-permute-start | bytes 12296 | tf_op jit(solution)/shard_map/ppermute | solution.py:652
  53.8 1.9 %collective-permute-start.8 = (f32[8,128]{1,0:T(8,128)S(1)}, f32[8,128]{1,0:T(8,128)S(1)}, u32[]{:S(2)}, u32[]{:S(2)}) collective-permute-start(f32[8,128]{1,0:T(8,128)S(1)} %add_add_fusion.1), channel_id=1, source_target_pairs={{0,8},{8,0},{16,24},{24,16},{32,40},{40,32},{48,56},{56,48},{64,72... | collective-permute-start | bytes 12296 | tf_op jit(solution)/shard_map/ppermute | solution.py:652
  55.8 1.8 %outer_slots.3 = f32[2,62,2,1800]{3,2,1,0:T(2,128)} custom-call(s32[2]{0:T(128)S(1)} %copy-done.5, f32[8,2,32,8,128]{4,3,2,1,0:T(8,128)S(1)} %get-tuple-element.31.moved, f32[8,2,8,8,128]{4,3,2,1,0:T(8,128)S(1)} %get-tuple-element.35.edges, f32[2,62,2,1800]{3,2,1,0:T(2,128)} %outer_slots.2.inner), custom_call_target="tpu_custom_call", output_to_operand_aliasing={{}: (3, {})} | custom-call | flops 2000000 | bytes 2000000 | tf_op jit(solution)/shard_map/outer_slots/pallas_call | solution.py:819
  57.7 1.6 %collective-permute-start.11 = (f32[8,128]{1,0:T(8,128)S(1)}, f32[8,128]{1,0:T(8,128)S(1)}, u32[]{:S(2)}, u32[]{:S(2)}) collective-permute-start(f32[8,128]{1,0:T(8,128)S(1)} %add_add_fusion.first), channel_id=1, source_target_pairs={{0,32},{8,40},{16,48},{24,56},{32,0},{40,8},{48,16},{56,24},{64,96... | collective-permute-start | bytes 12296 | tf_op jit(solution)/shard_map/ppermute | solution.py:652
  59.3 3.9 %collective-permute-start.12 = (f32[8,128]{1,0:T(8,128)S(1)}, f32[8,128]{1,0:T(8,128)S(1)}, u32[]{:S(2)}, u32[]{:S(2)}) collective-permute-start(f32[8,128]{1,0:T(8,128)S(1)} %add_add_fusion.first), channel_id=1, source_target_pairs={{0,64},{8,72},{16,80},{24,88},{32,96},{40,104},{48,112},{56,120},{... | collective-permute-start | bytes 12296 | tf_op jit(solution)/shard_map/ppermute | solution.py:652
  63.2 1.6 %collective-permute-done.12.third = f32[8,128]{1,0:T(8,128)S(1)} collective-permute-done((f32[8,128]{1,0:T(8,128)S(1)}, f32[8,128]{1,0:T(8,128)S(1)}, u32[]{:S(2)}, u32[]{:S(2)}) %collective-permute-start.12) | collective-permute-done | bytes 4128 | tf_op jit(solution)/shard_map/ppermute | solution.py:652
  64.8 3.2 %collective-permute-done.13.fourth = f32[8,128]{1,0:T(8,128)S(1)} collective-permute-done((f32[8,128]{1,0:T(8,128)S(1)}, f32[8,128]{1,0:T(8,128)S(1)}, u32[]{:S(2)}, u32[]{:S(2)}) %collective-permute-start.13) | collective-permute-done | bytes 4128 | tf_op jit(solution)/shard_map/ppermute | solution.py:652
  (33 shorter events, 4.1 us)
Async XLA Ops:
  0.6 2.1 %copy-start.6 = (f32[2,2,62,1800]{3,1,2,0:T(2,128)S(1)}, f32[2,2,62,1800]{3,1,2,0:T(2,128)}, u32[]{:S(2)}) copy-start(f32[2,2,62,1800]{3,1,2,0:T(2,128)} %param.10) | copy-start | bytes 5356804
  2.7 0.7 %copy-start.2 = (f32[40,90]{1,0:T(8,128)S(1)}, f32[40,90]{1,0:T(8,128)}, u32[]{:S(2)}) copy-start(f32[40,90]{1,0:T(8,128)} %damping.3) | copy-start | bytes 43204
  2.7 0.7 %copy-start.3 = (s32[2,1800]{1,0:T(2,128)S(1)}, s32[2,1800]{1,0:T(2,128)}, u32[]{:S(2)}) copy-start(s32[2,1800]{1,0:T(2,128)} %wet_levels.3) | copy-start | bytes 43204
  2.7 0.7 %copy-start.4 = (f32[2,1800]{1,0:T(2,128)S(1)}, f32[2,1800]{1,0:T(2,128)}, u32[]{:S(2)}) copy-start(f32[2,1800]{1,0:T(2,128)} %mixing.3) | copy-start | bytes 43204
  2.7 0.7 %copy-start.5 = (s32[2]{0:T(128)S(1)}, s32[2]{0:T(128)}, u32[]{:S(2)}) copy-start(s32[2]{0:T(128)} %block_list.9) | copy-start | bytes 28
  3.5 3.2 %copy-start = (f32[2,2,62,1800]{3,2,1,0:T(8,128)}, f32[2,2,62,1800]{3,2,1,0:T(8,128)S(1)}, u32[]{:S(2)}) copy-start(f32[2,2,62,1800]{3,2,1,0:T(8,128)S(1)} %copy.11.tracers) | copy-start | bytes 5356804
  6.7 15.2 %collective-permute-start = (f32[8,11,8,128]{3,2,1,0:T(8,128)}, f32[8,11,8,128]{3,2,1,0:T(8,128)S(1)}, u32[]{:S(2)}, u32[]{:S(2)}) collective-permute-start(f32[8,11,8,128]{3,2,1,0:T(8,128)} %get-tuple-element.24), channel_id=1, source_target_pairs={{0,8},{8,16},{16,24},{24,32},{32,40},{40,48},{48,56},{56,64},{64,7... | collective-permute-start | bytes 1081352 | tf_op jit(solution)/shard_map/ppermute | solution.py:716
  8.7 13.2 %collective-permute-start.1 = (f32[8,11,8,128]{3,2,1,0:T(8,128)}, f32[8,11,8,128]{3,2,1,0:T(8,128)S(1)}, u32[]{:S(2)}, u32[]{:S(2)}) collective-permute-start(f32[8,11,8,128]{3,2,1,0:T(8,128)} %get-tuple-element.25), channel_id=1, source_target_pairs={{8,0},{16,8},{24,16},{32,24},{40,32},{48,40},{56,48},{64,56},{72,6... | collective-permute-start | bytes 1081352 | tf_op jit(solution)/shard_map/ppermute | solution.py:717
  13.3 1.5 %copy-start.1 = (f32[2,2,62,1800]{3,2,1,0:T(8,128)S(1)}, f32[2,2,62,1800]{3,2,1,0:T(8,128)}, u32[]{:S(2)}) copy-start(f32[2,2,62,1800]{3,2,1,0:T(8,128)} %copy-done) | copy-start | bytes 5356804
  23.3 13.3 %collective-permute-start.2 = (f32[8,27,8,128]{3,2,1,0:T(8,128)S(1)}, f32[8,27,8,128]{3,2,1,0:T(8,128)S(1)}, u32[]{:S(2)}, u32[]{:S(2)}) collective-permute-start(f32[8,27,8,128]{3,2,1,0:T(8,128)S(1)} %get-tuple-element.28), channel_id=1, source_target_pairs={{0,1},{1,0},{2,3},{3,2},{4,5},{5,4},{6,7},{7,6},{8,9},{9,8},{10,11... | collective-permute-start | bytes 2654216 | tf_op jit(solution)/shard_map/ppermute | solution.py:755
  23.4 13.2 %collective-permute-start.3 = (f32[8,27,8,128]{3,2,1,0:T(8,128)S(1)}, f32[8,27,8,128]{3,2,1,0:T(8,128)S(1)}, u32[]{:S(2)}, u32[]{:S(2)}) collective-permute-start(f32[8,27,8,128]{3,2,1,0:T(8,128)S(1)} %get-tuple-element.29), channel_id=1, source_target_pairs={{1,2},{2,1},{3,4},{4,3},{5,6},{6,5},{9,10},{10,9},{11,12},{12,11},... | collective-permute-start | bytes 2654216 | tf_op jit(solution)/shard_map/ppermute | solution.py:757
  40.8 3.7 %collective-permute-start.4 = (f32[8,128]{1,0:T(8,128)S(1)}, f32[8,128]{1,0:T(8,128)S(1)}, u32[]{:S(2)}, u32[]{:S(2)}) collective-permute-start(f32[8,128]{1,0:T(8,128)S(1)} %get-tuple-element.34), channel_id=1, source_target_pairs={{0,1},{1,0},{2,3},{3,2},{4,5},{5,4},{6,7},{7,6},{8,9},{9,8},{10,11... | collective-permute-start | bytes 12296 | tf_op jit(solution)/shard_map/ppermute | solution.py:664
  44.5 5.9 %collective-permute-start.6 = (f32[8,128]{1,0:T(8,128)S(1)}, f32[8,128]{1,0:T(8,128)S(1)}, u32[]{:S(2)}, u32[]{:S(2)}) collective-permute-start(f32[8,128]{1,0:T(8,128)S(1)} %add.21), channel_id=1, source_target_pairs={{0,4},{1,5},{2,6},{3,7},{4,0},{5,1},{6,2},{7,3},{8,12},{9,13},{10,... | collective-permute-start | bytes 12296 | tf_op jit(solution)/shard_map/ppermute | solution.py:652
  47.2 4.8 %collective-permute-start.7 = (f32[8,128]{1,0:T(8,128)S(1)}, f32[8,128]{1,0:T(8,128)S(1)}, u32[]{:S(2)}, u32[]{:S(2)}) collective-permute-start(f32[8,128]{1,0:T(8,128)S(1)} %add.21), channel_id=1, source_target_pairs={{0,6},{1,7},{2,4},{3,5},{4,2},{5,3},{6,0},{7,1},{8,14},{9,15},{10,... | collective-permute-start | bytes 12296 | tf_op jit(solution)/shard_map/ppermute | solution.py:652
  48.7 3.6 %collective-permute-start.5 = (f32[8,128]{1,0:T(8,128)S(1)}, f32[8,128]{1,0:T(8,128)S(1)}, u32[]{:S(2)}, u32[]{:S(2)}) collective-permute-start(f32[8,128]{1,0:T(8,128)S(1)} %add.21), channel_id=1, source_target_pairs={{0,2},{1,3},{2,0},{3,1},{4,6},{5,7},{6,4},{7,5},{8,10},{9,11},{10,... | collective-permute-start | bytes 12296 | tf_op jit(solution)/shard_map/ppermute | solution.py:652
  52.3 5.3 %collective-permute-start.9 = (f32[8,128]{1,0:T(8,128)S(1)}, f32[8,128]{1,0:T(8,128)S(1)}, u32[]{:S(2)}, u32[]{:S(2)}) collective-permute-start(f32[8,128]{1,0:T(8,128)S(1)} %add_add_fusion.1), channel_id=1, source_target_pairs={{0,16},{8,24},{16,0},{24,8},{32,48},{40,56},{48,32},{56,40},{64,80... | collective-permute-start | bytes 12296 | tf_op jit(solution)/shard_map/ppermute | solution.py:652
  52.8 4.9 %collective-permute-start.10 = (f32[8,128]{1,0:T(8,128)S(1)}, f32[8,128]{1,0:T(8,128)S(1)}, u32[]{:S(2)}, u32[]{:S(2)}) collective-permute-start(f32[8,128]{1,0:T(8,128)S(1)} %add_add_fusion.1), channel_id=1, source_target_pairs={{0,24},{8,16},{16,8},{24,0},{32,56},{40,48},{48,40},{56,32},{64,88... | collective-permute-start | bytes 12296 | tf_op jit(solution)/shard_map/ppermute | solution.py:652
  53.8 3.8 %collective-permute-start.8 = (f32[8,128]{1,0:T(8,128)S(1)}, f32[8,128]{1,0:T(8,128)S(1)}, u32[]{:S(2)}, u32[]{:S(2)}) collective-permute-start(f32[8,128]{1,0:T(8,128)S(1)} %add_add_fusion.1), channel_id=1, source_target_pairs={{0,8},{8,0},{16,24},{24,16},{32,40},{40,32},{48,56},{56,48},{64,72... | collective-permute-start | bytes 12296 | tf_op jit(solution)/shard_map/ppermute | solution.py:652
  57.7 5.5 %collective-permute-start.11 = (f32[8,128]{1,0:T(8,128)S(1)}, f32[8,128]{1,0:T(8,128)S(1)}, u32[]{:S(2)}, u32[]{:S(2)}) collective-permute-start(f32[8,128]{1,0:T(8,128)S(1)} %add_add_fusion.first), channel_id=1, source_target_pairs={{0,32},{8,40},{16,48},{24,56},{32,0},{40,8},{48,16},{56,24},{64,96... | collective-permute-start | bytes 12296 | tf_op jit(solution)/shard_map/ppermute | solution.py:652
  59.3 5.5 %collective-permute-start.12 = (f32[8,128]{1,0:T(8,128)S(1)}, f32[8,128]{1,0:T(8,128)S(1)}, u32[]{:S(2)}, u32[]{:S(2)}) collective-permute-start(f32[8,128]{1,0:T(8,128)S(1)} %add_add_fusion.first), channel_id=1, source_target_pairs={{0,64},{8,72},{16,80},{24,88},{32,96},{40,104},{48,112},{56,120},{... | collective-permute-start | bytes 12296 | tf_op jit(solution)/shard_map/ppermute | solution.py:652
  63.1 4.8 %collective-permute-start.13 = (f32[8,128]{1,0:T(8,128)S(1)}, f32[8,128]{1,0:T(8,128)S(1)}, u32[]{:S(2)}, u32[]{:S(2)}) collective-permute-start(f32[8,128]{1,0:T(8,128)S(1)} %add_add_fusion.first), channel_id=1, source_target_pairs={{0,96},{8,104},{16,112},{24,120},{32,64},{40,72},{48,80},{56,88},{... | collective-permute-start | bytes 12296 | tf_op jit(solution)/shard_map/ppermute | solution.py:652

commit v8 on v7

--- a/solution.py
+++ b/solution.py
@@ -17,6 +17,8 @@
 REACH = 7
 ROWS = BY + 2 * REACH
 PARTS = 2
+INNER_PLAN = (2, 5, 2)
+OUTER_PLAN = (4, 3, 4)
 AHEAD = 26
 BASE = 8
 WIDE = 2 * BX
@@ -81,12 +83,10 @@
         return parts
 
 
-def pack_columns(source, lane):
-    east, west = [], []
-    for group in range(3):
-        rows = range(17 * group, min(17 * group + 17, BY))
-        east.append(merge([c for r in rows for c in source.cells(1, BX * r + BX - REACH, REACH)], lane))
-        west.append(merge([c for r in rows for c in source.cells(0, BX * r, REACH)], lane))
+def pack_columns(source, lane, group):
+    rows = range(17 * group, min(17 * group + 17, BY))
+    east = merge([c for r in rows for c in source.cells(1, BX * r + BX - REACH, REACH)], lane)
+    west = merge([c for r in rows for c in source.cells(0, BX * r, REACH)], lane)
     return east, west
 
 
@@ -180,38 +180,57 @@
     return load
 
 
-def columns_kernel(block_list, wet_levels, mixing, damping, velocity, tracers, east, west, padded):
+def columns_kernel(
+    block_list, wet_levels_far, mixing_far, damping_far, velocity, tracers,
+    east, west, padded, wet_levels, mixing, damping, semaphores,
+):
     lane = lane_ids()
     swap = slot_swap(block_list)
+    sides = (east, west)
+    copies = [
+        pltpu.make_async_copy(far, near, semaphores.at[number])
+        for number, (far, near) in enumerate(
+            ((wet_levels_far, wet_levels), (mixing_far, mixing), (damping_far, damping))
+        )
+    ]
+    for copy in copies:
+        copy.start()
 
     def work(block, levels):
-        lasts = []
-        for field in range(4):
-            ref = tracers if field < 2 else velocity
-            easts, wests = pack_columns(Source(field_loader(ref, field % 2, levels, swap)), lane)
-            scale = 1.0 if field < 2 else 0.25 * advect_rate
+        sources = [Source(field_loader(ref, n, levels, swap)) for ref in (tracers, velocity) for n in range(2)]
+        scales = (1.0, 1.0, 0.25 * advect_rate, 0.25 * advect_rate)
+        lasts = [pack_columns(source, lane, 2) for source in sources]
+        lasts = [[tile * scale for tile in both] for both, scale in zip(lasts, scales)]
+        lasts = [[turn(tile, SHARED * (field % 2)) for tile in both] for field, both in enumerate(lasts)]
+        for field, source in enumerate(sources):
             for number in range(2):
-                east[block, 2 * field + number] = easts[number] * scale
-                west[block, 2 * field + number] = wests[number] * scale
-            lasts.append((easts[2] * scale, wests[2] * scale))
+                for message, tile in zip(sides, pack_columns(source, lane, number)):
+                    message[block, 2 * field + number] = tile * scales[field]
         for pair in range(2):
-            for side, message in enumerate((east, west)):
+            for side, message in enumerate(sides):
                 first = BX - REACH if side == 0 else 0
                 lows = [BX * row + first for row in range(34, BY)]
-                one, two = lasts[2 * pair][side], turn(lasts[2 * pair + 1][side], SHARED)
+                one, two = lasts[2 * pair][side], lasts[2 * pair + 1][side]
                 parts = [(low, REACH, one) for low in lows] + [(low + SHARED, REACH, two) for low in lows]
                 message[block, 8 + pair] = merge(parts, lane)
 
     over_level_blocks(work)
-    easts, wests = pack_columns(Source(column_loader(wet_levels, mixing, swap)), lane)
+    for copy in copies:
+        copy.wait()
+    source = Source(column_loader(wet_levels, mixing, swap))
+    extras = [pack_columns(source, lane, number) for number in range(3)]
     padded[...] = jnp.zeros_like(padded)
     padded[:, 0:WIDE] = damping[...]
     tiles = [padded[8 * j : 8 * j + 8, :] for j in range(5)]
-    easts.append(merge([(2 * j, 2, turn(t, 2 * j - WIDE + 2)) for j, t in enumerate(tiles)], lane))
-    wests.append(merge([(2 * j, 2, turn(t, 2 * j)) for j, t in enumerate(tiles)], lane))
+    extras.append(
+        (
+            merge([(2 * j, 2, turn(t, 2 * j - WIDE + 2)) for j, t in enumerate(tiles)], lane),
+            merge([(2 * j, 2, turn(t, 2 * j)) for j, t in enumerate(tiles)], lane),
+        )
+    )
     for block in range(TILES):
-        east[block, EW - 1] = easts[min(block, 3)]
-        west[block, EW - 1] = wests[min(block, 3)]
+        for side, message in enumerate(sides):
+            message[block, EW - 1] = extras[min(block, 3)][side]
 
 
 def strips_kernel(block_list, wet_levels, mixing, damping, velocity, tracers, fields, columns, padded):
@@ -566,38 +585,45 @@
             basis[k] = turn(powers[k], LANES - BASE)[8 : 8 + BY, :]
 
 
-def to_slots(numbers, start, rows, load, block_list, out, group):
+def to_slots(numbers, start, rows, load, block_list, out, group, width, ahead):
     lane = lane_ids()
     swap = slot_swap(block_list)
-    cells = [c for t in numbers for c in range(t * LANES, min((t + 1) * LANES, CELLS))]
-    wanted = sorted({c // BX - p for c in cells for p in range(2)})
+    pieces = [numbers[i : i + width] for i in range(0, len(numbers), width)]
+
+    def rotations(block, n, piece):
+        cells = [c for t in piece for c in range(t * LANES, min((t + 1) * LANES, CELLS))]
+        turned = {}
+        for r in sorted({c // BX - p for c in cells for p in range(2)}):
+            low, high = (min(max(row, rows[0]), rows[1]) for row in (r, r + 1))
+            value = jnp.where(lane < BASE + BX, load(block, n, low), load(block, n, high))
+            turned[r] = turn(value, BX * r - BASE)
+        return turned
+
+    def place(block, last, n, piece, turned):
+        for number in piece:
+            for position in range(2):
+                slot = swap if position == 0 else 1 - swap
+                first, end = number * LANES, min((number + 1) * LANES, CELLS)
+                parts = []
+                for row in range(first // BX, (end - 1) // BX + 1):
+                    low = max(row * BX, first)
+                    parts.append((low, min((row + 1) * BX, end) - low, turned[row - position]))
+                value = merge(parts, lane)[:, 0 : end - first]
+                if last:
+                    rest = value[8 * TILES - LEVELS : 8]
+                    out[slot, 8 * TILES - 8 : LEVELS, n, first - start : end - start] = rest
+                else:
+                    out[slot, pl.ds(8 * block, 8), n, first - start : end - start] = value
 
     def work(blocks):
-        turned = {}
-        chosen = list(enumerate(blocks))
-        for index, (block, last) in chosen:
-            for n in range(2):
-                for r in wanted:
-                    low, high = (min(max(row, rows[0]), rows[1]) for row in (r, r + 1))
-                    value = jnp.where(lane < BASE + BX, load(block, n, low), load(block, n, high))
-                    turned[index, n, r] = turn(value, BX * r - BASE)
-        for index, (block, last) in chosen:
-            for n in range(2):
-                for number in numbers:
-                    for position in range(2):
-                        slot = swap if position == 0 else 1 - swap
-                        first, end = number * LANES, min((number + 1) * LANES, CELLS)
-                        parts = []
-                        for row in range(first // BX, (end - 1) // BX + 1):
-                            low = max(row * BX, first)
-                            width = min((row + 1) * BX, end) - low
-                            parts.append((low, width, turned[index, n, row - position]))
-                        value = merge(parts, lane)[:, 0 : end - first]
-                        if last:
-                            rest = value[8 * TILES - LEVELS : 8]
-                            out[slot, 8 * TILES - 8 : LEVELS, n, first - start : end - start] = rest
-                        else:
-                            out[slot, pl.ds(8 * block, 8), n, first - start : end - start] = value
+        jobs = [(block, last, n, piece) for block, last in blocks for n in range(2) for piece in pieces]
+        ready = [rotations(block, n, piece) for block, _, n, piece in jobs[:ahead]]
+        for index, (block, last, n, piece) in enumerate(jobs):
+            if index + ahead < len(jobs):
+                later = jobs[index + ahead]
+                ready.append(rotations(later[0], later[2], later[3]))
+            place(block, last, n, piece, ready[index])
+            ready[index] = None
 
     def body(index, carry):
         work([(group * index + i, False) for i in range(group)])
@@ -608,7 +634,7 @@
 
 
 def inner_slots_kernel(block_list, moved, out, cells, semaphore):
-    to_slots(range(2, 12), 2 * LANES, (4, 35), lambda block, n, row: moved[block, n, row - 4], block_list, cells, 1)
+    to_slots(tuple(range(2, 12)), 2 * LANES, (4, 35), lambda block, n, row: moved[block, n, row - 4], block_list, cells, *INNER_PLAN)
     copy = pltpu.make_async_copy(cells, out.at[:, :, :, 2 * LANES : 12 * LANES], semaphore)
     copy.start()
     copy.wait()
@@ -621,7 +647,7 @@
         return edges[block, n, row if row < 4 else row - 32]
 
     start, end = numbers[0] * LANES, min((numbers[-1] + 1) * LANES, CELLS)
-    to_slots(numbers, start, (0, BY - 1), load, block_list, cells, 2)
+    to_slots(numbers, start, (0, BY - 1), load, block_list, cells, *OUTER_PLAN)
     copy = pltpu.make_async_copy(cells, out.at[:, :, :, start:end], semaphore)
     copy.start()
     copy.wait()
@@ -705,13 +731,19 @@
 
     east, west = pl.pallas_call(
         columns_kernel,
-        in_specs=own_specs,
+        in_specs=own_specs[:1] + [pl.BlockSpec(memory_space=pl.ANY)] * 3 + [in_vmem] * 2,
         out_specs=[in_vmem] * 2,
         out_shape=[vmem(columns_type)] * 2,
-        scratch_shapes=[pltpu.VMEM((BY, LANES), f32)],
+        scratch_shapes=[
+            pltpu.VMEM((BY, LANES), f32),
+            pltpu.VMEM(wet_levels.shape, jnp.int32),
+            pltpu.VMEM(mixing.shape, f32),
+            pltpu.VMEM(damping.shape, f32),
+            pltpu.SemaphoreType.DMA((3,)),
+        ],
         compiler_params=whole_params,
         name="pack_columns",
-    )(*own)
+    )(block_list, wet_levels, mixing, damping, *own[4:])
     columns_total = lax.axis_size("gx")
     from_west = lax.ppermute(east, "gx", [(i, (i + 1) % columns_total) for i in range(columns_total)])
     from_east = lax.ppermute(west, "gx", [((i + 1) % columns_total, i) for i in range(columns_total)])

time: 68.9 us -> 69 us (level)
  transfers between devices with their start and end apart: 14 -> 14, of which waited for: 6 -> 7; matrix products, arithmetic and copies ran while one was open for 0% -> 0% of each run, Pallas kernels for 29% -> 28%
where the time goes in v8:
time: 69 us; the launch traced here: 68.8 us
  Pallas kernels  29.2 us (42%)
  starting transfers between devices  23.6 us (34%)
  waiting for transfers between devices  10.8 us (16%)
  local copies, waits for them, and re-layouts  4.37 us (6%)
  between operations  0.8 us (1%)
    ppermute x9, starting transfers between devices, quad(): lax.ppermute(values, axis, [(i, partner(i, turn)) for i in range(count)])  13.2 us
    ppermute x9, waiting for transfers between devices, quad(): lax.ppermute(values, axis, [(i, partner(i, turn)) for i in range(count)])  7.02 us
    pallas_call x1, Pallas kernels, per_device(): pl.pallas_call(inner_kernel, grid=(TILES,), in_specs=[fields_block, whole...  6.96 us
    ppermute x1, starting transfers between devices, per_device(): lax.ppermute(west, 'gx', [((i + 1) % columns_total, i) for i in range(col...  4.65 us
    unnamed x16, local copies, waits for them, and re-layouts  4.37 us
    pallas_call x1, Pallas kernels, per_device(): pl.pallas_call(outer_kernel, grid=(TILES // PARTS,), in_specs=[pl.BlockSp...  4.19 us
    pallas_call x1, Pallas kernels, per_device(): pl.pallas_call(strips_kernel, in_specs=own_specs, out_specs=[in_vmem] * 2...  4.01 us
    pallas_call x1, Pallas kernels, per_device(): pl.pallas_call(columns_kernel, in_specs=own_specs[:1] + [pl.BlockSpec(mem...  3.45 us
  transfers between devices with their start and end apart: 14, of which 7 were waited for; matrix products, arithmetic and copies ran while one was open for 0% of the time, Pallas kernels for 28%

profile of v8, /device:TPU:0, one launch (start us, length us, event | category | flops | bytes accessed | tf_op | source)
XLA Modules:
  0.0 68.8 jit_solution(8552489796801412915)
XLA Ops:
  0.6 1.8 %copy.10.velocity = f32[2,2,62,1800]{3,2,1,0:T(8,128)S(1)} copy(f32[2,2,62,1800]{3,1,2,0:T(2,128)} %param.9) | data formatting | bytes 3571200 | tf_op args[3]
  3.5 3.4 %pack_columns.1 = (f32[8,11,8,128]{3,2,1,0:T(8,128)}, f32[8,11,8,128]{3,2,1,0:T(8,128)}) custom-call(s32[2]{0:T(128)S(1)} %copy-done.5, s32[2,1800]{1,0:T(2,128)S(1)} %copy-done.3, f32[2,1800]{1,0:T(2,128)S(1)} %copy-done.4, f32[40,90]{1,0:T(8,128)S(1)} %copy-done.2, f32[2,2,62,1800]{3,2,1,0:T(8,128)S(1)} %copy.10.velocity, f32[2,2,62,1800]{3,2,1,0:T(8,128)S(1)} %copy.11.tracers), custom_call_target="tpu_custom_call" | custom-call | tf_op jit(solution)/shard_map/pack_columns/pallas_call | solution.py:732
  6.9 2.1 %collective-permute-start = (f32[8,11,8,128]{3,2,1,0:T(8,128)}, f32[8,11,8,128]{3,2,1,0:T(8,128)S(1)}, u32[]{:S(2)}, u32[]{:S(2)}) collective-permute-start(f32[8,11,8,128]{3,2,1,0:T(8,128)} %get-tuple-element.24), channel_id=1, source_target_pairs={{0,8},{8,16},{16,24},{24,32},{32,40},{40,48},{48,56},{56,64},{64,7... | collective-permute-start | bytes 1081352 | tf_op jit(solution)/shard_map/ppermute | solution.py:748
  9.0 4.7 %collective-permute-start.1 = (f32[8,11,8,128]{3,2,1,0:T(8,128)}, f32[8,11,8,128]{3,2,1,0:T(8,128)S(1)}, u32[]{:S(2)}, u32[]{:S(2)}) collective-permute-start(f32[8,11,8,128]{3,2,1,0:T(8,128)} %get-tuple-element.25), channel_id=1, source_target_pairs={{8,0},{16,8},{24,16},{32,24},{40,32},{48,40},{56,48},{64,56},{72,6... | collective-permute-start | bytes 1081352 | tf_op jit(solution)/shard_map/ppermute | solution.py:749
  13.7 1.5 %copy-done.1 = f32[2,2,62,1800]{3,2,1,0:T(8,128)S(1)} copy-done((f32[2,2,62,1800]{3,2,1,0:T(8,128)S(1)}, f32[2,2,62,1800]{3,2,1,0:T(8,128)}, u32[]{:S(2)}) %copy-start.1) | copy-done | bytes 1785624
  15.2 4.0 %strips.1 = (f32[8,4,40,8,128]{4,3,2,1,0:T(8,128)S(1)}, f32[40,8,128]{2,1,0:T(8,128)S(1)}) custom-call(s32[2]{0:T(128)S(1)} %copy-done.5, s32[2,1800]{1,0:T(2,128)S(1)} %copy-done.3, f32[2,1800]{1,0:T(2,128)S(1)} %copy-done.4, f32[40,90]{1,0:T(8,128)S(1)} %copy-done.2, f32[2,2,62,1800]{3,2,1,0:T(8,128)S(1)} %copy.10.velocity, f32[2,2,62,1800]{3,2,1,0:T(8,128)S(1)} %copy-done.1), custom_call_target="tpu_custom_call" | custom-call | flops 30000000 | bytes 9000000 | tf_op jit(solution)/shard_map/strips/pallas_call | solution.py:754
  19.2 3.0 %collective-permute-done.from_west = f32[8,11,8,128]{3,2,1,0:T(8,128)S(1)} collective-permute-done((f32[8,11,8,128]{3,2,1,0:T(8,128)}, f32[8,11,8,128]{3,2,1,0:T(8,128)S(1)}, u32[]{:S(2)}, u32[]{:S(2)}) %collective-permute-start) | collective-permute-done | bytes 360480 | tf_op jit(solution)/shard_map/ppermute | solution.py:748
  22.2 1.4 %row_message.1 = (f32[8,27,8,128]{3,2,1,0:T(8,128)S(1)}, f32[8,27,8,128]{3,2,1,0:T(8,128)S(1)}) custom-call(s32[1]{0:T(128)} %bitcast.parity, f32[8,4,40,8,128]{4,3,2,1,0:T(8,128)S(1)} %get-tuple-element.22.own_fields, f32[40,8,128]{2,1,0:T(8,128)S(1)} %get-tuple-element.23.own_columns, f32[8,11,8,128]{3,2,1,0:T(8,128)S(1)} %collective-permute-done.from_west, ...), custom_call_target="tpu_custom_call" | custom-call | tf_op jit(solution)/shard_map/row_message/pallas_call | solution.py:766
  24.5 2.4 %halos.1 = (f32[8,4,40,8,128]{4,3,2,1,0:T(8,128)S(1)}, f32[40,8,128]{2,1,0:T(8,128)S(1)}) custom-call(f32[8,4,40,8,128]{4,3,2,1,0:T(8,128)S(1)} %get-tuple-element.22.own_fields, f32[40,8,128]{2,1,0:T(8,128)S(1)} %get-tuple-element.23.own_columns, f32[8,11,8,128]{3,2,1,0:T(8,128)S(1)} %collective-permute-done.from_west, ...), custom_call_target="tpu_custom_call" | custom-call | flops 30000000 | bytes 9000000 | tf_op jit(solution)/shard_map/halos/pallas_call | solution.py:775
  26.9 7.0 %inner_rows.1 = (f32[8,2,8,8,128]{4,3,2,1,0:T(8,128)S(1)}, f32[8,2,32,8,128]{4,3,2,1,0:T(8,128)S(1)}, f32[40,8,128]{2,1,0:T(8,128)S(1)}) custom-call(f32[8,4,40,8,128]{4,3,2,1,0:T(8,128)S(1)} %get-tuple-element.26.fields.low_fields.high_fields, f32[40,8,128]{2,1,0:T(8,128)S(1)} %get-tuple-element.27.columns), custom_call_target="tpu_custom_call" | custom-call | flops 60000000 | bytes 10000000 | tf_op jit(solution)/shard_map/inner_rows/pallas_call | solution.py:795
  33.9 2.8 %inner_slots.1.inner = f32[2,62,2,1800]{3,2,1,0:T(2,128)} custom-call(s32[2]{0:T(128)S(1)} %copy-done.5, f32[8,2,32,8,128]{4,3,2,1,0:T(8,128)S(1)} %get-tuple-element.31.moved), custom_call_target="tpu_custom_call" | custom-call | flops 20000000 | bytes 6000000 | tf_op jit(solution)/shard_map/inner_slots/pallas_call | solution.py:808
  36.7 4.2 %outer_rows.1 = (f32[8,2,8,8,128]{4,3,2,1,0:T(8,128)S(1)}, f32[3,40,128]{2,1,0:T(8,128)S(1)}, f32[8,128]{1,0:T(8,128)S(1)}) custom-call(s32[1]{0:T(128)} %bitcast.parity, f32[8,4,40,8,128]{4,3,2,1,0:T(8,128)S(1)} %get-tuple-element.26.fields.low_fields.high_fields, f32[8,4,40,8,128]{4,3,2,1,0:T(8,128)S(1)} %get-tuple-element.26.fields.low_fields.high_fields, ...), custom_call_target="tpu_custom_call" | custom-call | tf_op jit(solution)/shard_map/outer_rows/pallas_call | solution.py:828
  40.9 2.9 %collective-permute-start.4 = (f32[8,128]{1,0:T(8,128)S(1)}, f32[8,128]{1,0:T(8,128)S(1)}, u32[]{:S(2)}, u32[]{:S(2)}) collective-permute-start(f32[8,128]{1,0:T(8,128)S(1)} %get-tuple-element.34), channel_id=1, source_target_pairs={{0,1},{1,0},{2,3},{3,2},{4,5},{5,4},{6,7},{7,6},{8,9},{9,8},{10,11... | collective-permute-start | bytes 12296 | tf_op jit(solution)/shard_map/ppermute | solution.py:690
  44.6 2.7 %collective-permute-start.6 = (f32[8,128]{1,0:T(8,128)S(1)}, f32[8,128]{1,0:T(8,128)S(1)}, u32[]{:S(2)}, u32[]{:S(2)}) collective-permute-start(f32[8,128]{1,0:T(8,128)S(1)} %add.21), channel_id=1, source_target_pairs={{0,4},{1,5},{2,6},{3,7},{4,0},{5,1},{6,2},{7,3},{8,12},{9,13},{10,... | collective-permute-start | bytes 12296 | tf_op jit(solution)/shard_map/ppermute | solution.py:678
  47.3 1.4 %collective-permute-start.7 = (f32[8,128]{1,0:T(8,128)S(1)}, f32[8,128]{1,0:T(8,128)S(1)}, u32[]{:S(2)}, u32[]{:S(2)}) collective-permute-start(f32[8,128]{1,0:T(8,128)S(1)} %add.21), channel_id=1, source_target_pairs={{0,6},{1,7},{2,4},{3,5},{4,2},{5,3},{6,0},{7,1},{8,14},{9,15},{10,... | collective-permute-start | bytes 12296 | tf_op jit(solution)/shard_map/ppermute | solution.py:678
  48.8 1.5 %outer_slots.2.inner = f32[2,62,2,1800]{3,2,1,0:T(2,128)} custom-call(s32[2]{0:T(128)S(1)} %copy-done.5, f32[8,2,32,8,128]{4,3,2,1,0:T(8,128)S(1)} %get-tuple-element.31.moved, f32[8,2,8,8,128]{4,3,2,1,0:T(8,128)S(1)} %get-tuple-element.35.edges, f32[2,62,2,1800]{3,2,1,0:T(2,128)} %inner_slots.1.inner), custom_call_target="tpu_custom_call", output_to_operand_aliasing={{}: (3, {})} | custom-call | flops 2000000 | bytes 2000000 | tf_op jit(solution)/shard_map/outer_slots/pallas_call | solution.py:851
  50.3 1.8 %collective-permute-done.7 = f32[8,128]{1,0:T(8,128)S(1)} collective-permute-done((f32[8,128]{1,0:T(8,128)S(1)}, f32[8,128]{1,0:T(8,128)S(1)}, u32[]{:S(2)}, u32[]{:S(2)}) %collective-permute-start.7) | collective-permute-done | bytes 4128 | tf_op jit(solution)/shard_map/ppermute | solution.py:678
  52.8 1.1 %collective-permute-start.10 = (f32[8,128]{1,0:T(8,128)S(1)}, f32[8,128]{1,0:T(8,128)S(1)}, u32[]{:S(2)}, u32[]{:S(2)}) collective-permute-start(f32[8,128]{1,0:T(8,128)S(1)} %add_add_fusion.1), channel_id=1, source_target_pairs={{0,24},{8,16},{16,8},{24,0},{32,56},{40,48},{48,40},{56,32},{64,88... | collective-permute-start | bytes 12296 | tf_op jit(solution)/shard_map/ppermute | solution.py:678
  53.9 1.9 %collective-permute-start.8 = (f32[8,128]{1,0:T(8,128)S(1)}, f32[8,128]{1,0:T(8,128)S(1)}, u32[]{:S(2)}, u32[]{:S(2)}) collective-permute-start(f32[8,128]{1,0:T(8,128)S(1)} %add_add_fusion.1), channel_id=1, source_target_pairs={{0,8},{8,0},{16,24},{24,16},{32,40},{40,32},{48,56},{56,48},{64,72... | collective-permute-start | bytes 12296 | tf_op jit(solution)/shard_map/ppermute | solution.py:678
  55.9 1.6 %outer_slots.3 = f32[2,62,2,1800]{3,2,1,0:T(2,128)} custom-call(s32[2]{0:T(128)S(1)} %copy-done.5, f32[8,2,32,8,128]{4,3,2,1,0:T(8,128)S(1)} %get-tuple-element.31.moved, f32[8,2,8,8,128]{4,3,2,1,0:T(8,128)S(1)} %get-tuple-element.35.edges, f32[2,62,2,1800]{3,2,1,0:T(2,128)} %outer_slots.2.inner), custom_call_target="tpu_custom_call", output_to_operand_aliasing={{}: (3, {})} | custom-call | flops 2000000 | bytes 2000000 | tf_op jit(solution)/shard_map/outer_slots/pallas_call | solution.py:851
  57.7 1.7 %collective-permute-start.11 = (f32[8,128]{1,0:T(8,128)S(1)}, f32[8,128]{1,0:T(8,128)S(1)}, u32[]{:S(2)}, u32[]{:S(2)}) collective-permute-start(f32[8,128]{1,0:T(8,128)S(1)} %add_add_fusion.first), channel_id=1, source_target_pairs={{0,32},{8,40},{16,48},{24,56},{32,0},{40,8},{48,16},{56,24},{64,96... | collective-permute-start | bytes 12296 | tf_op jit(solution)/shard_map/ppermute | solution.py:678
  59.3 3.9 %collective-permute-start.12 = (f32[8,128]{1,0:T(8,128)S(1)}, f32[8,128]{1,0:T(8,128)S(1)}, u32[]{:S(2)}, u32[]{:S(2)}) collective-permute-start(f32[8,128]{1,0:T(8,128)S(1)} %add_add_fusion.first), channel_id=1, source_target_pairs={{0,64},{8,72},{16,80},{24,88},{32,96},{40,104},{48,112},{56,120},{... | collective-permute-start | bytes 12296 | tf_op jit(solution)/shard_map/ppermute | solution.py:678
  63.2 1.6 %collective-permute-done.12.third = f32[8,128]{1,0:T(8,128)S(1)} collective-permute-done((f32[8,128]{1,0:T(8,128)S(1)}, f32[8,128]{1,0:T(8,128)S(1)}, u32[]{:S(2)}, u32[]{:S(2)}) %collective-permute-start.12) | collective-permute-done | bytes 4128 | tf_op jit(solution)/shard_map/ppermute | solution.py:678
  64.9 3.2 %collective-permute-done.13.fourth = f32[8,128]{1,0:T(8,128)S(1)} collective-permute-done((f32[8,128]{1,0:T(8,128)S(1)}, f32[8,128]{1,0:T(8,128)S(1)}, u32[]{:S(2)}, u32[]{:S(2)}) %collective-permute-start.13) | collective-permute-done | bytes 4128 | tf_op jit(solution)/shard_map/ppermute | solution.py:678
  (33 shorter events, 4.3 us)
Async XLA Ops:
  0.6 2.1 %copy-start.6 = (f32[2,2,62,1800]{3,1,2,0:T(2,128)S(1)}, f32[2,2,62,1800]{3,1,2,0:T(2,128)}, u32[]{:S(2)}) copy-start(f32[2,2,62,1800]{3,1,2,0:T(2,128)} %param.10) | copy-start | bytes 5356804
  2.7 0.7 %copy-start.2 = (f32[40,90]{1,0:T(8,128)S(1)}, f32[40,90]{1,0:T(8,128)}, u32[]{:S(2)}) copy-start(f32[40,90]{1,0:T(8,128)} %damping_far.1) | copy-start | bytes 43204
  2.7 0.7 %copy-start.3 = (s32[2,1800]{1,0:T(2,128)S(1)}, s32[2,1800]{1,0:T(2,128)}, u32[]{:S(2)}) copy-start(s32[2,1800]{1,0:T(2,128)} %wet_levels_far.1) | copy-start | bytes 43204
  2.7 0.7 %copy-start.4 = (f32[2,1800]{1,0:T(2,128)S(1)}, f32[2,1800]{1,0:T(2,128)}, u32[]{:S(2)}) copy-start(f32[2,1800]{1,0:T(2,128)} %mixing_far.1) | copy-start | bytes 43204
  2.7 0.7 %copy-start.5 = (s32[2]{0:T(128)S(1)}, s32[2]{0:T(128)}, u32[]{:S(2)}) copy-start(s32[2]{0:T(128)} %block_list.9) | copy-start | bytes 28
  3.5 3.5 %copy-start = (f32[2,2,62,1800]{3,2,1,0:T(8,128)}, f32[2,2,62,1800]{3,2,1,0:T(8,128)S(1)}, u32[]{:S(2)}) copy-start(f32[2,2,62,1800]{3,2,1,0:T(8,128)S(1)} %copy.11.tracers) | copy-start | bytes 5356804
  6.9 15.3 %collective-permute-start = (f32[8,11,8,128]{3,2,1,0:T(8,128)}, f32[8,11,8,128]{3,2,1,0:T(8,128)S(1)}, u32[]{:S(2)}, u32[]{:S(2)}) collective-permute-start(f32[8,11,8,128]{3,2,1,0:T(8,128)} %get-tuple-element.24), channel_id=1, source_target_pairs={{0,8},{8,16},{16,24},{24,32},{32,40},{40,48},{48,56},{56,64},{64,7... | collective-permute-start | bytes 1081352 | tf_op jit(solution)/shard_map/ppermute | solution.py:748
  9.0 13.2 %collective-permute-start.1 = (f32[8,11,8,128]{3,2,1,0:T(8,128)}, f32[8,11,8,128]{3,2,1,0:T(8,128)S(1)}, u32[]{:S(2)}, u32[]{:S(2)}) collective-permute-start(f32[8,11,8,128]{3,2,1,0:T(8,128)} %get-tuple-element.25), channel_id=1, source_target_pairs={{8,0},{16,8},{24,16},{32,24},{40,32},{48,40},{56,48},{64,56},{72,6... | collective-permute-start | bytes 1081352 | tf_op jit(solution)/shard_map/ppermute | solution.py:749
  13.7 1.5 %copy-start.1 = (f32[2,2,62,1800]{3,2,1,0:T(8,128)S(1)}, f32[2,2,62,1800]{3,2,1,0:T(8,128)}, u32[]{:S(2)}) copy-start(f32[2,2,62,1800]{3,2,1,0:T(8,128)} %copy-done) | copy-start | bytes 5356804
  23.7 13.0 %collective-permute-start.2 = (f32[8,27,8,128]{3,2,1,0:T(8,128)S(1)}, f32[8,27,8,128]{3,2,1,0:T(8,128)S(1)}, u32[]{:S(2)}, u32[]{:S(2)}) collective-permute-start(f32[8,27,8,128]{3,2,1,0:T(8,128)S(1)} %get-tuple-element.28), channel_id=1, source_target_pairs={{0,1},{1,0},{2,3},{3,2},{4,5},{5,4},{6,7},{7,6},{8,9},{9,8},{10,11... | collective-permute-start | bytes 2654216 | tf_op jit(solution)/shard_map/ppermute | solution.py:787
  23.8 12.9 %collective-permute-start.3 = (f32[8,27,8,128]{3,2,1,0:T(8,128)S(1)}, f32[8,27,8,128]{3,2,1,0:T(8,128)S(1)}, u32[]{:S(2)}, u32[]{:S(2)}) collective-permute-start(f32[8,27,8,128]{3,2,1,0:T(8,128)S(1)} %get-tuple-element.29), channel_id=1, source_target_pairs={{1,2},{2,1},{3,4},{4,3},{5,6},{6,5},{9,10},{10,9},{11,12},{12,11},... | collective-permute-start | bytes 2654216 | tf_op jit(solution)/shard_map/ppermute | solution.py:789
  40.9 3.7 %collective-permute-start.4 = (f32[8,128]{1,0:T(8,128)S(1)}, f32[8,128]{1,0:T(8,128)S(1)}, u32[]{:S(2)}, u32[]{:S(2)}) collective-permute-start(f32[8,128]{1,0:T(8,128)S(1)} %get-tuple-element.34), channel_id=1, source_target_pairs={{0,1},{1,0},{2,3},{3,2},{4,5},{5,4},{6,7},{7,6},{8,9},{9,8},{10,11... | collective-permute-start | bytes 12296 | tf_op jit(solution)/shard_map/ppermute | solution.py:690
  44.6 5.7 %collective-permute-start.6 = (f32[8,128]{1,0:T(8,128)S(1)}, f32[8,128]{1,0:T(8,128)S(1)}, u32[]{:S(2)}, u32[]{:S(2)}) collective-permute-start(f32[8,128]{1,0:T(8,128)S(1)} %add.21), channel_id=1, source_target_pairs={{0,4},{1,5},{2,6},{3,7},{4,0},{5,1},{6,2},{7,3},{8,12},{9,13},{10,... | collective-permute-start | bytes 12296 | tf_op jit(solution)/shard_map/ppermute | solution.py:678
  47.3 4.8 %collective-permute-start.7 = (f32[8,128]{1,0:T(8,128)S(1)}, f32[8,128]{1,0:T(8,128)S(1)}, u32[]{:S(2)}, u32[]{:S(2)}) collective-permute-start(f32[8,128]{1,0:T(8,128)S(1)} %add.21), channel_id=1, source_target_pairs={{0,6},{1,7},{2,4},{3,5},{4,2},{5,3},{6,0},{7,1},{8,14},{9,15},{10,... | collective-permute-start | bytes 12296 | tf_op jit(solution)/shard_map/ppermute | solution.py:678
  48.8 3.6 %collective-permute-start.5 = (f32[8,128]{1,0:T(8,128)S(1)}, f32[8,128]{1,0:T(8,128)S(1)}, u32[]{:S(2)}, u32[]{:S(2)}) collective-permute-start(f32[8,128]{1,0:T(8,128)S(1)} %add.21), channel_id=1, source_target_pairs={{0,2},{1,3},{2,0},{3,1},{4,6},{5,7},{6,4},{7,5},{8,10},{9,11},{10,... | collective-permute-start | bytes 12296 | tf_op jit(solution)/shard_map/ppermute | solution.py:678
  52.4 5.1 %collective-permute-start.9 = (f32[8,128]{1,0:T(8,128)S(1)}, f32[8,128]{1,0:T(8,128)S(1)}, u32[]{:S(2)}, u32[]{:S(2)}) collective-permute-start(f32[8,128]{1,0:T(8,128)S(1)} %add_add_fusion.1), channel_id=1, source_target_pairs={{0,16},{8,24},{16,0},{24,8},{32,48},{40,56},{48,32},{56,40},{64,80... | collective-permute-start | bytes 12296 | tf_op jit(solution)/shard_map/ppermute | solution.py:678
  52.8 4.8 %collective-permute-start.10 = (f32[8,128]{1,0:T(8,128)S(1)}, f32[8,128]{1,0:T(8,128)S(1)}, u32[]{:S(2)}, u32[]{:S(2)}) collective-permute-start(f32[8,128]{1,0:T(8,128)S(1)} %add_add_fusion.1), channel_id=1, source_target_pairs={{0,24},{8,16},{16,8},{24,0},{32,56},{40,48},{48,40},{56,32},{64,88... | collective-permute-start | bytes 12296 | tf_op jit(solution)/shard_map/ppermute | solution.py:678
  53.9 3.7 %collective-permute-start.8 = (f32[8,128]{1,0:T(8,128)S(1)}, f32[8,128]{1,0:T(8,128)S(1)}, u32[]{:S(2)}, u32[]{:S(2)}) collective-permute-start(f32[8,128]{1,0:T(8,128)S(1)} %add_add_fusion.1), channel_id=1, source_target_pairs={{0,8},{8,0},{16,24},{24,16},{32,40},{40,32},{48,56},{56,48},{64,72... | collective-permute-start | bytes 12296 | tf_op jit(solution)/shard_map/ppermute | solution.py:678
  57.7 5.6 %collective-permute-start.11 = (f32[8,128]{1,0:T(8,128)S(1)}, f32[8,128]{1,0:T(8,128)S(1)}, u32[]{:S(2)}, u32[]{:S(2)}) collective-permute-start(f32[8,128]{1,0:T(8,128)S(1)} %add_add_fusion.first), channel_id=1, source_target_pairs={{0,32},{8,40},{16,48},{24,56},{32,0},{40,8},{48,16},{56,24},{64,96... | collective-permute-start | bytes 12296 | tf_op jit(solution)/shard_map/ppermute | solution.py:678
  59.3 5.5 %collective-permute-start.12 = (f32[8,128]{1,0:T(8,128)S(1)}, f32[8,128]{1,0:T(8,128)S(1)}, u32[]{:S(2)}, u32[]{:S(2)}) collective-permute-start(f32[8,128]{1,0:T(8,128)S(1)} %add_add_fusion.first), channel_id=1, source_target_pairs={{0,64},{8,72},{16,80},{24,88},{32,96},{40,104},{48,112},{56,120},{... | collective-permute-start | bytes 12296 | tf_op jit(solution)/shard_map/ppermute | solution.py:678
  63.2 4.8 %collective-permute-start.13 = (f32[8,128]{1,0:T(8,128)S(1)}, f32[8,128]{1,0:T(8,128)S(1)}, u32[]{:S(2)}, u32[]{:S(2)}) collective-permute-start(f32[8,128]{1,0:T(8,128)S(1)} %add_add_fusion.first), channel_id=1, source_target_pairs={{0,96},{8,104},{16,112},{24,120},{32,64},{40,72},{48,80},{56,88},{... | collective-permute-start | bytes 12296 | tf_op jit(solution)/shard_map/ppermute | solution.py:678

commit v9 on v8

--- a/solution.py
+++ b/solution.py
@@ -711,7 +711,7 @@
     f32 = jnp.float32
     slots, fields_each, levels, cells = tracers.shape
     params = pltpu.CompilerParams(
-        dimension_semantics=("arbitrary",), vmem_limit_bytes=40 * 1024 * 1024
+        dimension_semantics=("arbitrary",), vmem_limit_bytes=20 * 1024 * 1024
     )
 
     def tiles(*shape):
@@ -727,7 +727,7 @@
     in_vmem = pl.BlockSpec(memory_space=pltpu.VMEM)
     own_specs = [pl.BlockSpec(memory_space=pltpu.SMEM)] + [in_vmem] * 5
     own = (block_list, *held_in_vmem((wet_levels, mixing, damping, velocity, tracers)))
-    whole_params = pltpu.CompilerParams(vmem_limit_bytes=40 * 1024 * 1024)
+    whole_params = pltpu.CompilerParams(vmem_limit_bytes=10 * 1024 * 1024)
 
     east, west = pl.pallas_call(
         columns_kernel,

time: 69 us -> 68.4 us (level)
    pallas_call x1, Pallas kernels: 3.45 us -> 2.6 us  [per_device(): pl.pallas_call(columns_kernel, in_specs=own_specs[:1] + [pl.BlockSpec(mem...]
  transfers between devices with their start and end apart: 14 -> 14, of which waited for: 7 -> 7; matrix products, arithmetic and copies ran while one was open for 0% -> 0% of each run, Pallas kernels for 28% -> 29%
where the time goes in v9:
time: 68.4 us; the launch traced here: 68.2 us
  Pallas kernels  28.8 us (42%)
  starting transfers between devices  23.6 us (35%)
  waiting for transfers between devices  10.6 us (15%)
  local copies, waits for them, and re-layouts  4.37 us (6%)
  between operations  0.8 us (1%)
    ppermute x9, starting transfers between devices, quad(): lax.ppermute(values, axis, [(i, partner(i, turn)) for i in range(count)])  13.2 us
    pallas_call x1, Pallas kernels, per_device(): pl.pallas_call(inner_kernel, grid=(TILES,), in_specs=[fields_block, whole...  7.44 us
    ppermute x9, waiting for transfers between devices, quad(): lax.ppermute(values, axis, [(i, partner(i, turn)) for i in range(count)])  7.01 us
    ppermute x1, starting transfers between devices, per_device(): lax.ppermute(west, 'gx', [((i + 1) % columns_total, i) for i in range(col...  4.65 us
    unnamed x16, local copies, waits for them, and re-layouts  4.37 us
    pallas_call x1, Pallas kernels, per_device(): pl.pallas_call(outer_kernel, grid=(TILES // PARTS,), in_specs=[pl.BlockSp...  4.19 us
    pallas_call x1, Pallas kernels, per_device(): pl.pallas_call(strips_kernel, in_specs=own_specs, out_specs=[in_vmem] * 2...  4.01 us
    pallas_call x2, Pallas kernels, outer_slots(): pl.pallas_call(functools.partial(outer_slots_kernel, numbers), in_specs=[...  3.17 us
  transfers between devices with their start and end apart: 14, of which 7 were waited for; matrix products, arithmetic and copies ran while one was open for 0% of the time, Pallas kernels for 29%

profile of v9, /device:TPU:0, one launch (start us, length us, event | category | flops | bytes accessed | tf_op | source)
XLA Modules:
  0.0 68.2 jit_solution(17675512864784457873)
XLA Ops:
  0.6 1.8 %copy.10.velocity = f32[2,2,62,1800]{3,2,1,0:T(8,128)S(1)} copy(f32[2,2,62,1800]{3,1,2,0:T(2,128)} %param.9) | data formatting | bytes 3571200 | tf_op args[3]
  3.5 2.6 %pack_columns.1 = (f32[8,11,8,128]{3,2,1,0:T(8,128)S(1)}, f32[8,11,8,128]{3,2,1,0:T(8,128)S(1)}) custom-call(s32[2]{0:T(128)S(1)} %copy-done.5, s32[2,1800]{1,0:T(2,128)S(1)} %copy-done.3, f32[2,1800]{1,0:T(2,128)S(1)} %copy-done.4, f32[40,90]{1,0:T(8,128)S(1)} %copy-done.2, f32[2,2,62,1800]{3,2,1,0:T(8,128)S(1)} %copy.10.velocity, ...), custom_call_target="tpu_custom_call" | custom-call | tf_op jit(solution)/shard_map/pack_columns/pallas_call | solution.py:732
  6.1 2.1 %collective-permute-start = (f32[8,11,8,128]{3,2,1,0:T(8,128)S(1)}, f32[8,11,8,128]{3,2,1,0:T(8,128)S(1)}, u32[]{:S(2)}, u32[]{:S(2)}) collective-permute-start(f32[8,11,8,128]{3,2,1,0:T(8,128)S(1)} %get-tuple-element.24), channel_id=1, source_target_pairs={{0,8},{8,16},{16,24},{24,32},{32,40},{40,48},{48,56},{56,64},{64,7... | collective-permute-start | bytes 1081352 | tf_op jit(solution)/shard_map/ppermute | solution.py:748
  8.2 4.7 %collective-permute-start.1 = (f32[8,11,8,128]{3,2,1,0:T(8,128)S(1)}, f32[8,11,8,128]{3,2,1,0:T(8,128)S(1)}, u32[]{:S(2)}, u32[]{:S(2)}) collective-permute-start(f32[8,11,8,128]{3,2,1,0:T(8,128)S(1)} %get-tuple-element.25), channel_id=1, source_target_pairs={{8,0},{16,8},{24,16},{32,24},{40,32},{48,40},{56,48},{64,56},{72,6... | collective-permute-start | bytes 1081352 | tf_op jit(solution)/shard_map/ppermute | solution.py:749
  12.8 1.5 %copy-done.1 = f32[2,2,62,1800]{3,2,1,0:T(8,128)S(1)} copy-done((f32[2,2,62,1800]{3,2,1,0:T(8,128)S(1)}, f32[2,2,62,1800]{3,2,1,0:T(8,128)}, u32[]{:S(2)}) %copy-start.1) | copy-done | bytes 1785624
  14.4 4.0 %strips.1 = (f32[8,4,40,8,128]{4,3,2,1,0:T(8,128)S(1)}, f32[40,8,128]{2,1,0:T(8,128)S(1)}) custom-call(s32[2]{0:T(128)S(1)} %copy-done.5, s32[2,1800]{1,0:T(2,128)S(1)} %copy-done.3, f32[2,1800]{1,0:T(2,128)S(1)} %copy-done.4, f32[40,90]{1,0:T(8,128)S(1)} %copy-done.2, f32[2,2,62,1800]{3,2,1,0:T(8,128)S(1)} %copy.10.velocity, f32[2,2,62,1800]{3,2,1,0:T(8,128)S(1)} %copy-done.1), custom_call_target="tpu_custom_call" | custom-call | flops 30000000 | bytes 9000000 | tf_op jit(solution)/shard_map/strips/pallas_call | solution.py:754
  18.4 2.8 %collective-permute-done.from_west = f32[8,11,8,128]{3,2,1,0:T(8,128)S(1)} collective-permute-done((f32[8,11,8,128]{3,2,1,0:T(8,128)S(1)}, f32[8,11,8,128]{3,2,1,0:T(8,128)S(1)}, u32[]{:S(2)}, u32[]{:S(2)}) %collective-permute-start) | collective-permute-done | bytes 360480 | tf_op jit(solution)/shard_map/ppermute | solution.py:748
  21.2 1.4 %row_message.1 = (f32[8,27,8,128]{3,2,1,0:T(8,128)S(1)}, f32[8,27,8,128]{3,2,1,0:T(8,128)S(1)}) custom-call(s32[1]{0:T(128)} %bitcast.parity, f32[8,4,40,8,128]{4,3,2,1,0:T(8,128)S(1)} %get-tuple-element.22.own_fields, f32[40,8,128]{2,1,0:T(8,128)S(1)} %get-tuple-element.23.own_columns, f32[8,11,8,128]{3,2,1,0:T(8,128)S(1)} %collective-permute-done.from_west, ...), custom_call_target="tpu_custom_call" | custom-call | tf_op jit(solution)/shard_map/row_message/pallas_call | solution.py:766
  23.4 2.4 %halos.1 = (f32[8,4,40,8,128]{4,3,2,1,0:T(8,128)S(1)}, f32[40,8,128]{2,1,0:T(8,128)S(1)}) custom-call(f32[8,4,40,8,128]{4,3,2,1,0:T(8,128)S(1)} %get-tuple-element.22.own_fields, f32[40,8,128]{2,1,0:T(8,128)S(1)} %get-tuple-element.23.own_columns, f32[8,11,8,128]{3,2,1,0:T(8,128)S(1)} %collective-permute-done.from_west, ...), custom_call_target="tpu_custom_call" | custom-call | flops 30000000 | bytes 9000000 | tf_op jit(solution)/shard_map/halos/pallas_call | solution.py:775
  25.8 7.4 %inner_rows.1 = (f32[8,2,8,8,128]{4,3,2,1,0:T(8,128)S(1)}, f32[8,2,32,8,128]{4,3,2,1,0:T(8,128)S(1)}, f32[40,8,128]{2,1,0:T(8,128)S(1)}) custom-call(f32[8,4,40,8,128]{4,3,2,1,0:T(8,128)S(1)} %get-tuple-element.26.fields.low_fields.high_fields, f32[40,8,128]{2,1,0:T(8,128)S(1)} %get-tuple-element.27.columns), custom_call_target="tpu_custom_call" | custom-call | flops 60000000 | bytes 10000000 | tf_op jit(solution)/shard_map/inner_rows/pallas_call | solution.py:795
  33.3 2.8 %inner_slots.1.inner = f32[2,62,2,1800]{3,2,1,0:T(2,128)} custom-call(s32[2]{0:T(128)S(1)} %copy-done.5, f32[8,2,32,8,128]{4,3,2,1,0:T(8,128)S(1)} %get-tuple-element.31.moved), custom_call_target="tpu_custom_call" | custom-call | flops 20000000 | bytes 6000000 | tf_op jit(solution)/shard_map/inner_slots/pallas_call | solution.py:808
  36.1 4.2 %outer_rows.1 = (f32[8,2,8,8,128]{4,3,2,1,0:T(8,128)S(1)}, f32[3,40,128]{2,1,0:T(8,128)S(1)}, f32[8,128]{1,0:T(8,128)S(1)}) custom-call(s32[1]{0:T(128)} %bitcast.parity, f32[8,4,40,8,128]{4,3,2,1,0:T(8,128)S(1)} %get-tuple-element.26.fields.low_fields.high_fields, f32[8,4,40,8,128]{4,3,2,1,0:T(8,128)S(1)} %get-tuple-element.26.fields.low_fields.high_fields, ...), custom_call_target="tpu_custom_call" | custom-call | tf_op jit(solution)/shard_map/outer_rows/pallas_call | solution.py:828
  40.3 2.9 %collective-permute-start.4 = (f32[8,128]{1,0:T(8,128)S(1)}, f32[8,128]{1,0:T(8,128)S(1)}, u32[]{:S(2)}, u32[]{:S(2)}) collective-permute-start(f32[8,128]{1,0:T(8,128)S(1)} %get-tuple-element.34), channel_id=1, source_target_pairs={{0,1},{1,0},{2,3},{3,2},{4,5},{5,4},{6,7},{7,6},{8,9},{9,8},{10,11... | collective-permute-start | bytes 12296 | tf_op jit(solution)/shard_map/ppermute | solution.py:690
  44.0 2.7 %collective-permute-start.6 = (f32[8,128]{1,0:T(8,128)S(1)}, f32[8,128]{1,0:T(8,128)S(1)}, u32[]{:S(2)}, u32[]{:S(2)}) collective-permute-start(f32[8,128]{1,0:T(8,128)S(1)} %add.21), channel_id=1, source_target_pairs={{0,4},{1,5},{2,6},{3,7},{4,0},{5,1},{6,2},{7,3},{8,12},{9,13},{10,... | collective-permute-start | bytes 12296 | tf_op jit(solution)/shard_map/ppermute | solution.py:678
  46.7 1.4 %collective-permute-start.7 = (f32[8,128]{1,0:T(8,128)S(1)}, f32[8,128]{1,0:T(8,128)S(1)}, u32[]{:S(2)}, u32[]{:S(2)}) collective-permute-start(f32[8,128]{1,0:T(8,128)S(1)} %add.21), channel_id=1, source_target_pairs={{0,6},{1,7},{2,4},{3,5},{4,2},{5,3},{6,0},{7,1},{8,14},{9,15},{10,... | collective-permute-start | bytes 12296 | tf_op jit(solution)/shard_map/ppermute | solution.py:678
  48.2 1.5 %outer_slots.2.inner = f32[2,62,2,1800]{3,2,1,0:T(2,128)} custom-call(s32[2]{0:T(128)S(1)} %copy-done.5, f32[8,2,32,8,128]{4,3,2,1,0:T(8,128)S(1)} %get-tuple-element.31.moved, f32[8,2,8,8,128]{4,3,2,1,0:T(8,128)S(1)} %get-tuple-element.35.edges, f32[2,62,2,1800]{3,2,1,0:T(2,128)} %inner_slots.1.inner), custom_call_target="tpu_custom_call", output_to_operand_aliasing={{}: (3, {})} | custom-call | flops 2000000 | bytes 2000000 | tf_op jit(solution)/shard_map/outer_slots/pallas_call | solution.py:851
  49.7 1.8 %collective-permute-done.7 = f32[8,128]{1,0:T(8,128)S(1)} collective-permute-done((f32[8,128]{1,0:T(8,128)S(1)}, f32[8,128]{1,0:T(8,128)S(1)}, u32[]{:S(2)}, u32[]{:S(2)}) %collective-permute-start.7) | collective-permute-done | bytes 4128 | tf_op jit(solution)/shard_map/ppermute | solution.py:678
  52.3 1.1 %collective-permute-start.10 = (f32[8,128]{1,0:T(8,128)S(1)}, f32[8,128]{1,0:T(8,128)S(1)}, u32[]{:S(2)}, u32[]{:S(2)}) collective-permute-start(f32[8,128]{1,0:T(8,128)S(1)} %add_add_fusion.1), channel_id=1, source_target_pairs={{0,24},{8,16},{16,8},{24,0},{32,56},{40,48},{48,40},{56,32},{64,88... | collective-permute-start | bytes 12296 | tf_op jit(solution)/shard_map/ppermute | solution.py:678
  53.3 1.9 %collective-permute-start.8 = (f32[8,128]{1,0:T(8,128)S(1)}, f32[8,128]{1,0:T(8,128)S(1)}, u32[]{:S(2)}, u32[]{:S(2)}) collective-permute-start(f32[8,128]{1,0:T(8,128)S(1)} %add_add_fusion.1), channel_id=1, source_target_pairs={{0,8},{8,0},{16,24},{24,16},{32,40},{40,32},{48,56},{56,48},{64,72... | collective-permute-start | bytes 12296 | tf_op jit(solution)/shard_map/ppermute | solution.py:678
  55.3 1.6 %outer_slots.3 = f32[2,62,2,1800]{3,2,1,0:T(2,128)} custom-call(s32[2]{0:T(128)S(1)} %copy-done.5, f32[8,2,32,8,128]{4,3,2,1,0:T(8,128)S(1)} %get-tuple-element.31.moved, f32[8,2,8,8,128]{4,3,2,1,0:T(8,128)S(1)} %get-tuple-element.35.edges, f32[2,62,2,1800]{3,2,1,0:T(2,128)} %outer_slots.2.inner), custom_call_target="tpu_custom_call", output_to_operand_aliasing={{}: (3, {})} | custom-call | flops 2000000 | bytes 2000000 | tf_op jit(solution)/shard_map/outer_slots/pallas_call | solution.py:851
  57.1 1.7 %collective-permute-start.11 = (f32[8,128]{1,0:T(8,128)S(1)}, f32[8,128]{1,0:T(8,128)S(1)}, u32[]{:S(2)}, u32[]{:S(2)}) collective-permute-start(f32[8,128]{1,0:T(8,128)S(1)} %add_add_fusion.first), channel_id=1, source_target_pairs={{0,32},{8,40},{16,48},{24,56},{32,0},{40,8},{48,16},{56,24},{64,96... | collective-permute-start | bytes 12296 | tf_op jit(solution)/shard_map/ppermute | solution.py:678
  58.7 3.9 %collective-permute-start.12 = (f32[8,128]{1,0:T(8,128)S(1)}, f32[8,128]{1,0:T(8,128)S(1)}, u32[]{:S(2)}, u32[]{:S(2)}) collective-permute-start(f32[8,128]{1,0:T(8,128)S(1)} %add_add_fusion.first), channel_id=1, source_target_pairs={{0,64},{8,72},{16,80},{24,88},{32,96},{40,104},{48,112},{56,120},{... | collective-permute-start | bytes 12296 | tf_op jit(solution)/shard_map/ppermute | solution.py:678
  62.7 1.6 %collective-permute-done.12.third = f32[8,128]{1,0:T(8,128)S(1)} collective-permute-done((f32[8,128]{1,0:T(8,128)S(1)}, f32[8,128]{1,0:T(8,128)S(1)}, u32[]{:S(2)}, u32[]{:S(2)}) %collective-permute-start.12) | collective-permute-done | bytes 4128 | tf_op jit(solution)/shard_map/ppermute | solution.py:678
  64.3 3.2 %collective-permute-done.13.fourth = f32[8,128]{1,0:T(8,128)S(1)} collective-permute-done((f32[8,128]{1,0:T(8,128)S(1)}, f32[8,128]{1,0:T(8,128)S(1)}, u32[]{:S(2)}, u32[]{:S(2)}) %collective-permute-start.13) | collective-permute-done | bytes 4128 | tf_op jit(solution)/shard_map/ppermute | solution.py:678
  (33 shorter events, 4.3 us)
Async XLA Ops:
  0.6 2.1 %copy-start.6 = (f32[2,2,62,1800]{3,1,2,0:T(2,128)S(1)}, f32[2,2,62,1800]{3,1,2,0:T(2,128)}, u32[]{:S(2)}) copy-start(f32[2,2,62,1800]{3,1,2,0:T(2,128)} %param.10) | copy-start | bytes 5356804
  2.7 0.7 %copy-start.2 = (f32[40,90]{1,0:T(8,128)S(1)}, f32[40,90]{1,0:T(8,128)}, u32[]{:S(2)}) copy-start(f32[40,90]{1,0:T(8,128)} %damping_far.1) | copy-start | bytes 43204
  2.7 0.7 %copy-start.3 = (s32[2,1800]{1,0:T(2,128)S(1)}, s32[2,1800]{1,0:T(2,128)}, u32[]{:S(2)}) copy-start(s32[2,1800]{1,0:T(2,128)} %wet_levels_far.1) | copy-start | bytes 43204
  2.7 0.7 %copy-start.4 = (f32[2,1800]{1,0:T(2,128)S(1)}, f32[2,1800]{1,0:T(2,128)}, u32[]{:S(2)}) copy-start(f32[2,1800]{1,0:T(2,128)} %mixing_far.1) | copy-start | bytes 43204
  2.7 0.7 %copy-start.5 = (s32[2]{0:T(128)S(1)}, s32[2]{0:T(128)}, u32[]{:S(2)}) copy-start(s32[2]{0:T(128)} %block_list.9) | copy-start | bytes 28
  3.5 2.6 %copy-start = (f32[2,2,62,1800]{3,2,1,0:T(8,128)}, f32[2,2,62,1800]{3,2,1,0:T(8,128)S(1)}, u32[]{:S(2)}) copy-start(f32[2,2,62,1800]{3,2,1,0:T(8,128)S(1)} %copy.11.tracers) | copy-start | bytes 5356804
  6.1 15.1 %collective-permute-start = (f32[8,11,8,128]{3,2,1,0:T(8,128)S(1)}, f32[8,11,8,128]{3,2,1,0:T(8,128)S(1)}, u32[]{:S(2)}, u32[]{:S(2)}) collective-permute-start(f32[8,11,8,128]{3,2,1,0:T(8,128)S(1)} %get-tuple-element.24), channel_id=1, source_target_pairs={{0,8},{8,16},{16,24},{24,32},{32,40},{40,48},{48,56},{56,64},{64,7... | collective-permute-start | bytes 1081352 | tf_op jit(solution)/shard_map/ppermute | solution.py:748
  8.2 13.0 %collective-permute-start.1 = (f32[8,11,8,128]{3,2,1,0:T(8,128)S(1)}, f32[8,11,8,128]{3,2,1,0:T(8,128)S(1)}, u32[]{:S(2)}, u32[]{:S(2)}) collective-permute-start(f32[8,11,8,128]{3,2,1,0:T(8,128)S(1)} %get-tuple-element.25), channel_id=1, source_target_pairs={{8,0},{16,8},{24,16},{32,24},{40,32},{48,40},{56,48},{64,56},{72,6... | collective-permute-start | bytes 1081352 | tf_op jit(solution)/shard_map/ppermute | solution.py:749
  12.8 1.5 %copy-start.1 = (f32[2,2,62,1800]{3,2,1,0:T(8,128)S(1)}, f32[2,2,62,1800]{3,2,1,0:T(8,128)}, u32[]{:S(2)}) copy-start(f32[2,2,62,1800]{3,2,1,0:T(8,128)} %copy-done) | copy-start | bytes 5356804
  22.6 13.5 %collective-permute-start.2 = (f32[8,27,8,128]{3,2,1,0:T(8,128)S(1)}, f32[8,27,8,128]{3,2,1,0:T(8,128)S(1)}, u32[]{:S(2)}, u32[]{:S(2)}) collective-permute-start(f32[8,27,8,128]{3,2,1,0:T(8,128)S(1)} %get-tuple-element.28), channel_id=1, source_target_pairs={{0,1},{1,0},{2,3},{3,2},{4,5},{5,4},{6,7},{7,6},{8,9},{9,8},{10,11... | collective-permute-start | bytes 2654216 | tf_op jit(solution)/shard_map/ppermute | solution.py:787
  22.7 13.4 %collective-permute-start.3 = (f32[8,27,8,128]{3,2,1,0:T(8,128)S(1)}, f32[8,27,8,128]{3,2,1,0:T(8,128)S(1)}, u32[]{:S(2)}, u32[]{:S(2)}) collective-permute-start(f32[8,27,8,128]{3,2,1,0:T(8,128)S(1)} %get-tuple-element.29), channel_id=1, source_target_pairs={{1,2},{2,1},{3,4},{4,3},{5,6},{6,5},{9,10},{10,9},{11,12},{12,11},... | collective-permute-start | bytes 2654216 | tf_op jit(solution)/shard_map/ppermute | solution.py:789
  40.3 3.7 %collective-permute-start.4 = (f32[8,128]{1,0:T(8,128)S(1)}, f32[8,128]{1,0:T(8,128)S(1)}, u32[]{:S(2)}, u32[]{:S(2)}) collective-permute-start(f32[8,128]{1,0:T(8,128)S(1)} %get-tuple-element.34), channel_id=1, source_target_pairs={{0,1},{1,0},{2,3},{3,2},{4,5},{5,4},{6,7},{7,6},{8,9},{9,8},{10,11... | collective-permute-start | bytes 12296 | tf_op jit(solution)/shard_map/ppermute | solution.py:690
  44.0 5.7 %collective-permute-start.6 = (f32[8,128]{1,0:T(8,128)S(1)}, f32[8,128]{1,0:T(8,128)S(1)}, u32[]{:S(2)}, u32[]{:S(2)}) collective-permute-start(f32[8,128]{1,0:T(8,128)S(1)} %add.21), channel_id=1, source_target_pairs={{0,4},{1,5},{2,6},{3,7},{4,0},{5,1},{6,2},{7,3},{8,12},{9,13},{10,... | collective-permute-start | bytes 12296 | tf_op jit(solution)/shard_map/ppermute | solution.py:678
  46.7 4.8 %collective-permute-start.7 = (f32[8,128]{1,0:T(8,128)S(1)}, f32[8,128]{1,0:T(8,128)S(1)}, u32[]{:S(2)}, u32[]{:S(2)}) collective-permute-start(f32[8,128]{1,0:T(8,128)S(1)} %add.21), channel_id=1, source_target_pairs={{0,6},{1,7},{2,4},{3,5},{4,2},{5,3},{6,0},{7,1},{8,14},{9,15},{10,... | collective-permute-start | bytes 12296 | tf_op jit(solution)/shard_map/ppermute | solution.py:678
  48.2 3.6 %collective-permute-start.5 = (f32[8,128]{1,0:T(8,128)S(1)}, f32[8,128]{1,0:T(8,128)S(1)}, u32[]{:S(2)}, u32[]{:S(2)}) collective-permute-start(f32[8,128]{1,0:T(8,128)S(1)} %add.21), channel_id=1, source_target_pairs={{0,2},{1,3},{2,0},{3,1},{4,6},{5,7},{6,4},{7,5},{8,10},{9,11},{10,... | collective-permute-start | bytes 12296 | tf_op jit(solution)/shard_map/ppermute | solution.py:678
  51.8 5.1 %collective-permute-start.9 = (f32[8,128]{1,0:T(8,128)S(1)}, f32[8,128]{1,0:T(8,128)S(1)}, u32[]{:S(2)}, u32[]{:S(2)}) collective-permute-start(f32[8,128]{1,0:T(8,128)S(1)} %add_add_fusion.1), channel_id=1, source_target_pairs={{0,16},{8,24},{16,0},{24,8},{32,48},{40,56},{48,32},{56,40},{64,80... | collective-permute-start | bytes 12296 | tf_op jit(solution)/shard_map/ppermute | solution.py:678
  52.3 4.8 %collective-permute-start.10 = (f32[8,128]{1,0:T(8,128)S(1)}, f32[8,128]{1,0:T(8,128)S(1)}, u32[]{:S(2)}, u32[]{:S(2)}) collective-permute-start(f32[8,128]{1,0:T(8,128)S(1)} %add_add_fusion.1), channel_id=1, source_target_pairs={{0,24},{8,16},{16,8},{24,0},{32,56},{40,48},{48,40},{56,32},{64,88... | collective-permute-start | bytes 12296 | tf_op jit(solution)/shard_map/ppermute | solution.py:678
  53.3 3.7 %collective-permute-start.8 = (f32[8,128]{1,0:T(8,128)S(1)}, f32[8,128]{1,0:T(8,128)S(1)}, u32[]{:S(2)}, u32[]{:S(2)}) collective-permute-start(f32[8,128]{1,0:T(8,128)S(1)} %add_add_fusion.1), channel_id=1, source_target_pairs={{0,8},{8,0},{16,24},{24,16},{32,40},{40,32},{48,56},{56,48},{64,72... | collective-permute-start | bytes 12296 | tf_op jit(solution)/shard_map/ppermute | solution.py:678
  57.1 5.6 %collective-permute-start.11 = (f32[8,128]{1,0:T(8,128)S(1)}, f32[8,128]{1,0:T(8,128)S(1)}, u32[]{:S(2)}, u32[]{:S(2)}) collective-permute-start(f32[8,128]{1,0:T(8,128)S(1)} %add_add_fusion.first), channel_id=1, source_target_pairs={{0,32},{8,40},{16,48},{24,56},{32,0},{40,8},{48,16},{56,24},{64,96... | collective-permute-start | bytes 12296 | tf_op jit(solution)/shard_map/ppermute | solution.py:678
  58.7 5.5 %collective-permute-start.12 = (f32[8,128]{1,0:T(8,128)S(1)}, f32[8,128]{1,0:T(8,128)S(1)}, u32[]{:S(2)}, u32[]{:S(2)}) collective-permute-start(f32[8,128]{1,0:T(8,128)S(1)} %add_add_fusion.first), channel_id=1, source_target_pairs={{0,64},{8,72},{16,80},{24,88},{32,96},{40,104},{48,112},{56,120},{... | collective-permute-start | bytes 12296 | tf_op jit(solution)/shard_map/ppermute | solution.py:678
  62.6 4.8 %collective-permute-start.13 = (f32[8,128]{1,0:T(8,128)S(1)}, f32[8,128]{1,0:T(8,128)S(1)}, u32[]{:S(2)}, u32[]{:S(2)}) collective-permute-start(f32[8,128]{1,0:T(8,128)S(1)} %add_add_fusion.first), channel_id=1, source_target_pairs={{0,96},{8,104},{16,112},{24,120},{32,64},{40,72},{48,80},{56,88},{... | collective-permute-start | bytes 12296 | tf_op jit(solution)/shard_map/ppermute | solution.py:678

commit v10 on v9

--- a/solution.py
+++ b/solution.py
@@ -19,7 +19,7 @@
 PARTS = 2
 INNER_PLAN = (2, 5, 2)
 OUTER_PLAN = (4, 3, 4)
-AHEAD = 26
+AHEAD = 40
 BASE = 8
 WIDE = 2 * BX
 NS = 27

time: 68.4 us -> 68 us (level)
  no operation moved by 1% of the time
where the time goes in v10:
time: 68 us; the launch traced here: 67.8 us
  Pallas kernels  28.4 us (42%)
  starting transfers between devices  23.6 us (35%)
  waiting for transfers between devices  10.6 us (16%)
  local copies, waits for them, and re-layouts  4.37 us (6%)
  between operations  0.8 us (1%)
    ppermute x9, starting transfers between devices, quad(): lax.ppermute(values, axis, [(i, partner(i, turn)) for i in range(count)])  13.2 us
    pallas_call x1, Pallas kernels, per_device(): pl.pallas_call(inner_kernel, grid=(TILES,), in_specs=[fields_block, whole...  7.02 us
    ppermute x9, waiting for transfers between devices, quad(): lax.ppermute(values, axis, [(i, partner(i, turn)) for i in range(count)])  7.01 us
    ppermute x1, starting transfers between devices, per_device(): lax.ppermute(west, 'gx', [((i + 1) % columns_total, i) for i in range(col...  4.65 us
    unnamed x16, local copies, waits for them, and re-layouts  4.37 us
    pallas_call x1, Pallas kernels, per_device(): pl.pallas_call(outer_kernel, grid=(TILES // PARTS,), in_specs=[pl.BlockSp...  4.19 us
    pallas_call x1, Pallas kernels, per_device(): pl.pallas_call(strips_kernel, in_specs=own_specs, out_specs=[in_vmem] * 2...  4.01 us
    pallas_call x2, Pallas kernels, outer_slots(): pl.pallas_call(functools.partial(outer_slots_kernel, numbers), in_specs=[...  3.17 us
  transfers between devices with their start and end apart: 14, of which 7 were waited for; matrix products, arithmetic and copies ran while one was open for 0% of the time, Pallas kernels for 29%

profile of v10, /device:TPU:0, one launch (start us, length us, event | category | flops | bytes accessed | tf_op | source)
XLA Modules:
  0.0 67.8 jit_solution(9744138818673667696)
XLA Ops:
  0.6 1.8 %copy.10.velocity = f32[2,2,62,1800]{3,2,1,0:T(8,128)S(1)} copy(f32[2,2,62,1800]{3,1,2,0:T(2,128)} %param.9) | data formatting | bytes 3571200 | tf_op args[3]
  3.5 2.6 %pack_columns.1 = (f32[8,11,8,128]{3,2,1,0:T(8,128)S(1)}, f32[8,11,8,128]{3,2,1,0:T(8,128)S(1)}) custom-call(s32[2]{0:T(128)S(1)} %copy-done.5, s32[2,1800]{1,0:T(2,128)S(1)} %copy-done.3, f32[2,1800]{1,0:T(2,128)S(1)} %copy-done.4, f32[40,90]{1,0:T(8,128)S(1)} %copy-done.2, f32[2,2,62,1800]{3,2,1,0:T(8,128)S(1)} %copy.10.velocity, ...), custom_call_target="tpu_custom_call" | custom-call | tf_op jit(solution)/shard_map/pack_columns/pallas_call | solution.py:732
  6.1 2.1 %collective-permute-start = (f32[8,11,8,128]{3,2,1,0:T(8,128)S(1)}, f32[8,11,8,128]{3,2,1,0:T(8,128)S(1)}, u32[]{:S(2)}, u32[]{:S(2)}) collective-permute-start(f32[8,11,8,128]{3,2,1,0:T(8,128)S(1)} %get-tuple-element.24), channel_id=1, source_target_pairs={{0,8},{8,16},{16,24},{24,32},{32,40},{40,48},{48,56},{56,64},{64,7... | collective-permute-start | bytes 1081352 | tf_op jit(solution)/shard_map/ppermute | solution.py:748
  8.2 4.7 %collective-permute-start.1 = (f32[8,11,8,128]{3,2,1,0:T(8,128)S(1)}, f32[8,11,8,128]{3,2,1,0:T(8,128)S(1)}, u32[]{:S(2)}, u32[]{:S(2)}) collective-permute-start(f32[8,11,8,128]{3,2,1,0:T(8,128)S(1)} %get-tuple-element.25), channel_id=1, source_target_pairs={{8,0},{16,8},{24,16},{32,24},{40,32},{48,40},{56,48},{64,56},{72,6... | collective-permute-start | bytes 1081352 | tf_op jit(solution)/shard_map/ppermute | solution.py:749
  12.8 1.5 %copy-done.1 = f32[2,2,62,1800]{3,2,1,0:T(8,128)S(1)} copy-done((f32[2,2,62,1800]{3,2,1,0:T(8,128)S(1)}, f32[2,2,62,1800]{3,2,1,0:T(8,128)}, u32[]{:S(2)}) %copy-start.1) | copy-done | bytes 1785624
  14.4 4.0 %strips.1 = (f32[8,4,40,8,128]{4,3,2,1,0:T(8,128)S(1)}, f32[40,8,128]{2,1,0:T(8,128)S(1)}) custom-call(s32[2]{0:T(128)S(1)} %copy-done.5, s32[2,1800]{1,0:T(2,128)S(1)} %copy-done.3, f32[2,1800]{1,0:T(2,128)S(1)} %copy-done.4, f32[40,90]{1,0:T(8,128)S(1)} %copy-done.2, f32[2,2,62,1800]{3,2,1,0:T(8,128)S(1)} %copy.10.velocity, f32[2,2,62,1800]{3,2,1,0:T(8,128)S(1)} %copy-done.1), custom_call_target="tpu_custom_call" | custom-call | flops 30000000 | bytes 9000000 | tf_op jit(solution)/shard_map/strips/pallas_call | solution.py:754
  18.4 2.8 %collective-permute-done.from_west = f32[8,11,8,128]{3,2,1,0:T(8,128)S(1)} collective-permute-done((f32[8,11,8,128]{3,2,1,0:T(8,128)S(1)}, f32[8,11,8,128]{3,2,1,0:T(8,128)S(1)}, u32[]{:S(2)}, u32[]{:S(2)}) %collective-permute-start) | collective-permute-done | bytes 360480 | tf_op jit(solution)/shard_map/ppermute | solution.py:748
  21.2 1.4 %row_message.1 = (f32[8,27,8,128]{3,2,1,0:T(8,128)S(1)}, f32[8,27,8,128]{3,2,1,0:T(8,128)S(1)}) custom-call(s32[1]{0:T(128)} %bitcast.parity, f32[8,4,40,8,128]{4,3,2,1,0:T(8,128)S(1)} %get-tuple-element.22.own_fields, f32[40,8,128]{2,1,0:T(8,128)S(1)} %get-tuple-element.23.own_columns, f32[8,11,8,128]{3,2,1,0:T(8,128)S(1)} %collective-permute-done.from_west, ...), custom_call_target="tpu_custom_call" | custom-call | tf_op jit(solution)/shard_map/row_message/pallas_call | solution.py:766
  23.4 2.4 %halos.1 = (f32[8,4,40,8,128]{4,3,2,1,0:T(8,128)S(1)}, f32[40,8,128]{2,1,0:T(8,128)S(1)}) custom-call(f32[8,4,40,8,128]{4,3,2,1,0:T(8,128)S(1)} %get-tuple-element.22.own_fields, f32[40,8,128]{2,1,0:T(8,128)S(1)} %get-tuple-element.23.own_columns, f32[8,11,8,128]{3,2,1,0:T(8,128)S(1)} %collective-permute-done.from_west, ...), custom_call_target="tpu_custom_call" | custom-call | flops 30000000 | bytes 9000000 | tf_op jit(solution)/shard_map/halos/pallas_call | solution.py:775
  25.8 7.0 %inner_rows.1 = (f32[8,2,8,8,128]{4,3,2,1,0:T(8,128)S(1)}, f32[8,2,32,8,128]{4,3,2,1,0:T(8,128)S(1)}, f32[40,8,128]{2,1,0:T(8,128)S(1)}) custom-call(f32[8,4,40,8,128]{4,3,2,1,0:T(8,128)S(1)} %get-tuple-element.26.fields.low_fields.high_fields, f32[40,8,128]{2,1,0:T(8,128)S(1)} %get-tuple-element.27.columns), custom_call_target="tpu_custom_call" | custom-call | flops 60000000 | bytes 10000000 | tf_op jit(solution)/shard_map/inner_rows/pallas_call | solution.py:795
  32.9 2.8 %inner_slots.1.inner = f32[2,62,2,1800]{3,2,1,0:T(2,128)} custom-call(s32[2]{0:T(128)S(1)} %copy-done.5, f32[8,2,32,8,128]{4,3,2,1,0:T(8,128)S(1)} %get-tuple-element.31.moved), custom_call_target="tpu_custom_call" | custom-call | flops 20000000 | bytes 6000000 | tf_op jit(solution)/shard_map/inner_slots/pallas_call | solution.py:808
  35.7 4.2 %outer_rows.1 = (f32[8,2,8,8,128]{4,3,2,1,0:T(8,128)S(1)}, f32[3,40,128]{2,1,0:T(8,128)S(1)}, f32[8,128]{1,0:T(8,128)S(1)}) custom-call(s32[1]{0:T(128)} %bitcast.parity, f32[8,4,40,8,128]{4,3,2,1,0:T(8,128)S(1)} %get-tuple-element.26.fields.low_fields.high_fields, f32[8,4,40,8,128]{4,3,2,1,0:T(8,128)S(1)} %get-tuple-element.26.fields.low_fields.high_fields, ...), custom_call_target="tpu_custom_call" | custom-call | tf_op jit(solution)/shard_map/outer_rows/pallas_call | solution.py:828
  39.9 2.9 %collective-permute-start.4 = (f32[8,128]{1,0:T(8,128)S(1)}, f32[8,128]{1,0:T(8,128)S(1)}, u32[]{:S(2)}, u32[]{:S(2)}) collective-permute-start(f32[8,128]{1,0:T(8,128)S(1)} %get-tuple-element.34), channel_id=1, source_target_pairs={{0,1},{1,0},{2,3},{3,2},{4,5},{5,4},{6,7},{7,6},{8,9},{9,8},{10,11... | collective-permute-start | bytes 12296 | tf_op jit(solution)/shard_map/ppermute | solution.py:690
  43.6 2.7 %collective-permute-start.6 = (f32[8,128]{1,0:T(8,128)S(1)}, f32[8,128]{1,0:T(8,128)S(1)}, u32[]{:S(2)}, u32[]{:S(2)}) collective-permute-start(f32[8,128]{1,0:T(8,128)S(1)} %add.21), channel_id=1, source_target_pairs={{0,4},{1,5},{2,6},{3,7},{4,0},{5,1},{6,2},{7,3},{8,12},{9,13},{10,... | collective-permute-start | bytes 12296 | tf_op jit(solution)/shard_map/ppermute | solution.py:678
  46.3 1.4 %collective-permute-start.7 = (f32[8,128]{1,0:T(8,128)S(1)}, f32[8,128]{1,0:T(8,128)S(1)}, u32[]{:S(2)}, u32[]{:S(2)}) collective-permute-start(f32[8,128]{1,0:T(8,128)S(1)} %add.21), channel_id=1, source_target_pairs={{0,6},{1,7},{2,4},{3,5},{4,2},{5,3},{6,0},{7,1},{8,14},{9,15},{10,... | collective-permute-start | bytes 12296 | tf_op jit(solution)/shard_map/ppermute | solution.py:678
  47.8 1.5 %outer_slots.2.inner = f32[2,62,2,1800]{3,2,1,0:T(2,128)} custom-call(s32[2]{0:T(128)S(1)} %copy-done.5, f32[8,2,32,8,128]{4,3,2,1,0:T(8,128)S(1)} %get-tuple-element.31.moved, f32[8,2,8,8,128]{4,3,2,1,0:T(8,128)S(1)} %get-tuple-element.35.edges, f32[2,62,2,1800]{3,2,1,0:T(2,128)} %inner_slots.1.inner), custom_call_target="tpu_custom_call", output_to_operand_aliasing={{}: (3, {})} | custom-call | flops 2000000 | bytes 2000000 | tf_op jit(solution)/shard_map/outer_slots/pallas_call | solution.py:851
  49.3 1.8 %collective-permute-done.7 = f32[8,128]{1,0:T(8,128)S(1)} collective-permute-done((f32[8,128]{1,0:T(8,128)S(1)}, f32[8,128]{1,0:T(8,128)S(1)}, u32[]{:S(2)}, u32[]{:S(2)}) %collective-permute-start.7) | collective-permute-done | bytes 4128 | tf_op jit(solution)/shard_map/ppermute | solution.py:678
  51.8 1.1 %collective-permute-start.10 = (f32[8,128]{1,0:T(8,128)S(1)}, f32[8,128]{1,0:T(8,128)S(1)}, u32[]{:S(2)}, u32[]{:S(2)}) collective-permute-start(f32[8,128]{1,0:T(8,128)S(1)} %add_add_fusion.1), channel_id=1, source_target_pairs={{0,24},{8,16},{16,8},{24,0},{32,56},{40,48},{48,40},{56,32},{64,88... | collective-permute-start | bytes 12296 | tf_op jit(solution)/shard_map/ppermute | solution.py:678
  52.9 1.9 %collective-permute-start.8 = (f32[8,128]{1,0:T(8,128)S(1)}, f32[8,128]{1,0:T(8,128)S(1)}, u32[]{:S(2)}, u32[]{:S(2)}) collective-permute-start(f32[8,128]{1,0:T(8,128)S(1)} %add_add_fusion.1), channel_id=1, source_target_pairs={{0,8},{8,0},{16,24},{24,16},{32,40},{40,32},{48,56},{56,48},{64,72... | collective-permute-start | bytes 12296 | tf_op jit(solution)/shard_map/ppermute | solution.py:678
  54.9 1.6 %outer_slots.3 = f32[2,62,2,1800]{3,2,1,0:T(2,128)} custom-call(s32[2]{0:T(128)S(1)} %copy-done.5, f32[8,2,32,8,128]{4,3,2,1,0:T(8,128)S(1)} %get-tuple-element.31.moved, f32[8,2,8,8,128]{4,3,2,1,0:T(8,128)S(1)} %get-tuple-element.35.edges, f32[2,62,2,1800]{3,2,1,0:T(2,128)} %outer_slots.2.inner), custom_call_target="tpu_custom_call", output_to_operand_aliasing={{}: (3, {})} | custom-call | flops 2000000 | bytes 2000000 | tf_op jit(solution)/shard_map/outer_slots/pallas_call | solution.py:851
  56.7 1.7 %collective-permute-start.11 = (f32[8,128]{1,0:T(8,128)S(1)}, f32[8,128]{1,0:T(8,128)S(1)}, u32[]{:S(2)}, u32[]{:S(2)}) collective-permute-start(f32[8,128]{1,0:T(8,128)S(1)} %add_add_fusion.first), channel_id=1, source_target_pairs={{0,32},{8,40},{16,48},{24,56},{32,0},{40,8},{48,16},{56,24},{64,96... | collective-permute-start | bytes 12296 | tf_op jit(solution)/shard_map/ppermute | solution.py:678
  58.3 3.9 %collective-permute-start.12 = (f32[8,128]{1,0:T(8,128)S(1)}, f32[8,128]{1,0:T(8,128)S(1)}, u32[]{:S(2)}, u32[]{:S(2)}) collective-permute-start(f32[8,128]{1,0:T(8,128)S(1)} %add_add_fusion.first), channel_id=1, source_target_pairs={{0,64},{8,72},{16,80},{24,88},{32,96},{40,104},{48,112},{56,120},{... | collective-permute-start | bytes 12296 | tf_op jit(solution)/shard_map/ppermute | solution.py:678
  62.2 1.6 %collective-permute-done.12.third = f32[8,128]{1,0:T(8,128)S(1)} collective-permute-done((f32[8,128]{1,0:T(8,128)S(1)}, f32[8,128]{1,0:T(8,128)S(1)}, u32[]{:S(2)}, u32[]{:S(2)}) %collective-permute-start.12) | collective-permute-done | bytes 4128 | tf_op jit(solution)/shard_map/ppermute | solution.py:678
  63.8 3.2 %collective-permute-done.13.fourth = f32[8,128]{1,0:T(8,128)S(1)} collective-permute-done((f32[8,128]{1,0:T(8,128)S(1)}, f32[8,128]{1,0:T(8,128)S(1)}, u32[]{:S(2)}, u32[]{:S(2)}) %collective-permute-start.13) | collective-permute-done | bytes 4128 | tf_op jit(solution)/shard_map/ppermute | solution.py:678
  (33 shorter events, 4.3 us)
Async XLA Ops:
  0.6 2.1 %copy-start.6 = (f32[2,2,62,1800]{3,1,2,0:T(2,128)S(1)}, f32[2,2,62,1800]{3,1,2,0:T(2,128)}, u32[]{:S(2)}) copy-start(f32[2,2,62,1800]{3,1,2,0:T(2,128)} %param.10) | copy-start | bytes 5356804
  2.7 0.7 %copy-start.2 = (f32[40,90]{1,0:T(8,128)S(1)}, f32[40,90]{1,0:T(8,128)}, u32[]{:S(2)}) copy-start(f32[40,90]{1,0:T(8,128)} %damping_far.1) | copy-start | bytes 43204
  2.7 0.7 %copy-start.3 = (s32[2,1800]{1,0:T(2,128)S(1)}, s32[2,1800]{1,0:T(2,128)}, u32[]{:S(2)}) copy-start(s32[2,1800]{1,0:T(2,128)} %wet_levels_far.1) | copy-start | bytes 43204
  2.7 0.7 %copy-start.4 = (f32[2,1800]{1,0:T(2,128)S(1)}, f32[2,1800]{1,0:T(2,128)}, u32[]{:S(2)}) copy-start(f32[2,1800]{1,0:T(2,128)} %mixing_far.1) | copy-start | bytes 43204
  2.7 0.7 %copy-start.5 = (s32[2]{0:T(128)S(1)}, s32[2]{0:T(128)}, u32[]{:S(2)}) copy-start(s32[2]{0:T(128)} %block_list.9) | copy-start | bytes 28
  3.5 2.6 %copy-start = (f32[2,2,62,1800]{3,2,1,0:T(8,128)}, f32[2,2,62,1800]{3,2,1,0:T(8,128)S(1)}, u32[]{:S(2)}) copy-start(f32[2,2,62,1800]{3,2,1,0:T(8,128)S(1)} %copy.11.tracers) | copy-start | bytes 5356804
  6.1 15.1 %collective-permute-start = (f32[8,11,8,128]{3,2,1,0:T(8,128)S(1)}, f32[8,11,8,128]{3,2,1,0:T(8,128)S(1)}, u32[]{:S(2)}, u32[]{:S(2)}) collective-permute-start(f32[8,11,8,128]{3,2,1,0:T(8,128)S(1)} %get-tuple-element.24), channel_id=1, source_target_pairs={{0,8},{8,16},{16,24},{24,32},{32,40},{40,48},{48,56},{56,64},{64,7... | collective-permute-start | bytes 1081352 | tf_op jit(solution)/shard_map/ppermute | solution.py:748
  8.2 13.0 %collective-permute-start.1 = (f32[8,11,8,128]{3,2,1,0:T(8,128)S(1)}, f32[8,11,8,128]{3,2,1,0:T(8,128)S(1)}, u32[]{:S(2)}, u32[]{:S(2)}) collective-permute-start(f32[8,11,8,128]{3,2,1,0:T(8,128)S(1)} %get-tuple-element.25), channel_id=1, source_target_pairs={{8,0},{16,8},{24,16},{32,24},{40,32},{48,40},{56,48},{64,56},{72,6... | collective-permute-start | bytes 1081352 | tf_op jit(solution)/shard_map/ppermute | solution.py:749
  12.8 1.5 %copy-start.1 = (f32[2,2,62,1800]{3,2,1,0:T(8,128)S(1)}, f32[2,2,62,1800]{3,2,1,0:T(8,128)}, u32[]{:S(2)}) copy-start(f32[2,2,62,1800]{3,2,1,0:T(8,128)} %copy-done) | copy-start | bytes 5356804
  22.6 13.0 %collective-permute-start.2 = (f32[8,27,8,128]{3,2,1,0:T(8,128)S(1)}, f32[8,27,8,128]{3,2,1,0:T(8,128)S(1)}, u32[]{:S(2)}, u32[]{:S(2)}) collective-permute-start(f32[8,27,8,128]{3,2,1,0:T(8,128)S(1)} %get-tuple-element.28), channel_id=1, source_target_pairs={{0,1},{1,0},{2,3},{3,2},{4,5},{5,4},{6,7},{7,6},{8,9},{9,8},{10,11... | collective-permute-start | bytes 2654216 | tf_op jit(solution)/shard_map/ppermute | solution.py:787
  22.7 13.0 %collective-permute-start.3 = (f32[8,27,8,128]{3,2,1,0:T(8,128)S(1)}, f32[8,27,8,128]{3,2,1,0:T(8,128)S(1)}, u32[]{:S(2)}, u32[]{:S(2)}) collective-permute-start(f32[8,27,8,128]{3,2,1,0:T(8,128)S(1)} %get-tuple-element.29), channel_id=1, source_target_pairs={{1,2},{2,1},{3,4},{4,3},{5,6},{6,5},{9,10},{10,9},{11,12},{12,11},... | collective-permute-start | bytes 2654216 | tf_op jit(solution)/shard_map/ppermute | solution.py:789
  39.9 3.7 %collective-permute-start.4 = (f32[8,128]{1,0:T(8,128)S(1)}, f32[8,128]{1,0:T(8,128)S(1)}, u32[]{:S(2)}, u32[]{:S(2)}) collective-permute-start(f32[8,128]{1,0:T(8,128)S(1)} %get-tuple-element.34), channel_id=1, source_target_pairs={{0,1},{1,0},{2,3},{3,2},{4,5},{5,4},{6,7},{7,6},{8,9},{9,8},{10,11... | collective-permute-start | bytes 12296 | tf_op jit(solution)/shard_map/ppermute | solution.py:690
  43.6 5.7 %collective-permute-start.6 = (f32[8,128]{1,0:T(8,128)S(1)}, f32[8,128]{1,0:T(8,128)S(1)}, u32[]{:S(2)}, u32[]{:S(2)}) collective-permute-start(f32[8,128]{1,0:T(8,128)S(1)} %add.21), channel_id=1, source_target_pairs={{0,4},{1,5},{2,6},{3,7},{4,0},{5,1},{6,2},{7,3},{8,12},{9,13},{10,... | collective-permute-start | bytes 12296 | tf_op jit(solution)/shard_map/ppermute | solution.py:678
  46.3 4.8 %collective-permute-start.7 = (f32[8,128]{1,0:T(8,128)S(1)}, f32[8,128]{1,0:T(8,128)S(1)}, u32[]{:S(2)}, u32[]{:S(2)}) collective-permute-start(f32[8,128]{1,0:T(8,128)S(1)} %add.21), channel_id=1, source_target_pairs={{0,6},{1,7},{2,4},{3,5},{4,2},{5,3},{6,0},{7,1},{8,14},{9,15},{10,... | collective-permute-start | bytes 12296 | tf_op jit(solution)/shard_map/ppermute | solution.py:678
  47.7 3.6 %collective-permute-start.5 = (f32[8,128]{1,0:T(8,128)S(1)}, f32[8,128]{1,0:T(8,128)S(1)}, u32[]{:S(2)}, u32[]{:S(2)}) collective-permute-start(f32[8,128]{1,0:T(8,128)S(1)} %add.21), channel_id=1, source_target_pairs={{0,2},{1,3},{2,0},{3,1},{4,6},{5,7},{6,4},{7,5},{8,10},{9,11},{10,... | collective-permute-start | bytes 12296 | tf_op jit(solution)/shard_map/ppermute | solution.py:678
  51.4 5.1 %collective-permute-start.9 = (f32[8,128]{1,0:T(8,128)S(1)}, f32[8,128]{1,0:T(8,128)S(1)}, u32[]{:S(2)}, u32[]{:S(2)}) collective-permute-start(f32[8,128]{1,0:T(8,128)S(1)} %add_add_fusion.1), channel_id=1, source_target_pairs={{0,16},{8,24},{16,0},{24,8},{32,48},{40,56},{48,32},{56,40},{64,80... | collective-permute-start | bytes 12296 | tf_op jit(solution)/shard_map/ppermute | solution.py:678
  51.8 4.8 %collective-permute-start.10 = (f32[8,128]{1,0:T(8,128)S(1)}, f32[8,128]{1,0:T(8,128)S(1)}, u32[]{:S(2)}, u32[]{:S(2)}) collective-permute-start(f32[8,128]{1,0:T(8,128)S(1)} %add_add_fusion.1), channel_id=1, source_target_pairs={{0,24},{8,16},{16,8},{24,0},{32,56},{40,48},{48,40},{56,32},{64,88... | collective-permute-start | bytes 12296 | tf_op jit(solution)/shard_map/ppermute | solution.py:678
  52.9 3.7 %collective-permute-start.8 = (f32[8,128]{1,0:T(8,128)S(1)}, f32[8,128]{1,0:T(8,128)S(1)}, u32[]{:S(2)}, u32[]{:S(2)}) collective-permute-start(f32[8,128]{1,0:T(8,128)S(1)} %add_add_fusion.1), channel_id=1, source_target_pairs={{0,8},{8,0},{16,24},{24,16},{32,40},{40,32},{48,56},{56,48},{64,72... | collective-permute-start | bytes 12296 | tf_op jit(solution)/shard_map/ppermute | solution.py:678
  56.7 5.6 %collective-permute-start.11 = (f32[8,128]{1,0:T(8,128)S(1)}, f32[8,128]{1,0:T(8,128)S(1)}, u32[]{:S(2)}, u32[]{:S(2)}) collective-permute-start(f32[8,128]{1,0:T(8,128)S(1)} %add_add_fusion.first), channel_id=1, source_target_pairs={{0,32},{8,40},{16,48},{24,56},{32,0},{40,8},{48,16},{56,24},{64,96... | collective-permute-start | bytes 12296 | tf_op jit(solution)/shard_map/ppermute | solution.py:678
  58.3 5.5 %collective-permute-start.12 = (f32[8,128]{1,0:T(8,128)S(1)}, f32[8,128]{1,0:T(8,128)S(1)}, u32[]{:S(2)}, u32[]{:S(2)}) collective-permute-start(f32[8,128]{1,0:T(8,128)S(1)} %add_add_fusion.first), channel_id=1, source_target_pairs={{0,64},{8,72},{16,80},{24,88},{32,96},{40,104},{48,112},{56,120},{... | collective-permute-start | bytes 12296 | tf_op jit(solution)/shard_map/ppermute | solution.py:678
  62.2 4.8 %collective-permute-start.13 = (f32[8,128]{1,0:T(8,128)S(1)}, f32[8,128]{1,0:T(8,128)S(1)}, u32[]{:S(2)}, u32[]{:S(2)}) collective-permute-start(f32[8,128]{1,0:T(8,128)S(1)} %add_add_fusion.first), channel_id=1, source_target_pairs={{0,96},{8,104},{16,112},{24,120},{32,64},{40,72},{48,80},{56,88},{... | collective-permute-start | bytes 12296 | tf_op jit(solution)/shard_map/ppermute | solution.py:678
